TPU v7x, 256 devices: a whole 4x4x8 slice. The times are simulated.
256 devices in a mesh: expert: 64 (over y, z, core), grid: 4 (over x).
Axes of the slice: x: 4, y: 4, z: 8, core: 2. Of those that a mesh axis runs over, the one named last changes fastest.
Arguments:
- tokens: bfloat16 [32768, 1024], P(('expert', 'grid')), may hold values from -6 to 6
- routes: int32 [32768, 2], P(('expert', 'grid')), may hold values from 0 to 63, all different within a row; in each aligned block of 128 rows (0 to 127, 128 to 255, ...) at most 8 rows name the same one
- route_gates: float32 [32768, 2], P(('expert', 'grid')), may hold values from 0.2 to 1
- caption_lengths: int32 [256, 4], P(('expert', 'grid')), may hold values from 1 to 64, 128 in all within a row
- image_embed: bfloat16 [1024, 1024], P(('expert', 'grid')), may hold values from -6 to 6
- final_gain: float32 [1024], replicated, may hold values from 0.1 to 1.9
- up_weight: bfloat16 [64, 1024, 4096], P('expert', None, 'grid'), may hold values from -0.1875 to 0.1875
- down_weight: bfloat16 [64, 1024, 4096], P('expert', None, 'grid'), may hold values from -0.09375 to 0.09375
Outputs:
- text_embed: float32 [1024, 1024], P(('expert', 'grid'))
- sentence_direction_slope: float32 [1024, 1024], P(('expert', 'grid'))
- picture_direction_slope: float32 [1024, 1024], P(('expert', 'grid'))
Inputs may be any that keep to these rules, and one draw needn't show every extreme that they name: `routes`: each token names two different experts; among the 128 tokens of one device no expert is named more than 8 times, and in every draw some device names some expert exactly 8 times. `caption_lengths`: each row gives the token counts of one device's 4 captions, summing to 128; the largest of a row is exactly 64.
All inputs are finite; a program needn't handle non-finite values.
Results may differ from a plain program's by a relative error of at most 0.003.
Values may be sent and summed in bfloat16 or wider, within the bound.
No kernel may reach another device: no remote copies, remote signals or barrier semaphores. Data moves between devices by JAX's collectives and lax.ppermute only.
A program may use at most 64 MiB of HBM per device.

v0:
```python
import math

import jax
import jax.numpy as jnp
from jax import lax
from jax.experimental import pallas as pl
from jax.experimental.pallas import tpu as pltpu
from jax.sharding import PartitionSpec as P

EPSILON = 1e-06
SIMILARITY_HEAT = 10.0
BF16 = jnp.bfloat16
F32 = jnp.float32


def layer_norm(values):
    centred = values - jnp.mean(values, axis=-1, keepdims=True)
    return centred * lax.rsqrt(jnp.mean(centred * centred, axis=-1, keepdims=True) + EPSILON)


def expert_kernel(rows_ref, up_ref, down_ref, out_ref, total_ref):
    step = pl.program_id(0)
    hidden = jnp.dot(rows_ref[...], up_ref[...], preferred_element_type=F32)
    hidden = (0.5 * hidden * (1.0 + lax.erf(hidden * math.sqrt(0.5)))).astype(BF16)
    term = lax.dot_general(
        hidden, down_ref[...], (((1,), (1,)), ((), ())), preferred_element_type=F32
    )

    @pl.when(step == 0)
    def _():
        total_ref[...] = term

    @pl.when(step > 0)
    def _():
        total_ref[...] += term

    @pl.when(step == pl.num_programs(0) - 1)
    def _():
        out_ref[...] = total_ref[...].astype(BF16)


def expert_part(rows, up_piece, down_piece):
    count, width = rows.shape
    units = up_piece.shape[1]
    tile = min(256, units)
    return pl.pallas_call(
        expert_kernel,
        grid=(units // tile,),
        in_specs=[
            pl.BlockSpec((count, width), lambda i: (0, 0)),
            pl.BlockSpec((width, tile), lambda i: (0, i)),
            pl.BlockSpec((width, tile), lambda i: (0, i)),
        ],
        out_specs=pl.BlockSpec((count, width), lambda i: (0, 0)),
        out_shape=jax.ShapeDtypeStruct((count, width), BF16),
        scratch_shapes=[pltpu.VMEM((count, width), F32)],
        compiler_params=pltpu.CompilerParams(vmem_limit_bytes=56 * 2**20),
        cost_estimate=pl.CostEstimate(
            flops=16 * count * width * units,
            bytes_accessed=4 * width * units + 4 * count * width,
            transcendentals=count * units,
        ),
    )(rows, up_piece, down_piece)


def split_pair(values):
    high = values.astype(BF16)
    return high, (values - high.astype(F32)).astype(BF16)


def pair_slope(logits, same):
    signs = jnp.where(same, 1.0, -1.0).astype(F32)
    return -signs * jax.nn.sigmoid(-signs * logits)


def weighted_sum(coeff, rows):
    high, low = split_pair(coeff)
    both = jnp.dot(jnp.concatenate([high, low], axis=0), rows, preferred_element_type=F32)
    count = coeff.shape[0]
    return SIMILARITY_HEAT * (both[:count] + both[count:])


def held(*values):
    return lax.optimization_barrier(values)


def moved(values, target, mesh_shape):
    wide, deep, cores = mesh_shape
    pairs = []
    for index in range(wide * deep * cores):
        y, z, core = index // (deep * cores), index // cores % deep, index % cores
        y, z, core = target(y, z, core)
        pairs.append((index, (y % wide * deep + z % deep) * cores + core % cores))
    return lax.ppermute(values, "expert", pairs)


def along_y(mine, shape):
    others = [moved(mine, lambda y, z, c, k=k: (y + k, z, c), shape) for k in range(1, shape[0])]
    return jnp.concatenate([mine] + others, axis=0)


def along_expert(mine, shape):
    wide, deep, cores = shape
    chips = wide * deep
    groups = [[chip * cores + core for chip in range(chips)] for core in range(cores)]
    copies = jnp.broadcast_to(mine[None], (chips,) + mine.shape)
    column = lax.all_to_all(
        copies, "expert", split_axis=0, concat_axis=0, axis_index_groups=groups, tiled=True
    ).reshape(chips * mine.shape[0], mine.shape[1])
    return on_chip(column, shape)


def on_chip(group, shape):
    return jnp.concatenate([group, moved(group, lambda y, z, c: (y, z, c + 1), shape)], axis=0)


def along_z(group, both, shape):
    deep = shape[1]
    here = [
        moved(both, lambda y, z, c, k=k: (y, z + (k if c == 0 else -k), c), shape)
        for k in range(1, deep // 2)
    ]
    here.append(moved(group, lambda y, z, c: (y, z + deep // 2, c), shape))
    return jnp.concatenate(here, axis=0)


def last_swap(both, here, shape):
    other = moved(here, lambda y, z, c: (y, z, c + 1), shape)
    return jnp.concatenate([both, here, other], axis=0)


def ring_shift(values, step, size):
    return lax.ppermute(values, "grid", [(i, (i + step) % size) for i in range(size)])


def unit_rows(values):
    return values * lax.rsqrt(jnp.mean(values * values, axis=-1, keepdims=True) + EPSILON)


def on_device(
    tokens, routes, route_gates, caption_lengths, image_embed, final_gain, up_weight, down_weight
):
    token_count, width = tokens.shape
    experts_all = lax.axis_size("expert")
    grid_all = lax.axis_size("grid")
    slots = 4 * token_count // experts_all
    places_all = experts_all * slots
    scale_root = math.sqrt(width)

    picture_unit = (unit_rows(image_embed.astype(F32)) / scale_root).astype(BF16)
    captions_here = picture_unit.shape[0]
    shape = (grid_all, experts_all // (2 * grid_all), 2)
    row_parts = [picture_unit] + [ring_shift(picture_unit, k, grid_all) for k in range(1, grid_all)]

    stream = tokens.astype(F32)
    normed = layer_norm(stream).astype(BF16)
    first, second = routes[:, 0:1], routes[:, 1:2]
    names = jnp.arange(experts_all, dtype=jnp.int32)[None, :]
    hot_first = first == names
    hot_second = second == names
    both_hot = jnp.concatenate([hot_first, hot_second], axis=1).astype(BF16)
    order = jnp.arange(token_count, dtype=jnp.int32)
    before = (order[None, :] < order[:, None]).astype(BF16)
    ranks = jnp.dot(before, both_hot, preferred_element_type=F32)
    totals = jnp.sum(hot_first.astype(F32), axis=0, keepdims=True)
    rank_first = jnp.sum(jnp.where(hot_first, ranks[:, :experts_all], 0.0), axis=1, keepdims=True)
    rank_second = jnp.sum(
        jnp.where(hot_second, ranks[:, experts_all:] + totals, 0.0), axis=1, keepdims=True
    )
    place_first = first * slots + rank_first.astype(jnp.int32)
    place_second = second * slots + rank_second.astype(jnp.int32)
    spots = jnp.arange(places_all, dtype=jnp.int32)[None, :]
    at_first = spots == place_first
    at_second = spots == place_second
    chosen = (at_first | at_second).astype(BF16)
    send = lax.dot_general(chosen, normed, (((0,), (0,)), ((), ())), preferred_element_type=F32)
    send = send.astype(BF16).reshape(experts_all, slots, width)
    arrived = lax.all_to_all(send, "expert", split_axis=0, concat_axis=0, tiled=True)
    arrived, picture_later, *row_parts = held(arrived, picture_unit, *row_parts)
    pictures_row = jnp.concatenate(row_parts, axis=0)
    rows = arrived.reshape(places_all, width)

    up_local = up_weight[0]
    down_local = down_weight[0]
    from_left = ring_shift(rows, 1, grid_all)
    from_right = ring_shift(rows, -1, grid_all)
    from_far = ring_shift(rows, 2, grid_all)
    own_term = expert_part(rows, up_local, down_local)
    own_term, picture_later = held(own_term, picture_later)
    picture_column = along_expert(picture_later, shape)
    from_left, from_right, own_term = held(from_left, from_right, own_term)
    from_far, picture_column = held(from_far, picture_column)
    back_left = ring_shift(expert_part(from_left, up_local, down_local), -1, grid_all)
    back_right = ring_shift(expert_part(from_right, up_local, down_local), 1, grid_all)
    back_far = ring_shift(expert_part(from_far, up_local, down_local), 2, grid_all)
    total = sum(term.astype(F32) for term in (own_term, back_left, back_right, back_far))
    results = total.astype(BF16).reshape(experts_all, slots, width)
    returned = lax.all_to_all(results, "expert", split_axis=0, concat_axis=0, tiled=True)
    returned = returned.reshape(places_all, width)

    gates = jnp.where(at_first, route_gates[:, 0:1], 0.0) + jnp.where(
        at_second, route_gates[:, 1:2], 0.0
    )
    gate_high, gate_low = split_pair(gates)
    mixed = (
        stream
        + jnp.dot(gate_high, returned, preferred_element_type=F32)
        + jnp.dot(gate_low, returned, preferred_element_type=F32)
    )
    final = layer_norm(mixed) * final_gain
    lengths = caption_lengths[0]
    ends = jnp.cumsum(lengths)
    starts = ends - lengths
    members = ((order[None, :] >= starts[:, None]) & (order[None, :] < ends[:, None])).astype(F32)
    pooled = jnp.dot(members, final, precision=lax.Precision.HIGHEST) / lengths[:, None].astype(F32)
    text_embed = unit_rows(pooled)
    text_unit = (text_embed / scale_root).astype(BF16)

    text_group = along_y(text_unit, shape)
    text_both = on_chip(text_group, shape)
    text_mine, text_both = held(text_unit, text_both)
    text_here = along_z(text_group, text_both, shape)
    text_parts = [text_mine] + [ring_shift(text_mine, k, grid_all) for k in range(1, grid_all)]
    text_column = last_swap(text_both, text_here, shape)
    text_row = jnp.concatenate(text_parts, axis=0)

    def slopes(mine, others, place):
        logits = SIMILARITY_HEAT * lax.dot_general(
            mine, others, (((1,), (1,)), ((), ())), preferred_element_type=F32
        )
        row_ids = lax.broadcasted_iota(jnp.int32, logits.shape, 0)
        column_ids = lax.broadcasted_iota(jnp.int32, logits.shape, 1)
        same = (row_ids < captions_here) & (row_ids + place == column_ids)
        return weighted_sum(pair_slope(logits, same), others)

    chip = lax.axis_index("expert") // shape[2]
    partial = jnp.concatenate(
        [
            slopes(text_row, picture_column, chip * captions_here).reshape(grid_all, captions_here, width),
            slopes(pictures_row, text_column, 0).reshape(grid_all, captions_here, width),
        ],
        axis=1,
    )
    slope = partial[0]
    for k in range(1, grid_all):
        slope = slope + ring_shift(partial[k], -k, grid_all)
    return (text_embed, slope[:captions_here], slope[captions_here:])


def solution(mesh):
    split = P(("expert", "grid"), None)
    weights = P("expert", None, "grid")
    return jax.shard_map(
        on_device,
        mesh=mesh,
        in_specs=(split, split, split, split, split, P(), weights, weights),
        out_specs=(split, split, split),
        check_vma=False,
    )
```

profile of v0, /device:TPU:32, one launch (start us, length us, event | category | flops | bytes accessed | tf_op | source)
XLA Modules:
  0.0 222.7 jit_solution(8399649712191184949)
XLA Ops:
  0.6 0.8 slice_bitcast_fusion.3
  1.5 1.1 convert_reduce_fusion
  2.6 1.2 fusion.18
  3.8 0.1 fusion.43
  4.0 0.8 fusion.92
  4.8 2.5 %fusion = bf16[64,8,1024]{2,1,0:T(8,128)(2,1)} fusion(bf16[128,1024]{1,0:T(8,128)(2,1)} %param.8, f32[128]{0:T(128)S(1)} %add_rsqrt_fusion.3, f32[128]{0:T(128)S(1)} %broadcast_multiply_fusion.2, s32[128]{0:T(128)S(1)} %get-tuple-element.49, s32[128]{0:T(128)S(1)} %get-tuple-element.48), kind=kOutput, calls=%fused_computation.2 | convolution fusion | flops 135462912 | bytes 1312768 | tf_op jit(solution)/shard_map/dot_general | solution.py:176
  7.3 11.8 %all-to-all-start = ((bf16[64,8,1024]{2,1,0:T(8,128)(2,1)}), bf16[64,8,1024]{2,1,0:T(8,128)(2,1)S(1)}, u32[]{:S(2)}, u32[]{:S(2)}) async-start(bf16[64,8,1024]{2,1,0:T(8,128)(2,1)} %fusion), calls=%async_computation | async-start | bytes 2097152 | tf_op jit(solution)/shard_map/all_to_all | solution.py:178
  19.3 1.5 collective-permute-start
  20.8 2.7 %collective-permute-start.1 = (bf16[4,1024]{1,0:T(4,128)(2,1)S(1)}, bf16[4,1024]{1,0:T(4,128)(2,1)S(1)}, u32[]{:S(2)}, u32[]{:S(2)}) collective-permute-start(bf16[4,1024]{1,0:T(4,128)(2,1)S(1)} %fusion.76), channel_id=1, source_target_pairs={{0,2},{1,3},{2,0},{3,1},{4,6},{5,7},{6,4},{7,5},{8,10},{9,11},{10,... | collective-permute-start | bytes 24584 | tf_op jit(solution)/shard_map/ppermute | solution.py:133
  23.6 1.4 collective-permute-start.2
  25.0 1.0 collective-permute-done.1
  26.0 1.2 collective-permute-done.2
  27.2 19.7 %all-to-all-done = bf16[64,8,1024]{2,1,0:T(8,128)(2,1)S(1)} async-done(((bf16[64,8,1024]{2,1,0:T(8,128)(2,1)}), bf16[64,8,1024]{2,1,0:T(8,128)(2,1)S(1)}, u32[]{:S(2)}, u32[]{:S(2)}) %all-to-all-start) | async-done | bytes 1048608 | tf_op jit(solution)/shard_map/all_to_all | solution.py:178
  47.0 1.5 collective-permute-start.3
  48.5 1.7 collective-permute-start.4
  50.2 8.4 %shard_map.103 = bf16[512,1024]{1,0:T(8,128)(2,1)} custom-call(bf16[512,1024]{1,0:T(8,128)(2,1)} %bitcast.60, bf16[1024,1024]{1,0:T(8,128)(2,1)} %bitcast.62, bf16[1024,1024]{1,0:T(8,128)(2,1)} %bitcast.66), custom_call_target="tpu_custom_call" | custom-call | flops 8589934592 | bytes 6291456 | tf_op jit(solution)/shard_map/pallas_call | solution.py:46
  58.7 18.1 %all_to_all.15 = bf16[32,4,1024]{2,1,0:T(4,128)(2,1)S(1)} all-to-all(bf16[32,4,1024]{2,1,0:T(4,128)(2,1)S(1)} %broadcast_in_dim.67), channel_id=1, replica_groups={{0,8,16,24,32,40,48,56,64,72,80,88,96,104,112,120,128,136,144,152,160,1..., dimensions={0} | all-to-all | bytes 524288 | tf_op jit(solution)/shard_map/all_to_all | solution.py:107
  76.9 1.9 collective-permute-start.7
  78.9 8.7 %shard_map.104 = bf16[512,1024]{1,0:T(8,128)(2,1)} custom-call(bf16[512,1024]{1,0:T(8,128)(2,1)} %collective-permute-done.3.rows_ref, bf16[1024,1024]{1,0:T(8,128)(2,1)} %bitcast.63, bf16[1024,1024]{1,0:T(8,128)(2,1)} %bitcast.67), custom_call_target="tpu_custom_call" | custom-call | flops 8589934592 | bytes 6291456 | tf_op jit(solution)/shard_map/pallas_call | solution.py:46
  87.6 1.2 collective-permute-start.5
  88.8 8.4 %shard_map.105 = bf16[512,1024]{1,0:T(8,128)(2,1)} custom-call(bf16[512,1024]{1,0:T(8,128)(2,1)} %copy-done.5, bf16[1024,1024]{1,0:T(8,128)(2,1)} %bitcast.64, bf16[1024,1024]{1,0:T(8,128)(2,1)} %bitcast.68), custom_call_target="tpu_custom_call" | custom-call | flops 8589934592 | bytes 6291456 | tf_op jit(solution)/shard_map/pallas_call | solution.py:46
  97.1 0.9 collective-permute-start.6
  98.0 6.8 %collective-permute-done.7.rows_ref = bf16[512,1024]{1,0:T(8,128)(2,1)S(1)} collective-permute-done((bf16[512,1024]{1,0:T(8,128)(2,1)}, bf16[512,1024]{1,0:T(8,128)(2,1)S(1)}, u32[]{:S(2)}, u32[]{:S(2)}) %collective-permute-start.7) | collective-permute-done | bytes 1048608 | tf_op jit(solution)/shard_map/ppermute | solution.py:133
  104.8 1.0 copy-done.6
  105.8 8.3 %shard_map.106 = bf16[512,1024]{1,0:T(8,128)(2,1)} custom-call(bf16[512,1024]{1,0:T(8,128)(2,1)} %copy-done.6, bf16[1024,1024]{1,0:T(8,128)(2,1)} %bitcast.65, bf16[1024,1024]{1,0:T(8,128)(2,1)} %bitcast.69), custom_call_target="tpu_custom_call" | custom-call | flops 8589934592 | bytes 6291456 | tf_op jit(solution)/shard_map/pallas_call | solution.py:46
  114.1 1.8 collective-permute-start.9
  115.9 10.2 %collective-permute-done.5 = bf16[512,1024]{1,0:T(8,128)(2,1)S(1)} collective-permute-done((bf16[512,1024]{1,0:T(8,128)(2,1)}, bf16[512,1024]{1,0:T(8,128)(2,1)S(1)}, u32[]{:S(2)}, u32[]{:S(2)}) %collective-permute-start.5) | collective-permute-done | bytes 1048608 | tf_op jit(solution)/shard_map/ppermute | solution.py:133
  126.1 1.0 collective-permute-done.6
  127.2 22.0 %collective-permute-done.9 = bf16[512,1024]{1,0:T(8,128)(2,1)S(1)} collective-permute-done((bf16[512,1024]{1,0:T(8,128)(2,1)}, bf16[512,1024]{1,0:T(8,128)(2,1)S(1)}, u32[]{:S(2)}, u32[]{:S(2)}) %collective-permute-start.9) | collective-permute-done | bytes 1048608 | tf_op jit(solution)/shard_map/ppermute | solution.py:133
  149.2 1.9 fusion.13
  151.1 5.1 %all-to-all-start.2 = ((bf16[64,8,1024]{2,1,0:T(8,128)(2,1)}), bf16[64,8,1024]{2,1,0:T(8,128)(2,1)S(1)}, u32[]{:S(2)}, u32[]{:S(2)}) async-start(bf16[64,8,1024]{2,1,0:T(8,128)(2,1)} %fusion.13), calls=%async_computation.2 | async-start | bytes 2097152 | tf_op jit(solution)/shard_map/all_to_all | solution.py:198
  156.2 0.2 reduce-window.7
  156.4 27.7 %all-to-all-done.2 = bf16[64,8,1024]{2,1,0:T(8,128)(2,1)S(1)} async-done(((bf16[64,8,1024]{2,1,0:T(8,128)(2,1)}), bf16[64,8,1024]{2,1,0:T(8,128)(2,1)S(1)}, u32[]{:S(2)}, u32[]{:S(2)}) %all-to-all-start.2) | async-done | bytes 1048608 | tf_op jit(solution)/shard_map/all_to_all | solution.py:198
  184.0 0.4 convolution_add_fusion.1
  184.4 0.5 fusion.101
  184.9 0.2 multiply_reduce_fusion
  185.1 0.5 multiply_reduce_fusion.1
  185.7 0.7 multiply_convert_fusion
  186.4 0.7 collective-permute-start.10
  187.0 2.9 %collective-permute-start.11 = (bf16[4,1024]{1,0:T(4,128)(2,1)S(1)}, bf16[4,1024]{1,0:T(4,128)(2,1)S(1)}, u32[]{:S(2)}, u32[]{:S(2)}) collective-permute-start(bf16[4,1024]{1,0:T(4,128)(2,1)S(1)} %get-tuple-element.26), channel_id=1, source_target_pairs={{0,128},{4,132},{8,136},{12,140},{16,144},{20,148},{24,152},{28,15... | collective-permute-start | bytes 24584 | tf_op jit(solution)/shard_map/ppermute | solution.py:94
  189.9 1.4 collective-permute-start.12
  191.3 0.9 collective-permute-done.11
  192.2 1.4 collective-permute-done.12
  193.7 1.7 collective-permute-start.20
  195.5 0.4 collective-permute-start.14
  195.8 2.7 %collective-permute-start.15 = (bf16[4,1024]{1,0:T(4,128)(2,1)S(1)}, bf16[4,1024]{1,0:T(4,128)(2,1)S(1)}, u32[]{:S(2)}, u32[]{:S(2)}) collective-permute-start(bf16[4,1024]{1,0:T(4,128)(2,1)S(1)} %get-tuple-element.26), channel_id=1, source_target_pairs={{0,2},{1,3},{2,0},{3,1},{4,6},{5,7},{6,4},{7,5},{8,10},{9,11},{10,... | collective-permute-start | bytes 24584 | tf_op jit(solution)/shard_map/ppermute | solution.py:133
  198.6 1.4 collective-permute-start.16
  200.0 1.8 collective-permute-start.17
  201.8 1.9 collective-permute-start.18
  203.7 2.2 collective-permute-start.19
  205.9 0.3 subtract_convert_fusion.3
  206.2 0.2 fusion.77
  206.4 2.2 collective-permute-done.18
  208.6 3.4 %collective-permute-done.19 = bf16[32,1024]{1,0:T(8,128)(2,1)S(1)} collective-permute-done((bf16[32,1024]{1,0:T(8,128)(2,1)S(1)}, bf16[32,1024]{1,0:T(8,128)(2,1)S(1)}, u32[]{:S(2)}, u32[]{:S(2)}) %collective-permute-start.19) | collective-permute-done | bytes 65568 | tf_op jit(solution)/shard_map/ppermute | solution.py:94
  212.2 1.4 collective-permute-done.21
  213.7 0.3 subtract_convert_fusion.2
  214.0 0.2 fusion.81
  214.2 0.6 collective-permute-start.22
  214.9 2.1 collective-permute-start.23
  217.0 0.5 collective-permute-start.24
  217.5 1.1 collective-permute-done.22
  218.6 1.7 collective-permute-done.23
  220.3 1.8 collective-permute-done.24
  222.1 0.6 fusion.100
  (65 shorter events, 1.3 us)
Async XLA Ops:
  0.6 18.5 %copy-start.3 = (bf16[4,1024]{1,0:T(4,128)(2,1)S(1)}, bf16[4,1024]{1,0:T(4,128)(2,1)}, u32[]{:S(2)}) copy-start(bf16[4,1024]{1,0:T(4,128)(2,1)} %param.12) | copy-start | bytes 24580
  7.3 39.6 %all-to-all-start = ((bf16[64,8,1024]{2,1,0:T(8,128)(2,1)}), bf16[64,8,1024]{2,1,0:T(8,128)(2,1)S(1)}, u32[]{:S(2)}, u32[]{:S(2)}) async-start(bf16[64,8,1024]{2,1,0:T(8,128)(2,1)} %fusion), calls=%async_computation | async-start | bytes 2097152 | tf_op jit(solution)/shard_map/all_to_all | solution.py:178
  19.3 5.7 %collective-permute-start = (bf16[4,1024]{1,0:T(4,128)(2,1)S(1)}, bf16[4,1024]{1,0:T(4,128)(2,1)S(1)}, u32[]{:S(2)}, u32[]{:S(2)}) collective-permute-start(bf16[4,1024]{1,0:T(4,128)(2,1)S(1)} %fusion.76), channel_id=1, source_target_pairs={{0,1},{1,2},{2,3},{3,0},{4,5},{5,6},{6,7},{7,4},{8,9},{9,10},{10,1... | collective-permute-start | bytes 24584 | tf_op jit(solution)/shard_map/ppermute | solution.py:133
  20.8 5.2 %collective-permute-start.1 = (bf16[4,1024]{1,0:T(4,128)(2,1)S(1)}, bf16[4,1024]{1,0:T(4,128)(2,1)S(1)}, u32[]{:S(2)}, u32[]{:S(2)}) collective-permute-start(bf16[4,1024]{1,0:T(4,128)(2,1)S(1)} %fusion.76), channel_id=1, source_target_pairs={{0,2},{1,3},{2,0},{3,1},{4,6},{5,7},{6,4},{7,5},{8,10},{9,11},{10,... | collective-permute-start | bytes 24584 | tf_op jit(solution)/shard_map/ppermute | solution.py:133
  23.6 3.7 %collective-permute-start.2 = (bf16[4,1024]{1,0:T(4,128)(2,1)S(1)}, bf16[4,1024]{1,0:T(4,128)(2,1)S(1)}, u32[]{:S(2)}, u32[]{:S(2)}) collective-permute-start(bf16[4,1024]{1,0:T(4,128)(2,1)S(1)} %fusion.76), channel_id=1, source_target_pairs={{0,3},{1,0},{2,1},{3,2},{4,7},{5,4},{6,5},{7,6},{8,11},{9,8},{10,9... | collective-permute-start | bytes 24584 | tf_op jit(solution)/shard_map/ppermute | solution.py:133
  47.0 3.2 %copy-start.2 = (bf16[64,8,1024]{2,1,0:T(8,128)(2,1)}, bf16[64,8,1024]{2,1,0:T(8,128)(2,1)S(1)}, u32[]{:S(2)}) copy-start(bf16[64,8,1024]{2,1,0:T(8,128)(2,1)S(1)} %all-to-all-done) | copy-start | bytes 3145732
  47.0 31.9 %collective-permute-start.3 = (bf16[512,1024]{1,0:T(8,128)(2,1)S(1)}, bf16[512,1024]{1,0:T(8,128)(2,1)}, u32[]{:S(2)}, u32[]{:S(2)}) collective-permute-start(bf16[512,1024]{1,0:T(8,128)(2,1)S(1)} %bitcast.58), channel_id=1, source_target_pairs={{0,1},{1,2},{2,3},{3,0},{4,5},{5,6},{6,7},{7,4},{8,9},{9,10},{10,1... | collective-permute-start | bytes 3145736 | tf_op jit(solution)/shard_map/ppermute | solution.py:133
  48.5 30.4 %collective-permute-start.4 = (bf16[512,1024]{1,0:T(8,128)(2,1)S(1)}, bf16[512,1024]{1,0:T(8,128)(2,1)S(1)}, u32[]{:S(2)}, u32[]{:S(2)}) collective-permute-start(bf16[512,1024]{1,0:T(8,128)(2,1)S(1)} %bitcast.59), channel_id=1, source_target_pairs={{0,3},{1,0},{2,1},{3,2},{4,7},{5,4},{6,5},{7,6},{8,11},{9,8},{10,9... | collective-permute-start | bytes 3145736 | tf_op jit(solution)/shard_map/ppermute | solution.py:133
  76.8 2.0 collective-permute-start.8
  76.9 27.9 %collective-permute-start.7 = (bf16[512,1024]{1,0:T(8,128)(2,1)}, bf16[512,1024]{1,0:T(8,128)(2,1)S(1)}, u32[]{:S(2)}, u32[]{:S(2)}) collective-permute-start(bf16[512,1024]{1,0:T(8,128)(2,1)} %bitcast.61), channel_id=1, source_target_pairs={{0,2},{1,3},{2,0},{3,1},{4,6},{5,7},{6,4},{7,5},{8,10},{9,11},{10,... | collective-permute-start | bytes 3145736 | tf_op jit(solution)/shard_map/ppermute | solution.py:133
  78.9 8.7 %copy-start.5 = (bf16[512,1024]{1,0:T(8,128)(2,1)}, bf16[512,1024]{1,0:T(8,128)(2,1)S(1)}, u32[]{:S(2)}) copy-start(bf16[512,1024]{1,0:T(8,128)(2,1)S(1)} %collective-permute-done.4.rows_ref) | copy-start | bytes 3145732
  87.6 38.5 %collective-permute-start.5 = (bf16[512,1024]{1,0:T(8,128)(2,1)}, bf16[512,1024]{1,0:T(8,128)(2,1)S(1)}, u32[]{:S(2)}, u32[]{:S(2)}) collective-permute-start(bf16[512,1024]{1,0:T(8,128)(2,1)} %shard_map.104), channel_id=1, source_target_pairs={{0,3},{1,0},{2,1},{3,2},{4,7},{5,4},{6,5},{7,6},{8,11},{9,8},{10,9... | collective-permute-start | bytes 3145736 | tf_op jit(solution)/shard_map/ppermute | solution.py:133
  97.1 52.0 %copy-start.1 = (bf16[512,1024]{1,0:T(8,128)(2,1)S(1)}, bf16[512,1024]{1,0:T(8,128)(2,1)}, u32[]{:S(2)}) copy-start(bf16[512,1024]{1,0:T(8,128)(2,1)} %shard_map.103) | copy-start | bytes 3145732
  97.1 30.0 %collective-permute-start.6 = (bf16[512,1024]{1,0:T(8,128)(2,1)}, bf16[512,1024]{1,0:T(8,128)(2,1)S(1)}, u32[]{:S(2)}, u32[]{:S(2)}) collective-permute-start(bf16[512,1024]{1,0:T(8,128)(2,1)} %shard_map.105), channel_id=1, source_target_pairs={{0,1},{1,2},{2,3},{3,0},{4,5},{5,6},{6,7},{7,4},{8,9},{9,10},{10,1... | collective-permute-start | bytes 3145736 | tf_op jit(solution)/shard_map/ppermute | solution.py:133
  104.8 1.0 copy-start.6
  114.1 35.1 %collective-permute-start.9 = (bf16[512,1024]{1,0:T(8,128)(2,1)}, bf16[512,1024]{1,0:T(8,128)(2,1)S(1)}, u32[]{:S(2)}, u32[]{:S(2)}) collective-permute-start(bf16[512,1024]{1,0:T(8,128)(2,1)} %shard_map.106), channel_id=1, source_target_pairs={{0,2},{1,3},{2,0},{3,1},{4,6},{5,7},{6,4},{7,5},{8,10},{9,11},{10,... | collective-permute-start | bytes 3145736 | tf_op jit(solution)/shard_map/ppermute | solution.py:133
  151.1 5.1 %copy-start.8 = (s32[1,4]{1,0:T(1,128)S(1)}, s32[1,4]{1,0:T(1,128)}, u32[]{:S(2)}) copy-start(s32[1,4]{1,0:T(1,128)} %param.11) | copy-start | bytes 52
  151.1 5.3 %copy-start.4 = (f32[128,2]{0,1:T(2,128)S(1)}, f32[128,2]{0,1:T(2,128)}, u32[]{:S(2)}) copy-start(f32[128,2]{0,1:T(2,128)} %param.10) | copy-start | bytes 3076
  151.1 33.0 %copy-start = (bf16[128,1024]{1,0:T(8,128)(2,1)S(1)}, bf16[128,1024]{1,0:T(8,128)(2,1)}, u32[]{:S(2)}) copy-start(bf16[128,1024]{1,0:T(8,128)(2,1)} %param.8) | copy-start | bytes 786436
  151.1 33.0 %all-to-all-start.2 = ((bf16[64,8,1024]{2,1,0:T(8,128)(2,1)}), bf16[64,8,1024]{2,1,0:T(8,128)(2,1)S(1)}, u32[]{:S(2)}, u32[]{:S(2)}) async-start(bf16[64,8,1024]{2,1,0:T(8,128)(2,1)} %fusion.13), calls=%async_computation.2 | async-start | bytes 2097152 | tf_op jit(solution)/shard_map/all_to_all | solution.py:198
  184.0 1.1 copy-start.7
  186.4 4.9 %collective-permute-start.10 = (bf16[4,1024]{1,0:T(4,128)(2,1)S(1)}, bf16[4,1024]{1,0:T(4,128)(2,1)S(1)}, u32[]{:S(2)}, u32[]{:S(2)}) collective-permute-start(bf16[4,1024]{1,0:T(4,128)(2,1)S(1)} %get-tuple-element.26), channel_id=1, source_target_pairs={{0,64},{4,68},{8,72},{12,76},{16,80},{20,84},{24,88},{28,92},{32,9... | collective-permute-start | bytes 24584 | tf_op jit(solution)/shard_map/ppermute | solution.py:94
  187.0 5.2 %collective-permute-start.11 = (bf16[4,1024]{1,0:T(4,128)(2,1)S(1)}, bf16[4,1024]{1,0:T(4,128)(2,1)S(1)}, u32[]{:S(2)}, u32[]{:S(2)}) collective-permute-start(bf16[4,1024]{1,0:T(4,128)(2,1)S(1)} %get-tuple-element.26), channel_id=1, source_target_pairs={{0,128},{4,132},{8,136},{12,140},{16,144},{20,148},{24,152},{28,15... | collective-permute-start | bytes 24584 | tf_op jit(solution)/shard_map/ppermute | solution.py:94
  189.9 3.7 %collective-permute-start.12 = (bf16[4,1024]{1,0:T(4,128)(2,1)S(1)}, bf16[4,1024]{1,0:T(4,128)(2,1)S(1)}, u32[]{:S(2)}, u32[]{:S(2)}) collective-permute-start(bf16[4,1024]{1,0:T(4,128)(2,1)S(1)} %get-tuple-element.26), channel_id=1, source_target_pairs={{0,192},{4,196},{8,200},{12,204},{16,208},{20,212},{24,216},{28,22... | collective-permute-start | bytes 24584 | tf_op jit(solution)/shard_map/ppermute | solution.py:94
  193.6 1.8 collective-permute-start.13
  193.7 12.7 %collective-permute-start.20 = (bf16[16,1024]{1,0:T(8,128)(2,1)S(1)}, bf16[16,1024]{1,0:T(8,128)(2,1)S(1)}, u32[]{:S(2)}, u32[]{:S(2)}) collective-permute-start(bf16[16,1024]{1,0:T(8,128)(2,1)S(1)} %pad_maximum_fusion.3), channel_id=1, source_target_pairs={{0,32},{4,36},{8,40},{12,44},{16,48},{20,52},{24,56},{28,60},{32,0... | collective-permute-start | bytes 98312 | tf_op jit(solution)/shard_map/ppermute | solution.py:94
  195.5 6.4 %collective-permute-start.14 = (bf16[4,1024]{1,0:T(4,128)(2,1)S(1)}, bf16[4,1024]{1,0:T(4,128)(2,1)S(1)}, u32[]{:S(2)}, u32[]{:S(2)}) collective-permute-start(bf16[4,1024]{1,0:T(4,128)(2,1)S(1)} %get-tuple-element.26), channel_id=1, source_target_pairs={{0,1},{1,2},{2,3},{3,0},{4,5},{5,6},{6,7},{7,4},{8,9},{9,10},{10,1... | collective-permute-start | bytes 24584 | tf_op jit(solution)/shard_map/ppermute | solution.py:133
  195.8 7.9 %collective-permute-start.15 = (bf16[4,1024]{1,0:T(4,128)(2,1)S(1)}, bf16[4,1024]{1,0:T(4,128)(2,1)S(1)}, u32[]{:S(2)}, u32[]{:S(2)}) collective-permute-start(bf16[4,1024]{1,0:T(4,128)(2,1)S(1)} %get-tuple-element.26), channel_id=1, source_target_pairs={{0,2},{1,3},{2,0},{3,1},{4,6},{5,7},{6,4},{7,5},{8,10},{9,11},{10,... | collective-permute-start | bytes 24584 | tf_op jit(solution)/shard_map/ppermute | solution.py:133
  198.6 7.3 %collective-permute-start.16 = (bf16[4,1024]{1,0:T(4,128)(2,1)S(1)}, bf16[4,1024]{1,0:T(4,128)(2,1)S(1)}, u32[]{:S(2)}, u32[]{:S(2)}) collective-permute-start(bf16[4,1024]{1,0:T(4,128)(2,1)S(1)} %get-tuple-element.26), channel_id=1, source_target_pairs={{0,3},{1,0},{2,1},{3,2},{4,7},{5,4},{6,5},{7,6},{8,11},{9,8},{10,9... | collective-permute-start | bytes 24584 | tf_op jit(solution)/shard_map/ppermute | solution.py:133
  200.0 6.4 %collective-permute-start.17 = (bf16[32,1024]{1,0:T(8,128)(2,1)S(1)}, bf16[32,1024]{1,0:T(8,128)(2,1)S(1)}, u32[]{:S(2)}, u32[]{:S(2)}) collective-permute-start(bf16[32,1024]{1,0:T(8,128)(2,1)S(1)} %concatenate.38), channel_id=1, source_target_pairs={{0,8},{4,60},{8,16},{12,4},{16,24},{20,12},{24,32},{28,20},{32,40}... | collective-permute-start | bytes 196616 | tf_op jit(solution)/shard_map/ppermute | solution.py:94
  201.8 6.8 %collective-permute-start.18 = (bf16[32,1024]{1,0:T(8,128)(2,1)S(1)}, bf16[32,1024]{1,0:T(8,128)(2,1)S(1)}, u32[]{:S(2)}, u32[]{:S(2)}) collective-permute-start(bf16[32,1024]{1,0:T(8,128)(2,1)S(1)} %concatenate.38), channel_id=1, source_target_pairs={{0,16},{4,52},{8,24},{12,60},{16,32},{20,4},{24,40},{28,12},{32,48... | collective-permute-start | bytes 196616 | tf_op jit(solution)/shard_map/ppermute | solution.py:94
  203.7 8.4 %collective-permute-start.19 = (bf16[32,1024]{1,0:T(8,128)(2,1)S(1)}, bf16[32,1024]{1,0:T(8,128)(2,1)S(1)}, u32[]{:S(2)}, u32[]{:S(2)}) collective-permute-start(bf16[32,1024]{1,0:T(8,128)(2,1)S(1)} %concatenate.38), channel_id=1, source_target_pairs={{0,24},{4,44},{8,32},{12,52},{16,40},{20,60},{24,48},{28,4},{32,56... | collective-permute-start | bytes 196616 | tf_op jit(solution)/shard_map/ppermute | solution.py:94
  212.1 1.6 collective-permute-start.21
  214.2 4.3 %collective-permute-start.22 = (f32[8,1024]{1,0:T(8,128)S(1)}, f32[8,1024]{1,0:T(8,128)S(1)}, u32[]{:S(2)}, u32[]{:S(2)}) collective-permute-start(f32[8,1024]{1,0:T(8,128)S(1)} %get-tuple-element.41), channel_id=1, source_target_pairs={{0,3},{1,0},{2,1},{3,2},{4,7},{5,4},{6,5},{7,6},{8,11},{9,8},{10,9... | collective-permute-start | bytes 98312 | tf_op jit(solution)/shard_map/ppermute | solution.py:133
  214.9 5.4 %collective-permute-start.23 = (f32[8,1024]{1,0:T(8,128)S(1)}, f32[8,1024]{1,0:T(8,128)S(1)}, u32[]{:S(2)}, u32[]{:S(2)}) collective-permute-start(f32[8,1024]{1,0:T(8,128)S(1)} %get-tuple-element.43), channel_id=1, source_target_pairs={{0,2},{1,3},{2,0},{3,1},{4,6},{5,7},{6,4},{7,5},{8,10},{9,11},{10,... | collective-permute-start | bytes 98312 | tf_op jit(solution)/shard_map/ppermute | solution.py:133
  217.0 5.1 %collective-permute-start.24 = (f32[8,1024]{1,0:T(8,128)S(1)}, f32[8,1024]{1,0:T(8,128)S(1)}, u32[]{:S(2)}, u32[]{:S(2)}) collective-permute-start(f32[8,1024]{1,0:T(8,128)S(1)} %get-tuple-element.42), channel_id=1, source_target_pairs={{0,1},{1,2},{2,3},{3,0},{4,5},{5,6},{6,7},{7,4},{8,9},{9,10},{10,1... | collective-permute-start | bytes 98312 | tf_op jit(solution)/shard_map/ppermute | solution.py:133
where the time goes:
time: 223 us
  waiting for transfers between devices  104 us (47%)
  starting transfers between devices  52 us (23%)
  Pallas kernels  33.8 us (15%)
  blocking collectives  18.1 us (8%)
  other arithmetic  6.61 us (3%)
  matrix products  4.97 us (2%)
  local copies, waits for them, and re-layouts  2.67 us (1%)
    ppermute x15, waiting for transfers between devices, ring_shift(): lax.ppermute(values, 'grid', [(i, (i + step) % size) for i in range(size)])  46.9 us
    pallas_call x4, Pallas kernels, expert_part(): pl.pallas_call(expert_kernel, grid=(units // tile,), in_specs=[pl.BlockSp...  33.8 us
    all_to_all x1, waiting for transfers between devices, on_device(): lax.all_to_all(results, 'expert', split_axis=0, concat_axis=0, tiled=True)  27.7 us
    ppermute x15, starting transfers between devices, ring_shift(): lax.ppermute(values, 'grid', [(i, (i + step) % size) for i in range(size)])  22.4 us
    all_to_all x1, waiting for transfers between devices, on_device(): lax.all_to_all(send, 'expert', split_axis=0, concat_axis=0, tiled=True)  19.7 us
    all_to_all x1, blocking collectives, along_expert(): lax.all_to_all(copies, 'expert', split_axis=0, concat_axis=0, axis_index_...  18.1 us
    ppermute x10, starting transfers between devices, moved(): return lax.ppermute(values, 'expert', pairs)  12.8 us
    all_to_all x1, starting transfers between devices, on_device(): lax.all_to_all(send, 'expert', split_axis=0, concat_axis=0, tiled=True)  11.8 us
  transfers between devices with their start and end apart: 27, of which 16 were waited for; matrix products, arithmetic and copies ran while one was open for 1% of the time, Pallas kernels for 15%

commit v1 on v0

--- a/solution.py
+++ b/solution.py
@@ -150,7 +150,7 @@
     picture_unit = (unit_rows(image_embed.astype(F32)) / scale_root).astype(BF16)
     captions_here = picture_unit.shape[0]
     shape = (grid_all, experts_all // (2 * grid_all), 2)
-    row_parts = [picture_unit] + [ring_shift(picture_unit, k, grid_all) for k in range(1, grid_all)]
+    chip = lax.axis_index("expert") // shape[2]
 
     stream = tokens.astype(F32)
     normed = layer_norm(stream).astype(BF16)
@@ -176,26 +176,51 @@
     send = lax.dot_general(chosen, normed, (((0,), (0,)), ((), ())), preferred_element_type=F32)
     send = send.astype(BF16).reshape(experts_all, slots, width)
     arrived = lax.all_to_all(send, "expert", split_axis=0, concat_axis=0, tiled=True)
-    arrived, picture_later, *row_parts = held(arrived, picture_unit, *row_parts)
-    pictures_row = jnp.concatenate(row_parts, axis=0)
     rows = arrived.reshape(places_all, width)
 
     up_local = up_weight[0]
     down_local = down_weight[0]
-    from_left = ring_shift(rows, 1, grid_all)
-    from_right = ring_shift(rows, -1, grid_all)
-    from_far = ring_shift(rows, 2, grid_all)
+    half = places_all // 2
+    top, bottom = rows[:half], rows[half:]
+    left_top = ring_shift(top, 1, grid_all)
+    right_bottom = ring_shift(bottom, -1, grid_all)
     own_term = expert_part(rows, up_local, down_local)
-    own_term, picture_later = held(own_term, picture_later)
+    own_term, top, bottom = held(own_term, top, bottom)
+    left_bottom = ring_shift(bottom, 1, grid_all)
+    right_top = ring_shift(top, -1, grid_all)
+    far_top = ring_shift(left_top, 1, grid_all)
+    far_bottom = ring_shift(right_bottom, -1, grid_all)
+    left_top = expert_part(left_top, up_local, down_local)
+    right_bottom = expert_part(right_bottom, up_local, down_local)
+    far_top = expert_part(far_top, up_local, down_local)
+    far_bottom = expert_part(far_bottom, up_local, down_local)
+    far_from_left = ring_shift(far_top, 1, grid_all)
+    far_from_right = ring_shift(far_bottom, -1, grid_all)
+    left_top, right_bottom, far_bottom = held(left_top, right_bottom, far_bottom)
+    home_top = ring_shift(left_top, -1, grid_all)
+    home_bottom = ring_shift(right_bottom, 1, grid_all)
+    right_top = expert_part(right_top, up_local, down_local)
+    left_bottom = expert_part(left_bottom, up_local, down_local)
+    right_top = (right_top.astype(F32) + far_from_left.astype(F32)).astype(BF16)
+    left_bottom = (left_bottom.astype(F32) + far_from_right.astype(F32)).astype(BF16)
+    last_top = ring_shift(right_top, 1, grid_all)
+    last_bottom = ring_shift(left_bottom, -1, grid_all)
+    right_top, left_bottom, picture_later = held(right_top, left_bottom, picture_unit)
     picture_column = along_expert(picture_later, shape)
-    from_left, from_right, own_term = held(from_left, from_right, own_term)
-    from_far, picture_column = held(from_far, picture_column)
-    back_left = ring_shift(expert_part(from_left, up_local, down_local), -1, grid_all)
-    back_right = ring_shift(expert_part(from_right, up_local, down_local), 1, grid_all)
-    back_far = ring_shift(expert_part(from_far, up_local, down_local), 2, grid_all)
-    total = sum(term.astype(F32) for term in (own_term, back_left, back_right, back_far))
-    results = total.astype(BF16).reshape(experts_all, slots, width)
+    total_top = own_term[:half].astype(F32) + home_top.astype(F32) + last_top.astype(F32)
+    total_bottom = own_term[half:].astype(F32) + home_bottom.astype(F32) + last_bottom.astype(F32)
+    total = jnp.concatenate([total_top, total_bottom], axis=0).astype(BF16)
+    total, picture_column = held(total, picture_column)
+    results = total.reshape(experts_all, slots, width)
     returned = lax.all_to_all(results, "expert", split_axis=0, concat_axis=0, tiled=True)
+    picture_parts = [picture_column] + [
+        ring_shift(picture_column, k, grid_all) for k in range(1, grid_all)
+    ]
+    pictures_all = jnp.concatenate(picture_parts, axis=0)
+    pictures_row = lax.dynamic_slice_in_dim(
+        jnp.stack(picture_parts), chip * captions_here, captions_here, axis=1
+    ).reshape(grid_all * captions_here, width)
+    returned, pictures_all, pictures_row = held(returned, pictures_all, pictures_row)
     returned = returned.reshape(places_all, width)
 
     gates = jnp.where(at_first, route_gates[:, 0:1], 0.0) + jnp.where(
@@ -218,11 +243,8 @@
 
     text_group = along_y(text_unit, shape)
     text_both = on_chip(text_group, shape)
-    text_mine, text_both = held(text_unit, text_both)
     text_here = along_z(text_group, text_both, shape)
-    text_parts = [text_mine] + [ring_shift(text_mine, k, grid_all) for k in range(1, grid_all)]
     text_column = last_swap(text_both, text_here, shape)
-    text_row = jnp.concatenate(text_parts, axis=0)
 
     def slopes(mine, others, place):
         logits = SIMILARITY_HEAT * lax.dot_general(
@@ -233,18 +255,12 @@
         same = (row_ids < captions_here) & (row_ids + place == column_ids)
         return weighted_sum(pair_slope(logits, same), others)
 
-    chip = lax.axis_index("expert") // shape[2]
-    partial = jnp.concatenate(
-        [
-            slopes(text_row, picture_column, chip * captions_here).reshape(grid_all, captions_here, width),
-            slopes(pictures_row, text_column, 0).reshape(grid_all, captions_here, width),
-        ],
-        axis=1,
-    )
-    slope = partial[0]
+    sentence_slope = slopes(text_unit, pictures_all, chip * captions_here)
+    partial = slopes(pictures_row, text_column, 0).reshape(grid_all, captions_here, width)
+    picture_slope = partial[0]
     for k in range(1, grid_all):
-        slope = slope + ring_shift(partial[k], -k, grid_all)
-    return (text_embed, slope[:captions_here], slope[captions_here:])
+        picture_slope = picture_slope + ring_shift(partial[k], -k, grid_all)
+    return (text_embed, sentence_slope, picture_slope)
 
 
 def solution(mesh):

time: 223 us -> 216 us (0.969)
  waiting for transfers between devices: 104 us -> 69.9 us
  Pallas kernels: 33.8 us -> 44.5 us
  starting transfers between devices: 52 us -> 58.6 us
  other arithmetic: 6.61 us -> 12.1 us
  local copies, waits for them, and re-layouts: 2.67 us -> 5.98 us
    all_to_all x1, waiting for transfers between devices: 27.7 us -> 0.01 us  [on_device(): lax.all_to_all(results, 'expert', split_axis=0, concat_axis=0, tiled=True)]
    ppermute x15 -> x18, waiting for transfers between devices: 46.9 us -> 33 us  [ring_shift(): lax.ppermute(values, 'grid', [(i, (i + step) % size) for i in range(size)])]
    pallas_call x4 -> x7, Pallas kernels: 33.8 us -> 44.5 us  [expert_part(): pl.pallas_call(expert_kernel, grid=(units // tile,), in_specs=[pl.BlockSp...]
    all_to_all x1, waiting for transfers between devices: 19.7 us -> 27.7 us  [on_device(): lax.all_to_all(send, 'expert', split_axis=0, concat_axis=0, tiled=True)]
    unnamed x23 -> x36, local copies, waits for them, and re-layouts: 1.04 us -> 4.79 us
    all_to_all x1, starting transfers between devices: 5.09 us -> 8.64 us  [on_device(): lax.all_to_all(results, 'expert', split_axis=0, concat_axis=0, tiled=True)]
    concatenate x0 -> x2, other arithmetic: none -> 2.77 us  [the longest x1 1.73 us: on_device(): pictures_all = jnp.concatenate(picture_parts, axis=0)]
    ppermute x10, starting transfers between devices: 12.8 us -> 15 us  [moved(): return lax.ppermute(values, 'expert', pairs)]
  transfers between devices with their start and end apart: 27 -> 30, of which waited for: 16 -> 12; matrix products, arithmetic and copies ran while one was open for 1% -> 4% of each run, Pallas kernels for 15% -> 21%
where the time goes in v1:
time: 216 us; the launch traced here: 215 us
  waiting for transfers between devices  69.9 us (32%)
  starting transfers between devices  58.6 us (27%)
  Pallas kernels  44.5 us (21%)
  blocking collectives  18 us (8%)
  other arithmetic  12.1 us (6%)
  local copies, waits for them, and re-layouts  5.98 us (3%)
  matrix products  5.55 us (3%)
    pallas_call x7, Pallas kernels, expert_part(): pl.pallas_call(expert_kernel, grid=(units // tile,), in_specs=[pl.BlockSp...  44.5 us
    ppermute x18, waiting for transfers between devices, ring_shift(): lax.ppermute(values, 'grid', [(i, (i + step) % size) for i in range(size)])  33 us
    all_to_all x1, waiting for transfers between devices, on_device(): lax.all_to_all(send, 'expert', split_axis=0, concat_axis=0, tiled=True)  27.7 us
    ppermute x18, starting transfers between devices, ring_shift(): lax.ppermute(values, 'grid', [(i, (i + step) % size) for i in range(size)])  23.1 us
    all_to_all x1, blocking collectives, along_expert(): lax.all_to_all(copies, 'expert', split_axis=0, concat_axis=0, axis_index_...  18 us
    ppermute x10, starting transfers between devices, moved(): return lax.ppermute(values, 'expert', pairs)  15 us
    all_to_all x1, starting transfers between devices, on_device(): lax.all_to_all(send, 'expert', split_axis=0, concat_axis=0, tiled=True)  11.8 us
    ppermute x10, waiting for transfers between devices, moved(): return lax.ppermute(values, 'expert', pairs)  9.16 us
  transfers between devices with their start and end apart: 30, of which 12 were waited for; matrix products, arithmetic and copies ran while one was open for 4% of the time, Pallas kernels for 21%

profile of v1, /device:TPU:32, one launch (start us, length us, event | category | flops | bytes accessed | tf_op | source)
XLA Modules:
  0.0 215.5 jit_solution(7923754513232873211)
XLA Ops:
  0.6 0.8 slice_bitcast_fusion.5
  1.5 1.1 convert_reduce_fusion
  2.6 1.2 fusion.17
  4.0 0.8 fusion.72
  4.8 2.5 %fusion = bf16[64,8,1024]{2,1,0:T(8,128)(2,1)} fusion(bf16[128,1024]{1,0:T(8,128)(2,1)} %param.8, f32[128]{0:T(128)S(1)} %add_rsqrt_fusion.3, f32[128]{0:T(128)S(1)} %broadcast_multiply_fusion.2, s32[128]{0:T(128)S(1)} %get-tuple-element.43, s32[128]{0:T(128)S(1)} %get-tuple-element.42), kind=kOutput, calls=%fused_computation.6 | convolution fusion | flops 135462912 | bytes 1312768 | tf_op jit(solution)/shard_map/dot_general | solution.py:176
  7.3 11.8 %all-to-all-start = ((bf16[64,8,1024]{2,1,0:T(8,128)(2,1)}), bf16[64,8,1024]{2,1,0:T(8,128)(2,1)S(1)}, u32[]{:S(2)}, u32[]{:S(2)}) async-start(bf16[64,8,1024]{2,1,0:T(8,128)(2,1)} %fusion), calls=%async_computation | async-start | bytes 2097152 | tf_op jit(solution)/shard_map/all_to_all | solution.py:178
  19.2 27.7 %all-to-all-done = bf16[64,8,1024]{2,1,0:T(8,128)(2,1)S(1)} async-done(((bf16[64,8,1024]{2,1,0:T(8,128)(2,1)}), bf16[64,8,1024]{2,1,0:T(8,128)(2,1)S(1)}, u32[]{:S(2)}, u32[]{:S(2)}) %all-to-all-start) | async-done | bytes 1048608 | tf_op jit(solution)/shard_map/all_to_all | solution.py:178
  47.0 2.8 %collective-permute-start.1 = (bf16[256,1024]{1,0:T(8,128)(2,1)S(1)}, bf16[256,1024]{1,0:T(8,128)(2,1)S(1)}, u32[]{:S(2)}, u32[]{:S(2)}) collective-permute-start(bf16[256,1024]{1,0:T(8,128)(2,1)S(1)} %get-tuple-element.18), channel_id=1, source_target_pairs={{0,3},{1,0},{2,1},{3,2},{4,7},{5,4},{6,5},{7,6},{8,11},{9,8},{10,9... | collective-permute-start | bytes 1572872 | tf_op jit(solution)/shard_map/ppermute | solution.py:133
  49.9 8.3 %shard_map.103 = bf16[512,1024]{1,0:T(8,128)(2,1)} custom-call(bf16[512,1024]{1,0:T(8,128)(2,1)} %bitcast.54, bf16[1024,1024]{1,0:T(8,128)(2,1)} %bitcast.58, bf16[1024,1024]{1,0:T(8,128)(2,1)} %bitcast.65), custom_call_target="tpu_custom_call" | custom-call | flops 8589934592 | bytes 6291456 | tf_op jit(solution)/shard_map/pallas_call | solution.py:46
  58.2 0.7 collective-permute-start.9
  59.0 2.5 %collective-permute-start.4 = (bf16[256,1024]{1,0:T(8,128)(2,1)S(1)}, bf16[256,1024]{1,0:T(8,128)(2,1)S(1)}, u32[]{:S(2)}, u32[]{:S(2)}) collective-permute-start(bf16[256,1024]{1,0:T(8,128)(2,1)S(1)} %get-tuple-element.16), channel_id=1, source_target_pairs={{0,3},{1,0},{2,1},{3,2},{4,7},{5,4},{6,5},{7,6},{8,11},{9,8},{10,9... | collective-permute-start | bytes 1572872 | tf_op jit(solution)/shard_map/ppermute | solution.py:133
  61.5 4.4 %collective-permute-done.rows_ref = bf16[256,1024]{1,0:T(8,128)(2,1)S(1)} collective-permute-done((bf16[256,1024]{1,0:T(8,128)(2,1)S(1)}, bf16[256,1024]{1,0:T(8,128)(2,1)S(1)}, u32[]{:S(2)}, u32[]{:S(2)}) %collective-permute-start) | collective-permute-done | bytes 524320 | tf_op jit(solution)/shard_map/ppermute | solution.py:133
  65.9 0.8 copy-done.11
  66.7 6.0 %shard_map.104 = bf16[256,1024]{1,0:T(8,128)(2,1)} custom-call(bf16[256,1024]{1,0:T(8,128)(2,1)} %copy-done.11, bf16[1024,1024]{1,0:T(8,128)(2,1)} %bitcast.59, bf16[1024,1024]{1,0:T(8,128)(2,1)} %bitcast.66), custom_call_target="tpu_custom_call" | custom-call | flops 4294967296 | bytes 5242880 | tf_op jit(solution)/shard_map/pallas_call | solution.py:46
  72.7 2.5 %collective-permute-start.2 = (bf16[256,1024]{1,0:T(8,128)(2,1)S(1)}, bf16[256,1024]{1,0:T(8,128)(2,1)S(1)}, u32[]{:S(2)}, u32[]{:S(2)}) collective-permute-start(bf16[256,1024]{1,0:T(8,128)(2,1)S(1)} %collective-permute-done.1.rows_ref), channel_id=1, source_target_pairs={{0,3},{1,0},{2,1},{3,2},{4,7},{5,4},{6,5},{7,6},{8,11},{9,8},{10,9... | collective-permute-start | bytes 1572872 | tf_op jit(solution)/shard_map/ppermute | solution.py:133
  75.2 6.0 %shard_map.105 = bf16[256,1024]{1,0:T(8,128)(2,1)} custom-call(bf16[256,1024]{1,0:T(8,128)(2,1)} %copy-done.12, bf16[1024,1024]{1,0:T(8,128)(2,1)} %bitcast.60, bf16[1024,1024]{1,0:T(8,128)(2,1)} %bitcast.67), custom_call_target="tpu_custom_call" | custom-call | flops 4294967296 | bytes 5242880 | tf_op jit(solution)/shard_map/pallas_call | solution.py:46
  81.2 0.8 copy-done.14
  82.0 6.0 %shard_map.109 = bf16[256,1024]{1,0:T(8,128)(2,1)} custom-call(bf16[256,1024]{1,0:T(8,128)(2,1)} %copy-done.14, bf16[1024,1024]{1,0:T(8,128)(2,1)} %bitcast.61, bf16[1024,1024]{1,0:T(8,128)(2,1)} %bitcast.68), custom_call_target="tpu_custom_call" | custom-call | flops 4294967296 | bytes 5242880 | tf_op jit(solution)/shard_map/pallas_call | solution.py:46
  88.1 0.8 copy-done.15
  88.8 6.0 %shard_map.106 = bf16[256,1024]{1,0:T(8,128)(2,1)} custom-call(bf16[256,1024]{1,0:T(8,128)(2,1)} %copy-done.15, bf16[1024,1024]{1,0:T(8,128)(2,1)} %bitcast.62, bf16[1024,1024]{1,0:T(8,128)(2,1)} %bitcast.69), custom_call_target="tpu_custom_call" | custom-call | flops 4294967296 | bytes 5242880 | tf_op jit(solution)/shard_map/pallas_call | solution.py:46
  94.9 0.7 collective-permute-start.10
  95.6 0.8 copy-done.13
  96.4 6.0 %shard_map.108 = bf16[256,1024]{1,0:T(8,128)(2,1)} custom-call(bf16[256,1024]{1,0:T(8,128)(2,1)} %copy-done.13, bf16[1024,1024]{1,0:T(8,128)(2,1)} %bitcast.63, bf16[1024,1024]{1,0:T(8,128)(2,1)} %bitcast.70), custom_call_target="tpu_custom_call" | custom-call | flops 4294967296 | bytes 5242880 | tf_op jit(solution)/shard_map/pallas_call | solution.py:46
  102.4 1.3 collective-permute-start.6
  103.7 0.8 copy-done.10
  104.5 6.0 %shard_map.107 = bf16[256,1024]{1,0:T(8,128)(2,1)} custom-call(bf16[256,1024]{1,0:T(8,128)(2,1)} %copy-done.10, bf16[1024,1024]{1,0:T(8,128)(2,1)} %bitcast.64, bf16[1024,1024]{1,0:T(8,128)(2,1)} %bitcast.71), custom_call_target="tpu_custom_call" | custom-call | flops 4294967296 | bytes 5242880 | tf_op jit(solution)/shard_map/pallas_call | solution.py:46
  110.5 1.9 collective-permute-start.3
  112.8 3.2 %collective-permute-start.11 = (bf16[256,1024]{1,0:T(8,128)(2,1)S(1)}, bf16[256,1024]{1,0:T(8,128)(2,1)}, u32[]{:S(2)}, u32[]{:S(2)}) collective-permute-start(bf16[256,1024]{1,0:T(8,128)(2,1)S(1)} %add_convert_fusion.1), channel_id=1, source_target_pairs={{0,3},{1,0},{2,1},{3,2},{4,7},{5,4},{6,5},{7,6},{8,11},{9,8},{10,9... | collective-permute-start | bytes 1572872 | tf_op jit(solution)/shard_map/ppermute | solution.py:133
  116.0 0.5 collective-permute-done.6
  116.5 1.2 add_convert_fusion.3
  117.7 0.6 collective-permute-start.7
  118.5 18.0 %all_to_all.15 = bf16[32,4,1024]{2,1,0:T(4,128)(2,1)S(1)} all-to-all(bf16[32,4,1024]{2,1,0:T(4,128)(2,1)S(1)} %broadcast_in_dim.73), channel_id=1, replica_groups={{0,8,16,24,32,40,48,56,64,72,80,88,96,104,112,120,128,136,144,152,160,1..., dimensions={0} | all-to-all | bytes 524288 | tf_op jit(solution)/shard_map/all_to_all | solution.py:107
  136.6 0.7 collective-permute-done.7
  137.3 2.0 add_convert_fusion.2
  139.3 1.0 pad_maximum_fusion.1
  140.4 8.6 %all-to-all-start.2 = ((bf16[64,8,1024]{2,1,0:T(8,128)(2,1)}), bf16[64,8,1024]{2,1,0:T(8,128)(2,1)S(1)}, u32[]{:S(2)}, u32[]{:S(2)}) async-start(bf16[64,8,1024]{2,1,0:T(8,128)(2,1)} %bitcast.17), calls=%async_computation.2 | async-start | bytes 2097152 | tf_op jit(solution)/shard_map/all_to_all | solution.py:215
  149.2 0.9 collective-permute-start.14
  150.1 2.3 %collective-permute-start.15 = (bf16[256,1024]{1,0:T(8,128)(2,1)S(1)}, bf16[256,1024]{1,0:T(8,128)(2,1)S(1)}, u32[]{:S(2)}, u32[]{:S(2)}) collective-permute-start(bf16[256,1024]{1,0:T(8,128)(2,1)S(1)} %pad_maximum_fusion.2), channel_id=1, source_target_pairs={{0,3},{1,0},{2,1},{3,2},{4,7},{5,4},{6,5},{7,6},{8,11},{9,8},{10,9... | collective-permute-start | bytes 1572872 | tf_op jit(solution)/shard_map/ppermute | solution.py:133
  152.5 23.1 %collective-permute-done.13 = bf16[256,1024]{1,0:T(8,128)(2,1)S(1)} collective-permute-done((bf16[256,1024]{1,0:T(8,128)(2,1)S(1)}, bf16[256,1024]{1,0:T(8,128)(2,1)S(1)}, u32[]{:S(2)}, u32[]{:S(2)}) %collective-permute-start.13) | collective-permute-done | bytes 524320 | tf_op jit(solution)/shard_map/ppermute | solution.py:133
  175.6 0.6 collective-permute-done.15
  176.6 0.4 copy-done.5
  177.1 1.7 pad_maximum_fusion
  178.9 0.4 convolution_add_fusion.1
  179.3 0.5 fusion.79
  180.0 0.5 multiply_reduce_fusion.1
  180.5 0.7 multiply_convert_fusion
  181.2 1.5 collective-permute-start.16
  182.7 2.9 %collective-permute-start.17 = (bf16[4,1024]{1,0:T(4,128)(2,1)S(1)}, bf16[4,1024]{1,0:T(4,128)(2,1)S(1)}, u32[]{:S(2)}, u32[]{:S(2)}) collective-permute-start(bf16[4,1024]{1,0:T(4,128)(2,1)S(1)} %get-tuple-element.31), channel_id=1, source_target_pairs={{0,128},{4,132},{8,136},{12,140},{16,144},{20,148},{24,152},{28,15... | collective-permute-start | bytes 24584 | tf_op jit(solution)/shard_map/ppermute | solution.py:94
  185.6 1.4 collective-permute-start.18
  186.9 0.9 collective-permute-done.17
  187.8 1.4 collective-permute-done.18
  189.4 4.6 %collective-permute-start.23 = (bf16[16,1024]{1,0:T(8,128)(2,1)S(1)}, bf16[16,1024]{1,0:T(8,128)(2,1)S(1)}, u32[]{:S(2)}, u32[]{:S(2)}) collective-permute-start(bf16[16,1024]{1,0:T(8,128)(2,1)S(1)} %pad_maximum_fusion.4), channel_id=1, source_target_pairs={{0,32},{4,36},{8,40},{12,44},{16,48},{20,52},{24,56},{28,60},{32,0... | collective-permute-start | bytes 98312 | tf_op jit(solution)/shard_map/ppermute | solution.py:94
  194.0 0.7 collective-permute-start.20
  194.7 1.1 collective-permute-start.21
  195.8 2.7 %collective-permute-start.22 = (bf16[32,1024]{1,0:T(8,128)(2,1)S(1)}, bf16[32,1024]{1,0:T(8,128)(2,1)S(1)}, u32[]{:S(2)}, u32[]{:S(2)}) collective-permute-start(bf16[32,1024]{1,0:T(8,128)(2,1)S(1)} %concatenate.39), channel_id=1, source_target_pairs={{0,24},{4,44},{8,32},{12,52},{16,40},{20,60},{24,48},{28,4},{32,56... | collective-permute-start | bytes 196616 | tf_op jit(solution)/shard_map/ppermute | solution.py:94
  198.5 0.7 subtract_convert_fusion.3
  199.2 2.1 collective-permute-done.21
  201.2 3.7 %collective-permute-done.22 = bf16[32,1024]{1,0:T(8,128)(2,1)S(1)} collective-permute-done((bf16[32,1024]{1,0:T(8,128)(2,1)S(1)}, bf16[32,1024]{1,0:T(8,128)(2,1)S(1)}, u32[]{:S(2)}, u32[]{:S(2)}) %collective-permute-start.22) | collective-permute-done | bytes 65568 | tf_op jit(solution)/shard_map/ppermute | solution.py:94
  205.4 1.1 collective-permute-done.24
  207.2 2.4 %collective-permute-start.25 = (f32[4,1024]{1,0:T(4,128)S(1)}, f32[4,1024]{1,0:T(4,128)S(1)}, u32[]{:S(2)}, u32[]{:S(2)}) collective-permute-start(f32[4,1024]{1,0:T(4,128)S(1)} %get-tuple-element.37), channel_id=1, source_target_pairs={{0,3},{1,0},{2,1},{3,2},{4,7},{5,4},{6,5},{7,6},{8,11},{9,8},{10,9... | collective-permute-start | bytes 49160 | tf_op jit(solution)/shard_map/ppermute | solution.py:133
  209.6 1.0 collective-permute-start.27
  210.6 0.6 fusion.56
  211.2 3.7 %collective-permute-done.26 = f32[4,1024]{1,0:T(4,128)S(1)} collective-permute-done((f32[4,1024]{1,0:T(4,128)S(1)}, f32[4,1024]{1,0:T(4,128)S(1)}, u32[]{:S(2)}, u32[]{:S(2)}) %collective-permute-start.26) | collective-permute-done | bytes 16416 | tf_op jit(solution)/shard_map/ppermute | solution.py:133
  214.9 0.6 fusion.55
  (92 shorter events, 3.5 us)
Async XLA Ops:
  0.6 18.5 %copy-start.8 = (bf16[4,1024]{1,0:T(4,128)(2,1)S(1)}, bf16[4,1024]{1,0:T(4,128)(2,1)}, u32[]{:S(2)}) copy-start(bf16[4,1024]{1,0:T(4,128)(2,1)} %param.12) | copy-start | bytes 24580
  7.3 39.6 %all-to-all-start = ((bf16[64,8,1024]{2,1,0:T(8,128)(2,1)}), bf16[64,8,1024]{2,1,0:T(8,128)(2,1)S(1)}, u32[]{:S(2)}, u32[]{:S(2)}) async-start(bf16[64,8,1024]{2,1,0:T(8,128)(2,1)} %fusion), calls=%async_computation | async-start | bytes 2097152 | tf_op jit(solution)/shard_map/all_to_all | solution.py:178
  47.0 2.9 %copy-start.1 = (bf16[64,8,1024]{2,1,0:T(8,128)(2,1)}, bf16[64,8,1024]{2,1,0:T(8,128)(2,1)S(1)}, u32[]{:S(2)}) copy-start(bf16[64,8,1024]{2,1,0:T(8,128)(2,1)S(1)} %all-to-all-done) | copy-start | bytes 3145732
  47.0 25.7 %collective-permute-start.1 = (bf16[256,1024]{1,0:T(8,128)(2,1)S(1)}, bf16[256,1024]{1,0:T(8,128)(2,1)S(1)}, u32[]{:S(2)}, u32[]{:S(2)}) collective-permute-start(bf16[256,1024]{1,0:T(8,128)(2,1)S(1)} %get-tuple-element.18), channel_id=1, source_target_pairs={{0,3},{1,0},{2,1},{3,2},{4,7},{5,4},{6,5},{7,6},{8,11},{9,8},{10,9... | collective-permute-start | bytes 1572872 | tf_op jit(solution)/shard_map/ppermute | solution.py:133
  49.9 16.0 %collective-permute-start = (bf16[256,1024]{1,0:T(8,128)(2,1)S(1)}, bf16[256,1024]{1,0:T(8,128)(2,1)S(1)}, u32[]{:S(2)}, u32[]{:S(2)}) collective-permute-start(bf16[256,1024]{1,0:T(8,128)(2,1)S(1)} %get-tuple-element.16), channel_id=1, source_target_pairs={{0,1},{1,2},{2,3},{3,0},{4,5},{5,6},{6,7},{7,4},{8,9},{9,10},{10,1... | collective-permute-start | bytes 1572872 | tf_op jit(solution)/shard_map/ppermute | solution.py:133
  58.2 23.0 %collective-permute-start.9 = (bf16[256,1024]{1,0:T(8,128)(2,1)S(1)}, bf16[256,1024]{1,0:T(8,128)(2,1)S(1)}, u32[]{:S(2)}, u32[]{:S(2)}) collective-permute-start(bf16[256,1024]{1,0:T(8,128)(2,1)S(1)} %get-tuple-element.18), channel_id=1, source_target_pairs={{0,1},{1,2},{2,3},{3,0},{4,5},{5,6},{6,7},{7,4},{8,9},{9,10},{10,1... | collective-permute-start | bytes 1572872 | tf_op jit(solution)/shard_map/ppermute | solution.py:133
  59.0 44.7 %collective-permute-start.4 = (bf16[256,1024]{1,0:T(8,128)(2,1)S(1)}, bf16[256,1024]{1,0:T(8,128)(2,1)S(1)}, u32[]{:S(2)}, u32[]{:S(2)}) collective-permute-start(bf16[256,1024]{1,0:T(8,128)(2,1)S(1)} %get-tuple-element.16), channel_id=1, source_target_pairs={{0,3},{1,0},{2,1},{3,2},{4,7},{5,4},{6,5},{7,6},{8,11},{9,8},{10,9... | collective-permute-start | bytes 1572872 | tf_op jit(solution)/shard_map/ppermute | solution.py:133
  65.9 0.8 copy-start.11
  65.9 29.7 %collective-permute-start.5 = (bf16[256,1024]{1,0:T(8,128)(2,1)S(1)}, bf16[256,1024]{1,0:T(8,128)(2,1)S(1)}, u32[]{:S(2)}, u32[]{:S(2)}) collective-permute-start(bf16[256,1024]{1,0:T(8,128)(2,1)S(1)} %collective-permute-done.rows_ref), channel_id=1, source_target_pairs={{0,1},{1,2},{2,3},{3,0},{4,5},{5,6},{6,7},{7,4},{8,9},{9,10},{10,1... | collective-permute-start | bytes 1572872 | tf_op jit(solution)/shard_map/ppermute | solution.py:133
  72.7 2.5 %copy-start.12 = (bf16[256,1024]{1,0:T(8,128)(2,1)}, bf16[256,1024]{1,0:T(8,128)(2,1)S(1)}, u32[]{:S(2)}) copy-start(bf16[256,1024]{1,0:T(8,128)(2,1)S(1)} %collective-permute-done.1.rows_ref) | copy-start | bytes 1572868
  72.7 15.4 %collective-permute-start.2 = (bf16[256,1024]{1,0:T(8,128)(2,1)S(1)}, bf16[256,1024]{1,0:T(8,128)(2,1)S(1)}, u32[]{:S(2)}, u32[]{:S(2)}) collective-permute-start(bf16[256,1024]{1,0:T(8,128)(2,1)S(1)} %collective-permute-done.1.rows_ref), channel_id=1, source_target_pairs={{0,3},{1,0},{2,1},{3,2},{4,7},{5,4},{6,5},{7,6},{8,11},{9,8},{10,9... | collective-permute-start | bytes 1572872 | tf_op jit(solution)/shard_map/ppermute | solution.py:133
  81.2 0.8 copy-start.14
  88.1 0.8 copy-start.15
  94.9 17.7 %collective-permute-start.10 = (bf16[256,1024]{1,0:T(8,128)(2,1)}, bf16[256,1024]{1,0:T(8,128)(2,1)S(1)}, u32[]{:S(2)}, u32[]{:S(2)}) collective-permute-start(bf16[256,1024]{1,0:T(8,128)(2,1)} %shard_map.106), channel_id=1, source_target_pairs={{0,3},{1,0},{2,1},{3,2},{4,7},{5,4},{6,5},{7,6},{8,11},{9,8},{10,9... | collective-permute-start | bytes 1572872 | tf_op jit(solution)/shard_map/ppermute | solution.py:133
  95.6 0.8 copy-start.13
  102.4 10.2 %copy-start.7 = (bf16[256,1024]{1,0:T(8,128)(2,1)S(1)}, bf16[256,1024]{1,0:T(8,128)(2,1)}, u32[]{:S(2)}) copy-start(bf16[256,1024]{1,0:T(8,128)(2,1)} %shard_map.109) | copy-start | bytes 1572868
  102.4 14.1 %collective-permute-start.6 = (bf16[256,1024]{1,0:T(8,128)(2,1)}, bf16[256,1024]{1,0:T(8,128)(2,1)S(1)}, u32[]{:S(2)}, u32[]{:S(2)}) collective-permute-start(bf16[256,1024]{1,0:T(8,128)(2,1)} %shard_map.108), channel_id=1, source_target_pairs={{0,1},{1,2},{2,3},{3,0},{4,5},{5,6},{6,7},{7,4},{8,9},{9,10},{10,1... | collective-permute-start | bytes 1572872 | tf_op jit(solution)/shard_map/ppermute | solution.py:133
  103.7 0.8 copy-start.10
  110.5 26.8 %copy-start.6 = (bf16[512,1024]{1,0:T(8,128)(2,1)S(1)}, bf16[512,1024]{1,0:T(8,128)(2,1)}, u32[]{:S(2)}) copy-start(bf16[512,1024]{1,0:T(8,128)(2,1)} %shard_map.103) | copy-start | bytes 3145732
  110.5 26.1 %collective-permute-start.3 = (bf16[256,1024]{1,0:T(8,128)(2,1)}, bf16[256,1024]{1,0:T(8,128)(2,1)S(1)}, u32[]{:S(2)}, u32[]{:S(2)}) collective-permute-start(bf16[256,1024]{1,0:T(8,128)(2,1)} %shard_map.104), channel_id=1, source_target_pairs={{0,3},{1,0},{2,1},{3,2},{4,7},{5,4},{6,5},{7,6},{8,11},{9,8},{10,9... | collective-permute-start | bytes 1572872 | tf_op jit(solution)/shard_map/ppermute | solution.py:133
  112.5 24.2 %collective-permute-start.8 = (bf16[256,1024]{1,0:T(8,128)(2,1)}, bf16[256,1024]{1,0:T(8,128)(2,1)}, u32[]{:S(2)}, u32[]{:S(2)}) collective-permute-start(bf16[256,1024]{1,0:T(8,128)(2,1)} %shard_map.105), channel_id=1, source_target_pairs={{0,1},{1,2},{2,3},{3,0},{4,5},{5,6},{6,7},{7,4},{8,9},{9,10},{10,1... | collective-permute-start | bytes 1572872 | tf_op jit(solution)/shard_map/ppermute | solution.py:133
  112.8 23.9 %collective-permute-start.11 = (bf16[256,1024]{1,0:T(8,128)(2,1)S(1)}, bf16[256,1024]{1,0:T(8,128)(2,1)}, u32[]{:S(2)}, u32[]{:S(2)}) collective-permute-start(bf16[256,1024]{1,0:T(8,128)(2,1)S(1)} %add_convert_fusion.1), channel_id=1, source_target_pairs={{0,3},{1,0},{2,1},{3,2},{4,7},{5,4},{6,5},{7,6},{8,11},{9,8},{10,9... | collective-permute-start | bytes 1572872 | tf_op jit(solution)/shard_map/ppermute | solution.py:133
  117.7 19.6 %collective-permute-start.7 = (bf16[256,1024]{1,0:T(8,128)(2,1)S(1)}, bf16[256,1024]{1,0:T(8,128)(2,1)}, u32[]{:S(2)}, u32[]{:S(2)}) collective-permute-start(bf16[256,1024]{1,0:T(8,128)(2,1)S(1)} %add_convert_fusion.3), channel_id=1, source_target_pairs={{0,1},{1,2},{2,3},{3,0},{4,5},{5,6},{6,7},{7,4},{8,9},{9,10},{10,1... | collective-permute-start | bytes 1572872 | tf_op jit(solution)/shard_map/ppermute | solution.py:133
  136.5 3.8 %collective-permute-start.12 = (bf16[128,1024]{1,0:T(8,128)(2,1)S(1)}, bf16[128,1024]{1,0:T(8,128)(2,1)S(1)}, u32[]{:S(2)}, u32[]{:S(2)}) collective-permute-start(bf16[128,1024]{1,0:T(8,128)(2,1)S(1)} %reshape.135), channel_id=1, source_target_pairs={{0,4},{4,0},{8,12},{12,8},{16,20},{20,16},{24,28},{28,24},{32,36},... | collective-permute-start | bytes 786440 | tf_op jit(solution)/shard_map/ppermute | solution.py:94
  140.3 8.7 %copy-start.17 = (s32[1,4]{1,0:T(1,128)S(1)}, s32[1,4]{1,0:T(1,128)}, u32[]{:S(2)}) copy-start(s32[1,4]{1,0:T(1,128)} %param.11) | copy-start | bytes 52
  140.3 12.2 %copy-start.9 = (f32[128,2]{0,1:T(2,128)S(1)}, f32[128,2]{0,1:T(2,128)}, u32[]{:S(2)}) copy-start(f32[128,2]{0,1:T(2,128)} %param.10) | copy-start | bytes 3076
  140.4 36.7 %copy-start = (bf16[256,1024]{1,0:T(8,128)(2,1)}, bf16[256,1024]{1,0:T(8,128)(2,1)S(1)}, u32[]{:S(2)}) copy-start(bf16[256,1024]{1,0:T(8,128)(2,1)S(1)} %pad_maximum_fusion.2) | copy-start | bytes 1572868
  140.4 38.5 %all-to-all-start.2 = ((bf16[64,8,1024]{2,1,0:T(8,128)(2,1)}), bf16[64,8,1024]{2,1,0:T(8,128)(2,1)S(1)}, u32[]{:S(2)}, u32[]{:S(2)}) async-start(bf16[64,8,1024]{2,1,0:T(8,128)(2,1)} %bitcast.17), calls=%async_computation.2 | async-start | bytes 2097152 | tf_op jit(solution)/shard_map/all_to_all | solution.py:215
  149.2 26.4 %collective-permute-start.13 = (bf16[256,1024]{1,0:T(8,128)(2,1)S(1)}, bf16[256,1024]{1,0:T(8,128)(2,1)S(1)}, u32[]{:S(2)}, u32[]{:S(2)}) collective-permute-start(bf16[256,1024]{1,0:T(8,128)(2,1)S(1)} %pad_maximum_fusion.2), channel_id=1, source_target_pairs={{0,1},{1,2},{2,3},{3,0},{4,5},{5,6},{6,7},{7,4},{8,9},{9,10},{10,1... | collective-permute-start | bytes 1572872 | tf_op jit(solution)/shard_map/ppermute | solution.py:133
  149.2 26.4 %collective-permute-start.14 = (bf16[256,1024]{1,0:T(8,128)(2,1)S(1)}, bf16[256,1024]{1,0:T(8,128)(2,1)S(1)}, u32[]{:S(2)}, u32[]{:S(2)}) collective-permute-start(bf16[256,1024]{1,0:T(8,128)(2,1)S(1)} %pad_maximum_fusion.2), channel_id=1, source_target_pairs={{0,2},{1,3},{2,0},{3,1},{4,6},{5,7},{6,4},{7,5},{8,10},{9,11},{10,... | collective-permute-start | bytes 1572872 | tf_op jit(solution)/shard_map/ppermute | solution.py:133
  150.1 26.1 %collective-permute-start.15 = (bf16[256,1024]{1,0:T(8,128)(2,1)S(1)}, bf16[256,1024]{1,0:T(8,128)(2,1)S(1)}, u32[]{:S(2)}, u32[]{:S(2)}) collective-permute-start(bf16[256,1024]{1,0:T(8,128)(2,1)S(1)} %pad_maximum_fusion.2), channel_id=1, source_target_pairs={{0,3},{1,0},{2,1},{3,2},{4,7},{5,4},{6,5},{7,6},{8,11},{9,8},{10,9... | collective-permute-start | bytes 1572872 | tf_op jit(solution)/shard_map/ppermute | solution.py:133
  175.6 0.8 copy-start.3
  175.6 1.0 copy-start.4
  176.2 0.8 copy-start.5
  177.1 1.8 copy-start.2
  178.9 1.1 copy-start.16
  181.2 5.7 %collective-permute-start.16 = (bf16[4,1024]{1,0:T(4,128)(2,1)S(1)}, bf16[4,1024]{1,0:T(4,128)(2,1)S(1)}, u32[]{:S(2)}, u32[]{:S(2)}) collective-permute-start(bf16[4,1024]{1,0:T(4,128)(2,1)S(1)} %get-tuple-element.31), channel_id=1, source_target_pairs={{0,64},{4,68},{8,72},{12,76},{16,80},{20,84},{24,88},{28,92},{32,9... | collective-permute-start | bytes 24584 | tf_op jit(solution)/shard_map/ppermute | solution.py:94
  182.7 5.2 %collective-permute-start.17 = (bf16[4,1024]{1,0:T(4,128)(2,1)S(1)}, bf16[4,1024]{1,0:T(4,128)(2,1)S(1)}, u32[]{:S(2)}, u32[]{:S(2)}) collective-permute-start(bf16[4,1024]{1,0:T(4,128)(2,1)S(1)} %get-tuple-element.31), channel_id=1, source_target_pairs={{0,128},{4,132},{8,136},{12,140},{16,144},{20,148},{24,152},{28,15... | collective-permute-start | bytes 24584 | tf_op jit(solution)/shard_map/ppermute | solution.py:94
  185.6 3.7 %collective-permute-start.18 = (bf16[4,1024]{1,0:T(4,128)(2,1)S(1)}, bf16[4,1024]{1,0:T(4,128)(2,1)S(1)}, u32[]{:S(2)}, u32[]{:S(2)}) collective-permute-start(bf16[4,1024]{1,0:T(4,128)(2,1)S(1)} %get-tuple-element.31), channel_id=1, source_target_pairs={{0,192},{4,196},{8,200},{12,204},{16,208},{20,212},{24,216},{28,22... | collective-permute-start | bytes 24584 | tf_op jit(solution)/shard_map/ppermute | solution.py:94
  189.3 4.7 %collective-permute-start.19 = (bf16[16,1024]{1,0:T(8,128)(2,1)S(1)}, bf16[16,1024]{1,0:T(8,128)(2,1)S(1)}, u32[]{:S(2)}, u32[]{:S(2)}) collective-permute-start(bf16[16,1024]{1,0:T(8,128)(2,1)S(1)} %pad_maximum_fusion.4), channel_id=1, source_target_pairs={{0,4},{4,0},{8,12},{12,8},{16,20},{20,16},{24,28},{28,24},{32,36},... | collective-permute-start | bytes 98312 | tf_op jit(solution)/shard_map/ppermute | solution.py:94
  189.4 9.8 %collective-permute-start.23 = (bf16[16,1024]{1,0:T(8,128)(2,1)S(1)}, bf16[16,1024]{1,0:T(8,128)(2,1)S(1)}, u32[]{:S(2)}, u32[]{:S(2)}) collective-permute-start(bf16[16,1024]{1,0:T(8,128)(2,1)S(1)} %pad_maximum_fusion.4), channel_id=1, source_target_pairs={{0,32},{4,36},{8,40},{12,44},{16,48},{20,52},{24,56},{28,60},{32,0... | collective-permute-start | bytes 98312 | tf_op jit(solution)/shard_map/ppermute | solution.py:94
  194.0 5.1 %collective-permute-start.20 = (bf16[32,1024]{1,0:T(8,128)(2,1)S(1)}, bf16[32,1024]{1,0:T(8,128)(2,1)S(1)}, u32[]{:S(2)}, u32[]{:S(2)}) collective-permute-start(bf16[32,1024]{1,0:T(8,128)(2,1)S(1)} %concatenate.39), channel_id=1, source_target_pairs={{0,8},{4,60},{8,16},{12,4},{16,24},{20,12},{24,32},{28,20},{32,40}... | collective-permute-start | bytes 196616 | tf_op jit(solution)/shard_map/ppermute | solution.py:94
  194.7 6.6 %collective-permute-start.21 = (bf16[32,1024]{1,0:T(8,128)(2,1)S(1)}, bf16[32,1024]{1,0:T(8,128)(2,1)S(1)}, u32[]{:S(2)}, u32[]{:S(2)}) collective-permute-start(bf16[32,1024]{1,0:T(8,128)(2,1)S(1)} %concatenate.39), channel_id=1, source_target_pairs={{0,16},{4,52},{8,24},{12,60},{16,32},{20,4},{24,40},{28,12},{32,48... | collective-permute-start | bytes 196616 | tf_op jit(solution)/shard_map/ppermute | solution.py:94
  195.8 9.2 %collective-permute-start.22 = (bf16[32,1024]{1,0:T(8,128)(2,1)S(1)}, bf16[32,1024]{1,0:T(8,128)(2,1)S(1)}, u32[]{:S(2)}, u32[]{:S(2)}) collective-permute-start(bf16[32,1024]{1,0:T(8,128)(2,1)S(1)} %concatenate.39), channel_id=1, source_target_pairs={{0,24},{4,44},{8,32},{12,52},{16,40},{20,60},{24,48},{28,4},{32,56... | collective-permute-start | bytes 196616 | tf_op jit(solution)/shard_map/ppermute | solution.py:94
  205.0 1.6 collective-permute-start.24
  207.2 4.0 %collective-permute-start.25 = (f32[4,1024]{1,0:T(4,128)S(1)}, f32[4,1024]{1,0:T(4,128)S(1)}, u32[]{:S(2)}, u32[]{:S(2)}) collective-permute-start(f32[4,1024]{1,0:T(4,128)S(1)} %get-tuple-element.37), channel_id=1, source_target_pairs={{0,3},{1,0},{2,1},{3,2},{4,7},{5,4},{6,5},{7,6},{8,11},{9,8},{10,9... | collective-permute-start | bytes 49160 | tf_op jit(solution)/shard_map/ppermute | solution.py:133
  209.6 5.2 %collective-permute-start.26 = (f32[4,1024]{1,0:T(4,128)S(1)}, f32[4,1024]{1,0:T(4,128)S(1)}, u32[]{:S(2)}, u32[]{:S(2)}) collective-permute-start(f32[4,1024]{1,0:T(4,128)S(1)} %get-tuple-element.39), channel_id=1, source_target_pairs={{0,2},{1,3},{2,0},{3,1},{4,6},{5,7},{6,4},{7,5},{8,10},{9,11},{10,... | collective-permute-start | bytes 49160 | tf_op jit(solution)/shard_map/ppermute | solution.py:133
  209.6 5.2 %collective-permute-start.27 = (f32[4,1024]{1,0:T(4,128)S(1)}, f32[4,1024]{1,0:T(4,128)S(1)}, u32[]{:S(2)}, u32[]{:S(2)}) collective-permute-start(f32[4,1024]{1,0:T(4,128)S(1)} %get-tuple-element.38), channel_id=1, source_target_pairs={{0,1},{1,2},{2,3},{3,0},{4,5},{5,6},{6,7},{7,4},{8,9},{9,10},{10,1... | collective-permute-start | bytes 49160 | tf_op jit(solution)/shard_map/ppermute | solution.py:133

commit v2 on v1

--- a/solution.py
+++ b/solution.py
@@ -1,3 +1,4 @@
+import functools
 import math
 
 import jax
@@ -18,9 +19,13 @@
     return centred * lax.rsqrt(jnp.mean(centred * centred, axis=-1, keepdims=True) + EPSILON)
 
 
-def expert_kernel(rows_ref, up_ref, down_ref, out_ref, total_ref):
+def expert_kernel(*refs):
+    blocks = (len(refs) - 3) // 2
+    rows_refs, (up_ref, down_ref) = refs[:blocks], refs[blocks : blocks + 2]
+    out_refs, total_ref = refs[blocks + 2 : -1], refs[-1]
     step = pl.program_id(0)
-    hidden = jnp.dot(rows_ref[...], up_ref[...], preferred_element_type=F32)
+    rows = jnp.concatenate([ref[...] for ref in rows_refs], axis=0)
+    hidden = jnp.dot(rows, up_ref[...], preferred_element_type=F32)
     hidden = (0.5 * hidden * (1.0 + lax.erf(hidden * math.sqrt(0.5)))).astype(BF16)
     term = lax.dot_general(
         hidden, down_ref[...], (((1,), (1,)), ((), ())), preferred_element_type=F32
@@ -36,23 +41,27 @@
 
     @pl.when(step == pl.num_programs(0) - 1)
     def _():
-        out_ref[...] = total_ref[...].astype(BF16)
-
-
-def expert_part(rows, up_piece, down_piece):
-    count, width = rows.shape
-    units = up_piece.shape[1]
+        start = 0
+        for ref in out_refs:
+            ref[...] = total_ref[start : start + ref.shape[0], :].astype(BF16)
+            start += ref.shape[0]
+
+
+def expert_part(blocks, up_piece, down_piece):
+    width, units = up_piece.shape
+    count = sum(block.shape[0] for block in blocks)
     tile = min(256, units)
+    whole = [pl.BlockSpec(block.shape, lambda i: (0, 0)) for block in blocks]
     return pl.pallas_call(
         expert_kernel,
         grid=(units // tile,),
-        in_specs=[
-            pl.BlockSpec((count, width), lambda i: (0, 0)),
+        in_specs=whole
+        + [
             pl.BlockSpec((width, tile), lambda i: (0, i)),
             pl.BlockSpec((width, tile), lambda i: (0, i)),
         ],
-        out_specs=pl.BlockSpec((count, width), lambda i: (0, 0)),
-        out_shape=jax.ShapeDtypeStruct((count, width), BF16),
+        out_specs=whole,
+        out_shape=[jax.ShapeDtypeStruct(block.shape, BF16) for block in blocks],
         scratch_shapes=[pltpu.VMEM((count, width), F32)],
         compiler_params=pltpu.CompilerParams(vmem_limit_bytes=56 * 2**20),
         cost_estimate=pl.CostEstimate(
@@ -60,7 +69,74 @@
             bytes_accessed=4 * width * units + 4 * count * width,
             transcendentals=count * units,
         ),
-    )(rows, up_piece, down_piece)
+    )(*blocks, up_piece, down_piece)
+
+
+def sum_kernel(own_ref, home_top, last_top, home_bottom, last_bottom, out_ref):
+    own = own_ref[...].astype(F32)
+    early = pl.program_id(0) < pl.num_programs(0) // 2
+
+    @pl.when(early)
+    def _():
+        out_ref[...] = (own + home_top[...].astype(F32) + last_top[...].astype(F32)).astype(BF16)
+
+    @pl.when(jnp.logical_not(early))
+    def _():
+        out_ref[...] = (
+            own + home_bottom[...].astype(F32) + last_bottom[...].astype(F32)
+        ).astype(BF16)
+
+
+def sum_terms(own, home_top, last_top, home_bottom, last_bottom):
+    count, width = own.shape
+    steps = 4
+    block = (count // steps, width)
+    top = pl.BlockSpec(block, lambda i: (jnp.minimum(i, steps // 2 - 1), 0))
+    bottom = pl.BlockSpec(block, lambda i: (jnp.maximum(i - steps // 2, 0), 0))
+    return pl.pallas_call(
+        sum_kernel,
+        grid=(steps,),
+        in_specs=[pl.BlockSpec(block, lambda i: (i, 0)), top, top, bottom, bottom],
+        out_specs=pl.BlockSpec(block, lambda i: (i, 0)),
+        out_shape=jax.ShapeDtypeStruct(own.shape, BF16),
+        compiler_params=pltpu.CompilerParams(vmem_limit_bytes=16 * 2**20),
+    )(own, home_top, last_top, home_bottom, last_bottom)
+
+
+def dispatch_kernel(slots, tokens_ref, routes_ref, send_ref, place_ref):
+    count = tokens_ref.shape[0]
+    places = send_ref.shape[0]
+    normed = layer_norm(tokens_ref[...].astype(F32)).astype(BF16)
+    first, second = routes_ref[:, 0:1], routes_ref[:, 1:2]
+    names = lax.broadcasted_iota(jnp.int32, (count, places // slots), 1)
+    hot_first = (first == names).astype(F32)
+    hot_second = (second == names).astype(F32)
+    row_ids = lax.broadcasted_iota(jnp.int32, (count, count), 0)
+    before = (lax.broadcasted_iota(jnp.int32, (count, count), 1) < row_ids).astype(F32).astype(BF16)
+    rank_first = jnp.dot(before, hot_first.astype(BF16), preferred_element_type=F32)
+    rank_second = jnp.dot(before, hot_second.astype(BF16), preferred_element_type=F32)
+    rank_second = rank_second + jnp.sum(hot_first, axis=0, keepdims=True)
+    rank_first = jnp.sum(rank_first * hot_first, axis=1, keepdims=True)
+    rank_second = jnp.sum(rank_second * hot_second, axis=1, keepdims=True)
+    place_first = first * slots + rank_first.astype(jnp.int32)
+    place_second = second * slots + rank_second.astype(jnp.int32)
+    place_ref[:, 0:1] = place_first
+    place_ref[:, 1:2] = place_second
+    spots = lax.broadcasted_iota(jnp.int32, (count, places), 1)
+    chosen = ((spots == place_first) | (spots == place_second)).astype(F32)
+    send = jnp.dot(chosen.T.astype(BF16), normed, preferred_element_type=F32)
+    send_ref[...] = send.astype(BF16)
+
+
+def dispatch(tokens, routes, places, slots):
+    return pl.pallas_call(
+        functools.partial(dispatch_kernel, slots),
+        out_shape=[
+            jax.ShapeDtypeStruct((places, tokens.shape[1]), BF16),
+            jax.ShapeDtypeStruct(routes.shape, jnp.int32),
+        ],
+        compiler_params=pltpu.CompilerParams(vmem_limit_bytes=16 * 2**20),
+    )(tokens, routes)
 
 
 def split_pair(values):
@@ -92,11 +168,6 @@
         y, z, core = target(y, z, core)
         pairs.append((index, (y % wide * deep + z % deep) * cores + core % cores))
     return lax.ppermute(values, "expert", pairs)
-
-
-def along_y(mine, shape):
-    others = [moved(mine, lambda y, z, c, k=k: (y + k, z, c), shape) for k in range(1, shape[0])]
-    return jnp.concatenate([mine] + others, axis=0)
 
 
 def along_expert(mine, shape):
@@ -114,21 +185,6 @@
     return jnp.concatenate([group, moved(group, lambda y, z, c: (y, z, c + 1), shape)], axis=0)
 
 
-def along_z(group, both, shape):
-    deep = shape[1]
-    here = [
-        moved(both, lambda y, z, c, k=k: (y, z + (k if c == 0 else -k), c), shape)
-        for k in range(1, deep // 2)
-    ]
-    here.append(moved(group, lambda y, z, c: (y, z + deep // 2, c), shape))
-    return jnp.concatenate(here, axis=0)
-
-
-def last_swap(both, here, shape):
-    other = moved(here, lambda y, z, c: (y, z, c + 1), shape)
-    return jnp.concatenate([both, here, other], axis=0)
-
-
 def ring_shift(values, step, size):
     return lax.ppermute(values, "grid", [(i, (i + step) % size) for i in range(size)])
 
@@ -153,28 +209,12 @@
     chip = lax.axis_index("expert") // shape[2]
 
     stream = tokens.astype(F32)
-    normed = layer_norm(stream).astype(BF16)
-    first, second = routes[:, 0:1], routes[:, 1:2]
-    names = jnp.arange(experts_all, dtype=jnp.int32)[None, :]
-    hot_first = first == names
-    hot_second = second == names
-    both_hot = jnp.concatenate([hot_first, hot_second], axis=1).astype(BF16)
+    send, place = dispatch(tokens, routes, places_all, slots)
+    spots = jnp.arange(places_all, dtype=jnp.int32)[None, :]
+    at_first = spots == place[:, 0:1]
+    at_second = spots == place[:, 1:2]
     order = jnp.arange(token_count, dtype=jnp.int32)
-    before = (order[None, :] < order[:, None]).astype(BF16)
-    ranks = jnp.dot(before, both_hot, preferred_element_type=F32)
-    totals = jnp.sum(hot_first.astype(F32), axis=0, keepdims=True)
-    rank_first = jnp.sum(jnp.where(hot_first, ranks[:, :experts_all], 0.0), axis=1, keepdims=True)
-    rank_second = jnp.sum(
-        jnp.where(hot_second, ranks[:, experts_all:] + totals, 0.0), axis=1, keepdims=True
-    )
-    place_first = first * slots + rank_first.astype(jnp.int32)
-    place_second = second * slots + rank_second.astype(jnp.int32)
-    spots = jnp.arange(places_all, dtype=jnp.int32)[None, :]
-    at_first = spots == place_first
-    at_second = spots == place_second
-    chosen = (at_first | at_second).astype(BF16)
-    send = lax.dot_general(chosen, normed, (((0,), (0,)), ((), ())), preferred_element_type=F32)
-    send = send.astype(BF16).reshape(experts_all, slots, width)
+    send = send.reshape(experts_all, slots, width)
     arrived = lax.all_to_all(send, "expert", split_axis=0, concat_axis=0, tiled=True)
     rows = arrived.reshape(places_all, width)
 
@@ -184,32 +224,37 @@
     top, bottom = rows[:half], rows[half:]
     left_top = ring_shift(top, 1, grid_all)
     right_bottom = ring_shift(bottom, -1, grid_all)
-    own_term = expert_part(rows, up_local, down_local)
-    own_term, top, bottom = held(own_term, top, bottom)
+    own_term = expert_part([rows], up_local, down_local)[0]
+    own_term, top, bottom, left_top, right_bottom = held(
+        own_term, top, bottom, left_top, right_bottom
+    )
     left_bottom = ring_shift(bottom, 1, grid_all)
     right_top = ring_shift(top, -1, grid_all)
     far_top = ring_shift(left_top, 1, grid_all)
     far_bottom = ring_shift(right_bottom, -1, grid_all)
-    left_top = expert_part(left_top, up_local, down_local)
-    right_bottom = expert_part(right_bottom, up_local, down_local)
-    far_top = expert_part(far_top, up_local, down_local)
-    far_bottom = expert_part(far_bottom, up_local, down_local)
+    left_top, right_bottom = expert_part([left_top, right_bottom], up_local, down_local)
+    home_top = ring_shift(left_top, -1, grid_all)
+    home_bottom = ring_shift(right_bottom, 1, grid_all)
+    right_top, left_bottom, left_top, right_bottom = held(
+        right_top, left_bottom, left_top, right_bottom
+    )
+    right_top, left_bottom = expert_part([right_top, left_bottom], up_local, down_local)
+    far_top, far_bottom, left_top, right_bottom, right_top, left_bottom = held(
+        far_top, far_bottom, left_top, right_bottom, right_top, left_bottom
+    )
+    far_top, far_bottom = expert_part([far_top, far_bottom], up_local, down_local)
     far_from_left = ring_shift(far_top, 1, grid_all)
     far_from_right = ring_shift(far_bottom, -1, grid_all)
-    left_top, right_bottom, far_bottom = held(left_top, right_bottom, far_bottom)
-    home_top = ring_shift(left_top, -1, grid_all)
-    home_bottom = ring_shift(right_bottom, 1, grid_all)
-    right_top = expert_part(right_top, up_local, down_local)
-    left_bottom = expert_part(left_bottom, up_local, down_local)
+    far_from_left, far_from_right, home_top, home_bottom = held(
+        far_from_left, far_from_right, home_top, home_bottom
+    )
     right_top = (right_top.astype(F32) + far_from_left.astype(F32)).astype(BF16)
     left_bottom = (left_bottom.astype(F32) + far_from_right.astype(F32)).astype(BF16)
     last_top = ring_shift(right_top, 1, grid_all)
     last_bottom = ring_shift(left_bottom, -1, grid_all)
     right_top, left_bottom, picture_later = held(right_top, left_bottom, picture_unit)
     picture_column = along_expert(picture_later, shape)
-    total_top = own_term[:half].astype(F32) + home_top.astype(F32) + last_top.astype(F32)
-    total_bottom = own_term[half:].astype(F32) + home_bottom.astype(F32) + last_bottom.astype(F32)
-    total = jnp.concatenate([total_top, total_bottom], axis=0).astype(BF16)
+    total = sum_terms(own_term, home_top, last_top, home_bottom, last_bottom)
     total, picture_column = held(total, picture_column)
     results = total.reshape(experts_all, slots, width)
     returned = lax.all_to_all(results, "expert", split_axis=0, concat_axis=0, tiled=True)
@@ -241,10 +286,7 @@
     text_embed = unit_rows(pooled)
     text_unit = (text_embed / scale_root).astype(BF16)
 
-    text_group = along_y(text_unit, shape)
-    text_both = on_chip(text_group, shape)
-    text_here = along_z(text_group, text_both, shape)
-    text_column = last_swap(text_both, text_here, shape)
+    text_column = along_expert(text_unit, shape)
 
     def slopes(mine, others, place):
         logits = SIMILARITY_HEAT * lax.dot_general(
@@ -256,7 +298,7 @@
         return weighted_sum(pair_slope(logits, same), others)
 
     sentence_slope = slopes(text_unit, pictures_all, chip * captions_here)
-    partial = slopes(pictures_row, text_column, 0).reshape(grid_all, captions_here, width)
+    partial = slopes(pictures_row, text_column, chip * captions_here).reshape(grid_all, captions_here, width)
     picture_slope = partial[0]
     for k in range(1, grid_all):
         picture_slope = picture_slope + ring_shift(partial[k], -k, grid_all)

time: 216 us -> 214 us (level)
  blocking collectives: 18 us -> 39.4 us
  Pallas kernels: 44.5 us -> 36.2 us
  starting transfers between devices: 58.6 us -> 51.6 us
  other arithmetic: 12.1 us -> 6.01 us
  waiting for transfers between devices: 69.9 us -> 67 us
    all_to_all x1, blocking collectives: 18 us -> 39.4 us  [on_device(): lax.all_to_all(send, 'expert', split_axis=0, concat_axis=0, tiled=True)]
    ppermute x10 -> x2, starting transfers between devices: 15 us -> 0.1 us  [moved(): return lax.ppermute(values, 'expert', pairs)]
    ppermute x18, waiting for transfers between devices: 33 us -> 46.8 us  [ring_shift(): lax.ppermute(values, 'grid', [(i, (i + step) % size) for i in range(size)])]
    all_to_all x1 -> x2, waiting for transfers between devices: 27.7 us -> 19.1 us  [along_expert(): lax.all_to_all(copies, 'expert', split_axis=0, concat_axis=0, axis_index_...]
    pallas_call x7 -> x6, Pallas kernels: 44.5 us -> 36.2 us  [the longest x4 33.5 us: expert_part(): pl.pallas_call(expert_kernel, grid=(units // tile,), in_specs=whole + [pl...]
    ppermute x10 -> x2, waiting for transfers between devices: 9.16 us -> 1.11 us  [moved(): return lax.ppermute(values, 'expert', pairs)]
    all_to_all x1 -> x2, starting transfers between devices: 11.8 us -> 18.2 us  [along_expert(): lax.all_to_all(copies, 'expert', split_axis=0, concat_axis=0, axis_index_...]
    dot_general x2 -> x0, matrix products: 2.67 us -> none  [the longest x1 2.52 us: on_device(): lax.dot_general(chosen, normed, (((0,), (0,)), ((), ())), preferred_eleme...]
  transfers between devices with their start and end apart: 30 -> 23, of which waited for: 12 -> 15; matrix products, arithmetic and copies ran while one was open for 4% -> 2% of each run, Pallas kernels for 21% -> 16%
where the time goes in v2:
time: 214 us
  waiting for transfers between devices  67 us (31%)
  starting transfers between devices  51.6 us (24%)
  blocking collectives  39.4 us (18%)
  Pallas kernels  36.2 us (17%)
  local copies, waits for them, and re-layouts  7.05 us (3%)
  other arithmetic  6.01 us (3%)
  matrix products  5.34 us (2%)
    ppermute x18, waiting for transfers between devices, ring_shift(): lax.ppermute(values, 'grid', [(i, (i + step) % size) for i in range(size)])  46.8 us
    all_to_all x1, blocking collectives, on_device(): lax.all_to_all(send, 'expert', split_axis=0, concat_axis=0, tiled=True)  39.4 us
    pallas_call x4, Pallas kernels, expert_part(): pl.pallas_call(expert_kernel, grid=(units // tile,), in_specs=whole + [pl...  33.5 us
    ppermute x18, starting transfers between devices, ring_shift(): lax.ppermute(values, 'grid', [(i, (i + step) % size) for i in range(size)])  23 us
    all_to_all x2, waiting for transfers between devices, along_expert(): lax.all_to_all(copies, 'expert', split_axis=0, concat_axis=0, axis_index_...  19.1 us
    all_to_all x2, starting transfers between devices, along_expert(): lax.all_to_all(copies, 'expert', split_axis=0, concat_axis=0, axis_index_...  18.2 us
    all_to_all x1, starting transfers between devices, on_device(): lax.all_to_all(results, 'expert', split_axis=0, concat_axis=0, tiled=True)  10.4 us
    unnamed x40, local copies, waits for them, and re-layouts  4.39 us
  transfers between devices with their start and end apart: 23, of which 15 were waited for; matrix products, arithmetic and copies ran while one was open for 2% of the time, Pallas kernels for 16%

profile of v2, /device:TPU:32, one launch (start us, length us, event | category | flops | bytes accessed | tf_op | source)
XLA Modules:
  0.0 213.6 jit_solution(6284140283327061076)
XLA Ops:
  0.6 0.8 copy.12.routes_ref
  1.4 0.9 copy-done
  2.4 0.9 shard_map.103
  3.3 39.4 %all_to_all.20 = bf16[64,8,1024]{2,1,0:T(8,128)(2,1)S(1)} all-to-all(bf16[64,8,1024]{2,1,0:T(8,128)(2,1)S(1)} %bitcast.36), channel_id=1, replica_groups=mesh['expert'=64,'grid'=4] {'expert'}, dimensions={0} | all-to-all | bytes 2097152 | tf_op jit(solution)/shard_map/all_to_all | solution.py:218
  42.8 2.8 %collective-permute-start.1 = (bf16[256,1024]{1,0:T(8,128)(2,1)S(1)}, bf16[256,1024]{1,0:T(8,128)(2,1)S(1)}, u32[]{:S(2)}, u32[]{:S(2)}) collective-permute-start(bf16[256,1024]{1,0:T(8,128)(2,1)S(1)} %get-tuple-element.38), channel_id=1, source_target_pairs={{0,3},{1,0},{2,1},{3,2},{4,7},{5,4},{6,5},{7,6},{8,11},{9,8},{10,9... | collective-permute-start | bytes 1572872 | tf_op jit(solution)/shard_map/ppermute | solution.py:189
  45.6 8.3 %shard_map.104.own_ref = bf16[512,1024]{1,0:T(8,128)(2,1)} custom-call(bf16[512,1024]{1,0:T(8,128)(2,1)} %bitcast.38, bf16[1024,1024]{1,0:T(8,128)(2,1)} %bitcast.42, bf16[1024,1024]{1,0:T(8,128)(2,1)} %bitcast.46), custom_call_target="tpu_custom_call" | custom-call | flops 8589934592 | bytes 6291456 | tf_op jit(solution)/shard_map/pallas_call | solution.py:55
  54.0 3.0 %collective-permute-done.1.refs_1_ = bf16[256,1024]{1,0:T(8,128)(2,1)S(1)} collective-permute-done((bf16[256,1024]{1,0:T(8,128)(2,1)S(1)}, bf16[256,1024]{1,0:T(8,128)(2,1)S(1)}, u32[]{:S(2)}, u32[]{:S(2)}) %collective-permute-start.1) | collective-permute-done | bytes 524320 | tf_op jit(solution)/shard_map/ppermute | solution.py:189
  57.0 3.4 %collective-permute-done.refs_0_ = bf16[256,1024]{1,0:T(8,128)(2,1)S(1)} collective-permute-done((bf16[256,1024]{1,0:T(8,128)(2,1)S(1)}, bf16[256,1024]{1,0:T(8,128)(2,1)S(1)}, u32[]{:S(2)}, u32[]{:S(2)}) %collective-permute-start) | collective-permute-done | bytes 524320 | tf_op jit(solution)/shard_map/ppermute | solution.py:189
  60.4 0.4 collective-permute-start.4
  60.8 1.7 collective-permute-start.5
  62.5 3.2 %collective-permute-start.3 = (bf16[256,1024]{1,0:T(8,128)(2,1)S(1)}, bf16[256,1024]{1,0:T(8,128)(2,1)S(1)}, u32[]{:S(2)}, u32[]{:S(2)}) collective-permute-start(bf16[256,1024]{1,0:T(8,128)(2,1)S(1)} %collective-permute-done.1.refs_1_), channel_id=1, source_target_pairs={{0,3},{1,0},{2,1},{3,2},{4,7},{5,4},{6,5},{7,6},{8,11},{9,8},{10,9... | collective-permute-start | bytes 1572872 | tf_op jit(solution)/shard_map/ppermute | solution.py:189
  65.7 8.4 %shard_map.105 = (bf16[256,1024]{1,0:T(8,128)(2,1)}, bf16[256,1024]{1,0:T(8,128)(2,1)}) custom-call(bf16[256,1024]{1,0:T(8,128)(2,1)} %copy-done.12, bf16[256,1024]{1,0:T(8,128)(2,1)} %copy-done.11, bf16[1024,1024]{1,0:T(8,128)(2,1)} %bitcast.43, bf16[1024,1024]{1,0:T(8,128)(2,1)} %bitcast.47), custom_call_target="tpu_custom_call" | custom-call | flops 8589934592 | bytes 6291456 | tf_op jit(solution)/shard_map/pallas_call | solution.py:55
  74.0 0.4 collective-permute-start.8
  74.4 0.8 collective-permute-done.4.refs_0_
  75.2 0.9 collective-permute-start.9
  76.1 0.7 collective-permute-done.5.refs_1_
  76.8 0.8 copy-done.16
  77.6 8.3 %shard_map.106 = (bf16[256,1024]{1,0:T(8,128)(2,1)}, bf16[256,1024]{1,0:T(8,128)(2,1)}) custom-call(bf16[256,1024]{1,0:T(8,128)(2,1)} %copy-done.15, bf16[256,1024]{1,0:T(8,128)(2,1)} %copy-done.16, bf16[1024,1024]{1,0:T(8,128)(2,1)} %bitcast.44, bf16[1024,1024]{1,0:T(8,128)(2,1)} %bitcast.48), custom_call_target="tpu_custom_call" | custom-call | flops 8589934592 | bytes 6291456 | tf_op jit(solution)/shard_map/pallas_call | solution.py:55
  85.9 2.1 collective-permute-done.2.refs_0_
  88.0 0.8 copy-done.13
  88.8 0.2 copy-done.14
  89.0 8.4 %shard_map.107 = (bf16[256,1024]{1,0:T(8,128)(2,1)}, bf16[256,1024]{1,0:T(8,128)(2,1)}) custom-call(bf16[256,1024]{1,0:T(8,128)(2,1)} %copy-done.13, bf16[256,1024]{1,0:T(8,128)(2,1)} %copy-done.14, bf16[1024,1024]{1,0:T(8,128)(2,1)} %bitcast.45, bf16[1024,1024]{1,0:T(8,128)(2,1)} %bitcast.49), custom_call_target="tpu_custom_call" | custom-call | flops 8589934592 | bytes 6291456 | tf_op jit(solution)/shard_map/pallas_call | solution.py:55
  97.5 0.5 collective-permute-start.6
  97.9 2.8 %collective-permute-start.7 = (bf16[256,1024]{1,0:T(8,128)(2,1)}, bf16[256,1024]{1,0:T(8,128)(2,1)S(1)}, u32[]{:S(2)}, u32[]{:S(2)}) collective-permute-start(bf16[256,1024]{1,0:T(8,128)(2,1)} %get-tuple-element.48), channel_id=1, source_target_pairs={{0,3},{1,0},{2,1},{3,2},{4,7},{5,4},{6,5},{7,6},{8,11},{9,8},{10,9... | collective-permute-start | bytes 1572872 | tf_op jit(solution)/shard_map/ppermute | solution.py:189
  100.9 7.7 %collective-permute-done.6 = bf16[256,1024]{1,0:T(8,128)(2,1)S(1)} collective-permute-done((bf16[256,1024]{1,0:T(8,128)(2,1)}, bf16[256,1024]{1,0:T(8,128)(2,1)S(1)}, u32[]{:S(2)}, u32[]{:S(2)}) %collective-permute-start.6) | collective-permute-done | bytes 524320 | tf_op jit(solution)/shard_map/ppermute | solution.py:189
  108.6 1.0 add_convert_fusion
  109.6 1.0 add_convert_fusion.1
  110.6 0.8 broadcast_in_dim.65
  111.4 8.2 %all-to-all-start.1 = ((bf16[32,4,1024]{2,1,0:T(4,128)(2,1)}), bf16[32,4,1024]{2,1,0:T(4,128)(2,1)S(1)}, u32[]{:S(2)}, u32[]{:S(2)}) async-start(bf16[32,4,1024]{2,1,0:T(4,128)(2,1)} %broadcast_in_dim.65), calls=%async_computation.1 | async-start | bytes 524288 | tf_op jit(solution)/shard_map/all_to_all | solution.py:178
  119.7 3.2 %collective-permute-start.11 = (bf16[256,1024]{1,0:T(8,128)(2,1)}, bf16[256,1024]{1,0:T(8,128)(2,1)S(1)}, u32[]{:S(2)}, u32[]{:S(2)}) collective-permute-start(bf16[256,1024]{1,0:T(8,128)(2,1)} %add_convert_fusion), channel_id=1, source_target_pairs={{0,3},{1,0},{2,1},{3,2},{4,7},{5,4},{6,5},{7,6},{8,11},{9,8},{10,9... | collective-permute-start | bytes 1572872 | tf_op jit(solution)/shard_map/ppermute | solution.py:189
  122.9 7.7 %all-to-all-done.1 = bf16[32,4,1024]{2,1,0:T(4,128)(2,1)S(1)} async-done(((bf16[32,4,1024]{2,1,0:T(4,128)(2,1)}), bf16[32,4,1024]{2,1,0:T(4,128)(2,1)S(1)}, u32[]{:S(2)}, u32[]{:S(2)}) %all-to-all-start.1) | async-done | bytes 262176 | tf_op jit(solution)/shard_map/all_to_all | solution.py:178
  130.6 0.8 reshape.108
  131.4 0.3 collective-permute-done.10.last_top
  131.7 1.8 shard_map.108
  133.5 10.4 %all-to-all-start.2 = ((bf16[64,8,1024]{2,1,0:T(8,128)(2,1)}), bf16[64,8,1024]{2,1,0:T(8,128)(2,1)}, u32[]{:S(2)}, u32[]{:S(2)}) async-start(bf16[64,8,1024]{2,1,0:T(8,128)(2,1)} %bitcast.11), calls=%async_computation.2 | async-start | bytes 2097152 | tf_op jit(solution)/shard_map/all_to_all | solution.py:260
  143.9 0.2 reduce-window.7
  144.1 0.2 slice_reduce_fusion.1
  144.3 3.0 %collective-permute-start.15 = (bf16[256,1024]{1,0:T(8,128)(2,1)S(1)}, bf16[256,1024]{1,0:T(8,128)(2,1)S(1)}, u32[]{:S(2)}, u32[]{:S(2)}) collective-permute-start(bf16[256,1024]{1,0:T(8,128)(2,1)S(1)} %pad_maximum_fusion.1), channel_id=1, source_target_pairs={{0,3},{1,0},{2,1},{3,2},{4,7},{5,4},{6,5},{7,6},{8,11},{9,8},{10,9... | collective-permute-start | bytes 1572872 | tf_op jit(solution)/shard_map/ppermute | solution.py:189
  147.3 1.1 collective-permute-start.13
  148.5 21.6 %collective-permute-done.15 = bf16[256,1024]{1,0:T(8,128)(2,1)S(1)} collective-permute-done((bf16[256,1024]{1,0:T(8,128)(2,1)S(1)}, bf16[256,1024]{1,0:T(8,128)(2,1)S(1)}, u32[]{:S(2)}, u32[]{:S(2)}) %collective-permute-start.15) | collective-permute-done | bytes 524320 | tf_op jit(solution)/shard_map/ppermute | solution.py:189
  170.0 3.4 %collective-permute-done.13 = bf16[256,1024]{1,0:T(8,128)(2,1)S(1)} collective-permute-done((bf16[256,1024]{1,0:T(8,128)(2,1)S(1)}, bf16[256,1024]{1,0:T(8,128)(2,1)S(1)}, u32[]{:S(2)}, u32[]{:S(2)}) %collective-permute-start.13) | collective-permute-done | bytes 524320 | tf_op jit(solution)/shard_map/ppermute | solution.py:189
  173.5 0.8 copy-done.5
  174.3 1.4 pad_maximum_fusion
  175.7 1.6 convolution_add_fusion.1
  177.3 1.7 fusion.57
  179.1 0.2 multiply_reduce_fusion
  179.3 0.5 multiply_reduce_fusion.1
  179.8 0.7 multiply_convert_fusion
  180.5 0.8 broadcast_in_dim.70
  181.3 9.9 %all-to-all-start.3 = ((bf16[32,4,1024]{2,1,0:T(4,128)(2,1)}), bf16[32,4,1024]{2,1,0:T(4,128)(2,1)S(1)}, u32[]{:S(2)}, u32[]{:S(2)}) async-start(bf16[32,4,1024]{2,1,0:T(4,128)(2,1)} %broadcast_in_dim.70), calls=%async_computation.3 | async-start | bytes 524288 | tf_op jit(solution)/shard_map/all_to_all | solution.py:178
  191.2 0.7 subtract_convert_fusion.3
  191.9 11.5 %all-to-all-done.3 = bf16[32,4,1024]{2,1,0:T(4,128)(2,1)S(1)} async-done(((bf16[32,4,1024]{2,1,0:T(4,128)(2,1)}), bf16[32,4,1024]{2,1,0:T(4,128)(2,1)S(1)}, u32[]{:S(2)}, u32[]{:S(2)}) %all-to-all-start.3) | async-done | bytes 262176 | tf_op jit(solution)/shard_map/all_to_all | solution.py:178
  203.5 0.4 fusion.38
  204.0 1.1 collective-permute-done.16
  205.1 0.3 subtract_convert_fusion.2
  205.4 0.2 fusion.42
  205.6 0.3 collective-permute-start.17
  205.9 1.8 collective-permute-start.19
  207.7 0.8 collective-permute-start.18
  208.5 0.6 fusion.37
  209.2 0.3 collective-permute-done.17
  209.4 1.4 collective-permute-done.19
  210.8 2.1 collective-permute-done.18
  212.9 0.6 fusion.36
  (69 shorter events, 0.8 us)
Async XLA Ops:
  1.4 0.9 copy-start
  42.7 2.9 %copy-start.3 = (bf16[64,8,1024]{2,1,0:T(8,128)(2,1)}, bf16[64,8,1024]{2,1,0:T(8,128)(2,1)S(1)}, u32[]{:S(2)}) copy-start(bf16[64,8,1024]{2,1,0:T(8,128)(2,1)S(1)} %all_to_all.20) | copy-start | bytes 3145732
  42.8 14.2 %collective-permute-start.1 = (bf16[256,1024]{1,0:T(8,128)(2,1)S(1)}, bf16[256,1024]{1,0:T(8,128)(2,1)S(1)}, u32[]{:S(2)}, u32[]{:S(2)}) collective-permute-start(bf16[256,1024]{1,0:T(8,128)(2,1)S(1)} %get-tuple-element.38), channel_id=1, source_target_pairs={{0,3},{1,0},{2,1},{3,2},{4,7},{5,4},{6,5},{7,6},{8,11},{9,8},{10,9... | collective-permute-start | bytes 1572872 | tf_op jit(solution)/shard_map/ppermute | solution.py:189
  45.6 14.8 %collective-permute-start = (bf16[256,1024]{1,0:T(8,128)(2,1)S(1)}, bf16[256,1024]{1,0:T(8,128)(2,1)S(1)}, u32[]{:S(2)}, u32[]{:S(2)}) collective-permute-start(bf16[256,1024]{1,0:T(8,128)(2,1)S(1)} %get-tuple-element.37), channel_id=1, source_target_pairs={{0,1},{1,2},{2,3},{3,0},{4,5},{5,6},{6,7},{7,4},{8,9},{9,10},{10,1... | collective-permute-start | bytes 1572872 | tf_op jit(solution)/shard_map/ppermute | solution.py:189
  57.0 8.7 %copy-start.11 = (bf16[256,1024]{1,0:T(8,128)(2,1)}, bf16[256,1024]{1,0:T(8,128)(2,1)S(1)}, u32[]{:S(2)}) copy-start(bf16[256,1024]{1,0:T(8,128)(2,1)S(1)} %collective-permute-done.1.refs_1_) | copy-start | bytes 1572868
  60.4 5.3 %copy-start.12 = (bf16[256,1024]{1,0:T(8,128)(2,1)}, bf16[256,1024]{1,0:T(8,128)(2,1)S(1)}, u32[]{:S(2)}) copy-start(bf16[256,1024]{1,0:T(8,128)(2,1)S(1)} %collective-permute-done.refs_0_) | copy-start | bytes 1572868
  60.4 14.8 %collective-permute-start.4 = (bf16[256,1024]{1,0:T(8,128)(2,1)S(1)}, bf16[256,1024]{1,0:T(8,128)(2,1)S(1)}, u32[]{:S(2)}, u32[]{:S(2)}) collective-permute-start(bf16[256,1024]{1,0:T(8,128)(2,1)S(1)} %get-tuple-element.37), channel_id=1, source_target_pairs={{0,3},{1,0},{2,1},{3,2},{4,7},{5,4},{6,5},{7,6},{8,11},{9,8},{10,9... | collective-permute-start | bytes 1572872 | tf_op jit(solution)/shard_map/ppermute | solution.py:189
  60.8 16.0 %collective-permute-start.5 = (bf16[256,1024]{1,0:T(8,128)(2,1)S(1)}, bf16[256,1024]{1,0:T(8,128)(2,1)S(1)}, u32[]{:S(2)}, u32[]{:S(2)}) collective-permute-start(bf16[256,1024]{1,0:T(8,128)(2,1)S(1)} %get-tuple-element.38), channel_id=1, source_target_pairs={{0,1},{1,2},{2,3},{3,0},{4,5},{5,6},{6,7},{7,4},{8,9},{9,10},{10,1... | collective-permute-start | bytes 1572872 | tf_op jit(solution)/shard_map/ppermute | solution.py:189
  62.4 25.6 %collective-permute-start.2 = (bf16[256,1024]{1,0:T(8,128)(2,1)S(1)}, bf16[256,1024]{1,0:T(8,128)(2,1)S(1)}, u32[]{:S(2)}, u32[]{:S(2)}) collective-permute-start(bf16[256,1024]{1,0:T(8,128)(2,1)S(1)} %collective-permute-done.refs_0_), channel_id=1, source_target_pairs={{0,1},{1,2},{2,3},{3,0},{4,5},{5,6},{6,7},{7,4},{8,9},{9,10},{10,1... | collective-permute-start | bytes 1572872 | tf_op jit(solution)/shard_map/ppermute | solution.py:189
  62.5 25.6 %collective-permute-start.3 = (bf16[256,1024]{1,0:T(8,128)(2,1)S(1)}, bf16[256,1024]{1,0:T(8,128)(2,1)S(1)}, u32[]{:S(2)}, u32[]{:S(2)}) collective-permute-start(bf16[256,1024]{1,0:T(8,128)(2,1)S(1)} %collective-permute-done.1.refs_1_), channel_id=1, source_target_pairs={{0,3},{1,0},{2,1},{3,2},{4,7},{5,4},{6,5},{7,6},{8,11},{9,8},{10,9... | collective-permute-start | bytes 1572872 | tf_op jit(solution)/shard_map/ppermute | solution.py:189
  74.0 26.9 %collective-permute-start.8 = (bf16[256,1024]{1,0:T(8,128)(2,1)}, bf16[256,1024]{1,0:T(8,128)(2,1)S(1)}, u32[]{:S(2)}, u32[]{:S(2)}) collective-permute-start(bf16[256,1024]{1,0:T(8,128)(2,1)} %get-tuple-element.39), channel_id=1, source_target_pairs={{0,3},{1,0},{2,1},{3,2},{4,7},{5,4},{6,5},{7,6},{8,11},{9,8},{10,9... | collective-permute-start | bytes 1572872 | tf_op jit(solution)/shard_map/ppermute | solution.py:189
  75.2 1.6 copy-start.15
  75.2 25.7 %collective-permute-start.9 = (bf16[256,1024]{1,0:T(8,128)(2,1)}, bf16[256,1024]{1,0:T(8,128)(2,1)S(1)}, u32[]{:S(2)}, u32[]{:S(2)}) collective-permute-start(bf16[256,1024]{1,0:T(8,128)(2,1)} %get-tuple-element.40), channel_id=1, source_target_pairs={{0,1},{1,2},{2,3},{3,0},{4,5},{5,6},{6,7},{7,4},{8,9},{9,10},{10,1... | collective-permute-start | bytes 1572872 | tf_op jit(solution)/shard_map/ppermute | solution.py:189
  76.8 0.8 copy-start.16
  88.0 0.8 copy-start.13
  88.0 1.0 copy-start.14
  89.0 11.7 %copy-start.9 = (bf16[4,1024]{1,0:T(4,128)(2,1)S(1)}, bf16[4,1024]{1,0:T(4,128)(2,1)}, u32[]{:S(2)}) copy-start(bf16[4,1024]{1,0:T(4,128)(2,1)} %param.12) | copy-start | bytes 24580
  89.0 19.6 %copy-start.8 = (bf16[256,1024]{1,0:T(8,128)(2,1)S(1)}, bf16[256,1024]{1,0:T(8,128)(2,1)}, u32[]{:S(2)}) copy-start(bf16[256,1024]{1,0:T(8,128)(2,1)} %get-tuple-element.53) | copy-start | bytes 1572868
  89.0 20.6 %copy-start.7 = (bf16[256,1024]{1,0:T(8,128)(2,1)S(1)}, bf16[256,1024]{1,0:T(8,128)(2,1)}, u32[]{:S(2)}) copy-start(bf16[256,1024]{1,0:T(8,128)(2,1)} %get-tuple-element.50) | copy-start | bytes 1572868
  97.5 11.2 %collective-permute-start.6 = (bf16[256,1024]{1,0:T(8,128)(2,1)}, bf16[256,1024]{1,0:T(8,128)(2,1)S(1)}, u32[]{:S(2)}, u32[]{:S(2)}) collective-permute-start(bf16[256,1024]{1,0:T(8,128)(2,1)} %get-tuple-element.47), channel_id=1, source_target_pairs={{0,1},{1,2},{2,3},{3,0},{4,5},{5,6},{6,7},{7,4},{8,9},{9,10},{10,1... | collective-permute-start | bytes 1572872 | tf_op jit(solution)/shard_map/ppermute | solution.py:189
  97.9 10.7 %collective-permute-start.7 = (bf16[256,1024]{1,0:T(8,128)(2,1)}, bf16[256,1024]{1,0:T(8,128)(2,1)S(1)}, u32[]{:S(2)}, u32[]{:S(2)}) collective-permute-start(bf16[256,1024]{1,0:T(8,128)(2,1)} %get-tuple-element.48), channel_id=1, source_target_pairs={{0,3},{1,0},{2,1},{3,2},{4,7},{5,4},{6,5},{7,6},{8,11},{9,8},{10,9... | collective-permute-start | bytes 1572872 | tf_op jit(solution)/shard_map/ppermute | solution.py:189
  100.9 30.8 %copy-start.2 = (bf16[512,1024]{1,0:T(8,128)(2,1)S(1)}, bf16[512,1024]{1,0:T(8,128)(2,1)}, u32[]{:S(2)}) copy-start(bf16[512,1024]{1,0:T(8,128)(2,1)} %shard_map.104.own_ref) | copy-start | bytes 3145732
  111.4 19.2 %all-to-all-start.1 = ((bf16[32,4,1024]{2,1,0:T(4,128)(2,1)}), bf16[32,4,1024]{2,1,0:T(4,128)(2,1)S(1)}, u32[]{:S(2)}, u32[]{:S(2)}) async-start(bf16[32,4,1024]{2,1,0:T(4,128)(2,1)} %broadcast_in_dim.65), calls=%async_computation.1 | async-start | bytes 524288 | tf_op jit(solution)/shard_map/all_to_all | solution.py:178
  119.6 12.1 %collective-permute-start.10 = (bf16[256,1024]{1,0:T(8,128)(2,1)}, bf16[256,1024]{1,0:T(8,128)(2,1)S(1)}, u32[]{:S(2)}, u32[]{:S(2)}) collective-permute-start(bf16[256,1024]{1,0:T(8,128)(2,1)} %add_convert_fusion.1), channel_id=1, source_target_pairs={{0,1},{1,2},{2,3},{3,0},{4,5},{5,6},{6,7},{7,4},{8,9},{9,10},{10,1... | collective-permute-start | bytes 1572872 | tf_op jit(solution)/shard_map/ppermute | solution.py:189
  119.7 12.0 %collective-permute-start.11 = (bf16[256,1024]{1,0:T(8,128)(2,1)}, bf16[256,1024]{1,0:T(8,128)(2,1)S(1)}, u32[]{:S(2)}, u32[]{:S(2)}) collective-permute-start(bf16[256,1024]{1,0:T(8,128)(2,1)} %add_convert_fusion), channel_id=1, source_target_pairs={{0,3},{1,0},{2,1},{3,2},{4,7},{5,4},{6,5},{7,6},{8,11},{9,8},{10,9... | collective-permute-start | bytes 1572872 | tf_op jit(solution)/shard_map/ppermute | solution.py:189
  131.4 2.1 copy-start.6
  131.4 2.1 collective-permute-start.12
  133.5 10.5 %copy-start.18 = (s32[1,4]{1,0:T(1,128)S(1)}, s32[1,4]{1,0:T(1,128)}, u32[]{:S(2)}) copy-start(s32[1,4]{1,0:T(1,128)} %param.11) | copy-start | bytes 52
  133.5 15.0 %copy-start.10 = (f32[128,2]{0,1:T(2,128)S(1)}, f32[128,2]{0,1:T(2,128)}, u32[]{:S(2)}) copy-start(f32[128,2]{0,1:T(2,128)} %param.10) | copy-start | bytes 3076
  133.5 42.2 %all-to-all-start.2 = ((bf16[64,8,1024]{2,1,0:T(8,128)(2,1)}), bf16[64,8,1024]{2,1,0:T(8,128)(2,1)}, u32[]{:S(2)}, u32[]{:S(2)}) async-start(bf16[64,8,1024]{2,1,0:T(8,128)(2,1)} %bitcast.11), calls=%async_computation.2 | async-start | bytes 2097152 | tf_op jit(solution)/shard_map/all_to_all | solution.py:260
  144.3 25.7 %collective-permute-start.15 = (bf16[256,1024]{1,0:T(8,128)(2,1)S(1)}, bf16[256,1024]{1,0:T(8,128)(2,1)S(1)}, u32[]{:S(2)}, u32[]{:S(2)}) collective-permute-start(bf16[256,1024]{1,0:T(8,128)(2,1)S(1)} %pad_maximum_fusion.1), channel_id=1, source_target_pairs={{0,3},{1,0},{2,1},{3,2},{4,7},{5,4},{6,5},{7,6},{8,11},{9,8},{10,9... | collective-permute-start | bytes 1572872 | tf_op jit(solution)/shard_map/ppermute | solution.py:189
  147.3 22.7 %collective-permute-start.14 = (bf16[256,1024]{1,0:T(8,128)(2,1)S(1)}, bf16[256,1024]{1,0:T(8,128)(2,1)S(1)}, u32[]{:S(2)}, u32[]{:S(2)}) collective-permute-start(bf16[256,1024]{1,0:T(8,128)(2,1)S(1)} %pad_maximum_fusion.1), channel_id=1, source_target_pairs={{0,2},{1,3},{2,0},{3,1},{4,6},{5,7},{6,4},{7,5},{8,10},{9,11},{10,... | collective-permute-start | bytes 1572872 | tf_op jit(solution)/shard_map/ppermute | solution.py:189
  147.3 26.1 %collective-permute-start.13 = (bf16[256,1024]{1,0:T(8,128)(2,1)S(1)}, bf16[256,1024]{1,0:T(8,128)(2,1)S(1)}, u32[]{:S(2)}, u32[]{:S(2)}) collective-permute-start(bf16[256,1024]{1,0:T(8,128)(2,1)S(1)} %pad_maximum_fusion.1), channel_id=1, source_target_pairs={{0,1},{1,2},{2,3},{3,0},{4,5},{5,6},{6,7},{7,4},{8,9},{9,10},{10,1... | collective-permute-start | bytes 1572872 | tf_op jit(solution)/shard_map/ppermute | solution.py:189
  170.0 3.4 %copy-start.4 = (bf16[256,1024]{1,0:T(8,128)(2,1)}, bf16[256,1024]{1,0:T(8,128)(2,1)S(1)}, u32[]{:S(2)}) copy-start(bf16[256,1024]{1,0:T(8,128)(2,1)S(1)} %collective-permute-done.14) | copy-start | bytes 1572868
  173.5 0.8 copy-start.5
  174.3 1.4 copy-start.1
  175.7 3.6 %copy-start.17 = (f32[1024]{0:T(1024)S(1)}, f32[1024]{0:T(1024)}, u32[]{:S(2)}) copy-start(f32[1024]{0:T(1024)} %param.13) | copy-start | bytes 12292
  181.3 22.1 %all-to-all-start.3 = ((bf16[32,4,1024]{2,1,0:T(4,128)(2,1)}), bf16[32,4,1024]{2,1,0:T(4,128)(2,1)S(1)}, u32[]{:S(2)}, u32[]{:S(2)}) async-start(bf16[32,4,1024]{2,1,0:T(4,128)(2,1)} %broadcast_in_dim.70), calls=%async_computation.3 | async-start | bytes 524288 | tf_op jit(solution)/shard_map/all_to_all | solution.py:178
  203.4 1.6 collective-permute-start.16
  205.6 3.8 %collective-permute-start.17 = (f32[4,1024]{1,0:T(4,128)S(1)}, f32[4,1024]{1,0:T(4,128)S(1)}, u32[]{:S(2)}, u32[]{:S(2)}) collective-permute-start(f32[4,1024]{1,0:T(4,128)S(1)} %get-tuple-element.71), channel_id=1, source_target_pairs={{0,3},{1,0},{2,1},{3,2},{4,7},{5,4},{6,5},{7,6},{8,11},{9,8},{10,9... | collective-permute-start | bytes 49160 | tf_op jit(solution)/shard_map/ppermute | solution.py:189
  205.9 4.9 %collective-permute-start.19 = (f32[4,1024]{1,0:T(4,128)S(1)}, f32[4,1024]{1,0:T(4,128)S(1)}, u32[]{:S(2)}, u32[]{:S(2)}) collective-permute-start(f32[4,1024]{1,0:T(4,128)S(1)} %get-tuple-element.72), channel_id=1, source_target_pairs={{0,1},{1,2},{2,3},{3,0},{4,5},{5,6},{6,7},{7,4},{8,9},{9,10},{10,1... | collective-permute-start | bytes 49160 | tf_op jit(solution)/shard_map/ppermute | solution.py:189
  207.7 5.2 %collective-permute-start.18 = (f32[4,1024]{1,0:T(4,128)S(1)}, f32[4,1024]{1,0:T(4,128)S(1)}, u32[]{:S(2)}, u32[]{:S(2)}) collective-permute-start(f32[4,1024]{1,0:T(4,128)S(1)} %get-tuple-element.73), channel_id=1, source_target_pairs={{0,2},{1,3},{2,0},{3,1},{4,6},{5,7},{6,4},{7,5},{8,10},{9,11},{10,... | collective-permute-start | bytes 49160 | tf_op jit(solution)/shard_map/ppermute | solution.py:189

commit v3 on v2

--- a/solution.py
+++ b/solution.py
@@ -139,6 +139,63 @@
     )(tokens, routes)
 
 
+def combine_kernel(
+    lengths_ref, returned_ref, tokens_ref, place_ref, gates_ref, gain_ref, embed_ref, copies_ref
+):
+    count = tokens_ref.shape[0]
+    captions = embed_ref.shape[0]
+    returned = returned_ref[...]
+    spots = lax.broadcasted_iota(jnp.int32, (count, returned.shape[0]), 1)
+    gates = jnp.where(spots == place_ref[:, 0:1], gates_ref[:, 0:1], 0.0) + jnp.where(
+        spots == place_ref[:, 1:2], gates_ref[:, 1:2], 0.0
+    )
+    high, low = split_pair(gates)
+    mixed = tokens_ref[...].astype(F32)
+    mixed += jnp.dot(high, returned, preferred_element_type=F32)
+    mixed += jnp.dot(low, returned, preferred_element_type=F32)
+    final = layer_norm(mixed) * gain_ref[...]
+    padded = 8
+    caption = lax.broadcasted_iota(jnp.int32, (padded, count), 0)
+    token = lax.broadcasted_iota(jnp.int32, (padded, count), 1)
+    row = lax.broadcasted_iota(jnp.int32, (padded, 1), 0)
+    inside = jnp.zeros((padded, count), F32)
+    sizes = jnp.ones((padded, 1), F32)
+    start = jnp.int32(0)
+    for index in range(captions):
+        size = lengths_ref[0, index]
+        here = (caption == index) & (token >= start) & (token < start + size)
+        inside = jnp.where(here, 1.0, inside)
+        sizes = jnp.where(row == index, size.astype(F32), sizes)
+        start = start + size
+    inside = inside.astype(BF16)
+    first, rest = final.astype(BF16), final
+    pooled = jnp.dot(inside, first, preferred_element_type=F32)
+    for _ in range(2):
+        rest = rest - first.astype(F32)
+        first = rest.astype(BF16)
+        pooled += jnp.dot(inside, first, preferred_element_type=F32)
+    embed = unit_rows(pooled / sizes)[:captions]
+    embed_ref[...] = embed
+    unit = (embed * (1.0 / math.sqrt(embed.shape[1]))).astype(BF16)
+    copies_ref[...] = jnp.broadcast_to(unit[None], copies_ref.shape)
+
+
+def combine(lengths, returned, tokens, place, gates, gain, copies):
+    captions = lengths.shape[1]
+    width = tokens.shape[1]
+    vmem = pl.BlockSpec(memory_space=pltpu.VMEM)
+    return pl.pallas_call(
+        combine_kernel,
+        in_specs=[pl.BlockSpec(memory_space=pltpu.SMEM)] + [vmem] * 5,
+        out_specs=[vmem, vmem],
+        out_shape=[
+            jax.ShapeDtypeStruct((captions, width), F32),
+            jax.ShapeDtypeStruct((copies, captions, width), BF16),
+        ],
+        compiler_params=pltpu.CompilerParams(vmem_limit_bytes=24 * 2**20),
+    )(lengths, returned, tokens, place, gates, gain.reshape(1, width))
+
+
 def split_pair(values):
     high = values.astype(BF16)
     return high, (values - high.astype(F32)).astype(BF16)
@@ -170,14 +227,13 @@
     return lax.ppermute(values, "expert", pairs)
 
 
-def along_expert(mine, shape):
+def along_expert(copies, shape):
     wide, deep, cores = shape
     chips = wide * deep
     groups = [[chip * cores + core for chip in range(chips)] for core in range(cores)]
-    copies = jnp.broadcast_to(mine[None], (chips,) + mine.shape)
     column = lax.all_to_all(
         copies, "expert", split_axis=0, concat_axis=0, axis_index_groups=groups, tiled=True
-    ).reshape(chips * mine.shape[0], mine.shape[1])
+    ).reshape(chips * copies.shape[1], copies.shape[2])
     return on_chip(column, shape)
 
 
@@ -208,14 +264,14 @@
     shape = (grid_all, experts_all // (2 * grid_all), 2)
     chip = lax.axis_index("expert") // shape[2]
 
-    stream = tokens.astype(F32)
+    row_parts = [picture_unit] + [ring_shift(picture_unit, k, grid_all) for k in range(1, grid_all)]
     send, place = dispatch(tokens, routes, places_all, slots)
-    spots = jnp.arange(places_all, dtype=jnp.int32)[None, :]
-    at_first = spots == place[:, 0:1]
-    at_second = spots == place[:, 1:2]
-    order = jnp.arange(token_count, dtype=jnp.int32)
     send = send.reshape(experts_all, slots, width)
     arrived = lax.all_to_all(send, "expert", split_axis=0, concat_axis=0, tiled=True)
+    pictures_row = jnp.concatenate(row_parts, axis=0)
+    chips = shape[0] * shape[1]
+    picture_copies = jnp.broadcast_to(pictures_row[None], (chips,) + pictures_row.shape)
+    arrived, picture_copies, pictures_row = held(arrived, picture_copies, pictures_row)
     rows = arrived.reshape(places_all, width)
 
     up_local = up_weight[0]
@@ -224,12 +280,11 @@
     top, bottom = rows[:half], rows[half:]
     left_top = ring_shift(top, 1, grid_all)
     right_bottom = ring_shift(bottom, -1, grid_all)
-    own_term = expert_part([rows], up_local, down_local)[0]
-    own_term, top, bottom, left_top, right_bottom = held(
-        own_term, top, bottom, left_top, right_bottom
-    )
+    pictures_all = along_expert(picture_copies, shape)
     left_bottom = ring_shift(bottom, 1, grid_all)
     right_top = ring_shift(top, -1, grid_all)
+    own_term = expert_part([rows], up_local, down_local)[0]
+    own_term, left_top, right_bottom = held(own_term, left_top, right_bottom)
     far_top = ring_shift(left_top, 1, grid_all)
     far_bottom = ring_shift(right_bottom, -1, grid_all)
     left_top, right_bottom = expert_part([left_top, right_bottom], up_local, down_local)
@@ -245,48 +300,23 @@
     far_top, far_bottom = expert_part([far_top, far_bottom], up_local, down_local)
     far_from_left = ring_shift(far_top, 1, grid_all)
     far_from_right = ring_shift(far_bottom, -1, grid_all)
-    far_from_left, far_from_right, home_top, home_bottom = held(
-        far_from_left, far_from_right, home_top, home_bottom
+    far_from_left, far_from_right, home_top, home_bottom, pictures_all = held(
+        far_from_left, far_from_right, home_top, home_bottom, pictures_all
     )
     right_top = (right_top.astype(F32) + far_from_left.astype(F32)).astype(BF16)
     left_bottom = (left_bottom.astype(F32) + far_from_right.astype(F32)).astype(BF16)
     last_top = ring_shift(right_top, 1, grid_all)
     last_bottom = ring_shift(left_bottom, -1, grid_all)
-    right_top, left_bottom, picture_later = held(right_top, left_bottom, picture_unit)
-    picture_column = along_expert(picture_later, shape)
     total = sum_terms(own_term, home_top, last_top, home_bottom, last_bottom)
-    total, picture_column = held(total, picture_column)
     results = total.reshape(experts_all, slots, width)
     returned = lax.all_to_all(results, "expert", split_axis=0, concat_axis=0, tiled=True)
-    picture_parts = [picture_column] + [
-        ring_shift(picture_column, k, grid_all) for k in range(1, grid_all)
-    ]
-    pictures_all = jnp.concatenate(picture_parts, axis=0)
-    pictures_row = lax.dynamic_slice_in_dim(
-        jnp.stack(picture_parts), chip * captions_here, captions_here, axis=1
-    ).reshape(grid_all * captions_here, width)
-    returned, pictures_all, pictures_row = held(returned, pictures_all, pictures_row)
     returned = returned.reshape(places_all, width)
 
-    gates = jnp.where(at_first, route_gates[:, 0:1], 0.0) + jnp.where(
-        at_second, route_gates[:, 1:2], 0.0
-    )
-    gate_high, gate_low = split_pair(gates)
-    mixed = (
-        stream
-        + jnp.dot(gate_high, returned, preferred_element_type=F32)
-        + jnp.dot(gate_low, returned, preferred_element_type=F32)
-    )
-    final = layer_norm(mixed) * final_gain
-    lengths = caption_lengths[0]
-    ends = jnp.cumsum(lengths)
-    starts = ends - lengths
-    members = ((order[None, :] >= starts[:, None]) & (order[None, :] < ends[:, None])).astype(F32)
-    pooled = jnp.dot(members, final, precision=lax.Precision.HIGHEST) / lengths[:, None].astype(F32)
-    text_embed = unit_rows(pooled)
-    text_unit = (text_embed / scale_root).astype(BF16)
-
-    text_column = along_expert(text_unit, shape)
+    text_embed, text_copies = combine(
+        caption_lengths, returned, tokens, place, route_gates, final_gain, chips
+    )
+    text_unit = text_copies[0]
+    text_column = along_expert(text_copies, shape)
 
     def slopes(mine, others, place):
         logits = SIMILARITY_HEAT * lax.dot_general(
@@ -297,7 +327,7 @@
         same = (row_ids < captions_here) & (row_ids + place == column_ids)
         return weighted_sum(pair_slope(logits, same), others)
 
-    sentence_slope = slopes(text_unit, pictures_all, chip * captions_here)
+    sentence_slope = slopes(text_unit, pictures_all, chip * pictures_row.shape[0])
     partial = slopes(pictures_row, text_column, chip * captions_here).reshape(grid_all, captions_here, width)
     picture_slope = partial[0]
     for k in range(1, grid_all):
@@ -308,6 +338,7 @@
 def solution(mesh):
     split = P(("expert", "grid"), None)
     weights = P("expert", None, "grid")
+
     return jax.shard_map(
         on_device,
         mesh=mesh,

time: 214 us -> 203 us (0.949)
  blocking collectives: 39.4 us -> 0 us
  waiting for transfers between devices: 67 us -> 91.9 us
  starting transfers between devices: 51.6 us -> 59.5 us
  Pallas kernels: 36.2 us -> 39.4 us
  matrix products: 5.34 us -> 2.21 us
  other arithmetic: 6.01 us -> 3.27 us
    all_to_all x1 -> x0, blocking collectives: 39.4 us -> none  [on_device(): lax.all_to_all(send, 'expert', split_axis=0, concat_axis=0, tiled=True)]
    all_to_all x1, waiting for transfers between devices: 0.01 us -> 27.7 us  [on_device(): lax.all_to_all(results, 'expert', split_axis=0, concat_axis=0, tiled=True)]
    all_to_all x0 -> x1, waiting for transfers between devices: none -> 19.2 us  [on_device(): lax.all_to_all(send, 'expert', split_axis=0, concat_axis=0, tiled=True)]
    ppermute x18, waiting for transfers between devices: 46.8 us -> 32.9 us  [ring_shift(): lax.ppermute(values, 'grid', [(i, (i + step) % size) for i in range(size)])]
    all_to_all x0 -> x1, starting transfers between devices: none -> 11.8 us  [on_device(): lax.all_to_all(send, 'expert', split_axis=0, concat_axis=0, tiled=True)]
    all_to_all x2, waiting for transfers between devices: 19.1 us -> 10.9 us  [along_expert(): lax.all_to_all(copies, 'expert', split_axis=0, concat_axis=0, axis_index_...]
    all_to_all x2, starting transfers between devices: 18.2 us -> 12.9 us  [along_expert(): lax.all_to_all(copies, 'expert', split_axis=0, concat_axis=0, axis_index_...]
    ppermute x18, starting transfers between devices: 23 us -> 27.4 us  [ring_shift(): lax.ppermute(values, 'grid', [(i, (i + step) % size) for i in range(size)])]
  transfers between devices with their start and end apart: 23 -> 24, of which waited for: 15 -> 11; matrix products, arithmetic and copies ran while one was open for 2% -> 2% of each run, Pallas kernels for 16% -> 16%
where the time goes in v3:
time: 203 us; the launch traced here: 202 us
  waiting for transfers between devices  91.9 us (45%)
  starting transfers between devices  59.5 us (29%)
  Pallas kernels  39.4 us (19%)
  local copies, waits for them, and re-layouts  4.95 us (2%)
  other arithmetic  3.27 us (2%)
  matrix products  2.21 us (1%)
    pallas_call x4, Pallas kernels, expert_part(): pl.pallas_call(expert_kernel, grid=(units // tile,), in_specs=whole + [pl...  33.3 us
    ppermute x18, waiting for transfers between devices, ring_shift(): lax.ppermute(values, 'grid', [(i, (i + step) % size) for i in range(size)])  32.9 us
    all_to_all x1, waiting for transfers between devices, on_device(): lax.all_to_all(results, 'expert', split_axis=0, concat_axis=0, tiled=True)  27.7 us
    ppermute x18, starting transfers between devices, ring_shift(): lax.ppermute(values, 'grid', [(i, (i + step) % size) for i in range(size)])  27.4 us
    all_to_all x1, waiting for transfers between devices, on_device(): lax.all_to_all(send, 'expert', split_axis=0, concat_axis=0, tiled=True)  19.2 us
    all_to_all x2, starting transfers between devices, along_expert(): lax.all_to_all(copies, 'expert', split_axis=0, concat_axis=0, axis_index_...  12.9 us
    all_to_all x1, starting transfers between devices, on_device(): lax.all_to_all(send, 'expert', split_axis=0, concat_axis=0, tiled=True)  11.8 us
    all_to_all x2, waiting for transfers between devices, along_expert(): lax.all_to_all(copies, 'expert', split_axis=0, concat_axis=0, axis_index_...  10.9 us
  transfers between devices with their start and end apart: 24, of which 11 were waited for; matrix products, arithmetic and copies ran while one was open for 2% of the time, Pallas kernels for 16%

profile of v3, /device:TPU:32, one launch (start us, length us, event | category | flops | bytes accessed | tf_op | source)
XLA Modules:
  0.0 202.1 jit_solution(11208353160415552126)
XLA Ops:
  0.6 0.8 copy.11.routes_ref
  1.4 0.9 copy-done
  2.4 1.9 shard_map.103
  4.3 11.8 %all-to-all-start = ((bf16[64,8,1024]{2,1,0:T(8,128)(2,1)}), bf16[64,8,1024]{2,1,0:T(8,128)(2,1)S(1)}, u32[]{:S(2)}, u32[]{:S(2)}) async-start(bf16[64,8,1024]{2,1,0:T(8,128)(2,1)} %bitcast), calls=%async_computation | async-start | bytes 2097152 | tf_op jit(solution)/shard_map/all_to_all | solution.py:270
  16.1 0.1 fusion.13
  16.2 0.1 fusion.15
  16.3 2.8 %collective-permute-start.2 = (bf16[4,1024]{1,0:T(4,128)(2,1)S(1)}, bf16[4,1024]{1,0:T(4,128)(2,1)S(1)}, u32[]{:S(2)}, u32[]{:S(2)}) collective-permute-start(bf16[4,1024]{1,0:T(4,128)(2,1)S(1)} %fusion.15), channel_id=1, source_target_pairs={{0,3},{1,0},{2,1},{3,2},{4,7},{5,4},{6,5},{7,6},{8,11},{9,8},{10,9... | collective-permute-start | bytes 24584 | tf_op jit(solution)/shard_map/ppermute | solution.py:245
  19.1 0.8 collective-permute-start.1
  19.9 0.9 collective-permute-start
  20.8 0.0 collective-permute-done.2
  20.8 3.5 %collective-permute-done.1 = bf16[4,1024]{1,0:T(4,128)(2,1)S(1)} collective-permute-done((bf16[4,1024]{1,0:T(4,128)(2,1)S(1)}, bf16[4,1024]{1,0:T(4,128)(2,1)S(1)}, u32[]{:S(2)}, u32[]{:S(2)}) %collective-permute-start.1) | collective-permute-done | bytes 8224 | tf_op jit(solution)/shard_map/ppermute | solution.py:245
  24.2 0.5 collective-permute-done
  24.8 19.2 %all-to-all-done = bf16[64,8,1024]{2,1,0:T(8,128)(2,1)S(1)} async-done(((bf16[64,8,1024]{2,1,0:T(8,128)(2,1)}), bf16[64,8,1024]{2,1,0:T(8,128)(2,1)S(1)}, u32[]{:S(2)}, u32[]{:S(2)}) %all-to-all-start) | async-done | bytes 1048608 | tf_op jit(solution)/shard_map/all_to_all | solution.py:270
  43.9 1.2 broadcast_in_dim.23
  45.2 0.9 slice_bitcast_fusion
  46.0 1.5 collective-permute-start.3
  47.5 1.7 collective-permute-start.7
  49.3 1.5 collective-permute-start.4
  50.8 0.5 collective-permute-start.8
  51.3 6.5 %all-to-all-start.1 = ((bf16[32,16,1024]{2,1,0:T(8,128)(2,1)}), bf16[32,16,1024]{2,1,0:T(8,128)(2,1)S(1)}, u32[]{:S(2)}, u32[]{:S(2)}) async-start(bf16[32,16,1024]{2,1,0:T(8,128)(2,1)} %broadcast_in_dim.23), calls=%async_computation.1 | async-start | bytes 2097152 | tf_op jit(solution)/shard_map/all_to_all | solution.py:234
  57.8 8.4 %shard_map.104.own_ref = bf16[512,1024]{1,0:T(8,128)(2,1)} custom-call(bf16[512,1024]{1,0:T(8,128)(2,1)} %bitcast.24, bf16[1024,1024]{1,0:T(8,128)(2,1)} %bitcast.27, bf16[1024,1024]{1,0:T(8,128)(2,1)} %bitcast.31), custom_call_target="tpu_custom_call" | custom-call | flops 8589934592 | bytes 6291456 | tf_op jit(solution)/shard_map/pallas_call | solution.py:55
  66.1 0.0 collective-permute-done.3.refs_0_
  66.1 6.3 %collective-permute-done.4.refs_1_ = bf16[256,1024]{1,0:T(8,128)(2,1)} collective-permute-done((bf16[256,1024]{1,0:T(8,128)(2,1)}, bf16[256,1024]{1,0:T(8,128)(2,1)}, u32[]{:S(2)}, u32[]{:S(2)}) %collective-permute-start.4) | collective-permute-done | bytes 524320 | tf_op jit(solution)/shard_map/ppermute | solution.py:245
  72.4 1.5 collective-permute-start.5
  73.9 1.7 collective-permute-start.6
  75.6 8.3 %shard_map.105 = (bf16[256,1024]{1,0:T(8,128)(2,1)}, bf16[256,1024]{1,0:T(8,128)(2,1)}) custom-call(bf16[256,1024]{1,0:T(8,128)(2,1)} %collective-permute-done.3.refs_0_, bf16[256,1024]{1,0:T(8,128)(2,1)} %collective-permute-done.4.refs_1_, bf16[1024,1024]{1,0:T(8,128)(2,1)} %bitcast.28, bf16[1024,1024]{1,0:T(8,128)(2,1)} %bitcast.32), custom_call_target="tpu_custom_call" | custom-call | flops 8589934592 | bytes 6291456 | tf_op jit(solution)/shard_map/pallas_call | solution.py:55
  84.0 1.7 collective-permute-start.11
  85.7 0.0 collective-permute-done.7.refs_0_
  85.7 0.3 collective-permute-start.12
  86.0 8.3 %shard_map.106 = (bf16[256,1024]{1,0:T(8,128)(2,1)}, bf16[256,1024]{1,0:T(8,128)(2,1)}) custom-call(bf16[256,1024]{1,0:T(8,128)(2,1)} %collective-permute-done.7.refs_0_, bf16[256,1024]{1,0:T(8,128)(2,1)} %collective-permute-done.8.refs_1_, bf16[1024,1024]{1,0:T(8,128)(2,1)} %bitcast.29, bf16[1024,1024]{1,0:T(8,128)(2,1)} %bitcast.33), custom_call_target="tpu_custom_call" | custom-call | flops 8589934592 | bytes 6291456 | tf_op jit(solution)/shard_map/pallas_call | solution.py:55
  94.4 0.1 collective-permute-start.13
  94.5 0.7 copy-done.13
  95.1 0.2 copy-done.14
  95.3 8.3 %shard_map.107 = (bf16[256,1024]{1,0:T(8,128)(2,1)}, bf16[256,1024]{1,0:T(8,128)(2,1)}) custom-call(bf16[256,1024]{1,0:T(8,128)(2,1)} %copy-done.13, bf16[256,1024]{1,0:T(8,128)(2,1)} %copy-done.14, bf16[1024,1024]{1,0:T(8,128)(2,1)} %bitcast.30, bf16[1024,1024]{1,0:T(8,128)(2,1)} %bitcast.34), custom_call_target="tpu_custom_call" | custom-call | flops 8589934592 | bytes 6291456 | tf_op jit(solution)/shard_map/pallas_call | solution.py:55
  103.7 0.3 collective-permute-start.9
  104.0 3.0 %collective-permute-start.10 = (bf16[256,1024]{1,0:T(8,128)(2,1)}, bf16[256,1024]{1,0:T(8,128)(2,1)S(1)}, u32[]{:S(2)}, u32[]{:S(2)}) collective-permute-start(bf16[256,1024]{1,0:T(8,128)(2,1)} %get-tuple-element.44), channel_id=1, source_target_pairs={{0,3},{1,0},{2,1},{3,2},{4,7},{5,4},{6,5},{7,6},{8,11},{9,8},{10,9... | collective-permute-start | bytes 1572872 | tf_op jit(solution)/shard_map/ppermute | solution.py:245
  106.9 1.4 pad_maximum_fusion
  108.3 10.2 %collective-permute-done.9 = bf16[256,1024]{1,0:T(8,128)(2,1)S(1)} collective-permute-done((bf16[256,1024]{1,0:T(8,128)(2,1)}, bf16[256,1024]{1,0:T(8,128)(2,1)S(1)}, u32[]{:S(2)}, u32[]{:S(2)}) %collective-permute-start.9) | collective-permute-done | bytes 524320 | tf_op jit(solution)/shard_map/ppermute | solution.py:245
  118.6 0.2 add_convert_fusion.1
  118.8 1.2 collective-permute-start.14
  120.0 0.2 add_convert_fusion
  120.2 2.2 %collective-permute-start.15 = (bf16[256,1024]{1,0:T(8,128)(2,1)S(1)}, bf16[256,1024]{1,0:T(8,128)(2,1)S(1)}, u32[]{:S(2)}, u32[]{:S(2)}) collective-permute-start(bf16[256,1024]{1,0:T(8,128)(2,1)S(1)} %add_convert_fusion), channel_id=1, source_target_pairs={{0,3},{1,0},{2,1},{3,2},{4,7},{5,4},{6,5},{7,6},{8,11},{9,8},{10,9... | collective-permute-start | bytes 1572872 | tf_op jit(solution)/shard_map/ppermute | solution.py:245
  122.4 10.3 %collective-permute-done.14.last_top = bf16[256,1024]{1,0:T(8,128)(2,1)S(1)} collective-permute-done((bf16[256,1024]{1,0:T(8,128)(2,1)S(1)}, bf16[256,1024]{1,0:T(8,128)(2,1)S(1)}, u32[]{:S(2)}, u32[]{:S(2)}) %collective-permute-start.14) | collective-permute-done | bytes 524320 | tf_op jit(solution)/shard_map/ppermute | solution.py:245
  132.7 1.8 shard_map.108
  134.5 6.9 %all-to-all-start.2 = ((bf16[64,8,1024]{2,1,0:T(8,128)(2,1)}), bf16[64,8,1024]{2,1,0:T(8,128)(2,1)S(1)}, u32[]{:S(2)}, u32[]{:S(2)}) async-start(bf16[64,8,1024]{2,1,0:T(8,128)(2,1)} %bitcast.7), calls=%async_computation.2 | async-start | bytes 2097152 | tf_op jit(solution)/shard_map/all_to_all | solution.py:312
  141.4 0.1 copy.12.gates_ref
  141.5 27.7 %all-to-all-done.2 = bf16[64,8,1024]{2,1,0:T(8,128)(2,1)S(1)} async-done(((bf16[64,8,1024]{2,1,0:T(8,128)(2,1)}), bf16[64,8,1024]{2,1,0:T(8,128)(2,1)S(1)}, u32[]{:S(2)}, u32[]{:S(2)}) %all-to-all-start.2) | async-done | bytes 1048608 | tf_op jit(solution)/shard_map/all_to_all | solution.py:312
  169.3 2.3 %shard_map.109 = (f32[4,1024]{1,0:T(4,128)}, bf16[32,4,1024]{2,1,0:T(4,128)(2,1)}) custom-call(s32[1,4]{1,0:T(1,128)S(1)} %copy-done.4, bf16[512,1024]{1,0:T(8,128)(2,1)S(1)} %bitcast.22, bf16[128,1024]{1,0:T(8,128)(2,1)S(1)} %copy-done.1, s32[128,2]{1,0:T(8,128)S(1)} %get-tuple-element.52.place_ref, f32[128,2]{1,0:T(8,128)S(1)} %copy.12.gates_ref, ...), custom_call_target="tpu_custom_call" | custom-call | tf_op jit(solution)/shard_map/pallas_call | solution.py:187
  171.6 6.5 %all-to-all-start.3 = ((bf16[32,4,1024]{2,1,0:T(4,128)(2,1)}), bf16[32,4,1024]{2,1,0:T(4,128)(2,1)S(1)}, u32[]{:S(2)}, u32[]{:S(2)}) async-start(bf16[32,4,1024]{2,1,0:T(4,128)(2,1)} %get-tuple-element.54), calls=%async_computation.3 | async-start | bytes 524288 | tf_op jit(solution)/shard_map/all_to_all | solution.py:234
  178.2 1.4 subtract_convert_fusion.1
  179.5 10.9 %all-to-all-done.3 = bf16[32,4,1024]{2,1,0:T(4,128)(2,1)S(1)} async-done(((bf16[32,4,1024]{2,1,0:T(4,128)(2,1)}), bf16[32,4,1024]{2,1,0:T(4,128)(2,1)S(1)}, u32[]{:S(2)}, u32[]{:S(2)}) %all-to-all-start.3) | async-done | bytes 262176 | tf_op jit(solution)/shard_map/all_to_all | solution.py:234
  190.5 0.1 reshape.53
  190.5 0.3 collective-permute-start.16
  190.9 0.4 fusion.19
  191.3 1.1 collective-permute-done.16
  192.4 0.3 subtract_convert_fusion
  192.7 0.2 fusion.23
  192.9 1.5 collective-permute-start.19
  194.4 3.3 %collective-permute-start.18 = (f32[4,1024]{1,0:T(4,128)S(1)}, f32[4,1024]{1,0:T(4,128)S(1)}, u32[]{:S(2)}, u32[]{:S(2)}) collective-permute-start(f32[4,1024]{1,0:T(4,128)S(1)} %get-tuple-element.65), channel_id=1, source_target_pairs={{0,2},{1,3},{2,0},{3,1},{4,6},{5,7},{6,4},{7,5},{8,10},{9,11},{10,... | collective-permute-start | bytes 49160 | tf_op jit(solution)/shard_map/ppermute | solution.py:245
  197.7 1.1 collective-permute-start.17
  198.8 0.6 fusion.18
  199.4 0.3 collective-permute-done.18
  199.6 1.8 collective-permute-done.17
  201.4 0.6 fusion.17
  (47 shorter events, 0.2 us)
Async XLA Ops:
  0.6 15.4 %copy-start.11 = (bf16[4,1024]{1,0:T(4,128)(2,1)S(1)}, bf16[4,1024]{1,0:T(4,128)(2,1)}, u32[]{:S(2)}) copy-start(bf16[4,1024]{1,0:T(4,128)(2,1)} %param.12) | copy-start | bytes 24580
  1.4 0.9 copy-start
  4.3 39.6 %all-to-all-start = ((bf16[64,8,1024]{2,1,0:T(8,128)(2,1)}), bf16[64,8,1024]{2,1,0:T(8,128)(2,1)S(1)}, u32[]{:S(2)}, u32[]{:S(2)}) async-start(bf16[64,8,1024]{2,1,0:T(8,128)(2,1)} %bitcast), calls=%async_computation | async-start | bytes 2097152 | tf_op jit(solution)/shard_map/all_to_all | solution.py:270
  16.3 4.5 %collective-permute-start.2 = (bf16[4,1024]{1,0:T(4,128)(2,1)S(1)}, bf16[4,1024]{1,0:T(4,128)(2,1)S(1)}, u32[]{:S(2)}, u32[]{:S(2)}) collective-permute-start(bf16[4,1024]{1,0:T(4,128)(2,1)S(1)} %fusion.15), channel_id=1, source_target_pairs={{0,3},{1,0},{2,1},{3,2},{4,7},{5,4},{6,5},{7,6},{8,11},{9,8},{10,9... | collective-permute-start | bytes 24584 | tf_op jit(solution)/shard_map/ppermute | solution.py:245
  19.1 5.2 %collective-permute-start.1 = (bf16[4,1024]{1,0:T(4,128)(2,1)S(1)}, bf16[4,1024]{1,0:T(4,128)(2,1)S(1)}, u32[]{:S(2)}, u32[]{:S(2)}) collective-permute-start(bf16[4,1024]{1,0:T(4,128)(2,1)S(1)} %fusion.15), channel_id=1, source_target_pairs={{0,2},{1,3},{2,0},{3,1},{4,6},{5,7},{6,4},{7,5},{8,10},{9,11},{10,... | collective-permute-start | bytes 24584 | tf_op jit(solution)/shard_map/ppermute | solution.py:245
  19.9 4.9 %collective-permute-start = (bf16[4,1024]{1,0:T(4,128)(2,1)S(1)}, bf16[4,1024]{1,0:T(4,128)(2,1)S(1)}, u32[]{:S(2)}, u32[]{:S(2)}) collective-permute-start(bf16[4,1024]{1,0:T(4,128)(2,1)S(1)} %fusion.15), channel_id=1, source_target_pairs={{0,1},{1,2},{2,3},{3,0},{4,5},{5,6},{6,7},{7,4},{8,9},{9,10},{10,1... | collective-permute-start | bytes 24584 | tf_op jit(solution)/shard_map/ppermute | solution.py:245
  24.8 26.5 %copy-start.9 = (bf16[16,1024]{1,0:T(8,128)(2,1)}, bf16[16,1024]{1,0:T(8,128)(2,1)S(1)}, u32[]{:S(2)}) copy-start(bf16[16,1024]{1,0:T(8,128)(2,1)S(1)} %pad_maximum_fusion.1) | copy-start | bytes 98308
  43.9 7.4 %copy-start.5 = (bf16[64,8,1024]{2,1,0:T(8,128)(2,1)}, bf16[64,8,1024]{2,1,0:T(8,128)(2,1)S(1)}, u32[]{:S(2)}) copy-start(bf16[64,8,1024]{2,1,0:T(8,128)(2,1)S(1)} %all-to-all-done) | copy-start | bytes 3145732
  46.0 20.1 %collective-permute-start.3 = (bf16[256,1024]{1,0:T(8,128)(2,1)S(1)}, bf16[256,1024]{1,0:T(8,128)(2,1)}, u32[]{:S(2)}, u32[]{:S(2)}) collective-permute-start(bf16[256,1024]{1,0:T(8,128)(2,1)S(1)} %get-tuple-element.62), channel_id=1, source_target_pairs={{0,1},{1,2},{2,3},{3,0},{4,5},{5,6},{6,7},{7,4},{8,9},{9,10},{10,1... | collective-permute-start | bytes 1572872 | tf_op jit(solution)/shard_map/ppermute | solution.py:245
  47.5 38.2 %collective-permute-start.7 = (bf16[256,1024]{1,0:T(8,128)(2,1)S(1)}, bf16[256,1024]{1,0:T(8,128)(2,1)}, u32[]{:S(2)}, u32[]{:S(2)}) collective-permute-start(bf16[256,1024]{1,0:T(8,128)(2,1)S(1)} %get-tuple-element.62), channel_id=1, source_target_pairs={{0,3},{1,0},{2,1},{3,2},{4,7},{5,4},{6,5},{7,6},{8,11},{9,8},{10,9... | collective-permute-start | bytes 1572872 | tf_op jit(solution)/shard_map/ppermute | solution.py:245
  49.3 23.1 %collective-permute-start.4 = (bf16[256,1024]{1,0:T(8,128)(2,1)}, bf16[256,1024]{1,0:T(8,128)(2,1)}, u32[]{:S(2)}, u32[]{:S(2)}) collective-permute-start(bf16[256,1024]{1,0:T(8,128)(2,1)} %get-tuple-element.61), channel_id=1, source_target_pairs={{0,3},{1,0},{2,1},{3,2},{4,7},{5,4},{6,5},{7,6},{8,11},{9,8},{10,9... | collective-permute-start | bytes 1572872 | tf_op jit(solution)/shard_map/ppermute | solution.py:245
  50.8 35.2 %collective-permute-start.8 = (bf16[256,1024]{1,0:T(8,128)(2,1)}, bf16[256,1024]{1,0:T(8,128)(2,1)}, u32[]{:S(2)}, u32[]{:S(2)}) collective-permute-start(bf16[256,1024]{1,0:T(8,128)(2,1)} %get-tuple-element.61), channel_id=1, source_target_pairs={{0,1},{1,2},{2,3},{3,0},{4,5},{5,6},{6,7},{7,4},{8,9},{9,10},{10,1... | collective-permute-start | bytes 1572872 | tf_op jit(solution)/shard_map/ppermute | solution.py:245
  51.3 43.1 %all-to-all-start.1 = ((bf16[32,16,1024]{2,1,0:T(8,128)(2,1)}), bf16[32,16,1024]{2,1,0:T(8,128)(2,1)S(1)}, u32[]{:S(2)}, u32[]{:S(2)}) async-start(bf16[32,16,1024]{2,1,0:T(8,128)(2,1)} %broadcast_in_dim.23), calls=%async_computation.1 | async-start | bytes 2097152 | tf_op jit(solution)/shard_map/all_to_all | solution.py:234
  72.4 21.9 %collective-permute-start.5 = (bf16[256,1024]{1,0:T(8,128)(2,1)}, bf16[256,1024]{1,0:T(8,128)(2,1)S(1)}, u32[]{:S(2)}, u32[]{:S(2)}) collective-permute-start(bf16[256,1024]{1,0:T(8,128)(2,1)} %collective-permute-done.3.refs_0_), channel_id=1, source_target_pairs={{0,1},{1,2},{2,3},{3,0},{4,5},{5,6},{6,7},{7,4},{8,9},{9,10},{10,1... | collective-permute-start | bytes 1572872 | tf_op jit(solution)/shard_map/ppermute | solution.py:245
  73.9 20.4 %collective-permute-start.6 = (bf16[256,1024]{1,0:T(8,128)(2,1)}, bf16[256,1024]{1,0:T(8,128)(2,1)S(1)}, u32[]{:S(2)}, u32[]{:S(2)}) collective-permute-start(bf16[256,1024]{1,0:T(8,128)(2,1)} %collective-permute-done.4.refs_1_), channel_id=1, source_target_pairs={{0,3},{1,0},{2,1},{3,2},{4,7},{5,4},{6,5},{7,6},{8,11},{9,8},{10,9... | collective-permute-start | bytes 1572872 | tf_op jit(solution)/shard_map/ppermute | solution.py:245
  84.0 24.4 %collective-permute-start.11 = (bf16[256,1024]{1,0:T(8,128)(2,1)}, bf16[256,1024]{1,0:T(8,128)(2,1)S(1)}, u32[]{:S(2)}, u32[]{:S(2)}) collective-permute-start(bf16[256,1024]{1,0:T(8,128)(2,1)} %get-tuple-element.35), channel_id=1, source_target_pairs={{0,3},{1,0},{2,1},{3,2},{4,7},{5,4},{6,5},{7,6},{8,11},{9,8},{10,9... | collective-permute-start | bytes 1572872 | tf_op jit(solution)/shard_map/ppermute | solution.py:245
  85.7 22.6 %collective-permute-start.12 = (bf16[256,1024]{1,0:T(8,128)(2,1)}, bf16[256,1024]{1,0:T(8,128)(2,1)S(1)}, u32[]{:S(2)}, u32[]{:S(2)}) collective-permute-start(bf16[256,1024]{1,0:T(8,128)(2,1)} %get-tuple-element.36), channel_id=1, source_target_pairs={{0,1},{1,2},{2,3},{3,0},{4,5},{5,6},{6,7},{7,4},{8,9},{9,10},{10,1... | collective-permute-start | bytes 1572872 | tf_op jit(solution)/shard_map/ppermute | solution.py:245
  94.3 0.8 copy-start.13
  94.3 1.0 copy-start.14
  94.4 9.3 %copy-start.6 = (bf16[32,16,1024]{2,1,0:T(8,128)(2,1)}, bf16[32,16,1024]{2,1,0:T(8,128)(2,1)S(1)}, u32[]{:S(2)}) copy-start(bf16[32,16,1024]{2,1,0:T(8,128)(2,1)S(1)} %all-to-all-done.1) | copy-start | bytes 3145732
  94.4 12.5 %collective-permute-start.13 = (bf16[512,1024]{1,0:T(8,128)(2,1)S(1)}, bf16[512,1024]{1,0:T(8,128)(2,1)S(1)}, u32[]{:S(2)}, u32[]{:S(2)}) collective-permute-start(bf16[512,1024]{1,0:T(8,128)(2,1)S(1)} %bitcast.25), channel_id=1, source_target_pairs={{0,4},{4,0},{8,12},{12,8},{16,20},{20,16},{24,28},{28,24},{32,36},... | collective-permute-start | bytes 3145736 | tf_op jit(solution)/shard_map/ppermute | solution.py:227
  103.7 14.9 %collective-permute-start.9 = (bf16[256,1024]{1,0:T(8,128)(2,1)}, bf16[256,1024]{1,0:T(8,128)(2,1)S(1)}, u32[]{:S(2)}, u32[]{:S(2)}) collective-permute-start(bf16[256,1024]{1,0:T(8,128)(2,1)} %get-tuple-element.43), channel_id=1, source_target_pairs={{0,1},{1,2},{2,3},{3,0},{4,5},{5,6},{6,7},{7,4},{8,9},{9,10},{10,1... | collective-permute-start | bytes 1572872 | tf_op jit(solution)/shard_map/ppermute | solution.py:245
  104.0 14.6 %copy-start.8 = (bf16[256,1024]{1,0:T(8,128)(2,1)S(1)}, bf16[256,1024]{1,0:T(8,128)(2,1)}, u32[]{:S(2)}) copy-start(bf16[256,1024]{1,0:T(8,128)(2,1)} %get-tuple-element.47) | copy-start | bytes 1572868
  104.0 16.0 %copy-start.7 = (bf16[256,1024]{1,0:T(8,128)(2,1)S(1)}, bf16[256,1024]{1,0:T(8,128)(2,1)}, u32[]{:S(2)}) copy-start(bf16[256,1024]{1,0:T(8,128)(2,1)} %get-tuple-element.50) | copy-start | bytes 1572868
  104.0 14.6 %collective-permute-start.10 = (bf16[256,1024]{1,0:T(8,128)(2,1)}, bf16[256,1024]{1,0:T(8,128)(2,1)S(1)}, u32[]{:S(2)}, u32[]{:S(2)}) collective-permute-start(bf16[256,1024]{1,0:T(8,128)(2,1)} %get-tuple-element.44), channel_id=1, source_target_pairs={{0,3},{1,0},{2,1},{3,2},{4,7},{5,4},{6,5},{7,6},{8,11},{9,8},{10,9... | collective-permute-start | bytes 1572872 | tf_op jit(solution)/shard_map/ppermute | solution.py:245
  108.3 24.4 %copy-start.2 = (bf16[512,1024]{1,0:T(8,128)(2,1)S(1)}, bf16[512,1024]{1,0:T(8,128)(2,1)}, u32[]{:S(2)}) copy-start(bf16[512,1024]{1,0:T(8,128)(2,1)} %shard_map.104.own_ref) | copy-start | bytes 3145732
  118.8 13.9 %collective-permute-start.14 = (bf16[256,1024]{1,0:T(8,128)(2,1)S(1)}, bf16[256,1024]{1,0:T(8,128)(2,1)S(1)}, u32[]{:S(2)}, u32[]{:S(2)}) collective-permute-start(bf16[256,1024]{1,0:T(8,128)(2,1)S(1)} %add_convert_fusion.1), channel_id=1, source_target_pairs={{0,1},{1,2},{2,3},{3,0},{4,5},{5,6},{6,7},{7,4},{8,9},{9,10},{10,1... | collective-permute-start | bytes 1572872 | tf_op jit(solution)/shard_map/ppermute | solution.py:245
  120.2 12.5 %collective-permute-start.15 = (bf16[256,1024]{1,0:T(8,128)(2,1)S(1)}, bf16[256,1024]{1,0:T(8,128)(2,1)S(1)}, u32[]{:S(2)}, u32[]{:S(2)}) collective-permute-start(bf16[256,1024]{1,0:T(8,128)(2,1)S(1)} %add_convert_fusion), channel_id=1, source_target_pairs={{0,3},{1,0},{2,1},{3,2},{4,7},{5,4},{6,5},{7,6},{8,11},{9,8},{10,9... | collective-permute-start | bytes 1572872 | tf_op jit(solution)/shard_map/ppermute | solution.py:245
  134.5 7.0 %copy-start.12 = (f32[128,2]{0,1:T(2,128)S(1)}, f32[128,2]{0,1:T(2,128)}, u32[]{:S(2)}) copy-start(f32[128,2]{0,1:T(2,128)} %param.10) | copy-start | bytes 3076
  134.5 34.8 %copy-start.1 = (bf16[128,1024]{1,0:T(8,128)(2,1)S(1)}, bf16[128,1024]{1,0:T(8,128)(2,1)}, u32[]{:S(2)}) copy-start(bf16[128,1024]{1,0:T(8,128)(2,1)} %tokens_ref.3) | copy-start | bytes 786436
  134.5 34.8 %copy-start.3 = (f32[1024]{0:T(1024)S(1)}, f32[1024]{0:T(1024)}, u32[]{:S(2)}) copy-start(f32[1024]{0:T(1024)} %param.13) | copy-start | bytes 12292
  134.5 34.8 %copy-start.4 = (s32[1,4]{1,0:T(1,128)S(1)}, s32[1,4]{1,0:T(1,128)}, u32[]{:S(2)}) copy-start(s32[1,4]{1,0:T(1,128)} %lengths_ref.1) | copy-start | bytes 52
  134.5 34.8 %all-to-all-start.2 = ((bf16[64,8,1024]{2,1,0:T(8,128)(2,1)}), bf16[64,8,1024]{2,1,0:T(8,128)(2,1)S(1)}, u32[]{:S(2)}, u32[]{:S(2)}) async-start(bf16[64,8,1024]{2,1,0:T(8,128)(2,1)} %bitcast.7), calls=%async_computation.2 | async-start | bytes 2097152 | tf_op jit(solution)/shard_map/all_to_all | solution.py:312
  171.6 18.8 %all-to-all-start.3 = ((bf16[32,4,1024]{2,1,0:T(4,128)(2,1)}), bf16[32,4,1024]{2,1,0:T(4,128)(2,1)S(1)}, u32[]{:S(2)}, u32[]{:S(2)}) async-start(bf16[32,4,1024]{2,1,0:T(4,128)(2,1)} %get-tuple-element.54), calls=%async_computation.3 | async-start | bytes 524288 | tf_op jit(solution)/shard_map/all_to_all | solution.py:234
  179.5 12.9 %copy-start.10 = (bf16[16,1024]{1,0:T(8,128)(2,1)S(1)}, bf16[16,1024]{1,0:T(8,128)(2,1)}, u32[]{:S(2)}) copy-start(bf16[16,1024]{1,0:T(8,128)(2,1)} %copy-done.9) | copy-start | bytes 98308
  190.5 1.8 collective-permute-start.16
  192.9 6.4 %collective-permute-start.19 = (f32[4,1024]{1,0:T(4,128)S(1)}, f32[4,1024]{1,0:T(4,128)S(1)}, u32[]{:S(2)}, u32[]{:S(2)}) collective-permute-start(f32[4,1024]{1,0:T(4,128)S(1)} %get-tuple-element.64), channel_id=1, source_target_pairs={{0,1},{1,2},{2,3},{3,0},{4,5},{5,6},{6,7},{7,4},{8,9},{9,10},{10,1... | collective-permute-start | bytes 49160 | tf_op jit(solution)/shard_map/ppermute | solution.py:245
  194.4 5.2 %collective-permute-start.18 = (f32[4,1024]{1,0:T(4,128)S(1)}, f32[4,1024]{1,0:T(4,128)S(1)}, u32[]{:S(2)}, u32[]{:S(2)}) collective-permute-start(f32[4,1024]{1,0:T(4,128)S(1)} %get-tuple-element.65), channel_id=1, source_target_pairs={{0,2},{1,3},{2,0},{3,1},{4,6},{5,7},{6,4},{7,5},{8,10},{9,11},{10,... | collective-permute-start | bytes 49160 | tf_op jit(solution)/shard_map/ppermute | solution.py:245
  197.7 3.7 %collective-permute-start.17 = (f32[4,1024]{1,0:T(4,128)S(1)}, f32[4,1024]{1,0:T(4,128)S(1)}, u32[]{:S(2)}, u32[]{:S(2)}) collective-permute-start(f32[4,1024]{1,0:T(4,128)S(1)} %get-tuple-element.63), channel_id=1, source_target_pairs={{0,3},{1,0},{2,1},{3,2},{4,7},{5,4},{6,5},{7,6},{8,11},{9,8},{10,9... | collective-permute-start | bytes 49160 | tf_op jit(solution)/shard_map/ppermute | solution.py:245

commit v4 on v3

--- a/solution.py
+++ b/solution.py
@@ -22,50 +22,51 @@
 def expert_kernel(*refs):
     blocks = (len(refs) - 3) // 2
     rows_refs, (up_ref, down_ref) = refs[:blocks], refs[blocks : blocks + 2]
-    out_refs, total_ref = refs[blocks + 2 : -1], refs[-1]
+    out_refs, hidden_ref = refs[blocks + 2 : -1], refs[-1]
     step = pl.program_id(0)
-    rows = jnp.concatenate([ref[...] for ref in rows_refs], axis=0)
-    hidden = jnp.dot(rows, up_ref[...], preferred_element_type=F32)
-    hidden = (0.5 * hidden * (1.0 + lax.erf(hidden * math.sqrt(0.5)))).astype(BF16)
-    term = lax.dot_general(
-        hidden, down_ref[...], (((1,), (1,)), ((), ())), preferred_element_type=F32
-    )
-
-    @pl.when(step == 0)
+    half = pl.num_programs(0) // 2
+    tile = up_ref.shape[1]
+
+    @pl.when(step < half)
     def _():
-        total_ref[...] = term
-
-    @pl.when(step > 0)
+        rows = jnp.concatenate([ref[...] for ref in rows_refs], axis=0)
+        hidden = jnp.dot(rows, up_ref[...], preferred_element_type=F32)
+        hidden = (0.5 * hidden * (1.0 + lax.erf(hidden * math.sqrt(0.5)))).astype(BF16)
+        hidden_ref[:, pl.ds(pl.multiple_of(step * tile, tile), tile)] = hidden
+
+    @pl.when(step >= half)
     def _():
-        total_ref[...] += term
-
-    @pl.when(step == pl.num_programs(0) - 1)
-    def _():
+        term = lax.dot_general(
+            hidden_ref[...], down_ref[...], (((1,), (1,)), ((), ())), preferred_element_type=F32
+        ).astype(BF16)
         start = 0
         for ref in out_refs:
-            ref[...] = total_ref[start : start + ref.shape[0], :].astype(BF16)
+            ref[...] = term[start : start + ref.shape[0]]
             start += ref.shape[0]
 
 
 def expert_part(blocks, up_piece, down_piece):
     width, units = up_piece.shape
     count = sum(block.shape[0] for block in blocks)
-    tile = min(256, units)
-    whole = [pl.BlockSpec(block.shape, lambda i: (0, 0)) for block in blocks]
+    tile = min(512, units)
+    half = units // tile
     return pl.pallas_call(
         expert_kernel,
-        grid=(units // tile,),
-        in_specs=whole
+        grid=(2 * half,),
+        in_specs=[pl.BlockSpec(block.shape, lambda i: (0, 0)) for block in blocks]
         + [
-            pl.BlockSpec((width, tile), lambda i: (0, i)),
-            pl.BlockSpec((width, tile), lambda i: (0, i)),
-        ],
-        out_specs=whole,
+            pl.BlockSpec((width, tile), lambda i: (0, jnp.minimum(i, half - 1))),
+            pl.BlockSpec((width // half, units), lambda i: (jnp.maximum(i - half, 0), 0)),
+        ],
+        out_specs=[
+            pl.BlockSpec((block.shape[0], width // half), lambda i: (0, jnp.maximum(i - half, 0)))
+            for block in blocks
+        ],
         out_shape=[jax.ShapeDtypeStruct(block.shape, BF16) for block in blocks],
-        scratch_shapes=[pltpu.VMEM((count, width), F32)],
+        scratch_shapes=[pltpu.VMEM((count, units), BF16)],
         compiler_params=pltpu.CompilerParams(vmem_limit_bytes=56 * 2**20),
         cost_estimate=pl.CostEstimate(
-            flops=16 * count * width * units,
+            flops=12 * count * width * units,
             bytes_accessed=4 * width * units + 4 * count * width,
             transcendentals=count * units,
         ),
@@ -196,6 +197,26 @@
     )(lengths, returned, tokens, place, gates, gain.reshape(1, width))
 
 
+def spread_kernel(*refs):
+    rows_ref, copies_ref = refs[-2:]
+    rows = jnp.concatenate([ref[...].astype(F32) for ref in refs[:-2]], axis=0).astype(BF16)
+    rows_ref[...] = rows
+    copies_ref[...] = jnp.broadcast_to(rows[None], copies_ref.shape)
+
+
+def spread(parts, copies):
+    count = sum(part.shape[0] for part in parts)
+    width = parts[0].shape[1]
+    return pl.pallas_call(
+        spread_kernel,
+        out_shape=[
+            jax.ShapeDtypeStruct((count, width), BF16),
+            jax.ShapeDtypeStruct((copies, count, width), BF16),
+        ],
+        compiler_params=pltpu.CompilerParams(vmem_limit_bytes=8 * 2**20),
+    )(*parts)
+
+
 def split_pair(values):
     high = values.astype(BF16)
     return high, (values - high.astype(F32)).astype(BF16)
@@ -268,9 +289,8 @@
     send, place = dispatch(tokens, routes, places_all, slots)
     send = send.reshape(experts_all, slots, width)
     arrived = lax.all_to_all(send, "expert", split_axis=0, concat_axis=0, tiled=True)
-    pictures_row = jnp.concatenate(row_parts, axis=0)
     chips = shape[0] * shape[1]
-    picture_copies = jnp.broadcast_to(pictures_row[None], (chips,) + pictures_row.shape)
+    pictures_row, picture_copies = spread(row_parts, chips)
     arrived, picture_copies, pictures_row = held(arrived, picture_copies, pictures_row)
     rows = arrived.reshape(places_all, width)
 

time: 203 us -> 205 us (level)
  Pallas kernels: 39.4 us -> 32.4 us
  waiting for transfers between devices: 91.9 us -> 98.1 us
  starting transfers between devices: 59.5 us -> 64 us
  local copies, waits for them, and re-layouts: 4.95 us -> 2.88 us
    ppermute x18, waiting for transfers between devices: 32.9 us -> 40.6 us  [ring_shift(): lax.ppermute(values, 'grid', [(i, (i + step) % size) for i in range(size)])]
    pallas_call x4 -> x5, Pallas kernels: 33.3 us -> 26.3 us  [the longest x4 25.2 us: expert_part(): pl.pallas_call(expert_kernel, grid=(2 * half,), in_specs=[pl.BlockSpec(bl...]
    all_to_all x1, starting transfers between devices: 6.93 us -> 10.3 us  [on_device(): lax.all_to_all(results, 'expert', split_axis=0, concat_axis=0, tiled=True)]
  transfers between devices with their start and end apart: 24 -> 24, of which waited for: 11 -> 12; matrix products, arithmetic and copies ran while one was open for 2% -> 3% of each run, Pallas kernels for 16% -> 13%
where the time goes in v4:
time: 205 us
  waiting for transfers between devices  98.1 us (48%)
  starting transfers between devices  64 us (31%)
  Pallas kernels  32.4 us (16%)
  other arithmetic  3.35 us (2%)
  matrix products  3.12 us (2%)
  local copies, waits for them, and re-layouts  2.88 us (1%)
    ppermute x18, waiting for transfers between devices, ring_shift(): lax.ppermute(values, 'grid', [(i, (i + step) % size) for i in range(size)])  40.6 us
    ppermute x18, starting transfers between devices, ring_shift(): lax.ppermute(values, 'grid', [(i, (i + step) % size) for i in range(size)])  28.7 us
    all_to_all x1, waiting for transfers between devices, on_device(): lax.all_to_all(results, 'expert', split_axis=0, concat_axis=0, tiled=True)  27.7 us
    pallas_call x4, Pallas kernels, expert_part(): pl.pallas_call(expert_kernel, grid=(2 * half,), in_specs=[pl.BlockSpec(bl...  25.2 us
    all_to_all x1, waiting for transfers between devices, on_device(): lax.all_to_all(send, 'expert', split_axis=0, concat_axis=0, tiled=True)  18.6 us
    all_to_all x2, starting transfers between devices, along_expert(): lax.all_to_all(copies, 'expert', split_axis=0, concat_axis=0, axis_index_...  13 us
    all_to_all x1, starting transfers between devices, on_device(): lax.all_to_all(send, 'expert', split_axis=0, concat_axis=0, tiled=True)  11.8 us
    all_to_all x1, starting transfers between devices, on_device(): lax.all_to_all(results, 'expert', split_axis=0, concat_axis=0, tiled=True)  10.3 us
  transfers between devices with their start and end apart: 24, of which 12 were waited for; matrix products, arithmetic and copies ran while one was open for 3% of the time, Pallas kernels for 13%

profile of v4, /device:TPU:32, one launch (start us, length us, event | category | flops | bytes accessed | tf_op | source)
XLA Modules:
  0.0 204.7 jit_solution(9341383496256345548)
XLA Ops:
  0.6 0.8 copy.11.routes_ref
  1.4 0.9 copy-done
  2.4 1.9 shard_map.103
  4.3 11.8 %all-to-all-start = ((bf16[64,8,1024]{2,1,0:T(8,128)(2,1)}), bf16[64,8,1024]{2,1,0:T(8,128)(2,1)S(1)}, u32[]{:S(2)}, u32[]{:S(2)}) async-start(bf16[64,8,1024]{2,1,0:T(8,128)(2,1)} %bitcast), calls=%async_computation | async-start | bytes 2097152 | tf_op jit(solution)/shard_map/all_to_all | solution.py:291
  16.1 0.1 fusion.13
  16.2 0.1 fusion.15.refs_0_
  16.3 1.5 collective-permute-start
  17.8 2.7 %collective-permute-start.1 = (bf16[4,1024]{1,0:T(4,128)(2,1)S(1)}, bf16[4,1024]{1,0:T(4,128)(2,1)S(1)}, u32[]{:S(2)}, u32[]{:S(2)}) collective-permute-start(bf16[4,1024]{1,0:T(4,128)(2,1)S(1)} %fusion.15.refs_0_), channel_id=1, source_target_pairs={{0,2},{1,3},{2,0},{3,1},{4,6},{5,7},{6,4},{7,5},{8,10},{9,11},{10,... | collective-permute-start | bytes 24584 | tf_op jit(solution)/shard_map/ppermute | solution.py:266
  20.5 1.4 collective-permute-start.2
  22.0 0.0 collective-permute-done.refs_1_
  22.0 1.0 collective-permute-done.1.refs_2_
  23.0 1.2 collective-permute-done.2.refs_3_
  24.2 1.1 shard_map.104
  25.3 18.6 %all-to-all-done = bf16[64,8,1024]{2,1,0:T(8,128)(2,1)S(1)} async-done(((bf16[64,8,1024]{2,1,0:T(8,128)(2,1)}), bf16[64,8,1024]{2,1,0:T(8,128)(2,1)S(1)}, u32[]{:S(2)}, u32[]{:S(2)}) %all-to-all-start) | async-done | bytes 1048608 | tf_op jit(solution)/shard_map/all_to_all | solution.py:291
  43.9 6.5 %all-to-all-start.1 = ((bf16[32,16,1024]{2,1,0:T(8,128)(2,1)}), bf16[32,16,1024]{2,1,0:T(8,128)(2,1)S(1)}, u32[]{:S(2)}, u32[]{:S(2)}) async-start(bf16[32,16,1024]{2,1,0:T(8,128)(2,1)} %get-tuple-element.49), calls=%async_computation.1 | async-start | bytes 2097152 | tf_op jit(solution)/shard_map/all_to_all | solution.py:255
  50.4 0.1 slice_bitcast_fusion
  50.5 1.6 collective-permute-start.3
  52.1 1.7 collective-permute-start.7
  53.8 1.5 collective-permute-start.4
  55.4 0.5 collective-permute-start.8
  55.8 6.3 %shard_map.105.own_ref = bf16[512,1024]{1,0:T(8,128)(2,1)} custom-call(bf16[512,1024]{1,0:T(8,128)(2,1)} %bitcast.24, bf16[1024,1024]{1,0:T(8,128)(2,1)} %bitcast.27, bf16[1024,1024]{1,0:T(8,128)(2,1)} %bitcast.31), custom_call_target="tpu_custom_call" | custom-call | flops 6442450944 | bytes 6291456 | tf_op jit(solution)/shard_map/pallas_call | solution.py:53
  62.1 4.5 %collective-permute-done.3.refs_0_ = bf16[256,1024]{1,0:T(8,128)(2,1)S(1)} collective-permute-done((bf16[256,1024]{1,0:T(8,128)(2,1)S(1)}, bf16[256,1024]{1,0:T(8,128)(2,1)S(1)}, u32[]{:S(2)}, u32[]{:S(2)}) %collective-permute-start.3) | collective-permute-done | bytes 524320 | tf_op jit(solution)/shard_map/ppermute | solution.py:266
  66.6 9.6 %collective-permute-done.4.refs_1_ = bf16[256,1024]{1,0:T(8,128)(2,1)S(1)} collective-permute-done((bf16[256,1024]{1,0:T(8,128)(2,1)S(1)}, bf16[256,1024]{1,0:T(8,128)(2,1)S(1)}, u32[]{:S(2)}, u32[]{:S(2)}) %collective-permute-start.4) | collective-permute-done | bytes 524320 | tf_op jit(solution)/shard_map/ppermute | solution.py:266
  76.2 1.5 collective-permute-start.5
  77.7 1.7 collective-permute-start.6
  79.5 6.3 %shard_map.106 = (bf16[256,1024]{1,0:T(8,128)(2,1)}, bf16[256,1024]{1,0:T(8,128)(2,1)}) custom-call(bf16[256,1024]{1,0:T(8,128)(2,1)} %copy-done.11, bf16[256,1024]{1,0:T(8,128)(2,1)} %copy-done.12, bf16[1024,1024]{1,0:T(8,128)(2,1)} %bitcast.28, bf16[1024,1024]{1,0:T(8,128)(2,1)} %bitcast.32), custom_call_target="tpu_custom_call" | custom-call | flops 6442450944 | bytes 6291456 | tf_op jit(solution)/shard_map/pallas_call | solution.py:53
  85.8 1.7 collective-permute-start.11
  87.6 0.8 copy-done.13
  88.4 0.3 collective-permute-start.12
  88.6 0.0 collective-permute-done.8.refs_1_
  88.6 0.0 all-to-all-done.1
  88.6 0.0 collective-permute-start.13
  88.7 6.3 %shard_map.107 = (bf16[256,1024]{1,0:T(8,128)(2,1)}, bf16[256,1024]{1,0:T(8,128)(2,1)}) custom-call(bf16[256,1024]{1,0:T(8,128)(2,1)} %copy-done.13, bf16[256,1024]{1,0:T(8,128)(2,1)} %collective-permute-done.8.refs_1_, bf16[1024,1024]{1,0:T(8,128)(2,1)} %bitcast.29, bf16[1024,1024]{1,0:T(8,128)(2,1)} %bitcast.33), custom_call_target="tpu_custom_call" | custom-call | flops 6442450944 | bytes 6291456 | tf_op jit(solution)/shard_map/pallas_call | solution.py:53
  95.0 6.3 %shard_map.108 = (bf16[256,1024]{1,0:T(8,128)(2,1)}, bf16[256,1024]{1,0:T(8,128)(2,1)}) custom-call(bf16[256,1024]{1,0:T(8,128)(2,1)} %collective-permute-done.5.refs_0_, bf16[256,1024]{1,0:T(8,128)(2,1)} %collective-permute-done.6.refs_1_, bf16[1024,1024]{1,0:T(8,128)(2,1)} %bitcast.30, bf16[1024,1024]{1,0:T(8,128)(2,1)} %bitcast.34), custom_call_target="tpu_custom_call" | custom-call | flops 6442450944 | bytes 6291456 | tf_op jit(solution)/shard_map/pallas_call | solution.py:53
  101.3 0.3 collective-permute-start.9
  101.5 3.0 %collective-permute-start.10 = (bf16[256,1024]{1,0:T(8,128)(2,1)}, bf16[256,1024]{1,0:T(8,128)(2,1)S(1)}, u32[]{:S(2)}, u32[]{:S(2)}) collective-permute-start(bf16[256,1024]{1,0:T(8,128)(2,1)} %get-tuple-element.48), channel_id=1, source_target_pairs={{0,3},{1,0},{2,1},{3,2},{4,7},{5,4},{6,5},{7,6},{8,11},{9,8},{10,9... | collective-permute-start | bytes 1572872 | tf_op jit(solution)/shard_map/ppermute | solution.py:266
  104.5 1.5 pad_maximum_fusion
  106.0 11.0 %collective-permute-done.9 = bf16[256,1024]{1,0:T(8,128)(2,1)S(1)} collective-permute-done((bf16[256,1024]{1,0:T(8,128)(2,1)}, bf16[256,1024]{1,0:T(8,128)(2,1)S(1)}, u32[]{:S(2)}, u32[]{:S(2)}) %collective-permute-start.9) | collective-permute-done | bytes 524320 | tf_op jit(solution)/shard_map/ppermute | solution.py:266
  117.0 0.2 add_convert_fusion.1
  117.2 1.2 collective-permute-start.14
  118.4 0.2 add_convert_fusion
  118.6 2.2 %collective-permute-start.15 = (bf16[256,1024]{1,0:T(8,128)(2,1)S(1)}, bf16[256,1024]{1,0:T(8,128)(2,1)S(1)}, u32[]{:S(2)}, u32[]{:S(2)}) collective-permute-start(bf16[256,1024]{1,0:T(8,128)(2,1)S(1)} %add_convert_fusion), channel_id=1, source_target_pairs={{0,3},{1,0},{2,1},{3,2},{4,7},{5,4},{6,5},{7,6},{8,11},{9,8},{10,9... | collective-permute-start | bytes 1572872 | tf_op jit(solution)/shard_map/ppermute | solution.py:266
  120.8 11.2 %collective-permute-done.14.last_top = bf16[256,1024]{1,0:T(8,128)(2,1)S(1)} collective-permute-done((bf16[256,1024]{1,0:T(8,128)(2,1)S(1)}, bf16[256,1024]{1,0:T(8,128)(2,1)S(1)}, u32[]{:S(2)}, u32[]{:S(2)}) %collective-permute-start.14) | collective-permute-done | bytes 524320 | tf_op jit(solution)/shard_map/ppermute | solution.py:266
  132.0 1.8 shard_map.109
  133.7 10.3 %all-to-all-start.2 = ((bf16[64,8,1024]{2,1,0:T(8,128)(2,1)}), bf16[64,8,1024]{2,1,0:T(8,128)(2,1)S(1)}, u32[]{:S(2)}, u32[]{:S(2)}) async-start(bf16[64,8,1024]{2,1,0:T(8,128)(2,1)} %bitcast.7), calls=%async_computation.2 | async-start | bytes 2097152 | tf_op jit(solution)/shard_map/all_to_all | solution.py:332
  144.1 0.1 copy.12.gates_ref
  144.2 27.7 %all-to-all-done.2 = bf16[64,8,1024]{2,1,0:T(8,128)(2,1)S(1)} async-done(((bf16[64,8,1024]{2,1,0:T(8,128)(2,1)}), bf16[64,8,1024]{2,1,0:T(8,128)(2,1)S(1)}, u32[]{:S(2)}, u32[]{:S(2)}) %all-to-all-start.2) | async-done | bytes 1048608 | tf_op jit(solution)/shard_map/all_to_all | solution.py:332
  172.0 2.4 %shard_map.110 = (f32[4,1024]{1,0:T(4,128)}, bf16[32,4,1024]{2,1,0:T(4,128)(2,1)}) custom-call(s32[1,4]{1,0:T(1,128)S(1)} %copy-done.4, bf16[512,1024]{1,0:T(8,128)(2,1)S(1)} %bitcast.22, bf16[128,1024]{1,0:T(8,128)(2,1)S(1)} %copy-done.1, s32[128,2]{1,0:T(8,128)S(1)} %get-tuple-element.56.place_ref, f32[128,2]{1,0:T(8,128)S(1)} %copy.12.gates_ref, ...), custom_call_target="tpu_custom_call" | custom-call | tf_op jit(solution)/shard_map/pallas_call | solution.py:188
  174.3 6.6 %all-to-all-start.3 = ((bf16[32,4,1024]{2,1,0:T(4,128)(2,1)}), bf16[32,4,1024]{2,1,0:T(4,128)(2,1)S(1)}, u32[]{:S(2)}, u32[]{:S(2)}) async-start(bf16[32,4,1024]{2,1,0:T(4,128)(2,1)} %get-tuple-element.58), calls=%async_computation.3 | async-start | bytes 524288 | tf_op jit(solution)/shard_map/all_to_all | solution.py:255
  181.0 2.3 %subtract_convert_fusion.1 = (bf16[4,1024]{1,0:T(4,128)(2,1)S(1)}, bf16[4,1024]{1,0:T(4,128)(2,1)S(1)}) fusion(bf16[1024,1024]{1,0:T(8,128)(2,1)} %pad_maximum_fusion, bf16[32,4,1024]{2,1,0:T(4,128)(2,1)} %get-tuple-element.58, s32[4]{0:T(128)S(1)} %iota_add_fusion.1, pred[4]{0:T(512)(128)(4,1)S(1)} %iota_compare_fusion.3), kind=kOutput, calls=%fused_computation.41 | convolution fusion | flops 8445952 | bytes 2121748 | tf_op jit(solution)/shard_map/dot_general | solution.py:342
  183.3 10.0 %all-to-all-done.3 = bf16[32,4,1024]{2,1,0:T(4,128)(2,1)S(1)} async-done(((bf16[32,4,1024]{2,1,0:T(4,128)(2,1)}), bf16[32,4,1024]{2,1,0:T(4,128)(2,1)S(1)}, u32[]{:S(2)}, u32[]{:S(2)}) %all-to-all-start.3) | async-done | bytes 262176 | tf_op jit(solution)/shard_map/all_to_all | solution.py:255
  193.3 0.1 reshape.52
  193.4 0.1 collective-permute-start.16
  193.5 0.4 fusion.19
  193.9 1.1 collective-permute-done.16
  195.0 0.3 subtract_convert_fusion
  195.3 0.2 fusion.23
  195.5 1.4 collective-permute-start.19
  197.0 3.3 %collective-permute-start.18 = (f32[4,1024]{1,0:T(4,128)S(1)}, f32[4,1024]{1,0:T(4,128)S(1)}, u32[]{:S(2)}, u32[]{:S(2)}) collective-permute-start(f32[4,1024]{1,0:T(4,128)S(1)} %get-tuple-element.69), channel_id=1, source_target_pairs={{0,2},{1,3},{2,0},{3,1},{4,6},{5,7},{6,4},{7,5},{8,10},{9,11},{10,... | collective-permute-start | bytes 49160 | tf_op jit(solution)/shard_map/ppermute | solution.py:266
  200.3 1.0 collective-permute-start.17
  201.3 0.6 fusion.18
  202.0 0.3 collective-permute-done.18
  202.2 1.8 collective-permute-done.17
  204.0 0.6 fusion.17
  (44 shorter events, 0.2 us)
Async XLA Ops:
  0.6 15.5 %copy-start.9 = (bf16[4,1024]{1,0:T(4,128)(2,1)S(1)}, bf16[4,1024]{1,0:T(4,128)(2,1)}, u32[]{:S(2)}) copy-start(bf16[4,1024]{1,0:T(4,128)(2,1)} %param.12) | copy-start | bytes 24580
  1.4 0.9 copy-start
  4.3 39.6 %all-to-all-start = ((bf16[64,8,1024]{2,1,0:T(8,128)(2,1)}), bf16[64,8,1024]{2,1,0:T(8,128)(2,1)S(1)}, u32[]{:S(2)}, u32[]{:S(2)}) async-start(bf16[64,8,1024]{2,1,0:T(8,128)(2,1)} %bitcast), calls=%async_computation | async-start | bytes 2097152 | tf_op jit(solution)/shard_map/all_to_all | solution.py:291
  16.3 5.7 %collective-permute-start = (bf16[4,1024]{1,0:T(4,128)(2,1)S(1)}, bf16[4,1024]{1,0:T(4,128)(2,1)S(1)}, u32[]{:S(2)}, u32[]{:S(2)}) collective-permute-start(bf16[4,1024]{1,0:T(4,128)(2,1)S(1)} %fusion.15.refs_0_), channel_id=1, source_target_pairs={{0,1},{1,2},{2,3},{3,0},{4,5},{5,6},{6,7},{7,4},{8,9},{9,10},{10,1... | collective-permute-start | bytes 24584 | tf_op jit(solution)/shard_map/ppermute | solution.py:266
  17.8 5.2 %collective-permute-start.1 = (bf16[4,1024]{1,0:T(4,128)(2,1)S(1)}, bf16[4,1024]{1,0:T(4,128)(2,1)S(1)}, u32[]{:S(2)}, u32[]{:S(2)}) collective-permute-start(bf16[4,1024]{1,0:T(4,128)(2,1)S(1)} %fusion.15.refs_0_), channel_id=1, source_target_pairs={{0,2},{1,3},{2,0},{3,1},{4,6},{5,7},{6,4},{7,5},{8,10},{9,11},{10,... | collective-permute-start | bytes 24584 | tf_op jit(solution)/shard_map/ppermute | solution.py:266
  20.5 3.7 %collective-permute-start.2 = (bf16[4,1024]{1,0:T(4,128)(2,1)S(1)}, bf16[4,1024]{1,0:T(4,128)(2,1)S(1)}, u32[]{:S(2)}, u32[]{:S(2)}) collective-permute-start(bf16[4,1024]{1,0:T(4,128)(2,1)S(1)} %fusion.15.refs_0_), channel_id=1, source_target_pairs={{0,3},{1,0},{2,1},{3,2},{4,7},{5,4},{6,5},{7,6},{8,11},{9,8},{10,9... | collective-permute-start | bytes 24584 | tf_op jit(solution)/shard_map/ppermute | solution.py:266
  43.9 6.5 %copy-start.6 = (bf16[64,8,1024]{2,1,0:T(8,128)(2,1)}, bf16[64,8,1024]{2,1,0:T(8,128)(2,1)S(1)}, u32[]{:S(2)}) copy-start(bf16[64,8,1024]{2,1,0:T(8,128)(2,1)S(1)} %all-to-all-done) | copy-start | bytes 3145732
  43.9 44.7 %all-to-all-start.1 = ((bf16[32,16,1024]{2,1,0:T(8,128)(2,1)}), bf16[32,16,1024]{2,1,0:T(8,128)(2,1)S(1)}, u32[]{:S(2)}, u32[]{:S(2)}) async-start(bf16[32,16,1024]{2,1,0:T(8,128)(2,1)} %get-tuple-element.49), calls=%async_computation.1 | async-start | bytes 2097152 | tf_op jit(solution)/shard_map/all_to_all | solution.py:255
  50.5 16.1 %collective-permute-start.3 = (bf16[256,1024]{1,0:T(8,128)(2,1)S(1)}, bf16[256,1024]{1,0:T(8,128)(2,1)S(1)}, u32[]{:S(2)}, u32[]{:S(2)}) collective-permute-start(bf16[256,1024]{1,0:T(8,128)(2,1)S(1)} %get-tuple-element.66), channel_id=1, source_target_pairs={{0,1},{1,2},{2,3},{3,0},{4,5},{5,6},{6,7},{7,4},{8,9},{9,10},{10,1... | collective-permute-start | bytes 1572872 | tf_op jit(solution)/shard_map/ppermute | solution.py:266
  52.1 35.5 %collective-permute-start.7 = (bf16[256,1024]{1,0:T(8,128)(2,1)S(1)}, bf16[256,1024]{1,0:T(8,128)(2,1)S(1)}, u32[]{:S(2)}, u32[]{:S(2)}) collective-permute-start(bf16[256,1024]{1,0:T(8,128)(2,1)S(1)} %get-tuple-element.66), channel_id=1, source_target_pairs={{0,3},{1,0},{2,1},{3,2},{4,7},{5,4},{6,5},{7,6},{8,11},{9,8},{10,9... | collective-permute-start | bytes 1572872 | tf_op jit(solution)/shard_map/ppermute | solution.py:266
  53.8 22.4 %collective-permute-start.4 = (bf16[256,1024]{1,0:T(8,128)(2,1)S(1)}, bf16[256,1024]{1,0:T(8,128)(2,1)S(1)}, u32[]{:S(2)}, u32[]{:S(2)}) collective-permute-start(bf16[256,1024]{1,0:T(8,128)(2,1)S(1)} %get-tuple-element.65), channel_id=1, source_target_pairs={{0,3},{1,0},{2,1},{3,2},{4,7},{5,4},{6,5},{7,6},{8,11},{9,8},{10,9... | collective-permute-start | bytes 1572872 | tf_op jit(solution)/shard_map/ppermute | solution.py:266
  55.4 33.3 %collective-permute-start.8 = (bf16[256,1024]{1,0:T(8,128)(2,1)S(1)}, bf16[256,1024]{1,0:T(8,128)(2,1)}, u32[]{:S(2)}, u32[]{:S(2)}) collective-permute-start(bf16[256,1024]{1,0:T(8,128)(2,1)S(1)} %get-tuple-element.65), channel_id=1, source_target_pairs={{0,1},{1,2},{2,3},{3,0},{4,5},{5,6},{6,7},{7,4},{8,9},{9,10},{10,1... | collective-permute-start | bytes 1572872 | tf_op jit(solution)/shard_map/ppermute | solution.py:266
  66.6 12.9 %copy-start.11 = (bf16[256,1024]{1,0:T(8,128)(2,1)}, bf16[256,1024]{1,0:T(8,128)(2,1)S(1)}, u32[]{:S(2)}) copy-start(bf16[256,1024]{1,0:T(8,128)(2,1)S(1)} %collective-permute-done.3.refs_0_) | copy-start | bytes 1572868
  76.2 3.2 %copy-start.12 = (bf16[256,1024]{1,0:T(8,128)(2,1)}, bf16[256,1024]{1,0:T(8,128)(2,1)S(1)}, u32[]{:S(2)}) copy-start(bf16[256,1024]{1,0:T(8,128)(2,1)S(1)} %collective-permute-done.4.refs_1_) | copy-start | bytes 1572868
  76.2 18.8 %collective-permute-start.5 = (bf16[256,1024]{1,0:T(8,128)(2,1)S(1)}, bf16[256,1024]{1,0:T(8,128)(2,1)}, u32[]{:S(2)}, u32[]{:S(2)}) collective-permute-start(bf16[256,1024]{1,0:T(8,128)(2,1)S(1)} %collective-permute-done.3.refs_0_), channel_id=1, source_target_pairs={{0,1},{1,2},{2,3},{3,0},{4,5},{5,6},{6,7},{7,4},{8,9},{9,10},{10,1... | collective-permute-start | bytes 1572872 | tf_op jit(solution)/shard_map/ppermute | solution.py:266
  77.7 17.3 %collective-permute-start.6 = (bf16[256,1024]{1,0:T(8,128)(2,1)S(1)}, bf16[256,1024]{1,0:T(8,128)(2,1)}, u32[]{:S(2)}, u32[]{:S(2)}) collective-permute-start(bf16[256,1024]{1,0:T(8,128)(2,1)S(1)} %collective-permute-done.4.refs_1_), channel_id=1, source_target_pairs={{0,3},{1,0},{2,1},{3,2},{4,7},{5,4},{6,5},{7,6},{8,11},{9,8},{10,9... | collective-permute-start | bytes 1572872 | tf_op jit(solution)/shard_map/ppermute | solution.py:266
  85.8 20.2 %collective-permute-start.11 = (bf16[256,1024]{1,0:T(8,128)(2,1)}, bf16[256,1024]{1,0:T(8,128)(2,1)S(1)}, u32[]{:S(2)}, u32[]{:S(2)}) collective-permute-start(bf16[256,1024]{1,0:T(8,128)(2,1)} %get-tuple-element.39), channel_id=1, source_target_pairs={{0,3},{1,0},{2,1},{3,2},{4,7},{5,4},{6,5},{7,6},{8,11},{9,8},{10,9... | collective-permute-start | bytes 1572872 | tf_op jit(solution)/shard_map/ppermute | solution.py:266
  87.6 0.8 copy-start.13
  88.4 17.7 %collective-permute-start.12 = (bf16[256,1024]{1,0:T(8,128)(2,1)}, bf16[256,1024]{1,0:T(8,128)(2,1)S(1)}, u32[]{:S(2)}, u32[]{:S(2)}) collective-permute-start(bf16[256,1024]{1,0:T(8,128)(2,1)} %get-tuple-element.40), channel_id=1, source_target_pairs={{0,1},{1,2},{2,3},{3,0},{4,5},{5,6},{6,7},{7,4},{8,9},{9,10},{10,1... | collective-permute-start | bytes 1572872 | tf_op jit(solution)/shard_map/ppermute | solution.py:266
  88.6 15.9 %collective-permute-start.13 = (bf16[512,1024]{1,0:T(8,128)(2,1)S(1)}, bf16[512,1024]{1,0:T(8,128)(2,1)S(1)}, u32[]{:S(2)}, u32[]{:S(2)}) collective-permute-start(bf16[512,1024]{1,0:T(8,128)(2,1)S(1)} %bitcast.25), channel_id=1, source_target_pairs={{0,4},{4,0},{8,12},{12,8},{16,20},{20,16},{24,28},{28,24},{32,36},... | collective-permute-start | bytes 3145736 | tf_op jit(solution)/shard_map/ppermute | solution.py:248
  101.3 15.7 %collective-permute-start.9 = (bf16[256,1024]{1,0:T(8,128)(2,1)}, bf16[256,1024]{1,0:T(8,128)(2,1)S(1)}, u32[]{:S(2)}, u32[]{:S(2)}) collective-permute-start(bf16[256,1024]{1,0:T(8,128)(2,1)} %get-tuple-element.47), channel_id=1, source_target_pairs={{0,1},{1,2},{2,3},{3,0},{4,5},{5,6},{6,7},{7,4},{8,9},{9,10},{10,1... | collective-permute-start | bytes 1572872 | tf_op jit(solution)/shard_map/ppermute | solution.py:266
  101.5 15.5 %copy-start.8 = (bf16[256,1024]{1,0:T(8,128)(2,1)S(1)}, bf16[256,1024]{1,0:T(8,128)(2,1)}, u32[]{:S(2)}) copy-start(bf16[256,1024]{1,0:T(8,128)(2,1)} %get-tuple-element.51) | copy-start | bytes 1572868
  101.5 16.9 %copy-start.7 = (bf16[256,1024]{1,0:T(8,128)(2,1)S(1)}, bf16[256,1024]{1,0:T(8,128)(2,1)}, u32[]{:S(2)}) copy-start(bf16[256,1024]{1,0:T(8,128)(2,1)} %get-tuple-element.54) | copy-start | bytes 1572868
  101.5 15.5 %collective-permute-start.10 = (bf16[256,1024]{1,0:T(8,128)(2,1)}, bf16[256,1024]{1,0:T(8,128)(2,1)S(1)}, u32[]{:S(2)}, u32[]{:S(2)}) collective-permute-start(bf16[256,1024]{1,0:T(8,128)(2,1)} %get-tuple-element.48), channel_id=1, source_target_pairs={{0,3},{1,0},{2,1},{3,2},{4,7},{5,4},{6,5},{7,6},{8,11},{9,8},{10,9... | collective-permute-start | bytes 1572872 | tf_op jit(solution)/shard_map/ppermute | solution.py:266
  106.0 26.0 %copy-start.2 = (bf16[512,1024]{1,0:T(8,128)(2,1)S(1)}, bf16[512,1024]{1,0:T(8,128)(2,1)}, u32[]{:S(2)}) copy-start(bf16[512,1024]{1,0:T(8,128)(2,1)} %shard_map.105.own_ref) | copy-start | bytes 3145732
  117.2 14.7 %collective-permute-start.14 = (bf16[256,1024]{1,0:T(8,128)(2,1)S(1)}, bf16[256,1024]{1,0:T(8,128)(2,1)S(1)}, u32[]{:S(2)}, u32[]{:S(2)}) collective-permute-start(bf16[256,1024]{1,0:T(8,128)(2,1)S(1)} %add_convert_fusion.1), channel_id=1, source_target_pairs={{0,1},{1,2},{2,3},{3,0},{4,5},{5,6},{6,7},{7,4},{8,9},{9,10},{10,1... | collective-permute-start | bytes 1572872 | tf_op jit(solution)/shard_map/ppermute | solution.py:266
  118.6 13.3 %collective-permute-start.15 = (bf16[256,1024]{1,0:T(8,128)(2,1)S(1)}, bf16[256,1024]{1,0:T(8,128)(2,1)S(1)}, u32[]{:S(2)}, u32[]{:S(2)}) collective-permute-start(bf16[256,1024]{1,0:T(8,128)(2,1)S(1)} %add_convert_fusion), channel_id=1, source_target_pairs={{0,3},{1,0},{2,1},{3,2},{4,7},{5,4},{6,5},{7,6},{8,11},{9,8},{10,9... | collective-permute-start | bytes 1572872 | tf_op jit(solution)/shard_map/ppermute | solution.py:266
  133.7 10.4 %copy-start.10 = (f32[128,2]{0,1:T(2,128)S(1)}, f32[128,2]{0,1:T(2,128)}, u32[]{:S(2)}) copy-start(f32[128,2]{0,1:T(2,128)} %param.10) | copy-start | bytes 3076
  133.7 38.2 %copy-start.1 = (bf16[128,1024]{1,0:T(8,128)(2,1)S(1)}, bf16[128,1024]{1,0:T(8,128)(2,1)}, u32[]{:S(2)}) copy-start(bf16[128,1024]{1,0:T(8,128)(2,1)} %tokens_ref.3) | copy-start | bytes 786436
  133.7 38.2 %copy-start.3 = (f32[1024]{0:T(1024)S(1)}, f32[1024]{0:T(1024)}, u32[]{:S(2)}) copy-start(f32[1024]{0:T(1024)} %param.13) | copy-start | bytes 12292
  133.7 38.2 %copy-start.4 = (s32[1,4]{1,0:T(1,128)S(1)}, s32[1,4]{1,0:T(1,128)}, u32[]{:S(2)}) copy-start(s32[1,4]{1,0:T(1,128)} %lengths_ref.1) | copy-start | bytes 52
  133.7 38.2 %all-to-all-start.2 = ((bf16[64,8,1024]{2,1,0:T(8,128)(2,1)}), bf16[64,8,1024]{2,1,0:T(8,128)(2,1)S(1)}, u32[]{:S(2)}, u32[]{:S(2)}) async-start(bf16[64,8,1024]{2,1,0:T(8,128)(2,1)} %bitcast.7), calls=%async_computation.2 | async-start | bytes 2097152 | tf_op jit(solution)/shard_map/all_to_all | solution.py:332
  174.3 19.1 %copy-start.5 = (bf16[1024,1024]{1,0:T(8,128)(2,1)S(1)}, bf16[1024,1024]{1,0:T(8,128)(2,1)}, u32[]{:S(2)}) copy-start(bf16[1024,1024]{1,0:T(8,128)(2,1)} %pad_maximum_fusion) | copy-start | bytes 6291460
  174.3 19.0 %all-to-all-start.3 = ((bf16[32,4,1024]{2,1,0:T(4,128)(2,1)}), bf16[32,4,1024]{2,1,0:T(4,128)(2,1)S(1)}, u32[]{:S(2)}, u32[]{:S(2)}) async-start(bf16[32,4,1024]{2,1,0:T(4,128)(2,1)} %get-tuple-element.58), calls=%async_computation.3 | async-start | bytes 524288 | tf_op jit(solution)/shard_map/all_to_all | solution.py:255
  193.4 1.6 collective-permute-start.16
  195.5 6.4 %collective-permute-start.19 = (f32[4,1024]{1,0:T(4,128)S(1)}, f32[4,1024]{1,0:T(4,128)S(1)}, u32[]{:S(2)}, u32[]{:S(2)}) collective-permute-start(f32[4,1024]{1,0:T(4,128)S(1)} %get-tuple-element.68), channel_id=1, source_target_pairs={{0,1},{1,2},{2,3},{3,0},{4,5},{5,6},{6,7},{7,4},{8,9},{9,10},{10,1... | collective-permute-start | bytes 49160 | tf_op jit(solution)/shard_map/ppermute | solution.py:266
  197.0 5.2 %collective-permute-start.18 = (f32[4,1024]{1,0:T(4,128)S(1)}, f32[4,1024]{1,0:T(4,128)S(1)}, u32[]{:S(2)}, u32[]{:S(2)}) collective-permute-start(f32[4,1024]{1,0:T(4,128)S(1)} %get-tuple-element.69), channel_id=1, source_target_pairs={{0,2},{1,3},{2,0},{3,1},{4,6},{5,7},{6,4},{7,5},{8,10},{9,11},{10,... | collective-permute-start | bytes 49160 | tf_op jit(solution)/shard_map/ppermute | solution.py:266
  200.3 3.7 %collective-permute-start.17 = (f32[4,1024]{1,0:T(4,128)S(1)}, f32[4,1024]{1,0:T(4,128)S(1)}, u32[]{:S(2)}, u32[]{:S(2)}) collective-permute-start(f32[4,1024]{1,0:T(4,128)S(1)} %get-tuple-element.67), channel_id=1, source_target_pairs={{0,3},{1,0},{2,1},{3,2},{4,7},{5,4},{6,5},{7,6},{8,11},{9,8},{10,9... | collective-permute-start | bytes 49160 | tf_op jit(solution)/shard_map/ppermute | solution.py:266

commit v5 on v4

--- a/solution.py
+++ b/solution.py
@@ -64,7 +64,7 @@
         ],
         out_shape=[jax.ShapeDtypeStruct(block.shape, BF16) for block in blocks],
         scratch_shapes=[pltpu.VMEM((count, units), BF16)],
-        compiler_params=pltpu.CompilerParams(vmem_limit_bytes=56 * 2**20),
+        compiler_params=pltpu.CompilerParams(vmem_limit_bytes=63 * 2**20),
         cost_estimate=pl.CostEstimate(
             flops=12 * count * width * units,
             bytes_accessed=4 * width * units + 4 * count * width,
@@ -104,39 +104,56 @@
     )(own, home_top, last_top, home_bottom, last_bottom)
 
 
-def dispatch_kernel(slots, tokens_ref, routes_ref, send_ref, place_ref):
+def dispatch_kernel(slots, tokens_ref, routes_ref, send_ref, place_ref, normed_ref):
     count = tokens_ref.shape[0]
-    places = send_ref.shape[0]
-    normed = layer_norm(tokens_ref[...].astype(F32)).astype(BF16)
-    first, second = routes_ref[:, 0:1], routes_ref[:, 1:2]
-    names = lax.broadcasted_iota(jnp.int32, (count, places // slots), 1)
-    hot_first = (first == names).astype(F32)
-    hot_second = (second == names).astype(F32)
-    row_ids = lax.broadcasted_iota(jnp.int32, (count, count), 0)
-    before = (lax.broadcasted_iota(jnp.int32, (count, count), 1) < row_ids).astype(F32).astype(BF16)
-    rank_first = jnp.dot(before, hot_first.astype(BF16), preferred_element_type=F32)
-    rank_second = jnp.dot(before, hot_second.astype(BF16), preferred_element_type=F32)
-    rank_second = rank_second + jnp.sum(hot_first, axis=0, keepdims=True)
-    rank_first = jnp.sum(rank_first * hot_first, axis=1, keepdims=True)
-    rank_second = jnp.sum(rank_second * hot_second, axis=1, keepdims=True)
-    place_first = first * slots + rank_first.astype(jnp.int32)
-    place_second = second * slots + rank_second.astype(jnp.int32)
-    place_ref[:, 0:1] = place_first
-    place_ref[:, 1:2] = place_second
-    spots = lax.broadcasted_iota(jnp.int32, (count, places), 1)
-    chosen = ((spots == place_first) | (spots == place_second)).astype(F32)
-    send = jnp.dot(chosen.T.astype(BF16), normed, preferred_element_type=F32)
+    rows = send_ref.shape[0]
+    step = pl.program_id(0)
+
+    @pl.when(step == 0)
+    def _():
+        normed_ref[...] = layer_norm(tokens_ref[...].astype(F32)).astype(BF16)
+        first, second = routes_ref[0:1, :], routes_ref[1:2, :]
+        experts = rows * pl.num_programs(0) // slots
+        names = lax.broadcasted_iota(jnp.int32, (experts, count), 0)
+        hot_first = (first == names).astype(F32)
+        hot_second = (second == names).astype(F32)
+        column_ids = lax.broadcasted_iota(jnp.int32, (count, count), 1)
+        row_ids = lax.broadcasted_iota(jnp.int32, (count, count), 0)
+        before = (row_ids < column_ids).astype(F32).astype(BF16)
+        rank_first = jnp.dot(hot_first.astype(BF16), before, preferred_element_type=F32)
+        rank_second = jnp.dot(hot_second.astype(BF16), before, preferred_element_type=F32)
+        rank_second = rank_second + jnp.sum(hot_first, axis=1, keepdims=True)
+        rank_first = jnp.sum(rank_first * hot_first, axis=0, keepdims=True)
+        rank_second = jnp.sum(rank_second * hot_second, axis=0, keepdims=True)
+        place_ref[0:1, :] = first * slots + rank_first.astype(jnp.int32)
+        place_ref[1:2, :] = second * slots + rank_second.astype(jnp.int32)
+
+    spots = lax.broadcasted_iota(jnp.int32, (rows, count), 0) + step * rows
+    chosen = ((spots == place_ref[0:1, :]) | (spots == place_ref[1:2, :])).astype(F32)
+    send = jnp.dot(chosen.astype(BF16), normed_ref[...], preferred_element_type=F32)
     send_ref[...] = send.astype(BF16)
 
 
 def dispatch(tokens, routes, places, slots):
+    steps = 4
+    count, width = tokens.shape
     return pl.pallas_call(
         functools.partial(dispatch_kernel, slots),
+        grid=(steps,),
+        in_specs=[
+            pl.BlockSpec(tokens.shape, lambda i: (0, 0)),
+            pl.BlockSpec(routes.shape, lambda i: (0, 0)),
+        ],
+        out_specs=[
+            pl.BlockSpec((places // steps, width), lambda i: (i, 0)),
+            pl.BlockSpec(routes.shape, lambda i: (0, 0)),
+        ],
         out_shape=[
-            jax.ShapeDtypeStruct((places, tokens.shape[1]), BF16),
+            jax.ShapeDtypeStruct((places, width), BF16),
             jax.ShapeDtypeStruct(routes.shape, jnp.int32),
         ],
-        compiler_params=pltpu.CompilerParams(vmem_limit_bytes=16 * 2**20),
+        scratch_shapes=[pltpu.VMEM((count, width), BF16)],
+        compiler_params=pltpu.CompilerParams(vmem_limit_bytes=63 * 2**20),
     )(tokens, routes)
 
 
@@ -147,8 +164,11 @@
     captions = embed_ref.shape[0]
     returned = returned_ref[...]
     spots = lax.broadcasted_iota(jnp.int32, (count, returned.shape[0]), 1)
-    gates = jnp.where(spots == place_ref[:, 0:1], gates_ref[:, 0:1], 0.0) + jnp.where(
-        spots == place_ref[:, 1:2], gates_ref[:, 1:2], 0.0
+    zeros = jnp.zeros((4, count), F32)
+    columns = jnp.concatenate([place_ref[...].astype(F32), gates_ref[...], zeros], axis=0).T
+    places = columns[:, 0:2].astype(jnp.int32)
+    gates = jnp.where(spots == places[:, 0:1], columns[:, 2:3], 0.0) + jnp.where(
+        spots == places[:, 1:2], columns[:, 3:4], 0.0
     )
     high, low = split_pair(gates)
     mixed = tokens_ref[...].astype(F32)
@@ -286,7 +306,7 @@
     chip = lax.axis_index("expert") // shape[2]
 
     row_parts = [picture_unit] + [ring_shift(picture_unit, k, grid_all) for k in range(1, grid_all)]
-    send, place = dispatch(tokens, routes, places_all, slots)
+    send, place = dispatch(tokens, routes.T, places_all, slots)
     send = send.reshape(experts_all, slots, width)
     arrived = lax.all_to_all(send, "expert", split_axis=0, concat_axis=0, tiled=True)
     chips = shape[0] * shape[1]
@@ -303,8 +323,6 @@
     pictures_all = along_expert(picture_copies, shape)
     left_bottom = ring_shift(bottom, 1, grid_all)
     right_top = ring_shift(top, -1, grid_all)
-    own_term = expert_part([rows], up_local, down_local)[0]
-    own_term, left_top, right_bottom = held(own_term, left_top, right_bottom)
     far_top = ring_shift(left_top, 1, grid_all)
     far_bottom = ring_shift(right_bottom, -1, grid_all)
     left_top, right_bottom = expert_part([left_top, right_bottom], up_local, down_local)
@@ -318,10 +336,12 @@
         far_top, far_bottom, left_top, right_bottom, right_top, left_bottom
     )
     far_top, far_bottom = expert_part([far_top, far_bottom], up_local, down_local)
+    rows, far_top, far_bottom = held(rows, far_top, far_bottom)
+    own_term = expert_part([rows], up_local, down_local)[0]
     far_from_left = ring_shift(far_top, 1, grid_all)
     far_from_right = ring_shift(far_bottom, -1, grid_all)
-    far_from_left, far_from_right, home_top, home_bottom, pictures_all = held(
-        far_from_left, far_from_right, home_top, home_bottom, pictures_all
+    far_from_left, far_from_right, home_top, home_bottom, pictures_all, own_term = held(
+        far_from_left, far_from_right, home_top, home_bottom, pictures_all, own_term
     )
     right_top = (right_top.astype(F32) + far_from_left.astype(F32)).astype(BF16)
     left_bottom = (left_bottom.astype(F32) + far_from_right.astype(F32)).astype(BF16)
@@ -333,7 +353,7 @@
     returned = returned.reshape(places_all, width)
 
     text_embed, text_copies = combine(
-        caption_lengths, returned, tokens, place, route_gates, final_gain, chips
+        caption_lengths, returned, tokens, place, route_gates.T, final_gain, chips
     )
     text_unit = text_copies[0]
     text_column = along_expert(text_copies, shape)

time: 205 us -> 216 us (1.054)
  waiting for transfers between devices: 98.1 us -> 108 us
  starting transfers between devices: 64 us -> 59.3 us
  other arithmetic: 3.35 us -> 7.08 us
  Pallas kernels: 32.4 us -> 35.6 us
    ppermute x18, waiting for transfers between devices: 40.6 us -> 49.8 us  [ring_shift(): lax.ppermute(values, 'grid', [(i, (i + step) % size) for i in range(size)])]
    ppermute x18, starting transfers between devices: 28.7 us -> 24.2 us  [ring_shift(): lax.ppermute(values, 'grid', [(i, (i + step) % size) for i in range(size)])]
    unnamed x31 -> x25, local copies, waits for them, and re-layouts: 2.72 us -> 0.47 us
  transfers between devices with their start and end apart: 24 -> 24, of which waited for: 12 -> 17; matrix products, arithmetic and copies ran while one was open for 3% -> 4% of each run, Pallas kernels for 13% -> 12%
where the time goes in v5:
time: 216 us; the launch traced here: 215 us
  waiting for transfers between devices  108 us (50%)
  starting transfers between devices  59.3 us (27%)
  Pallas kernels  35.6 us (16%)
  other arithmetic  7.08 us (3%)
  matrix products  2.21 us (1%)
    ppermute x18, waiting for transfers between devices, ring_shift(): lax.ppermute(values, 'grid', [(i, (i + step) % size) for i in range(size)])  49.8 us
    all_to_all x1, waiting for transfers between devices, on_device(): lax.all_to_all(results, 'expert', split_axis=0, concat_axis=0, tiled=True)  27.9 us
    pallas_call x4, Pallas kernels, expert_part(): pl.pallas_call(expert_kernel, grid=(2 * half,), in_specs=[pl.BlockSpec(bl...  25.2 us
    ppermute x18, starting transfers between devices, ring_shift(): lax.ppermute(values, 'grid', [(i, (i + step) % size) for i in range(size)])  24.2 us
    all_to_all x1, waiting for transfers between devices, on_device(): lax.all_to_all(send, 'expert', split_axis=0, concat_axis=0, tiled=True)  18.6 us
    all_to_all x2, starting transfers between devices, along_expert(): lax.all_to_all(copies, 'expert', split_axis=0, concat_axis=0, axis_index_...  13 us
    all_to_all x1, starting transfers between devices, on_device(): lax.all_to_all(send, 'expert', split_axis=0, concat_axis=0, tiled=True)  11.8 us
    all_to_all x2, waiting for transfers between devices, along_expert(): lax.all_to_all(copies, 'expert', split_axis=0, concat_axis=0, axis_index_...  10.9 us
  transfers between devices with their start and end apart: 24, of which 17 were waited for; matrix products, arithmetic and copies ran while one was open for 4% of the time, Pallas kernels for 12%

profile of v5, /device:TPU:32, one launch (start us, length us, event | category | flops | bytes accessed | tf_op | source)
XLA Modules:
  0.0 215.1 jit_solution(3844402192588033489)
XLA Ops:
  0.6 3.3 %shard_map.103 = (bf16[512,1024]{1,0:T(8,128)(2,1)}, s32[2,128]{1,0:T(2,128)}) custom-call(bf16[128,1024]{1,0:T(8,128)(2,1)} %tokens_ref.3, s32[2,128]{1,0:T(2,128)} %bitcast.29), custom_call_target="tpu_custom_call" | custom-call | tf_op jit(solution)/shard_map/pallas_call | solution.py:140
  4.0 11.8 %all-to-all-start = ((bf16[64,8,1024]{2,1,0:T(8,128)(2,1)}), bf16[64,8,1024]{2,1,0:T(8,128)(2,1)S(1)}, u32[]{:S(2)}, u32[]{:S(2)}) async-start(bf16[64,8,1024]{2,1,0:T(8,128)(2,1)} %bitcast.28), calls=%async_computation | async-start | bytes 2097152 | tf_op jit(solution)/shard_map/all_to_all | solution.py:311
  15.7 0.1 fusion.13
  15.9 0.1 fusion.15.refs_0_
  15.9 1.5 collective-permute-start
  17.5 2.7 %collective-permute-start.1 = (bf16[4,1024]{1,0:T(4,128)(2,1)S(1)}, bf16[4,1024]{1,0:T(4,128)(2,1)S(1)}, u32[]{:S(2)}, u32[]{:S(2)}) collective-permute-start(bf16[4,1024]{1,0:T(4,128)(2,1)S(1)} %fusion.15.refs_0_), channel_id=1, source_target_pairs={{0,2},{1,3},{2,0},{3,1},{4,6},{5,7},{6,4},{7,5},{8,10},{9,11},{10,... | collective-permute-start | bytes 24584 | tf_op jit(solution)/shard_map/ppermute | solution.py:286
  20.2 1.4 collective-permute-start.2
  21.6 1.0 collective-permute-done.1.refs_2_
  22.6 1.2 collective-permute-done.2.refs_3_
  23.8 1.1 shard_map.104
  25.0 18.6 %all-to-all-done = bf16[64,8,1024]{2,1,0:T(8,128)(2,1)S(1)} async-done(((bf16[64,8,1024]{2,1,0:T(8,128)(2,1)}), bf16[64,8,1024]{2,1,0:T(8,128)(2,1)S(1)}, u32[]{:S(2)}, u32[]{:S(2)}) %all-to-all-start) | async-done | bytes 1048608 | tf_op jit(solution)/shard_map/all_to_all | solution.py:311
  43.6 6.5 %all-to-all-start.1 = ((bf16[32,16,1024]{2,1,0:T(8,128)(2,1)}), bf16[32,16,1024]{2,1,0:T(8,128)(2,1)}, u32[]{:S(2)}, u32[]{:S(2)}) async-start(bf16[32,16,1024]{2,1,0:T(8,128)(2,1)} %get-tuple-element.49), calls=%async_computation.1 | async-start | bytes 2097152 | tf_op jit(solution)/shard_map/all_to_all | solution.py:275
  50.1 1.1 slice_bitcast_fusion
  51.2 1.5 collective-permute-start.3
  52.7 1.7 collective-permute-start.5
  54.4 1.6 collective-permute-start.7
  56.0 0.5 collective-permute-start.8
  56.5 11.0 %collective-permute-done.3.refs_0_ = bf16[256,1024]{1,0:T(8,128)(2,1)S(1)} collective-permute-done((bf16[256,1024]{1,0:T(8,128)(2,1)}, bf16[256,1024]{1,0:T(8,128)(2,1)S(1)}, u32[]{:S(2)}, u32[]{:S(2)}) %collective-permute-start.3) | collective-permute-done | bytes 524320 | tf_op jit(solution)/shard_map/ppermute | solution.py:286
  67.4 0.4 collective-permute-done.5.refs_1_
  67.8 0.4 copy-done.11
  68.2 6.3 %shard_map.105 = (bf16[256,1024]{1,0:T(8,128)(2,1)}, bf16[256,1024]{1,0:T(8,128)(2,1)}) custom-call(bf16[256,1024]{1,0:T(8,128)(2,1)} %copy-done.11, bf16[256,1024]{1,0:T(8,128)(2,1)} %collective-permute-done.5.refs_1_, bf16[1024,1024]{1,0:T(8,128)(2,1)} %bitcast.30, bf16[1024,1024]{1,0:T(8,128)(2,1)} %bitcast.34), custom_call_target="tpu_custom_call" | custom-call | flops 6442450944 | bytes 6291456 | tf_op jit(solution)/shard_map/pallas_call | solution.py:53
  74.5 2.6 %collective-permute-start.11 = (bf16[256,1024]{1,0:T(8,128)(2,1)}, bf16[256,1024]{1,0:T(8,128)(2,1)S(1)}, u32[]{:S(2)}, u32[]{:S(2)}) collective-permute-start(bf16[256,1024]{1,0:T(8,128)(2,1)} %get-tuple-element.37), channel_id=1, source_target_pairs={{0,3},{1,0},{2,1},{3,2},{4,7},{5,4},{6,5},{7,6},{8,11},{9,8},{10,9... | collective-permute-start | bytes 1572872 | tf_op jit(solution)/shard_map/ppermute | solution.py:286
  77.0 0.0 collective-permute-start.12
  77.0 2.0 collective-permute-done.7.refs_0_
  79.0 0.0 collective-permute-done.8.refs_1_
  79.0 1.5 collective-permute-start.4
  80.5 1.7 collective-permute-start.6
  82.3 6.3 %shard_map.106 = (bf16[256,1024]{1,0:T(8,128)(2,1)}, bf16[256,1024]{1,0:T(8,128)(2,1)}) custom-call(bf16[256,1024]{1,0:T(8,128)(2,1)} %collective-permute-done.7.refs_0_, bf16[256,1024]{1,0:T(8,128)(2,1)} %collective-permute-done.8.refs_1_, bf16[1024,1024]{1,0:T(8,128)(2,1)} %bitcast.31, bf16[1024,1024]{1,0:T(8,128)(2,1)} %bitcast.35), custom_call_target="tpu_custom_call" | custom-call | flops 6442450944 | bytes 6291456 | tf_op jit(solution)/shard_map/pallas_call | solution.py:53
  88.6 11.1 %collective-permute-done.4.refs_0_ = bf16[256,1024]{1,0:T(8,128)(2,1)} collective-permute-done((bf16[256,1024]{1,0:T(8,128)(2,1)}, bf16[256,1024]{1,0:T(8,128)(2,1)}, u32[]{:S(2)}, u32[]{:S(2)}) %collective-permute-start.4) | collective-permute-done | bytes 524320 | tf_op jit(solution)/shard_map/ppermute | solution.py:286
  99.7 0.0 collective-permute-done.6.refs_1_
  99.7 0.0 all-to-all-done.1
  99.8 6.3 %shard_map.107 = (bf16[256,1024]{1,0:T(8,128)(2,1)}, bf16[256,1024]{1,0:T(8,128)(2,1)}) custom-call(bf16[256,1024]{1,0:T(8,128)(2,1)} %collective-permute-done.4.refs_0_, bf16[256,1024]{1,0:T(8,128)(2,1)} %collective-permute-done.6.refs_1_, bf16[1024,1024]{1,0:T(8,128)(2,1)} %bitcast.32, bf16[1024,1024]{1,0:T(8,128)(2,1)} %bitcast.36), custom_call_target="tpu_custom_call" | custom-call | flops 6442450944 | bytes 6291456 | tf_op jit(solution)/shard_map/pallas_call | solution.py:53
  106.1 2.8 %collective-permute-start.10 = (bf16[256,1024]{1,0:T(8,128)(2,1)}, bf16[256,1024]{1,0:T(8,128)(2,1)}, u32[]{:S(2)}, u32[]{:S(2)}) collective-permute-start(bf16[256,1024]{1,0:T(8,128)(2,1)} %get-tuple-element.48), channel_id=1, source_target_pairs={{0,3},{1,0},{2,1},{3,2},{4,7},{5,4},{6,5},{7,6},{8,11},{9,8},{10,9... | collective-permute-start | bytes 1572872 | tf_op jit(solution)/shard_map/ppermute | solution.py:286
  108.9 6.3 %shard_map.108.own_ref = bf16[512,1024]{1,0:T(8,128)(2,1)} custom-call(bf16[512,1024]{1,0:T(8,128)(2,1)} %bitcast.27, bf16[1024,1024]{1,0:T(8,128)(2,1)} %bitcast.33, bf16[1024,1024]{1,0:T(8,128)(2,1)} %bitcast.37), custom_call_target="tpu_custom_call" | custom-call | flops 6442450944 | bytes 6291456 | tf_op jit(solution)/shard_map/pallas_call | solution.py:53
  115.2 3.1 %pad_maximum_fusion = bf16[1024,1024]{1,0:T(8,128)(2,1)} fusion(bf16[512,1024]{1,0:T(8,128)(2,1)} %collective-permute-done.13, bf16[512,1024]{1,0:T(8,128)(2,1)} %bitcast.7), kind=kLoop, calls=%fused_computation | loop fusion | flops 4194304 | bytes 4194304 | tf_op jit(solution)/shard_map/concatenate | solution.py:282
  118.3 2.7 %collective-permute-done.10 = bf16[256,1024]{1,0:T(8,128)(2,1)} collective-permute-done((bf16[256,1024]{1,0:T(8,128)(2,1)}, bf16[256,1024]{1,0:T(8,128)(2,1)}, u32[]{:S(2)}, u32[]{:S(2)}) %collective-permute-start.10) | collective-permute-done | bytes 524320 | tf_op jit(solution)/shard_map/ppermute | solution.py:286
  121.1 3.4 %collective-permute-done.9 = bf16[256,1024]{1,0:T(8,128)(2,1)} collective-permute-done((bf16[256,1024]{1,0:T(8,128)(2,1)}, bf16[256,1024]{1,0:T(8,128)(2,1)}, u32[]{:S(2)}, u32[]{:S(2)}) %collective-permute-start.9) | collective-permute-done | bytes 524320 | tf_op jit(solution)/shard_map/ppermute | solution.py:286
  124.5 1.2 add_convert_fusion
  125.7 0.4 collective-permute-start.15
  126.1 1.2 add_convert_fusion.1
  127.3 1.8 collective-permute-start.14
  129.1 9.8 %collective-permute-done.15.last_bottom = bf16[256,1024]{1,0:T(8,128)(2,1)S(1)} collective-permute-done((bf16[256,1024]{1,0:T(8,128)(2,1)S(1)}, bf16[256,1024]{1,0:T(8,128)(2,1)S(1)}, u32[]{:S(2)}, u32[]{:S(2)}) %collective-permute-start.15) | collective-permute-done | bytes 524320 | tf_op jit(solution)/shard_map/ppermute | solution.py:286
  139.0 2.8 %collective-permute-done.14.last_top = bf16[256,1024]{1,0:T(8,128)(2,1)S(1)} collective-permute-done((bf16[256,1024]{1,0:T(8,128)(2,1)S(1)}, bf16[256,1024]{1,0:T(8,128)(2,1)S(1)}, u32[]{:S(2)}, u32[]{:S(2)}) %collective-permute-start.14) | collective-permute-done | bytes 524320 | tf_op jit(solution)/shard_map/ppermute | solution.py:286
  141.8 3.5 %shard_map.109 = bf16[512,1024]{1,0:T(8,128)(2,1)} custom-call(bf16[512,1024]{1,0:T(8,128)(2,1)S(1)} %copy-done.1, bf16[256,1024]{1,0:T(8,128)(2,1)S(1)} %collective-permute-done.11.home_top, bf16[256,1024]{1,0:T(8,128)(2,1)S(1)} %collective-permute-done.14.last_top, bf16[256,1024]{1,0:T(8,128)(2,1)} %collective-permute-done.12.home_bottom, ...), custom_call_target="tpu_custom_call" | custom-call | tf_op jit(solution)/shard_map/pallas_call | solution.py:97
  145.3 0.0 copy-start.5
  145.4 10.3 %all-to-all-start.2 = ((bf16[64,8,1024]{2,1,0:T(8,128)(2,1)}), bf16[64,8,1024]{2,1,0:T(8,128)(2,1)S(1)}, u32[]{:S(2)}, u32[]{:S(2)}) async-start(bf16[64,8,1024]{2,1,0:T(8,128)(2,1)} %bitcast.8), calls=%async_computation.2 | async-start | bytes 2097152 | tf_op jit(solution)/shard_map/all_to_all | solution.py:352
  155.7 27.9 %all-to-all-done.2 = bf16[64,8,1024]{2,1,0:T(8,128)(2,1)S(1)} async-done(((bf16[64,8,1024]{2,1,0:T(8,128)(2,1)}), bf16[64,8,1024]{2,1,0:T(8,128)(2,1)S(1)}, u32[]{:S(2)}, u32[]{:S(2)}) %all-to-all-start.2) | async-done | bytes 1048608 | tf_op jit(solution)/shard_map/all_to_all | solution.py:352
  183.6 2.5 %shard_map.110 = (f32[4,1024]{1,0:T(4,128)}, bf16[32,4,1024]{2,1,0:T(4,128)(2,1)}) custom-call(s32[1,4]{1,0:T(1,128)S(1)} %copy-done.5, bf16[512,1024]{1,0:T(8,128)(2,1)S(1)} %bitcast.24, bf16[128,1024]{1,0:T(8,128)(2,1)S(1)} %copy-done, s32[2,128]{1,0:T(2,128)S(1)} %copy-done.4, f32[2,128]{1,0:T(2,128)S(1)} %bitcast.26, f32[1,1024]{1,0:T(1,128)S(1)} %bitcast.25), custom_call_target="tpu_custom_call" | custom-call | tf_op jit(solution)/shard_map/pallas_call | solution.py:208
  186.0 6.5 %all-to-all-start.3 = ((bf16[32,4,1024]{2,1,0:T(4,128)(2,1)}), bf16[32,4,1024]{2,1,0:T(4,128)(2,1)S(1)}, u32[]{:S(2)}, u32[]{:S(2)}) async-start(bf16[32,4,1024]{2,1,0:T(4,128)(2,1)} %get-tuple-element.60), calls=%async_computation.3 | async-start | bytes 524288 | tf_op jit(solution)/shard_map/all_to_all | solution.py:275
  192.6 1.4 subtract_convert_fusion.1
  193.9 10.9 %all-to-all-done.3 = bf16[32,4,1024]{2,1,0:T(4,128)(2,1)S(1)} async-done(((bf16[32,4,1024]{2,1,0:T(4,128)(2,1)}), bf16[32,4,1024]{2,1,0:T(4,128)(2,1)S(1)}, u32[]{:S(2)}, u32[]{:S(2)}) %all-to-all-start.3) | async-done | bytes 262176 | tf_op jit(solution)/shard_map/all_to_all | solution.py:275
  204.9 0.1 reshape.52
  205.0 0.1 collective-permute-start.16
  205.1 0.4 fusion.19
  205.5 1.1 collective-permute-done.16
  206.6 0.3 subtract_convert_fusion
  206.9 0.2 fusion.23
  207.1 0.1 collective-permute-start.17
  207.2 2.3 %collective-permute-start.18 = (f32[4,1024]{1,0:T(4,128)S(1)}, f32[4,1024]{1,0:T(4,128)S(1)}, u32[]{:S(2)}, u32[]{:S(2)}) collective-permute-start(f32[4,1024]{1,0:T(4,128)S(1)} %get-tuple-element.71), channel_id=1, source_target_pairs={{0,2},{1,3},{2,0},{3,1},{4,6},{5,7},{6,4},{7,5},{8,10},{9,11},{10,... | collective-permute-start | bytes 49160 | tf_op jit(solution)/shard_map/ppermute | solution.py:286
  209.5 0.6 fusion.18
  210.1 0.8 collective-permute-done.17
  210.9 1.6 collective-permute-done.18
  212.5 1.9 collective-permute-done.19
  214.5 0.6 fusion.17
  (38 shorter events, 0.2 us)
Async XLA Ops:
  0.6 15.1 %copy-start.10 = (bf16[4,1024]{1,0:T(4,128)(2,1)S(1)}, bf16[4,1024]{1,0:T(4,128)(2,1)}, u32[]{:S(2)}) copy-start(bf16[4,1024]{1,0:T(4,128)(2,1)} %param.12) | copy-start | bytes 24580
  4.0 39.6 %all-to-all-start = ((bf16[64,8,1024]{2,1,0:T(8,128)(2,1)}), bf16[64,8,1024]{2,1,0:T(8,128)(2,1)S(1)}, u32[]{:S(2)}, u32[]{:S(2)}) async-start(bf16[64,8,1024]{2,1,0:T(8,128)(2,1)} %bitcast.28), calls=%async_computation | async-start | bytes 2097152 | tf_op jit(solution)/shard_map/all_to_all | solution.py:311
  15.9 5.7 %collective-permute-start = (bf16[4,1024]{1,0:T(4,128)(2,1)S(1)}, bf16[4,1024]{1,0:T(4,128)(2,1)S(1)}, u32[]{:S(2)}, u32[]{:S(2)}) collective-permute-start(bf16[4,1024]{1,0:T(4,128)(2,1)S(1)} %fusion.15.refs_0_), channel_id=1, source_target_pairs={{0,1},{1,2},{2,3},{3,0},{4,5},{5,6},{6,7},{7,4},{8,9},{9,10},{10,1... | collective-permute-start | bytes 24584 | tf_op jit(solution)/shard_map/ppermute | solution.py:286
  17.5 5.2 %collective-permute-start.1 = (bf16[4,1024]{1,0:T(4,128)(2,1)S(1)}, bf16[4,1024]{1,0:T(4,128)(2,1)S(1)}, u32[]{:S(2)}, u32[]{:S(2)}) collective-permute-start(bf16[4,1024]{1,0:T(4,128)(2,1)S(1)} %fusion.15.refs_0_), channel_id=1, source_target_pairs={{0,2},{1,3},{2,0},{3,1},{4,6},{5,7},{6,4},{7,5},{8,10},{9,11},{10,... | collective-permute-start | bytes 24584 | tf_op jit(solution)/shard_map/ppermute | solution.py:286
  20.2 3.7 %collective-permute-start.2 = (bf16[4,1024]{1,0:T(4,128)(2,1)S(1)}, bf16[4,1024]{1,0:T(4,128)(2,1)S(1)}, u32[]{:S(2)}, u32[]{:S(2)}) collective-permute-start(bf16[4,1024]{1,0:T(4,128)(2,1)S(1)} %fusion.15.refs_0_), channel_id=1, source_target_pairs={{0,3},{1,0},{2,1},{3,2},{4,7},{5,4},{6,5},{7,6},{8,11},{9,8},{10,9... | collective-permute-start | bytes 24584 | tf_op jit(solution)/shard_map/ppermute | solution.py:286
  43.6 7.6 %copy-start.7 = (bf16[64,8,1024]{2,1,0:T(8,128)(2,1)}, bf16[64,8,1024]{2,1,0:T(8,128)(2,1)S(1)}, u32[]{:S(2)}) copy-start(bf16[64,8,1024]{2,1,0:T(8,128)(2,1)S(1)} %all-to-all-done) | copy-start | bytes 3145732
  43.6 56.2 %all-to-all-start.1 = ((bf16[32,16,1024]{2,1,0:T(8,128)(2,1)}), bf16[32,16,1024]{2,1,0:T(8,128)(2,1)}, u32[]{:S(2)}, u32[]{:S(2)}) async-start(bf16[32,16,1024]{2,1,0:T(8,128)(2,1)} %get-tuple-element.49), calls=%async_computation.1 | async-start | bytes 2097152 | tf_op jit(solution)/shard_map/all_to_all | solution.py:275
  51.2 16.2 %collective-permute-start.3 = (bf16[256,1024]{1,0:T(8,128)(2,1)}, bf16[256,1024]{1,0:T(8,128)(2,1)S(1)}, u32[]{:S(2)}, u32[]{:S(2)}) collective-permute-start(bf16[256,1024]{1,0:T(8,128)(2,1)} %get-tuple-element.68), channel_id=1, source_target_pairs={{0,1},{1,2},{2,3},{3,0},{4,5},{5,6},{6,7},{7,4},{8,9},{9,10},{10,1... | collective-permute-start | bytes 1572872 | tf_op jit(solution)/shard_map/ppermute | solution.py:286
  52.7 15.1 %collective-permute-start.5 = (bf16[256,1024]{1,0:T(8,128)(2,1)}, bf16[256,1024]{1,0:T(8,128)(2,1)}, u32[]{:S(2)}, u32[]{:S(2)}) collective-permute-start(bf16[256,1024]{1,0:T(8,128)(2,1)} %get-tuple-element.67), channel_id=1, source_target_pairs={{0,3},{1,0},{2,1},{3,2},{4,7},{5,4},{6,5},{7,6},{8,11},{9,8},{10,9... | collective-permute-start | bytes 1572872 | tf_op jit(solution)/shard_map/ppermute | solution.py:286
  54.4 24.6 %collective-permute-start.7 = (bf16[256,1024]{1,0:T(8,128)(2,1)}, bf16[256,1024]{1,0:T(8,128)(2,1)}, u32[]{:S(2)}, u32[]{:S(2)}) collective-permute-start(bf16[256,1024]{1,0:T(8,128)(2,1)} %get-tuple-element.68), channel_id=1, source_target_pairs={{0,3},{1,0},{2,1},{3,2},{4,7},{5,4},{6,5},{7,6},{8,11},{9,8},{10,9... | collective-permute-start | bytes 1572872 | tf_op jit(solution)/shard_map/ppermute | solution.py:286
  56.0 23.1 %collective-permute-start.8 = (bf16[256,1024]{1,0:T(8,128)(2,1)}, bf16[256,1024]{1,0:T(8,128)(2,1)}, u32[]{:S(2)}, u32[]{:S(2)}) collective-permute-start(bf16[256,1024]{1,0:T(8,128)(2,1)} %get-tuple-element.67), channel_id=1, source_target_pairs={{0,1},{1,2},{2,3},{3,0},{4,5},{5,6},{6,7},{7,4},{8,9},{9,10},{10,1... | collective-permute-start | bytes 1572872 | tf_op jit(solution)/shard_map/ppermute | solution.py:286
  67.4 0.8 copy-start.11
  74.5 43.9 %collective-permute-start.11 = (bf16[256,1024]{1,0:T(8,128)(2,1)}, bf16[256,1024]{1,0:T(8,128)(2,1)S(1)}, u32[]{:S(2)}, u32[]{:S(2)}) collective-permute-start(bf16[256,1024]{1,0:T(8,128)(2,1)} %get-tuple-element.37), channel_id=1, source_target_pairs={{0,3},{1,0},{2,1},{3,2},{4,7},{5,4},{6,5},{7,6},{8,11},{9,8},{10,9... | collective-permute-start | bytes 1572872 | tf_op jit(solution)/shard_map/ppermute | solution.py:286
  77.0 41.3 %collective-permute-start.12 = (bf16[256,1024]{1,0:T(8,128)(2,1)}, bf16[256,1024]{1,0:T(8,128)(2,1)}, u32[]{:S(2)}, u32[]{:S(2)}) collective-permute-start(bf16[256,1024]{1,0:T(8,128)(2,1)} %get-tuple-element.38), channel_id=1, source_target_pairs={{0,1},{1,2},{2,3},{3,0},{4,5},{5,6},{6,7},{7,4},{8,9},{9,10},{10,1... | collective-permute-start | bytes 1572872 | tf_op jit(solution)/shard_map/ppermute | solution.py:286
  79.0 20.7 %collective-permute-start.4 = (bf16[256,1024]{1,0:T(8,128)(2,1)}, bf16[256,1024]{1,0:T(8,128)(2,1)}, u32[]{:S(2)}, u32[]{:S(2)}) collective-permute-start(bf16[256,1024]{1,0:T(8,128)(2,1)} %copy-done.11), channel_id=1, source_target_pairs={{0,1},{1,2},{2,3},{3,0},{4,5},{5,6},{6,7},{7,4},{8,9},{9,10},{10,1... | collective-permute-start | bytes 1572872 | tf_op jit(solution)/shard_map/ppermute | solution.py:286
  80.5 19.2 %collective-permute-start.6 = (bf16[256,1024]{1,0:T(8,128)(2,1)}, bf16[256,1024]{1,0:T(8,128)(2,1)}, u32[]{:S(2)}, u32[]{:S(2)}) collective-permute-start(bf16[256,1024]{1,0:T(8,128)(2,1)} %collective-permute-done.5.refs_1_), channel_id=1, source_target_pairs={{0,3},{1,0},{2,1},{3,2},{4,7},{5,4},{6,5},{7,6},{8,11},{9,8},{10,9... | collective-permute-start | bytes 1572872 | tf_op jit(solution)/shard_map/ppermute | solution.py:286
  99.7 15.5 %collective-permute-start.13 = (bf16[512,1024]{1,0:T(8,128)(2,1)}, bf16[512,1024]{1,0:T(8,128)(2,1)}, u32[]{:S(2)}, u32[]{:S(2)}) collective-permute-start(bf16[512,1024]{1,0:T(8,128)(2,1)} %bitcast.7), channel_id=1, source_target_pairs={{0,4},{4,0},{8,12},{12,8},{16,20},{20,16},{24,28},{28,24},{32,36},... | collective-permute-start | bytes 3145736 | tf_op jit(solution)/shard_map/ppermute | solution.py:268
  106.1 15.0 %collective-permute-start.10 = (bf16[256,1024]{1,0:T(8,128)(2,1)}, bf16[256,1024]{1,0:T(8,128)(2,1)}, u32[]{:S(2)}, u32[]{:S(2)}) collective-permute-start(bf16[256,1024]{1,0:T(8,128)(2,1)} %get-tuple-element.48), channel_id=1, source_target_pairs={{0,3},{1,0},{2,1},{3,2},{4,7},{5,4},{6,5},{7,6},{8,11},{9,8},{10,9... | collective-permute-start | bytes 1572872 | tf_op jit(solution)/shard_map/ppermute | solution.py:286
  108.9 15.6 %collective-permute-start.9 = (bf16[256,1024]{1,0:T(8,128)(2,1)}, bf16[256,1024]{1,0:T(8,128)(2,1)}, u32[]{:S(2)}, u32[]{:S(2)}) collective-permute-start(bf16[256,1024]{1,0:T(8,128)(2,1)} %get-tuple-element.47), channel_id=1, source_target_pairs={{0,1},{1,2},{2,3},{3,0},{4,5},{5,6},{6,7},{7,4},{8,9},{9,10},{10,1... | collective-permute-start | bytes 1572872 | tf_op jit(solution)/shard_map/ppermute | solution.py:286
  115.2 9.3 %copy-start.9 = (bf16[256,1024]{1,0:T(8,128)(2,1)S(1)}, bf16[256,1024]{1,0:T(8,128)(2,1)}, u32[]{:S(2)}) copy-start(bf16[256,1024]{1,0:T(8,128)(2,1)} %get-tuple-element.56) | copy-start | bytes 1572868
  115.2 10.9 %copy-start.8 = (bf16[256,1024]{1,0:T(8,128)(2,1)S(1)}, bf16[256,1024]{1,0:T(8,128)(2,1)}, u32[]{:S(2)}) copy-start(bf16[256,1024]{1,0:T(8,128)(2,1)} %get-tuple-element.53) | copy-start | bytes 1572868
  118.3 23.5 %copy-start.1 = (bf16[512,1024]{1,0:T(8,128)(2,1)S(1)}, bf16[512,1024]{1,0:T(8,128)(2,1)}, u32[]{:S(2)}) copy-start(bf16[512,1024]{1,0:T(8,128)(2,1)} %shard_map.108.own_ref) | copy-start | bytes 3145732
  125.7 13.3 %collective-permute-start.15 = (bf16[256,1024]{1,0:T(8,128)(2,1)S(1)}, bf16[256,1024]{1,0:T(8,128)(2,1)S(1)}, u32[]{:S(2)}, u32[]{:S(2)}) collective-permute-start(bf16[256,1024]{1,0:T(8,128)(2,1)S(1)} %add_convert_fusion), channel_id=1, source_target_pairs={{0,3},{1,0},{2,1},{3,2},{4,7},{5,4},{6,5},{7,6},{8,11},{9,8},{10,9... | collective-permute-start | bytes 1572872 | tf_op jit(solution)/shard_map/ppermute | solution.py:286
  127.3 14.5 %collective-permute-start.14 = (bf16[256,1024]{1,0:T(8,128)(2,1)S(1)}, bf16[256,1024]{1,0:T(8,128)(2,1)S(1)}, u32[]{:S(2)}, u32[]{:S(2)}) collective-permute-start(bf16[256,1024]{1,0:T(8,128)(2,1)S(1)} %add_convert_fusion.1), channel_id=1, source_target_pairs={{0,1},{1,2},{2,3},{3,0},{4,5},{5,6},{6,7},{7,4},{8,9},{9,10},{10,1... | collective-permute-start | bytes 1572872 | tf_op jit(solution)/shard_map/ppermute | solution.py:286
  145.3 38.2 %copy-start = (bf16[128,1024]{1,0:T(8,128)(2,1)S(1)}, bf16[128,1024]{1,0:T(8,128)(2,1)}, u32[]{:S(2)}) copy-start(bf16[128,1024]{1,0:T(8,128)(2,1)} %tokens_ref.3) | copy-start | bytes 786436
  145.3 38.2 %copy-start.2 = (f32[1024]{0:T(1024)S(1)}, f32[1024]{0:T(1024)}, u32[]{:S(2)}) copy-start(f32[1024]{0:T(1024)} %param.13) | copy-start | bytes 12292
  145.3 38.2 %copy-start.3 = (f32[128,2]{0,1:T(2,128)S(1)}, f32[128,2]{0,1:T(2,128)}, u32[]{:S(2)}) copy-start(f32[128,2]{0,1:T(2,128)} %param.10) | copy-start | bytes 3076
  145.3 38.2 %copy-start.4 = (s32[2,128]{1,0:T(2,128)S(1)}, s32[2,128]{1,0:T(2,128)}, u32[]{:S(2)}) copy-start(s32[2,128]{1,0:T(2,128)} %get-tuple-element.58.place_ref) | copy-start | bytes 3076
  145.3 38.2 %copy-start.5 = (s32[1,4]{1,0:T(1,128)S(1)}, s32[1,4]{1,0:T(1,128)}, u32[]{:S(2)}) copy-start(s32[1,4]{1,0:T(1,128)} %lengths_ref.1) | copy-start | bytes 52
  145.4 47.2 %copy-start.6 = (bf16[1024,1024]{1,0:T(8,128)(2,1)S(1)}, bf16[1024,1024]{1,0:T(8,128)(2,1)}, u32[]{:S(2)}) copy-start(bf16[1024,1024]{1,0:T(8,128)(2,1)} %pad_maximum_fusion) | copy-start | bytes 6291460
  145.4 38.2 %all-to-all-start.2 = ((bf16[64,8,1024]{2,1,0:T(8,128)(2,1)}), bf16[64,8,1024]{2,1,0:T(8,128)(2,1)S(1)}, u32[]{:S(2)}, u32[]{:S(2)}) async-start(bf16[64,8,1024]{2,1,0:T(8,128)(2,1)} %bitcast.8), calls=%async_computation.2 | async-start | bytes 2097152 | tf_op jit(solution)/shard_map/all_to_all | solution.py:352
  186.0 18.8 %all-to-all-start.3 = ((bf16[32,4,1024]{2,1,0:T(4,128)(2,1)}), bf16[32,4,1024]{2,1,0:T(4,128)(2,1)S(1)}, u32[]{:S(2)}, u32[]{:S(2)}) async-start(bf16[32,4,1024]{2,1,0:T(4,128)(2,1)} %get-tuple-element.60), calls=%async_computation.3 | async-start | bytes 524288 | tf_op jit(solution)/shard_map/all_to_all | solution.py:275
  205.0 1.6 collective-permute-start.16
  207.1 3.8 %collective-permute-start.17 = (f32[4,1024]{1,0:T(4,128)S(1)}, f32[4,1024]{1,0:T(4,128)S(1)}, u32[]{:S(2)}, u32[]{:S(2)}) collective-permute-start(f32[4,1024]{1,0:T(4,128)S(1)} %get-tuple-element.69), channel_id=1, source_target_pairs={{0,3},{1,0},{2,1},{3,2},{4,7},{5,4},{6,5},{7,6},{8,11},{9,8},{10,9... | collective-permute-start | bytes 49160 | tf_op jit(solution)/shard_map/ppermute | solution.py:286
  207.2 5.3 %collective-permute-start.18 = (f32[4,1024]{1,0:T(4,128)S(1)}, f32[4,1024]{1,0:T(4,128)S(1)}, u32[]{:S(2)}, u32[]{:S(2)}) collective-permute-start(f32[4,1024]{1,0:T(4,128)S(1)} %get-tuple-element.71), channel_id=1, source_target_pairs={{0,2},{1,3},{2,0},{3,1},{4,6},{5,7},{6,4},{7,5},{8,10},{9,11},{10,... | collective-permute-start | bytes 49160 | tf_op jit(solution)/shard_map/ppermute | solution.py:286
  209.5 4.9 %collective-permute-start.19 = (f32[4,1024]{1,0:T(4,128)S(1)}, f32[4,1024]{1,0:T(4,128)S(1)}, u32[]{:S(2)}, u32[]{:S(2)}) collective-permute-start(f32[4,1024]{1,0:T(4,128)S(1)} %get-tuple-element.70), channel_id=1, source_target_pairs={{0,1},{1,2},{2,3},{3,0},{4,5},{5,6},{6,7},{7,4},{8,9},{9,10},{10,1... | collective-permute-start | bytes 49160 | tf_op jit(solution)/shard_map/ppermute | solution.py:286

commit v6 on v5

--- a/solution.py
+++ b/solution.py
@@ -64,7 +64,7 @@
         ],
         out_shape=[jax.ShapeDtypeStruct(block.shape, BF16) for block in blocks],
         scratch_shapes=[pltpu.VMEM((count, units), BF16)],
-        compiler_params=pltpu.CompilerParams(vmem_limit_bytes=63 * 2**20),
+        compiler_params=pltpu.CompilerParams(vmem_limit_bytes=12 * 2**20),
         cost_estimate=pl.CostEstimate(
             flops=12 * count * width * units,
             bytes_accessed=4 * width * units + 4 * count * width,
@@ -100,7 +100,7 @@
         in_specs=[pl.BlockSpec(block, lambda i: (i, 0)), top, top, bottom, bottom],
         out_specs=pl.BlockSpec(block, lambda i: (i, 0)),
         out_shape=jax.ShapeDtypeStruct(own.shape, BF16),
-        compiler_params=pltpu.CompilerParams(vmem_limit_bytes=16 * 2**20),
+        compiler_params=pltpu.CompilerParams(vmem_limit_bytes=12 * 2**20),
     )(own, home_top, last_top, home_bottom, last_bottom)
 
 
@@ -153,7 +153,7 @@
             jax.ShapeDtypeStruct(routes.shape, jnp.int32),
         ],
         scratch_shapes=[pltpu.VMEM((count, width), BF16)],
-        compiler_params=pltpu.CompilerParams(vmem_limit_bytes=63 * 2**20),
+        compiler_params=pltpu.CompilerParams(vmem_limit_bytes=12 * 2**20),
     )(tokens, routes)
 
 
@@ -213,7 +213,7 @@
             jax.ShapeDtypeStruct((captions, width), F32),
             jax.ShapeDtypeStruct((copies, captions, width), BF16),
         ],
-        compiler_params=pltpu.CompilerParams(vmem_limit_bytes=24 * 2**20),
+        compiler_params=pltpu.CompilerParams(vmem_limit_bytes=12 * 2**20),
     )(lengths, returned, tokens, place, gates, gain.reshape(1, width))
 
 
@@ -340,8 +340,8 @@
     own_term = expert_part([rows], up_local, down_local)[0]
     far_from_left = ring_shift(far_top, 1, grid_all)
     far_from_right = ring_shift(far_bottom, -1, grid_all)
-    far_from_left, far_from_right, home_top, home_bottom, pictures_all, own_term = held(
-        far_from_left, far_from_right, home_top, home_bottom, pictures_all, own_term
+    far_from_left, far_from_right, home_top, home_bottom, own_term = held(
+        far_from_left, far_from_right, home_top, home_bottom, own_term
     )
     right_top = (right_top.astype(F32) + far_from_left.astype(F32)).astype(BF16)
     left_bottom = (left_bottom.astype(F32) + far_from_right.astype(F32)).astype(BF16)
@@ -350,6 +350,7 @@
     total = sum_terms(own_term, home_top, last_top, home_bottom, last_bottom)
     results = total.reshape(experts_all, slots, width)
     returned = lax.all_to_all(results, "expert", split_axis=0, concat_axis=0, tiled=True)
+    returned, pictures_all = held(returned, pictures_all)
     returned = returned.reshape(places_all, width)
 
     text_embed, text_copies = combine(

time: 216 us -> 199 us (0.921)
  Pallas kernels: 35.6 us -> 23.5 us
  other arithmetic: 7.08 us -> 3.33 us
  waiting for transfers between devices: 108 us -> 105 us
  local copies, waits for them, and re-layouts: 1.64 us -> 4.4 us
    pallas_call x4, Pallas kernels: 25.2 us -> 15.9 us  [expert_part(): pl.pallas_call(expert_kernel, grid=(2 * half,), in_specs=[pl.BlockSpec(bl...]
    all_to_all x1, waiting for transfers between devices: 27.9 us -> 23.4 us  [on_device(): lax.all_to_all(results, 'expert', split_axis=0, concat_axis=0, tiled=True)]
    unnamed x25 -> x19, local copies, waits for them, and re-layouts: 0.47 us -> 3.26 us
    ppermute x2, waiting for transfers between devices: 1.11 us -> 3.83 us  [moved(): return lax.ppermute(values, 'expert', pairs)]
  transfers between devices with their start and end apart: 24 -> 24, of which waited for: 17 -> 18; matrix products, arithmetic and copies ran while one was open for 4% -> 2% of each run, Pallas kernels for 12% -> 9%
where the time goes in v6:
time: 199 us; the launch traced here: 198 us
  waiting for transfers between devices  105 us (53%)
  starting transfers between devices  58.2 us (29%)
  Pallas kernels  23.5 us (12%)
  local copies, waits for them, and re-layouts  4.4 us (2%)
  other arithmetic  3.33 us (2%)
  matrix products  2.21 us (1%)
    ppermute x18, waiting for transfers between devices, ring_shift(): lax.ppermute(values, 'grid', [(i, (i + step) % size) for i in range(size)])  48.4 us
    ppermute x18, starting transfers between devices, ring_shift(): lax.ppermute(values, 'grid', [(i, (i + step) % size) for i in range(size)])  24.4 us
    all_to_all x1, waiting for transfers between devices, on_device(): lax.all_to_all(results, 'expert', split_axis=0, concat_axis=0, tiled=True)  23.4 us
    all_to_all x1, waiting for transfers between devices, on_device(): lax.all_to_all(send, 'expert', split_axis=0, concat_axis=0, tiled=True)  18.6 us
    pallas_call x4, Pallas kernels, expert_part(): pl.pallas_call(expert_kernel, grid=(2 * half,), in_specs=[pl.BlockSpec(bl...  15.9 us
    all_to_all x2, starting transfers between devices, along_expert(): lax.all_to_all(copies, 'expert', split_axis=0, concat_axis=0, axis_index_...  13 us
    all_to_all x1, starting transfers between devices, on_device(): lax.all_to_all(send, 'expert', split_axis=0, concat_axis=0, tiled=True)  11.8 us
    all_to_all x2, waiting for transfers between devices, along_expert(): lax.all_to_all(copies, 'expert', split_axis=0, concat_axis=0, axis_index_...  11 us
  transfers between devices with their start and end apart: 24, of which 18 were waited for; matrix products, arithmetic and copies ran while one was open for 2% of the time, Pallas kernels for 9%

profile of v6, /device:TPU:32, one launch (start us, length us, event | category | flops | bytes accessed | tf_op | source)
XLA Modules:
  0.0 197.9 jit_solution(7944224036009525610)
XLA Ops:
  0.6 0.9 copy-done
  1.6 0.7 copy-done.3
  2.3 2.3 %shard_map.103 = (bf16[512,1024]{1,0:T(8,128)(2,1)}, s32[2,128]{1,0:T(2,128)S(1)}) custom-call(bf16[128,1024]{1,0:T(8,128)(2,1)S(1)} %copy-done, s32[2,128]{1,0:T(2,128)S(1)} %bitcast.27), custom_call_target="tpu_custom_call" | custom-call | tf_op jit(solution)/shard_map/pallas_call | solution.py:140
  4.6 11.8 %all-to-all-start = ((bf16[64,8,1024]{2,1,0:T(8,128)(2,1)}), bf16[64,8,1024]{2,1,0:T(8,128)(2,1)S(1)}, u32[]{:S(2)}, u32[]{:S(2)}) async-start(bf16[64,8,1024]{2,1,0:T(8,128)(2,1)} %bitcast.1), calls=%async_computation | async-start | bytes 2097152 | tf_op jit(solution)/shard_map/all_to_all | solution.py:311
  16.4 0.1 fusion.13
  16.5 0.1 fusion.15.refs_0_
  16.6 1.5 collective-permute-start
  18.1 2.7 %collective-permute-start.1 = (bf16[4,1024]{1,0:T(4,128)(2,1)S(1)}, bf16[4,1024]{1,0:T(4,128)(2,1)S(1)}, u32[]{:S(2)}, u32[]{:S(2)}) collective-permute-start(bf16[4,1024]{1,0:T(4,128)(2,1)S(1)} %fusion.15.refs_0_), channel_id=1, source_target_pairs={{0,2},{1,3},{2,0},{3,1},{4,6},{5,7},{6,4},{7,5},{8,10},{9,11},{10,... | collective-permute-start | bytes 24584 | tf_op jit(solution)/shard_map/ppermute | solution.py:286
  20.8 1.4 collective-permute-start.2
  22.3 1.0 collective-permute-done.1.refs_2_
  23.3 1.2 collective-permute-done.2.refs_3_
  24.5 1.1 shard_map.104
  25.6 18.6 %all-to-all-done = bf16[64,8,1024]{2,1,0:T(8,128)(2,1)S(1)} async-done(((bf16[64,8,1024]{2,1,0:T(8,128)(2,1)}), bf16[64,8,1024]{2,1,0:T(8,128)(2,1)S(1)}, u32[]{:S(2)}, u32[]{:S(2)}) %all-to-all-start) | async-done | bytes 1048608 | tf_op jit(solution)/shard_map/all_to_all | solution.py:311
  44.2 1.0 slice_bitcast_fusion
  45.3 1.5 collective-permute-start.3
  46.8 1.7 collective-permute-start.5
  48.5 1.5 collective-permute-start.7
  50.1 0.5 collective-permute-start.8
  50.5 6.5 %all-to-all-start.2 = ((bf16[32,16,1024]{2,1,0:T(8,128)(2,1)}), bf16[32,16,1024]{2,1,0:T(8,128)(2,1)}, u32[]{:S(2)}, u32[]{:S(2)}) async-start(bf16[32,16,1024]{2,1,0:T(8,128)(2,1)} %get-tuple-element.58), calls=%async_computation.2 | async-start | bytes 2097152 | tf_op jit(solution)/shard_map/all_to_all | solution.py:275
  57.1 4.5 %collective-permute-done.3.refs_0_ = bf16[256,1024]{1,0:T(8,128)(2,1)} collective-permute-done((bf16[256,1024]{1,0:T(8,128)(2,1)}, bf16[256,1024]{1,0:T(8,128)(2,1)}, u32[]{:S(2)}, u32[]{:S(2)}) %collective-permute-start.3) | collective-permute-done | bytes 524320 | tf_op jit(solution)/shard_map/ppermute | solution.py:286
  61.6 0.3 collective-permute-done.5.refs_1_
  61.9 1.6 copy-done.7
  63.5 4.5 %shard_map.105 = (bf16[256,1024]{1,0:T(8,128)(2,1)S(1)}, bf16[256,1024]{1,0:T(8,128)(2,1)S(1)}) custom-call(bf16[256,1024]{1,0:T(8,128)(2,1)} %collective-permute-done.3.refs_0_, bf16[256,1024]{1,0:T(8,128)(2,1)} %collective-permute-done.5.refs_1_, bf16[1024,1024]{1,0:T(8,128)(2,1)S(1)} %bitcast.29, bf16[1024,1024]{1,0:T(8,128)(2,1)S(1)} %bitcast.33), custom_call_target="tpu_custom_call" | custom-call | flops 6442450944 | bytes 6291456 | tf_op jit(solution)/shard_map/pallas_call | solution.py:53
  68.0 3.0 %collective-permute-start.11 = (bf16[256,1024]{1,0:T(8,128)(2,1)S(1)}, bf16[256,1024]{1,0:T(8,128)(2,1)S(1)}, u32[]{:S(2)}, u32[]{:S(2)}) collective-permute-start(bf16[256,1024]{1,0:T(8,128)(2,1)S(1)} %get-tuple-element.38), channel_id=1, source_target_pairs={{0,3},{1,0},{2,1},{3,2},{4,7},{5,4},{6,5},{7,6},{8,11},{9,8},{10,9... | collective-permute-start | bytes 1572872 | tf_op jit(solution)/shard_map/ppermute | solution.py:286
  71.1 2.1 %collective-permute-done.7.refs_0_ = bf16[256,1024]{1,0:T(8,128)(2,1)} collective-permute-done((bf16[256,1024]{1,0:T(8,128)(2,1)}, bf16[256,1024]{1,0:T(8,128)(2,1)}, u32[]{:S(2)}, u32[]{:S(2)}) %collective-permute-start.7) | collective-permute-done | bytes 524320 | tf_op jit(solution)/shard_map/ppermute | solution.py:286
  73.1 1.5 collective-permute-start.4
  74.6 1.7 collective-permute-start.6
  76.4 4.5 %shard_map.106 = (bf16[256,1024]{1,0:T(8,128)(2,1)S(1)}, bf16[256,1024]{1,0:T(8,128)(2,1)S(1)}) custom-call(bf16[256,1024]{1,0:T(8,128)(2,1)} %collective-permute-done.7.refs_0_, bf16[256,1024]{1,0:T(8,128)(2,1)} %collective-permute-done.8.refs_1_, bf16[1024,1024]{1,0:T(8,128)(2,1)S(1)} %bitcast.30, bf16[1024,1024]{1,0:T(8,128)(2,1)S(1)} %bitcast.34), custom_call_target="tpu_custom_call" | custom-call | flops 6442450944 | bytes 6291456 | tf_op jit(solution)/shard_map/pallas_call | solution.py:53
  80.9 13.8 %collective-permute-done.4.refs_0_ = bf16[256,1024]{1,0:T(8,128)(2,1)S(1)} collective-permute-done((bf16[256,1024]{1,0:T(8,128)(2,1)}, bf16[256,1024]{1,0:T(8,128)(2,1)S(1)}, u32[]{:S(2)}, u32[]{:S(2)}) %collective-permute-start.4) | collective-permute-done | bytes 524320 | tf_op jit(solution)/shard_map/ppermute | solution.py:286
  94.7 3.4 %shard_map.107 = (bf16[256,1024]{1,0:T(8,128)(2,1)S(1)}, bf16[256,1024]{1,0:T(8,128)(2,1)S(1)}) custom-call(bf16[256,1024]{1,0:T(8,128)(2,1)S(1)} %collective-permute-done.4.refs_0_, bf16[256,1024]{1,0:T(8,128)(2,1)S(1)} %collective-permute-done.6.refs_1_, bf16[1024,1024]{1,0:T(8,128)(2,1)S(1)} %bitcast.31, bf16[1024,1024]{1,0:T(8,128)(2,1)S(1)} %bitcast.35), custom_call_target="tpu_custom_call" | custom-call | flops 6442450944 | bytes 6291456 | tf_op jit(solution)/shard_map/pallas_call | solution.py:53
  98.1 2.6 %collective-permute-start.10 = (bf16[256,1024]{1,0:T(8,128)(2,1)S(1)}, bf16[256,1024]{1,0:T(8,128)(2,1)S(1)}, u32[]{:S(2)}, u32[]{:S(2)}) collective-permute-start(bf16[256,1024]{1,0:T(8,128)(2,1)S(1)} %get-tuple-element.49), channel_id=1, source_target_pairs={{0,3},{1,0},{2,1},{3,2},{4,7},{5,4},{6,5},{7,6},{8,11},{9,8},{10,9... | collective-permute-start | bytes 1572872 | tf_op jit(solution)/shard_map/ppermute | solution.py:286
  100.7 3.4 %shard_map.108.own_ref = bf16[512,1024]{1,0:T(8,128)(2,1)S(1)} custom-call(bf16[512,1024]{1,0:T(8,128)(2,1)S(1)} %bitcast.24, bf16[1024,1024]{1,0:T(8,128)(2,1)S(1)} %bitcast.32, bf16[1024,1024]{1,0:T(8,128)(2,1)S(1)} %bitcast.36), custom_call_target="tpu_custom_call" | custom-call | flops 6442450944 | bytes 6291456 | tf_op jit(solution)/shard_map/pallas_call | solution.py:53
  104.1 6.8 %collective-permute-done.10 = bf16[256,1024]{1,0:T(8,128)(2,1)S(1)} collective-permute-done((bf16[256,1024]{1,0:T(8,128)(2,1)S(1)}, bf16[256,1024]{1,0:T(8,128)(2,1)S(1)}, u32[]{:S(2)}, u32[]{:S(2)}) %collective-permute-start.10) | collective-permute-done | bytes 524320 | tf_op jit(solution)/shard_map/ppermute | solution.py:286
  110.9 3.4 %collective-permute-done.9 = bf16[256,1024]{1,0:T(8,128)(2,1)S(1)} collective-permute-done((bf16[256,1024]{1,0:T(8,128)(2,1)S(1)}, bf16[256,1024]{1,0:T(8,128)(2,1)S(1)}, u32[]{:S(2)}, u32[]{:S(2)}) %collective-permute-start.9) | collective-permute-done | bytes 524320 | tf_op jit(solution)/shard_map/ppermute | solution.py:286
  114.3 0.2 add_convert_fusion
  114.5 0.4 collective-permute-start.14
  114.9 0.2 add_convert_fusion.1
  115.1 1.8 collective-permute-start.13
  116.9 9.3 %collective-permute-done.14.last_bottom = bf16[256,1024]{1,0:T(8,128)(2,1)S(1)} collective-permute-done((bf16[256,1024]{1,0:T(8,128)(2,1)S(1)}, bf16[256,1024]{1,0:T(8,128)(2,1)S(1)}, u32[]{:S(2)}, u32[]{:S(2)}) %collective-permute-start.14) | collective-permute-done | bytes 524320 | tf_op jit(solution)/shard_map/ppermute | solution.py:286
  126.2 1.8 collective-permute-done.13.last_top
  127.9 1.8 shard_map.109
  129.7 8.8 %all-to-all-start.1 = ((bf16[64,8,1024]{2,1,0:T(8,128)(2,1)}), bf16[64,8,1024]{2,1,0:T(8,128)(2,1)S(1)}, u32[]{:S(2)}, u32[]{:S(2)}) async-start(bf16[64,8,1024]{2,1,0:T(8,128)(2,1)} %bitcast.7), calls=%async_computation.1 | async-start | bytes 2097152 | tf_op jit(solution)/shard_map/all_to_all | solution.py:352
  138.5 0.2 collective-permute-start.15
  138.8 0.0 copy-start.5
  138.8 2.7 %collective-permute-done.15 = bf16[512,1024]{1,0:T(8,128)(2,1)S(1)} collective-permute-done((bf16[512,1024]{1,0:T(8,128)(2,1)}, bf16[512,1024]{1,0:T(8,128)(2,1)S(1)}, u32[]{:S(2)}, u32[]{:S(2)}) %collective-permute-start.15) | collective-permute-done | bytes 1048608 | tf_op jit(solution)/shard_map/ppermute | solution.py:268
  141.5 1.5 pad_maximum_fusion
  143.0 23.4 %all-to-all-done.1 = bf16[64,8,1024]{2,1,0:T(8,128)(2,1)S(1)} async-done(((bf16[64,8,1024]{2,1,0:T(8,128)(2,1)}), bf16[64,8,1024]{2,1,0:T(8,128)(2,1)S(1)}, u32[]{:S(2)}, u32[]{:S(2)}) %all-to-all-start.1) | async-done | bytes 1048608 | tf_op jit(solution)/shard_map/all_to_all | solution.py:352
  166.4 2.4 %shard_map.110 = (f32[4,1024]{1,0:T(4,128)}, bf16[32,4,1024]{2,1,0:T(4,128)(2,1)}) custom-call(s32[1,4]{1,0:T(1,128)S(1)} %copy-done.5, bf16[512,1024]{1,0:T(8,128)(2,1)S(1)} %bitcast.25, bf16[128,1024]{1,0:T(8,128)(2,1)S(1)} %copy-done.1, s32[2,128]{1,0:T(2,128)S(1)} %get-tuple-element.60.place_ref, f32[2,128]{1,0:T(2,128)S(1)} %bitcast.28, ...), custom_call_target="tpu_custom_call" | custom-call | tf_op jit(solution)/shard_map/pallas_call | solution.py:208
  168.8 6.5 %all-to-all-start.3 = ((bf16[32,4,1024]{2,1,0:T(4,128)(2,1)}), bf16[32,4,1024]{2,1,0:T(4,128)(2,1)S(1)}, u32[]{:S(2)}, u32[]{:S(2)}) async-start(bf16[32,4,1024]{2,1,0:T(4,128)(2,1)} %get-tuple-element.62), calls=%async_computation.3 | async-start | bytes 524288 | tf_op jit(solution)/shard_map/all_to_all | solution.py:275
  175.4 1.4 subtract_convert_fusion.1
  176.7 11.0 %all-to-all-done.3 = bf16[32,4,1024]{2,1,0:T(4,128)(2,1)S(1)} async-done(((bf16[32,4,1024]{2,1,0:T(4,128)(2,1)}), bf16[32,4,1024]{2,1,0:T(4,128)(2,1)S(1)}, u32[]{:S(2)}, u32[]{:S(2)}) %all-to-all-start.3) | async-done | bytes 262176 | tf_op jit(solution)/shard_map/all_to_all | solution.py:275
  187.7 0.1 reshape.52
  187.8 0.1 collective-permute-start.16
  187.9 0.4 fusion.19
  188.3 1.1 collective-permute-done.16
  189.4 0.3 subtract_convert_fusion
  189.7 0.2 fusion.23
  189.9 0.1 collective-permute-start.17
  190.0 2.3 %collective-permute-start.18 = (f32[4,1024]{1,0:T(4,128)S(1)}, f32[4,1024]{1,0:T(4,128)S(1)}, u32[]{:S(2)}, u32[]{:S(2)}) collective-permute-start(f32[4,1024]{1,0:T(4,128)S(1)} %get-tuple-element.73), channel_id=1, source_target_pairs={{0,2},{1,3},{2,0},{3,1},{4,6},{5,7},{6,4},{7,5},{8,10},{9,11},{10,... | collective-permute-start | bytes 49160 | tf_op jit(solution)/shard_map/ppermute | solution.py:286
  192.3 0.6 fusion.18
  192.9 0.8 collective-permute-done.17
  193.7 1.6 collective-permute-done.18
  195.3 1.9 collective-permute-done.19
  197.3 0.6 fusion.17
  (32 shorter events, 0.1 us)
Async XLA Ops:
  0.6 1.0 copy-start
  1.6 0.7 copy-start.3
  2.3 14.1 %copy-start.8 = (bf16[4,1024]{1,0:T(4,128)(2,1)S(1)}, bf16[4,1024]{1,0:T(4,128)(2,1)}, u32[]{:S(2)}) copy-start(bf16[4,1024]{1,0:T(4,128)(2,1)} %param.12) | copy-start | bytes 24580
  4.6 39.6 %all-to-all-start = ((bf16[64,8,1024]{2,1,0:T(8,128)(2,1)}), bf16[64,8,1024]{2,1,0:T(8,128)(2,1)S(1)}, u32[]{:S(2)}, u32[]{:S(2)}) async-start(bf16[64,8,1024]{2,1,0:T(8,128)(2,1)} %bitcast.1), calls=%async_computation | async-start | bytes 2097152 | tf_op jit(solution)/shard_map/all_to_all | solution.py:311
  16.6 5.7 %collective-permute-start = (bf16[4,1024]{1,0:T(4,128)(2,1)S(1)}, bf16[4,1024]{1,0:T(4,128)(2,1)S(1)}, u32[]{:S(2)}, u32[]{:S(2)}) collective-permute-start(bf16[4,1024]{1,0:T(4,128)(2,1)S(1)} %fusion.15.refs_0_), channel_id=1, source_target_pairs={{0,1},{1,2},{2,3},{3,0},{4,5},{5,6},{6,7},{7,4},{8,9},{9,10},{10,1... | collective-permute-start | bytes 24584 | tf_op jit(solution)/shard_map/ppermute | solution.py:286
  18.1 5.2 %collective-permute-start.1 = (bf16[4,1024]{1,0:T(4,128)(2,1)S(1)}, bf16[4,1024]{1,0:T(4,128)(2,1)S(1)}, u32[]{:S(2)}, u32[]{:S(2)}) collective-permute-start(bf16[4,1024]{1,0:T(4,128)(2,1)S(1)} %fusion.15.refs_0_), channel_id=1, source_target_pairs={{0,2},{1,3},{2,0},{3,1},{4,6},{5,7},{6,4},{7,5},{8,10},{9,11},{10,... | collective-permute-start | bytes 24584 | tf_op jit(solution)/shard_map/ppermute | solution.py:286
  20.8 3.7 %collective-permute-start.2 = (bf16[4,1024]{1,0:T(4,128)(2,1)S(1)}, bf16[4,1024]{1,0:T(4,128)(2,1)S(1)}, u32[]{:S(2)}, u32[]{:S(2)}) collective-permute-start(bf16[4,1024]{1,0:T(4,128)(2,1)S(1)} %fusion.15.refs_0_), channel_id=1, source_target_pairs={{0,3},{1,0},{2,1},{3,2},{4,7},{5,4},{6,5},{7,6},{8,11},{9,8},{10,9... | collective-permute-start | bytes 24584 | tf_op jit(solution)/shard_map/ppermute | solution.py:286
  44.2 17.7 %copy-start.6 = (bf16[1,1024,1024]{2,1,0:T(8,128)(2,1)S(1)}, bf16[1,1024,1024]{2,1,0:T(8,128)(2,1)}, u32[]{:S(2)}) copy-start(bf16[1,1024,1024]{2,1,0:T(8,128)(2,1)} %param.14) | copy-start | bytes 6291460
  45.3 16.3 %collective-permute-start.3 = (bf16[256,1024]{1,0:T(8,128)(2,1)}, bf16[256,1024]{1,0:T(8,128)(2,1)}, u32[]{:S(2)}, u32[]{:S(2)}) collective-permute-start(bf16[256,1024]{1,0:T(8,128)(2,1)} %get-tuple-element.70), channel_id=1, source_target_pairs={{0,1},{1,2},{2,3},{3,0},{4,5},{5,6},{6,7},{7,4},{8,9},{9,10},{10,1... | collective-permute-start | bytes 1572872 | tf_op jit(solution)/shard_map/ppermute | solution.py:286
  46.8 15.1 %collective-permute-start.5 = (bf16[256,1024]{1,0:T(8,128)(2,1)}, bf16[256,1024]{1,0:T(8,128)(2,1)}, u32[]{:S(2)}, u32[]{:S(2)}) collective-permute-start(bf16[256,1024]{1,0:T(8,128)(2,1)} %get-tuple-element.69), channel_id=1, source_target_pairs={{0,3},{1,0},{2,1},{3,2},{4,7},{5,4},{6,5},{7,6},{8,11},{9,8},{10,9... | collective-permute-start | bytes 1572872 | tf_op jit(solution)/shard_map/ppermute | solution.py:286
  48.5 24.6 %collective-permute-start.7 = (bf16[256,1024]{1,0:T(8,128)(2,1)}, bf16[256,1024]{1,0:T(8,128)(2,1)}, u32[]{:S(2)}, u32[]{:S(2)}) collective-permute-start(bf16[256,1024]{1,0:T(8,128)(2,1)} %get-tuple-element.70), channel_id=1, source_target_pairs={{0,3},{1,0},{2,1},{3,2},{4,7},{5,4},{6,5},{7,6},{8,11},{9,8},{10,9... | collective-permute-start | bytes 1572872 | tf_op jit(solution)/shard_map/ppermute | solution.py:286
  50.1 23.1 %collective-permute-start.8 = (bf16[256,1024]{1,0:T(8,128)(2,1)}, bf16[256,1024]{1,0:T(8,128)(2,1)}, u32[]{:S(2)}, u32[]{:S(2)}) collective-permute-start(bf16[256,1024]{1,0:T(8,128)(2,1)} %get-tuple-element.69), channel_id=1, source_target_pairs={{0,1},{1,2},{2,3},{3,0},{4,5},{5,6},{6,7},{7,4},{8,9},{9,10},{10,1... | collective-permute-start | bytes 1572872 | tf_op jit(solution)/shard_map/ppermute | solution.py:286
  50.5 79.2 %all-to-all-start.2 = ((bf16[32,16,1024]{2,1,0:T(8,128)(2,1)}), bf16[32,16,1024]{2,1,0:T(8,128)(2,1)}, u32[]{:S(2)}, u32[]{:S(2)}) async-start(bf16[32,16,1024]{2,1,0:T(8,128)(2,1)} %get-tuple-element.58), calls=%async_computation.2 | async-start | bytes 2097152 | tf_op jit(solution)/shard_map/all_to_all | solution.py:275
  61.9 1.6 copy-start.7
  68.0 36.1 %collective-permute-start.11 = (bf16[256,1024]{1,0:T(8,128)(2,1)S(1)}, bf16[256,1024]{1,0:T(8,128)(2,1)S(1)}, u32[]{:S(2)}, u32[]{:S(2)}) collective-permute-start(bf16[256,1024]{1,0:T(8,128)(2,1)S(1)} %get-tuple-element.38), channel_id=1, source_target_pairs={{0,3},{1,0},{2,1},{3,2},{4,7},{5,4},{6,5},{7,6},{8,11},{9,8},{10,9... | collective-permute-start | bytes 1572872 | tf_op jit(solution)/shard_map/ppermute | solution.py:286
  71.1 33.1 %collective-permute-start.12 = (bf16[256,1024]{1,0:T(8,128)(2,1)S(1)}, bf16[256,1024]{1,0:T(8,128)(2,1)S(1)}, u32[]{:S(2)}, u32[]{:S(2)}) collective-permute-start(bf16[256,1024]{1,0:T(8,128)(2,1)S(1)} %get-tuple-element.39), channel_id=1, source_target_pairs={{0,1},{1,2},{2,3},{3,0},{4,5},{5,6},{6,7},{7,4},{8,9},{9,10},{10,1... | collective-permute-start | bytes 1572872 | tf_op jit(solution)/shard_map/ppermute | solution.py:286
  73.1 21.6 %collective-permute-start.4 = (bf16[256,1024]{1,0:T(8,128)(2,1)}, bf16[256,1024]{1,0:T(8,128)(2,1)S(1)}, u32[]{:S(2)}, u32[]{:S(2)}) collective-permute-start(bf16[256,1024]{1,0:T(8,128)(2,1)} %collective-permute-done.3.refs_0_), channel_id=1, source_target_pairs={{0,1},{1,2},{2,3},{3,0},{4,5},{5,6},{6,7},{7,4},{8,9},{9,10},{10,1... | collective-permute-start | bytes 1572872 | tf_op jit(solution)/shard_map/ppermute | solution.py:286
  74.6 20.1 %collective-permute-start.6 = (bf16[256,1024]{1,0:T(8,128)(2,1)}, bf16[256,1024]{1,0:T(8,128)(2,1)S(1)}, u32[]{:S(2)}, u32[]{:S(2)}) collective-permute-start(bf16[256,1024]{1,0:T(8,128)(2,1)} %collective-permute-done.5.refs_1_), channel_id=1, source_target_pairs={{0,3},{1,0},{2,1},{3,2},{4,7},{5,4},{6,5},{7,6},{8,11},{9,8},{10,9... | collective-permute-start | bytes 1572872 | tf_op jit(solution)/shard_map/ppermute | solution.py:286
  98.1 12.8 %collective-permute-start.10 = (bf16[256,1024]{1,0:T(8,128)(2,1)S(1)}, bf16[256,1024]{1,0:T(8,128)(2,1)S(1)}, u32[]{:S(2)}, u32[]{:S(2)}) collective-permute-start(bf16[256,1024]{1,0:T(8,128)(2,1)S(1)} %get-tuple-element.49), channel_id=1, source_target_pairs={{0,3},{1,0},{2,1},{3,2},{4,7},{5,4},{6,5},{7,6},{8,11},{9,8},{10,9... | collective-permute-start | bytes 1572872 | tf_op jit(solution)/shard_map/ppermute | solution.py:286
  100.7 13.6 %collective-permute-start.9 = (bf16[256,1024]{1,0:T(8,128)(2,1)S(1)}, bf16[256,1024]{1,0:T(8,128)(2,1)S(1)}, u32[]{:S(2)}, u32[]{:S(2)}) collective-permute-start(bf16[256,1024]{1,0:T(8,128)(2,1)S(1)} %get-tuple-element.48), channel_id=1, source_target_pairs={{0,1},{1,2},{2,3},{3,0},{4,5},{5,6},{6,7},{7,4},{8,9},{9,10},{10,1... | collective-permute-start | bytes 1572872 | tf_op jit(solution)/shard_map/ppermute | solution.py:286
  114.5 11.6 %collective-permute-start.14 = (bf16[256,1024]{1,0:T(8,128)(2,1)S(1)}, bf16[256,1024]{1,0:T(8,128)(2,1)S(1)}, u32[]{:S(2)}, u32[]{:S(2)}) collective-permute-start(bf16[256,1024]{1,0:T(8,128)(2,1)S(1)} %add_convert_fusion), channel_id=1, source_target_pairs={{0,3},{1,0},{2,1},{3,2},{4,7},{5,4},{6,5},{7,6},{8,11},{9,8},{10,9... | collective-permute-start | bytes 1572872 | tf_op jit(solution)/shard_map/ppermute | solution.py:286
  115.1 12.8 %collective-permute-start.13 = (bf16[256,1024]{1,0:T(8,128)(2,1)S(1)}, bf16[256,1024]{1,0:T(8,128)(2,1)S(1)}, u32[]{:S(2)}, u32[]{:S(2)}) collective-permute-start(bf16[256,1024]{1,0:T(8,128)(2,1)S(1)} %add_convert_fusion.1), channel_id=1, source_target_pairs={{0,1},{1,2},{2,3},{3,0},{4,5},{5,6},{6,7},{7,4},{8,9},{9,10},{10,1... | collective-permute-start | bytes 1572872 | tf_op jit(solution)/shard_map/ppermute | solution.py:286
  129.7 36.7 %all-to-all-start.1 = ((bf16[64,8,1024]{2,1,0:T(8,128)(2,1)}), bf16[64,8,1024]{2,1,0:T(8,128)(2,1)S(1)}, u32[]{:S(2)}, u32[]{:S(2)}) async-start(bf16[64,8,1024]{2,1,0:T(8,128)(2,1)} %bitcast.7), calls=%async_computation.1 | async-start | bytes 2097152 | tf_op jit(solution)/shard_map/all_to_all | solution.py:352
  138.5 3.0 %collective-permute-start.15 = (bf16[512,1024]{1,0:T(8,128)(2,1)}, bf16[512,1024]{1,0:T(8,128)(2,1)S(1)}, u32[]{:S(2)}, u32[]{:S(2)}) collective-permute-start(bf16[512,1024]{1,0:T(8,128)(2,1)} %bitcast.8), channel_id=1, source_target_pairs={{0,4},{4,0},{8,12},{12,8},{16,20},{20,16},{24,28},{28,24},{32,36},... | collective-permute-start | bytes 3145736 | tf_op jit(solution)/shard_map/ppermute | solution.py:268
  138.7 27.7 %copy-start.1 = (bf16[128,1024]{1,0:T(8,128)(2,1)S(1)}, bf16[128,1024]{1,0:T(8,128)(2,1)}, u32[]{:S(2)}) copy-start(bf16[128,1024]{1,0:T(8,128)(2,1)} %tokens_ref.3) | copy-start | bytes 786436
  138.7 27.7 %copy-start.2 = (f32[1024]{0:T(1024)S(1)}, f32[1024]{0:T(1024)}, u32[]{:S(2)}) copy-start(f32[1024]{0:T(1024)} %param.13) | copy-start | bytes 12292
  138.7 27.7 %copy-start.4 = (f32[128,2]{0,1:T(2,128)S(1)}, f32[128,2]{0,1:T(2,128)}, u32[]{:S(2)}) copy-start(f32[128,2]{0,1:T(2,128)} %param.10) | copy-start | bytes 3076
  138.8 27.6 %copy-start.5 = (s32[1,4]{1,0:T(1,128)S(1)}, s32[1,4]{1,0:T(1,128)}, u32[]{:S(2)}) copy-start(s32[1,4]{1,0:T(1,128)} %lengths_ref.1) | copy-start | bytes 52
  168.8 18.8 %all-to-all-start.3 = ((bf16[32,4,1024]{2,1,0:T(4,128)(2,1)}), bf16[32,4,1024]{2,1,0:T(4,128)(2,1)S(1)}, u32[]{:S(2)}, u32[]{:S(2)}) async-start(bf16[32,4,1024]{2,1,0:T(4,128)(2,1)} %get-tuple-element.62), calls=%async_computation.3 | async-start | bytes 524288 | tf_op jit(solution)/shard_map/all_to_all | solution.py:275
  187.8 1.6 collective-permute-start.16
  189.9 3.8 %collective-permute-start.17 = (f32[4,1024]{1,0:T(4,128)S(1)}, f32[4,1024]{1,0:T(4,128)S(1)}, u32[]{:S(2)}, u32[]{:S(2)}) collective-permute-start(f32[4,1024]{1,0:T(4,128)S(1)} %get-tuple-element.71), channel_id=1, source_target_pairs={{0,3},{1,0},{2,1},{3,2},{4,7},{5,4},{6,5},{7,6},{8,11},{9,8},{10,9... | collective-permute-start | bytes 49160 | tf_op jit(solution)/shard_map/ppermute | solution.py:286
  190.0 5.3 %collective-permute-start.18 = (f32[4,1024]{1,0:T(4,128)S(1)}, f32[4,1024]{1,0:T(4,128)S(1)}, u32[]{:S(2)}, u32[]{:S(2)}) collective-permute-start(f32[4,1024]{1,0:T(4,128)S(1)} %get-tuple-element.73), channel_id=1, source_target_pairs={{0,2},{1,3},{2,0},{3,1},{4,6},{5,7},{6,4},{7,5},{8,10},{9,11},{10,... | collective-permute-start | bytes 49160 | tf_op jit(solution)/shard_map/ppermute | solution.py:286
  192.3 4.9 %collective-permute-start.19 = (f32[4,1024]{1,0:T(4,128)S(1)}, f32[4,1024]{1,0:T(4,128)S(1)}, u32[]{:S(2)}, u32[]{:S(2)}) collective-permute-start(f32[4,1024]{1,0:T(4,128)S(1)} %get-tuple-element.72), channel_id=1, source_target_pairs={{0,1},{1,2},{2,3},{3,0},{4,5},{5,6},{6,7},{7,4},{8,9},{9,10},{10,1... | collective-permute-start | bytes 49160 | tf_op jit(solution)/shard_map/ppermute | solution.py:286

commit v7 on v6

--- a/solution.py
+++ b/solution.py
@@ -153,7 +153,7 @@
             jax.ShapeDtypeStruct(routes.shape, jnp.int32),
         ],
         scratch_shapes=[pltpu.VMEM((count, width), BF16)],
-        compiler_params=pltpu.CompilerParams(vmem_limit_bytes=12 * 2**20),
+        compiler_params=pltpu.CompilerParams(vmem_limit_bytes=63 * 2**20),
     )(tokens, routes)
 
 
@@ -323,6 +323,8 @@
     pictures_all = along_expert(picture_copies, shape)
     left_bottom = ring_shift(bottom, 1, grid_all)
     right_top = ring_shift(top, -1, grid_all)
+    own_term = expert_part([rows], up_local, down_local)[0]
+    own_term, left_top, right_bottom = held(own_term, left_top, right_bottom)
     far_top = ring_shift(left_top, 1, grid_all)
     far_bottom = ring_shift(right_bottom, -1, grid_all)
     left_top, right_bottom = expert_part([left_top, right_bottom], up_local, down_local)
@@ -336,12 +338,10 @@
         far_top, far_bottom, left_top, right_bottom, right_top, left_bottom
     )
     far_top, far_bottom = expert_part([far_top, far_bottom], up_local, down_local)
-    rows, far_top, far_bottom = held(rows, far_top, far_bottom)
-    own_term = expert_part([rows], up_local, down_local)[0]
     far_from_left = ring_shift(far_top, 1, grid_all)
     far_from_right = ring_shift(far_bottom, -1, grid_all)
-    far_from_left, far_from_right, home_top, home_bottom, own_term = held(
-        far_from_left, far_from_right, home_top, home_bottom, own_term
+    far_from_left, far_from_right, home_top, home_bottom = held(
+        far_from_left, far_from_right, home_top, home_bottom
     )
     right_top = (right_top.astype(F32) + far_from_left.astype(F32)).astype(BF16)
     left_bottom = (left_bottom.astype(F32) + far_from_right.astype(F32)).astype(BF16)

time: 199 us -> 193 us (0.970)
  waiting for transfers between devices: 105 us -> 96.1 us
  starting transfers between devices: 58.2 us -> 62.4 us
    ppermute x18, waiting for transfers between devices: 48.4 us -> 39.3 us  [ring_shift(): lax.ppermute(values, 'grid', [(i, (i + step) % size) for i in range(size)])]
    ppermute x18, starting transfers between devices: 24.4 us -> 28.6 us  [ring_shift(): lax.ppermute(values, 'grid', [(i, (i + step) % size) for i in range(size)])]
  transfers between devices with their start and end apart: 24 -> 24, of which waited for: 18 -> 15; matrix products, arithmetic and copies ran while one was open for 2% -> 2% of each run, Pallas kernels for 9% -> 10%
where the time goes in v7:
time: 193 us; the launch traced here: 192 us
  waiting for transfers between devices  96.1 us (50%)
  starting transfers between devices  62.4 us (32%)
  Pallas kernels  24.4 us (13%)
  other arithmetic  3.35 us (2%)
  local copies, waits for them, and re-layouts  2.79 us (1%)
  matrix products  2.21 us (1%)
    ppermute x18, waiting for transfers between devices, ring_shift(): lax.ppermute(values, 'grid', [(i, (i + step) % size) for i in range(size)])  39.3 us
    ppermute x18, starting transfers between devices, ring_shift(): lax.ppermute(values, 'grid', [(i, (i + step) % size) for i in range(size)])  28.6 us
    all_to_all x1, waiting for transfers between devices, on_device(): lax.all_to_all(results, 'expert', split_axis=0, concat_axis=0, tiled=True)  23.4 us
    all_to_all x1, waiting for transfers between devices, on_device(): lax.all_to_all(send, 'expert', split_axis=0, concat_axis=0, tiled=True)  18.6 us
    pallas_call x4, Pallas kernels, expert_part(): pl.pallas_call(expert_kernel, grid=(2 * half,), in_specs=[pl.BlockSpec(bl...  15.8 us
    all_to_all x2, starting transfers between devices, along_expert(): lax.all_to_all(copies, 'expert', split_axis=0, concat_axis=0, axis_index_...  13 us
    all_to_all x1, starting transfers between devices, on_device(): lax.all_to_all(send, 'expert', split_axis=0, concat_axis=0, tiled=True)  11.8 us
    all_to_all x2, waiting for transfers between devices, along_expert(): lax.all_to_all(copies, 'expert', split_axis=0, concat_axis=0, axis_index_...  11 us
  transfers between devices with their start and end apart: 24, of which 15 were waited for; matrix products, arithmetic and copies ran while one was open for 2% of the time, Pallas kernels for 10%

profile of v7, /device:TPU:32, one launch (start us, length us, event | category | flops | bytes accessed | tf_op | source)
XLA Modules:
  0.0 192.3 jit_solution(17014686652273342971)
XLA Ops:
  0.6 3.3 %shard_map.103 = (bf16[512,1024]{1,0:T(8,128)(2,1)}, s32[2,128]{1,0:T(2,128)}) custom-call(bf16[128,1024]{1,0:T(8,128)(2,1)} %tokens_ref.3, s32[2,128]{1,0:T(2,128)} %bitcast.37), custom_call_target="tpu_custom_call" | custom-call | tf_op jit(solution)/shard_map/pallas_call | solution.py:140
  3.9 11.8 %all-to-all-start = ((bf16[64,8,1024]{2,1,0:T(8,128)(2,1)}), bf16[64,8,1024]{2,1,0:T(8,128)(2,1)S(1)}, u32[]{:S(2)}, u32[]{:S(2)}) async-start(bf16[64,8,1024]{2,1,0:T(8,128)(2,1)} %bitcast.36), calls=%async_computation | async-start | bytes 2097152 | tf_op jit(solution)/shard_map/all_to_all | solution.py:311
  15.7 0.1 fusion.13
  15.8 0.1 fusion.15.refs_0_
  15.9 1.5 collective-permute-start
  17.4 2.7 %collective-permute-start.1 = (bf16[4,1024]{1,0:T(4,128)(2,1)S(1)}, bf16[4,1024]{1,0:T(4,128)(2,1)S(1)}, u32[]{:S(2)}, u32[]{:S(2)}) collective-permute-start(bf16[4,1024]{1,0:T(4,128)(2,1)S(1)} %fusion.15.refs_0_), channel_id=1, source_target_pairs={{0,2},{1,3},{2,0},{3,1},{4,6},{5,7},{6,4},{7,5},{8,10},{9,11},{10,... | collective-permute-start | bytes 24584 | tf_op jit(solution)/shard_map/ppermute | solution.py:286
  20.2 1.4 collective-permute-start.2
  21.6 1.0 collective-permute-done.1.refs_2_
  22.6 1.2 collective-permute-done.2.refs_3_
  23.8 1.1 shard_map.104
  24.9 18.6 %all-to-all-done = bf16[64,8,1024]{2,1,0:T(8,128)(2,1)S(1)} async-done(((bf16[64,8,1024]{2,1,0:T(8,128)(2,1)}), bf16[64,8,1024]{2,1,0:T(8,128)(2,1)S(1)}, u32[]{:S(2)}, u32[]{:S(2)}) %all-to-all-start) | async-done | bytes 1048608 | tf_op jit(solution)/shard_map/all_to_all | solution.py:311
  43.6 1.1 slice_bitcast_fusion
  44.6 1.5 collective-permute-start.3
  46.1 1.7 collective-permute-start.7
  47.9 1.5 collective-permute-start.4
  49.4 0.5 collective-permute-start.8
  49.9 6.5 %all-to-all-start.2 = ((bf16[32,16,1024]{2,1,0:T(8,128)(2,1)}), bf16[32,16,1024]{2,1,0:T(8,128)(2,1)}, u32[]{:S(2)}, u32[]{:S(2)}) async-start(bf16[32,16,1024]{2,1,0:T(8,128)(2,1)} %get-tuple-element.56), calls=%async_computation.2 | async-start | bytes 2097152 | tf_op jit(solution)/shard_map/all_to_all | solution.py:275
  56.4 0.0 copy-start.6
  56.4 1.6 copy-done.6
  58.0 3.4 %shard_map.105.own_ref = bf16[512,1024]{1,0:T(8,128)(2,1)S(1)} custom-call(bf16[512,1024]{1,0:T(8,128)(2,1)S(1)} %bitcast.24, bf16[1024,1024]{1,0:T(8,128)(2,1)S(1)} %bitcast.28, bf16[1024,1024]{1,0:T(8,128)(2,1)S(1)} %bitcast.32), custom_call_target="tpu_custom_call" | custom-call | flops 6442450944 | bytes 6291456 | tf_op jit(solution)/shard_map/pallas_call | solution.py:53
  61.4 9.8 %collective-permute-done.4.refs_1_ = bf16[256,1024]{1,0:T(8,128)(2,1)} collective-permute-done((bf16[256,1024]{1,0:T(8,128)(2,1)}, bf16[256,1024]{1,0:T(8,128)(2,1)}, u32[]{:S(2)}, u32[]{:S(2)}) %collective-permute-start.4) | collective-permute-done | bytes 524320 | tf_op jit(solution)/shard_map/ppermute | solution.py:286
  71.2 1.5 collective-permute-start.5
  72.7 1.7 collective-permute-start.6
  74.5 4.5 %shard_map.106 = (bf16[256,1024]{1,0:T(8,128)(2,1)S(1)}, bf16[256,1024]{1,0:T(8,128)(2,1)S(1)}) custom-call(bf16[256,1024]{1,0:T(8,128)(2,1)} %collective-permute-done.3.refs_0_, bf16[256,1024]{1,0:T(8,128)(2,1)} %collective-permute-done.4.refs_1_, bf16[1024,1024]{1,0:T(8,128)(2,1)S(1)} %bitcast.29, bf16[1024,1024]{1,0:T(8,128)(2,1)S(1)} %bitcast.33), custom_call_target="tpu_custom_call" | custom-call | flops 6442450944 | bytes 6291456 | tf_op jit(solution)/shard_map/pallas_call | solution.py:53
  79.0 1.8 collective-permute-start.11
  80.8 0.3 collective-permute-start.12
  81.1 4.5 %shard_map.107 = (bf16[256,1024]{1,0:T(8,128)(2,1)S(1)}, bf16[256,1024]{1,0:T(8,128)(2,1)S(1)}) custom-call(bf16[256,1024]{1,0:T(8,128)(2,1)} %collective-permute-done.7.refs_0_, bf16[256,1024]{1,0:T(8,128)(2,1)} %collective-permute-done.8.refs_1_, bf16[1024,1024]{1,0:T(8,128)(2,1)S(1)} %bitcast.30, bf16[1024,1024]{1,0:T(8,128)(2,1)S(1)} %bitcast.34), custom_call_target="tpu_custom_call" | custom-call | flops 6442450944 | bytes 6291456 | tf_op jit(solution)/shard_map/pallas_call | solution.py:53
  85.6 1.8 collective-permute-done.5.refs_0_
  87.4 0.3 collective-permute-done.6.refs_1_
  87.7 3.4 %shard_map.108 = (bf16[256,1024]{1,0:T(8,128)(2,1)S(1)}, bf16[256,1024]{1,0:T(8,128)(2,1)S(1)}) custom-call(bf16[256,1024]{1,0:T(8,128)(2,1)S(1)} %collective-permute-done.5.refs_0_, bf16[256,1024]{1,0:T(8,128)(2,1)S(1)} %collective-permute-done.6.refs_1_, bf16[1024,1024]{1,0:T(8,128)(2,1)S(1)} %bitcast.31, bf16[1024,1024]{1,0:T(8,128)(2,1)S(1)} %bitcast.35), custom_call_target="tpu_custom_call" | custom-call | flops 6442450944 | bytes 6291456 | tf_op jit(solution)/shard_map/pallas_call | solution.py:53
  91.1 1.3 collective-permute-start.9
  92.4 2.0 %collective-permute-start.10 = (bf16[256,1024]{1,0:T(8,128)(2,1)S(1)}, bf16[256,1024]{1,0:T(8,128)(2,1)S(1)}, u32[]{:S(2)}, u32[]{:S(2)}) collective-permute-start(bf16[256,1024]{1,0:T(8,128)(2,1)S(1)} %get-tuple-element.49), channel_id=1, source_target_pairs={{0,3},{1,0},{2,1},{3,2},{4,7},{5,4},{6,5},{7,6},{8,11},{9,8},{10,9... | collective-permute-start | bytes 1572872 | tf_op jit(solution)/shard_map/ppermute | solution.py:286
  94.4 4.5 %collective-permute-done.11.home_top = bf16[256,1024]{1,0:T(8,128)(2,1)S(1)} collective-permute-done((bf16[256,1024]{1,0:T(8,128)(2,1)S(1)}, bf16[256,1024]{1,0:T(8,128)(2,1)S(1)}, u32[]{:S(2)}, u32[]{:S(2)}) %collective-permute-start.11) | collective-permute-done | bytes 524320 | tf_op jit(solution)/shard_map/ppermute | solution.py:286
  99.0 8.9 %collective-permute-done.9 = bf16[256,1024]{1,0:T(8,128)(2,1)S(1)} collective-permute-done((bf16[256,1024]{1,0:T(8,128)(2,1)S(1)}, bf16[256,1024]{1,0:T(8,128)(2,1)S(1)}, u32[]{:S(2)}, u32[]{:S(2)}) %collective-permute-start.9) | collective-permute-done | bytes 524320 | tf_op jit(solution)/shard_map/ppermute | solution.py:286
  107.8 0.2 add_convert_fusion.1
  108.0 1.3 collective-permute-start.13
  109.3 0.2 add_convert_fusion
  109.5 2.1 %collective-permute-start.14 = (bf16[256,1024]{1,0:T(8,128)(2,1)S(1)}, bf16[256,1024]{1,0:T(8,128)(2,1)S(1)}, u32[]{:S(2)}, u32[]{:S(2)}) collective-permute-start(bf16[256,1024]{1,0:T(8,128)(2,1)S(1)} %add_convert_fusion), channel_id=1, source_target_pairs={{0,3},{1,0},{2,1},{3,2},{4,7},{5,4},{6,5},{7,6},{8,11},{9,8},{10,9... | collective-permute-start | bytes 1572872 | tf_op jit(solution)/shard_map/ppermute | solution.py:286
  111.6 9.5 %collective-permute-done.13.last_top = bf16[256,1024]{1,0:T(8,128)(2,1)S(1)} collective-permute-done((bf16[256,1024]{1,0:T(8,128)(2,1)S(1)}, bf16[256,1024]{1,0:T(8,128)(2,1)S(1)}, u32[]{:S(2)}, u32[]{:S(2)}) %collective-permute-start.13) | collective-permute-done | bytes 524320 | tf_op jit(solution)/shard_map/ppermute | solution.py:286
  121.2 1.8 shard_map.109
  123.0 8.8 %all-to-all-start.1 = ((bf16[64,8,1024]{2,1,0:T(8,128)(2,1)}), bf16[64,8,1024]{2,1,0:T(8,128)(2,1)S(1)}, u32[]{:S(2)}, u32[]{:S(2)}) async-start(bf16[64,8,1024]{2,1,0:T(8,128)(2,1)} %bitcast.7), calls=%async_computation.1 | async-start | bytes 2097152 | tf_op jit(solution)/shard_map/all_to_all | solution.py:352
  131.7 0.2 collective-permute-start.15
  132.0 0.0 copy-start.2
  132.0 0.0 copy-start.4
  132.0 2.7 %collective-permute-done.15 = bf16[512,1024]{1,0:T(8,128)(2,1)S(1)} collective-permute-done((bf16[512,1024]{1,0:T(8,128)(2,1)}, bf16[512,1024]{1,0:T(8,128)(2,1)S(1)}, u32[]{:S(2)}, u32[]{:S(2)}) %collective-permute-start.15) | collective-permute-done | bytes 1048608 | tf_op jit(solution)/shard_map/ppermute | solution.py:268
  134.7 1.5 pad_maximum_fusion
  136.2 23.4 %all-to-all-done.1 = bf16[64,8,1024]{2,1,0:T(8,128)(2,1)S(1)} async-done(((bf16[64,8,1024]{2,1,0:T(8,128)(2,1)}), bf16[64,8,1024]{2,1,0:T(8,128)(2,1)S(1)}, u32[]{:S(2)}, u32[]{:S(2)}) %all-to-all-start.1) | async-done | bytes 1048608 | tf_op jit(solution)/shard_map/all_to_all | solution.py:352
  159.6 2.4 %shard_map.110 = (f32[4,1024]{1,0:T(4,128)}, bf16[32,4,1024]{2,1,0:T(4,128)(2,1)}) custom-call(s32[1,4]{1,0:T(1,128)S(1)} %copy-done.4, bf16[512,1024]{1,0:T(8,128)(2,1)S(1)} %bitcast.25, bf16[128,1024]{1,0:T(8,128)(2,1)S(1)} %copy-done, s32[2,128]{1,0:T(2,128)S(1)} %copy-done.3, f32[2,128]{1,0:T(2,128)S(1)} %bitcast.27, f32[1,1024]{1,0:T(1,128)S(1)} %bitcast.26), custom_call_target="tpu_custom_call" | custom-call | tf_op jit(solution)/shard_map/pallas_call | solution.py:208
  162.1 6.5 %all-to-all-start.3 = ((bf16[32,4,1024]{2,1,0:T(4,128)(2,1)}), bf16[32,4,1024]{2,1,0:T(4,128)(2,1)S(1)}, u32[]{:S(2)}, u32[]{:S(2)}) async-start(bf16[32,4,1024]{2,1,0:T(4,128)(2,1)} %get-tuple-element.60), calls=%async_computation.3 | async-start | bytes 524288 | tf_op jit(solution)/shard_map/all_to_all | solution.py:275
  168.6 1.4 subtract_convert_fusion.1
  170.0 11.0 %all-to-all-done.3 = bf16[32,4,1024]{2,1,0:T(4,128)(2,1)S(1)} async-done(((bf16[32,4,1024]{2,1,0:T(4,128)(2,1)}), bf16[32,4,1024]{2,1,0:T(4,128)(2,1)S(1)}, u32[]{:S(2)}, u32[]{:S(2)}) %all-to-all-start.3) | async-done | bytes 262176 | tf_op jit(solution)/shard_map/all_to_all | solution.py:275
  180.9 0.1 reshape.52
  181.0 0.1 collective-permute-start.16
  181.1 0.4 fusion.19
  181.5 1.1 collective-permute-done.16
  182.6 0.3 subtract_convert_fusion
  182.9 0.2 fusion.23
  183.1 1.5 collective-permute-start.19
  184.6 3.3 %collective-permute-start.18 = (f32[4,1024]{1,0:T(4,128)S(1)}, f32[4,1024]{1,0:T(4,128)S(1)}, u32[]{:S(2)}, u32[]{:S(2)}) collective-permute-start(f32[4,1024]{1,0:T(4,128)S(1)} %get-tuple-element.71), channel_id=1, source_target_pairs={{0,2},{1,3},{2,0},{3,1},{4,6},{5,7},{6,4},{7,5},{8,10},{9,11},{10,... | collective-permute-start | bytes 49160 | tf_op jit(solution)/shard_map/ppermute | solution.py:286
  187.9 0.9 collective-permute-start.17
  188.8 0.6 fusion.18
  189.4 0.5 collective-permute-done.18
  189.8 1.8 collective-permute-done.17
  191.6 0.6 fusion.17
  (30 shorter events, 0.1 us)
Async XLA Ops:
  0.6 15.1 %copy-start.7 = (bf16[4,1024]{1,0:T(4,128)(2,1)S(1)}, bf16[4,1024]{1,0:T(4,128)(2,1)}, u32[]{:S(2)}) copy-start(bf16[4,1024]{1,0:T(4,128)(2,1)} %param.12) | copy-start | bytes 24580
  3.9 39.6 %all-to-all-start = ((bf16[64,8,1024]{2,1,0:T(8,128)(2,1)}), bf16[64,8,1024]{2,1,0:T(8,128)(2,1)S(1)}, u32[]{:S(2)}, u32[]{:S(2)}) async-start(bf16[64,8,1024]{2,1,0:T(8,128)(2,1)} %bitcast.36), calls=%async_computation | async-start | bytes 2097152 | tf_op jit(solution)/shard_map/all_to_all | solution.py:311
  15.9 5.7 %collective-permute-start = (bf16[4,1024]{1,0:T(4,128)(2,1)S(1)}, bf16[4,1024]{1,0:T(4,128)(2,1)S(1)}, u32[]{:S(2)}, u32[]{:S(2)}) collective-permute-start(bf16[4,1024]{1,0:T(4,128)(2,1)S(1)} %fusion.15.refs_0_), channel_id=1, source_target_pairs={{0,1},{1,2},{2,3},{3,0},{4,5},{5,6},{6,7},{7,4},{8,9},{9,10},{10,1... | collective-permute-start | bytes 24584 | tf_op jit(solution)/shard_map/ppermute | solution.py:286
  17.4 5.2 %collective-permute-start.1 = (bf16[4,1024]{1,0:T(4,128)(2,1)S(1)}, bf16[4,1024]{1,0:T(4,128)(2,1)S(1)}, u32[]{:S(2)}, u32[]{:S(2)}) collective-permute-start(bf16[4,1024]{1,0:T(4,128)(2,1)S(1)} %fusion.15.refs_0_), channel_id=1, source_target_pairs={{0,2},{1,3},{2,0},{3,1},{4,6},{5,7},{6,4},{7,5},{8,10},{9,11},{10,... | collective-permute-start | bytes 24584 | tf_op jit(solution)/shard_map/ppermute | solution.py:286
  20.2 3.7 %collective-permute-start.2 = (bf16[4,1024]{1,0:T(4,128)(2,1)S(1)}, bf16[4,1024]{1,0:T(4,128)(2,1)S(1)}, u32[]{:S(2)}, u32[]{:S(2)}) collective-permute-start(bf16[4,1024]{1,0:T(4,128)(2,1)S(1)} %fusion.15.refs_0_), channel_id=1, source_target_pairs={{0,3},{1,0},{2,1},{3,2},{4,7},{5,4},{6,5},{7,6},{8,11},{9,8},{10,9... | collective-permute-start | bytes 24584 | tf_op jit(solution)/shard_map/ppermute | solution.py:286
  43.6 12.9 %copy-start.5 = (bf16[1,1024,1024]{2,1,0:T(8,128)(2,1)S(1)}, bf16[1,1024,1024]{2,1,0:T(8,128)(2,1)}, u32[]{:S(2)}) copy-start(bf16[1,1024,1024]{2,1,0:T(8,128)(2,1)} %param.14) | copy-start | bytes 6291460
  44.6 16.8 %collective-permute-start.3 = (bf16[256,1024]{1,0:T(8,128)(2,1)}, bf16[256,1024]{1,0:T(8,128)(2,1)}, u32[]{:S(2)}, u32[]{:S(2)}) collective-permute-start(bf16[256,1024]{1,0:T(8,128)(2,1)} %get-tuple-element.68), channel_id=1, source_target_pairs={{0,1},{1,2},{2,3},{3,0},{4,5},{5,6},{6,7},{7,4},{8,9},{9,10},{10,1... | collective-permute-start | bytes 1572872 | tf_op jit(solution)/shard_map/ppermute | solution.py:286
  46.1 34.7 %collective-permute-start.7 = (bf16[256,1024]{1,0:T(8,128)(2,1)}, bf16[256,1024]{1,0:T(8,128)(2,1)}, u32[]{:S(2)}, u32[]{:S(2)}) collective-permute-start(bf16[256,1024]{1,0:T(8,128)(2,1)} %get-tuple-element.68), channel_id=1, source_target_pairs={{0,3},{1,0},{2,1},{3,2},{4,7},{5,4},{6,5},{7,6},{8,11},{9,8},{10,9... | collective-permute-start | bytes 1572872 | tf_op jit(solution)/shard_map/ppermute | solution.py:286
  47.9 23.4 %collective-permute-start.4 = (bf16[256,1024]{1,0:T(8,128)(2,1)}, bf16[256,1024]{1,0:T(8,128)(2,1)}, u32[]{:S(2)}, u32[]{:S(2)}) collective-permute-start(bf16[256,1024]{1,0:T(8,128)(2,1)} %get-tuple-element.67), channel_id=1, source_target_pairs={{0,3},{1,0},{2,1},{3,2},{4,7},{5,4},{6,5},{7,6},{8,11},{9,8},{10,9... | collective-permute-start | bytes 1572872 | tf_op jit(solution)/shard_map/ppermute | solution.py:286
  49.4 31.7 %collective-permute-start.8 = (bf16[256,1024]{1,0:T(8,128)(2,1)}, bf16[256,1024]{1,0:T(8,128)(2,1)}, u32[]{:S(2)}, u32[]{:S(2)}) collective-permute-start(bf16[256,1024]{1,0:T(8,128)(2,1)} %get-tuple-element.67), channel_id=1, source_target_pairs={{0,1},{1,2},{2,3},{3,0},{4,5},{5,6},{6,7},{7,4},{8,9},{9,10},{10,1... | collective-permute-start | bytes 1572872 | tf_op jit(solution)/shard_map/ppermute | solution.py:286
  49.9 73.1 %all-to-all-start.2 = ((bf16[32,16,1024]{2,1,0:T(8,128)(2,1)}), bf16[32,16,1024]{2,1,0:T(8,128)(2,1)}, u32[]{:S(2)}, u32[]{:S(2)}) async-start(bf16[32,16,1024]{2,1,0:T(8,128)(2,1)} %get-tuple-element.56), calls=%async_computation.2 | async-start | bytes 2097152 | tf_op jit(solution)/shard_map/all_to_all | solution.py:275
  56.4 1.6 copy-start.6
  71.2 16.2 %collective-permute-start.5 = (bf16[256,1024]{1,0:T(8,128)(2,1)}, bf16[256,1024]{1,0:T(8,128)(2,1)S(1)}, u32[]{:S(2)}, u32[]{:S(2)}) collective-permute-start(bf16[256,1024]{1,0:T(8,128)(2,1)} %collective-permute-done.3.refs_0_), channel_id=1, source_target_pairs={{0,1},{1,2},{2,3},{3,0},{4,5},{5,6},{6,7},{7,4},{8,9},{9,10},{10,1... | collective-permute-start | bytes 1572872 | tf_op jit(solution)/shard_map/ppermute | solution.py:286
  72.7 15.0 %collective-permute-start.6 = (bf16[256,1024]{1,0:T(8,128)(2,1)}, bf16[256,1024]{1,0:T(8,128)(2,1)S(1)}, u32[]{:S(2)}, u32[]{:S(2)}) collective-permute-start(bf16[256,1024]{1,0:T(8,128)(2,1)} %collective-permute-done.4.refs_1_), channel_id=1, source_target_pairs={{0,3},{1,0},{2,1},{3,2},{4,7},{5,4},{6,5},{7,6},{8,11},{9,8},{10,9... | collective-permute-start | bytes 1572872 | tf_op jit(solution)/shard_map/ppermute | solution.py:286
  79.0 20.0 %collective-permute-start.11 = (bf16[256,1024]{1,0:T(8,128)(2,1)S(1)}, bf16[256,1024]{1,0:T(8,128)(2,1)S(1)}, u32[]{:S(2)}, u32[]{:S(2)}) collective-permute-start(bf16[256,1024]{1,0:T(8,128)(2,1)S(1)} %get-tuple-element.40), channel_id=1, source_target_pairs={{0,3},{1,0},{2,1},{3,2},{4,7},{5,4},{6,5},{7,6},{8,11},{9,8},{10,9... | collective-permute-start | bytes 1572872 | tf_op jit(solution)/shard_map/ppermute | solution.py:286
  80.8 18.1 %collective-permute-start.12 = (bf16[256,1024]{1,0:T(8,128)(2,1)S(1)}, bf16[256,1024]{1,0:T(8,128)(2,1)S(1)}, u32[]{:S(2)}, u32[]{:S(2)}) collective-permute-start(bf16[256,1024]{1,0:T(8,128)(2,1)S(1)} %get-tuple-element.41), channel_id=1, source_target_pairs={{0,1},{1,2},{2,3},{3,0},{4,5},{5,6},{6,7},{7,4},{8,9},{9,10},{10,1... | collective-permute-start | bytes 1572872 | tf_op jit(solution)/shard_map/ppermute | solution.py:286
  91.1 16.7 %collective-permute-start.9 = (bf16[256,1024]{1,0:T(8,128)(2,1)S(1)}, bf16[256,1024]{1,0:T(8,128)(2,1)S(1)}, u32[]{:S(2)}, u32[]{:S(2)}) collective-permute-start(bf16[256,1024]{1,0:T(8,128)(2,1)S(1)} %get-tuple-element.48), channel_id=1, source_target_pairs={{0,1},{1,2},{2,3},{3,0},{4,5},{5,6},{6,7},{7,4},{8,9},{9,10},{10,1... | collective-permute-start | bytes 1572872 | tf_op jit(solution)/shard_map/ppermute | solution.py:286
  92.4 15.4 %collective-permute-start.10 = (bf16[256,1024]{1,0:T(8,128)(2,1)S(1)}, bf16[256,1024]{1,0:T(8,128)(2,1)S(1)}, u32[]{:S(2)}, u32[]{:S(2)}) collective-permute-start(bf16[256,1024]{1,0:T(8,128)(2,1)S(1)} %get-tuple-element.49), channel_id=1, source_target_pairs={{0,3},{1,0},{2,1},{3,2},{4,7},{5,4},{6,5},{7,6},{8,11},{9,8},{10,9... | collective-permute-start | bytes 1572872 | tf_op jit(solution)/shard_map/ppermute | solution.py:286
  108.0 13.1 %collective-permute-start.13 = (bf16[256,1024]{1,0:T(8,128)(2,1)S(1)}, bf16[256,1024]{1,0:T(8,128)(2,1)S(1)}, u32[]{:S(2)}, u32[]{:S(2)}) collective-permute-start(bf16[256,1024]{1,0:T(8,128)(2,1)S(1)} %add_convert_fusion.1), channel_id=1, source_target_pairs={{0,1},{1,2},{2,3},{3,0},{4,5},{5,6},{6,7},{7,4},{8,9},{9,10},{10,1... | collective-permute-start | bytes 1572872 | tf_op jit(solution)/shard_map/ppermute | solution.py:286
  109.5 11.7 %collective-permute-start.14 = (bf16[256,1024]{1,0:T(8,128)(2,1)S(1)}, bf16[256,1024]{1,0:T(8,128)(2,1)S(1)}, u32[]{:S(2)}, u32[]{:S(2)}) collective-permute-start(bf16[256,1024]{1,0:T(8,128)(2,1)S(1)} %add_convert_fusion), channel_id=1, source_target_pairs={{0,3},{1,0},{2,1},{3,2},{4,7},{5,4},{6,5},{7,6},{8,11},{9,8},{10,9... | collective-permute-start | bytes 1572872 | tf_op jit(solution)/shard_map/ppermute | solution.py:286
  123.0 36.7 %all-to-all-start.1 = ((bf16[64,8,1024]{2,1,0:T(8,128)(2,1)}), bf16[64,8,1024]{2,1,0:T(8,128)(2,1)S(1)}, u32[]{:S(2)}, u32[]{:S(2)}) async-start(bf16[64,8,1024]{2,1,0:T(8,128)(2,1)} %bitcast.7), calls=%async_computation.1 | async-start | bytes 2097152 | tf_op jit(solution)/shard_map/all_to_all | solution.py:352
  131.7 3.0 %collective-permute-start.15 = (bf16[512,1024]{1,0:T(8,128)(2,1)}, bf16[512,1024]{1,0:T(8,128)(2,1)S(1)}, u32[]{:S(2)}, u32[]{:S(2)}) collective-permute-start(bf16[512,1024]{1,0:T(8,128)(2,1)} %bitcast.8), channel_id=1, source_target_pairs={{0,4},{4,0},{8,12},{12,8},{16,20},{20,16},{24,28},{28,24},{32,36},... | collective-permute-start | bytes 3145736 | tf_op jit(solution)/shard_map/ppermute | solution.py:268
  132.0 27.7 %copy-start = (bf16[128,1024]{1,0:T(8,128)(2,1)S(1)}, bf16[128,1024]{1,0:T(8,128)(2,1)}, u32[]{:S(2)}) copy-start(bf16[128,1024]{1,0:T(8,128)(2,1)} %tokens_ref.3) | copy-start | bytes 786436
  132.0 27.7 %copy-start.1 = (f32[1024]{0:T(1024)S(1)}, f32[1024]{0:T(1024)}, u32[]{:S(2)}) copy-start(f32[1024]{0:T(1024)} %param.13) | copy-start | bytes 12292
  132.0 27.7 %copy-start.2 = (f32[128,2]{0,1:T(2,128)S(1)}, f32[128,2]{0,1:T(2,128)}, u32[]{:S(2)}) copy-start(f32[128,2]{0,1:T(2,128)} %param.10) | copy-start | bytes 3076
  132.0 27.6 %copy-start.3 = (s32[2,128]{1,0:T(2,128)S(1)}, s32[2,128]{1,0:T(2,128)}, u32[]{:S(2)}) copy-start(s32[2,128]{1,0:T(2,128)} %get-tuple-element.58.place_ref) | copy-start | bytes 3076
  132.0 27.6 %copy-start.4 = (s32[1,4]{1,0:T(1,128)S(1)}, s32[1,4]{1,0:T(1,128)}, u32[]{:S(2)}) copy-start(s32[1,4]{1,0:T(1,128)} %lengths_ref.1) | copy-start | bytes 52
  162.1 18.8 %all-to-all-start.3 = ((bf16[32,4,1024]{2,1,0:T(4,128)(2,1)}), bf16[32,4,1024]{2,1,0:T(4,128)(2,1)S(1)}, u32[]{:S(2)}, u32[]{:S(2)}) async-start(bf16[32,4,1024]{2,1,0:T(4,128)(2,1)} %get-tuple-element.60), calls=%async_computation.3 | async-start | bytes 524288 | tf_op jit(solution)/shard_map/all_to_all | solution.py:275
  181.0 1.6 collective-permute-start.16
  183.1 6.2 %collective-permute-start.19 = (f32[4,1024]{1,0:T(4,128)S(1)}, f32[4,1024]{1,0:T(4,128)S(1)}, u32[]{:S(2)}, u32[]{:S(2)}) collective-permute-start(f32[4,1024]{1,0:T(4,128)S(1)} %get-tuple-element.70), channel_id=1, source_target_pairs={{0,1},{1,2},{2,3},{3,0},{4,5},{5,6},{6,7},{7,4},{8,9},{9,10},{10,1... | collective-permute-start | bytes 49160 | tf_op jit(solution)/shard_map/ppermute | solution.py:286
  184.6 5.2 %collective-permute-start.18 = (f32[4,1024]{1,0:T(4,128)S(1)}, f32[4,1024]{1,0:T(4,128)S(1)}, u32[]{:S(2)}, u32[]{:S(2)}) collective-permute-start(f32[4,1024]{1,0:T(4,128)S(1)} %get-tuple-element.71), channel_id=1, source_target_pairs={{0,2},{1,3},{2,0},{3,1},{4,6},{5,7},{6,4},{7,5},{8,10},{9,11},{10,... | collective-permute-start | bytes 49160 | tf_op jit(solution)/shard_map/ppermute | solution.py:286
  187.9 3.7 %collective-permute-start.17 = (f32[4,1024]{1,0:T(4,128)S(1)}, f32[4,1024]{1,0:T(4,128)S(1)}, u32[]{:S(2)}, u32[]{:S(2)}) collective-permute-start(f32[4,1024]{1,0:T(4,128)S(1)} %get-tuple-element.69), channel_id=1, source_target_pairs={{0,3},{1,0},{2,1},{3,2},{4,7},{5,4},{6,5},{7,6},{8,11},{9,8},{10,9... | collective-permute-start | bytes 49160 | tf_op jit(solution)/shard_map/ppermute | solution.py:286

commit v8 on v7

--- a/solution.py
+++ b/solution.py
@@ -64,7 +64,7 @@
         ],
         out_shape=[jax.ShapeDtypeStruct(block.shape, BF16) for block in blocks],
         scratch_shapes=[pltpu.VMEM((count, units), BF16)],
-        compiler_params=pltpu.CompilerParams(vmem_limit_bytes=12 * 2**20),
+        compiler_params=pltpu.CompilerParams(vmem_limit_bytes=56 * 2**20),
         cost_estimate=pl.CostEstimate(
             flops=12 * count * width * units,
             bytes_accessed=4 * width * units + 4 * count * width,
@@ -100,7 +100,7 @@
         in_specs=[pl.BlockSpec(block, lambda i: (i, 0)), top, top, bottom, bottom],
         out_specs=pl.BlockSpec(block, lambda i: (i, 0)),
         out_shape=jax.ShapeDtypeStruct(own.shape, BF16),
-        compiler_params=pltpu.CompilerParams(vmem_limit_bytes=12 * 2**20),
+        compiler_params=pltpu.CompilerParams(vmem_limit_bytes=16 * 2**20),
     )(own, home_top, last_top, home_bottom, last_bottom)
 
 
@@ -213,7 +213,7 @@
             jax.ShapeDtypeStruct((captions, width), F32),
             jax.ShapeDtypeStruct((copies, captions, width), BF16),
         ],
-        compiler_params=pltpu.CompilerParams(vmem_limit_bytes=12 * 2**20),
+        compiler_params=pltpu.CompilerParams(vmem_limit_bytes=24 * 2**20),
     )(lengths, returned, tokens, place, gates, gain.reshape(1, width))
 
 

time: 193 us -> 192 us (level)
  Pallas kernels: 24.4 us -> 33.9 us
  waiting for transfers between devices: 96.1 us -> 87.7 us
    pallas_call x4, Pallas kernels: 15.8 us -> 25.2 us  [expert_part(): pl.pallas_call(expert_kernel, grid=(2 * half,), in_specs=[pl.BlockSpec(bl...]
    ppermute x18, waiting for transfers between devices: 39.3 us -> 30.9 us  [ring_shift(): lax.ppermute(values, 'grid', [(i, (i + step) % size) for i in range(size)])]
  transfers between devices with their start and end apart: 24 -> 24, of which waited for: 15 -> 12; matrix products, arithmetic and copies ran while one was open for 2% -> 2% of each run, Pallas kernels for 10% -> 15%
where the time goes in v8:
time: 192 us
  waiting for transfers between devices  87.7 us (46%)
  starting transfers between devices  62.4 us (32%)
  Pallas kernels  33.9 us (18%)
  other arithmetic  3.35 us (2%)
  matrix products  2.21 us (1%)
    ppermute x18, waiting for transfers between devices, ring_shift(): lax.ppermute(values, 'grid', [(i, (i + step) % size) for i in range(size)])  30.9 us
    ppermute x18, starting transfers between devices, ring_shift(): lax.ppermute(values, 'grid', [(i, (i + step) % size) for i in range(size)])  28.7 us
    pallas_call x4, Pallas kernels, expert_part(): pl.pallas_call(expert_kernel, grid=(2 * half,), in_specs=[pl.BlockSpec(bl...  25.2 us
    all_to_all x1, waiting for transfers between devices, on_device(): lax.all_to_all(results, 'expert', split_axis=0, concat_axis=0, tiled=True)  23.6 us
    all_to_all x1, waiting for transfers between devices, on_device(): lax.all_to_all(send, 'expert', split_axis=0, concat_axis=0, tiled=True)  18.6 us
    all_to_all x2, starting transfers between devices, along_expert(): lax.all_to_all(copies, 'expert', split_axis=0, concat_axis=0, axis_index_...  12.9 us
    all_to_all x1, starting transfers between devices, on_device(): lax.all_to_all(send, 'expert', split_axis=0, concat_axis=0, tiled=True)  11.8 us
    all_to_all x2, waiting for transfers between devices, along_expert(): lax.all_to_all(copies, 'expert', split_axis=0, concat_axis=0, axis_index_...  11 us
  transfers between devices with their start and end apart: 24, of which 12 were waited for; matrix products, arithmetic and copies ran while one was open for 2% of the time, Pallas kernels for 15%

profile of v8, /device:TPU:32, one launch (start us, length us, event | category | flops | bytes accessed | tf_op | source)
XLA Modules:
  0.0 191.7 jit_solution(9696084633457674056)
XLA Ops:
  0.6 3.3 %shard_map.103 = (bf16[512,1024]{1,0:T(8,128)(2,1)}, s32[2,128]{1,0:T(2,128)}) custom-call(bf16[128,1024]{1,0:T(8,128)(2,1)} %tokens_ref.3, s32[2,128]{1,0:T(2,128)} %bitcast.31), custom_call_target="tpu_custom_call" | custom-call | tf_op jit(solution)/shard_map/pallas_call | solution.py:140
  4.0 11.8 %all-to-all-start = ((bf16[64,8,1024]{2,1,0:T(8,128)(2,1)}), bf16[64,8,1024]{2,1,0:T(8,128)(2,1)S(1)}, u32[]{:S(2)}, u32[]{:S(2)}) async-start(bf16[64,8,1024]{2,1,0:T(8,128)(2,1)} %bitcast.30), calls=%async_computation | async-start | bytes 2097152 | tf_op jit(solution)/shard_map/all_to_all | solution.py:311
  15.8 0.1 fusion.13
  15.9 0.1 fusion.15.refs_0_
  16.0 1.5 collective-permute-start
  17.5 2.7 %collective-permute-start.1 = (bf16[4,1024]{1,0:T(4,128)(2,1)S(1)}, bf16[4,1024]{1,0:T(4,128)(2,1)S(1)}, u32[]{:S(2)}, u32[]{:S(2)}) collective-permute-start(bf16[4,1024]{1,0:T(4,128)(2,1)S(1)} %fusion.15.refs_0_), channel_id=1, source_target_pairs={{0,2},{1,3},{2,0},{3,1},{4,6},{5,7},{6,4},{7,5},{8,10},{9,11},{10,... | collective-permute-start | bytes 24584 | tf_op jit(solution)/shard_map/ppermute | solution.py:286
  20.2 1.4 collective-permute-start.2
  21.6 0.0 collective-permute-done.refs_1_
  21.6 1.0 collective-permute-done.1.refs_2_
  22.6 1.2 collective-permute-done.2.refs_3_
  23.9 1.1 shard_map.104
  25.0 18.6 %all-to-all-done = bf16[64,8,1024]{2,1,0:T(8,128)(2,1)S(1)} async-done(((bf16[64,8,1024]{2,1,0:T(8,128)(2,1)}), bf16[64,8,1024]{2,1,0:T(8,128)(2,1)S(1)}, u32[]{:S(2)}, u32[]{:S(2)}) %all-to-all-start) | async-done | bytes 1048608 | tf_op jit(solution)/shard_map/all_to_all | solution.py:311
  43.6 0.1 slice_bitcast_fusion
  43.7 1.6 collective-permute-start.3
  45.3 1.7 collective-permute-start.7
  47.0 1.5 collective-permute-start.4
  48.5 0.5 collective-permute-start.8
  49.0 6.5 %all-to-all-start.2 = ((bf16[32,16,1024]{2,1,0:T(8,128)(2,1)}), bf16[32,16,1024]{2,1,0:T(8,128)(2,1)S(1)}, u32[]{:S(2)}, u32[]{:S(2)}) async-start(bf16[32,16,1024]{2,1,0:T(8,128)(2,1)} %get-tuple-element.56), calls=%async_computation.2 | async-start | bytes 2097152 | tf_op jit(solution)/shard_map/all_to_all | solution.py:275
  55.5 6.3 %shard_map.105.own_ref = bf16[512,1024]{1,0:T(8,128)(2,1)} custom-call(bf16[512,1024]{1,0:T(8,128)(2,1)} %bitcast.27, bf16[1024,1024]{1,0:T(8,128)(2,1)} %bitcast.32, bf16[1024,1024]{1,0:T(8,128)(2,1)} %bitcast.36), custom_call_target="tpu_custom_call" | custom-call | flops 6442450944 | bytes 6291456 | tf_op jit(solution)/shard_map/pallas_call | solution.py:53
  61.8 8.4 %collective-permute-done.4.refs_1_ = bf16[256,1024]{1,0:T(8,128)(2,1)} collective-permute-done((bf16[256,1024]{1,0:T(8,128)(2,1)S(1)}, bf16[256,1024]{1,0:T(8,128)(2,1)}, u32[]{:S(2)}, u32[]{:S(2)}) %collective-permute-start.4) | collective-permute-done | bytes 524320 | tf_op jit(solution)/shard_map/ppermute | solution.py:286
  70.2 1.5 collective-permute-start.5
  71.6 1.7 collective-permute-start.6
  73.4 6.3 %shard_map.106 = (bf16[256,1024]{1,0:T(8,128)(2,1)}, bf16[256,1024]{1,0:T(8,128)(2,1)}) custom-call(bf16[256,1024]{1,0:T(8,128)(2,1)} %collective-permute-done.3.refs_0_, bf16[256,1024]{1,0:T(8,128)(2,1)} %collective-permute-done.4.refs_1_, bf16[1024,1024]{1,0:T(8,128)(2,1)} %bitcast.33, bf16[1024,1024]{1,0:T(8,128)(2,1)} %bitcast.37), custom_call_target="tpu_custom_call" | custom-call | flops 6442450944 | bytes 6291456 | tf_op jit(solution)/shard_map/pallas_call | solution.py:53
  79.7 1.7 collective-permute-start.11
  81.4 0.3 collective-permute-start.12
  81.7 6.2 %shard_map.107 = (bf16[256,1024]{1,0:T(8,128)(2,1)}, bf16[256,1024]{1,0:T(8,128)(2,1)}) custom-call(bf16[256,1024]{1,0:T(8,128)(2,1)} %collective-permute-done.7.refs_0_, bf16[256,1024]{1,0:T(8,128)(2,1)} %collective-permute-done.8.refs_1_, bf16[1024,1024]{1,0:T(8,128)(2,1)} %bitcast.34, bf16[1024,1024]{1,0:T(8,128)(2,1)} %bitcast.38), custom_call_target="tpu_custom_call" | custom-call | flops 6442450944 | bytes 6291456 | tf_op jit(solution)/shard_map/pallas_call | solution.py:53
  88.0 0.8 copy-done.11
  88.8 0.1 copy-done.12
  88.9 6.4 %shard_map.108 = (bf16[256,1024]{1,0:T(8,128)(2,1)}, bf16[256,1024]{1,0:T(8,128)(2,1)}) custom-call(bf16[256,1024]{1,0:T(8,128)(2,1)} %copy-done.11, bf16[256,1024]{1,0:T(8,128)(2,1)} %copy-done.12, bf16[1024,1024]{1,0:T(8,128)(2,1)} %bitcast.35, bf16[1024,1024]{1,0:T(8,128)(2,1)} %bitcast.39), custom_call_target="tpu_custom_call" | custom-call | flops 6442450944 | bytes 6291456 | tf_op jit(solution)/shard_map/pallas_call | solution.py:53
  95.3 0.3 collective-permute-start.9
  95.6 3.0 %collective-permute-start.10 = (bf16[256,1024]{1,0:T(8,128)(2,1)}, bf16[256,1024]{1,0:T(8,128)(2,1)S(1)}, u32[]{:S(2)}, u32[]{:S(2)}) collective-permute-start(bf16[256,1024]{1,0:T(8,128)(2,1)} %get-tuple-element.49), channel_id=1, source_target_pairs={{0,3},{1,0},{2,1},{3,2},{4,7},{5,4},{6,5},{7,6},{8,11},{9,8},{10,9... | collective-permute-start | bytes 1572872 | tf_op jit(solution)/shard_map/ppermute | solution.py:286
  98.6 9.8 %collective-permute-done.9 = bf16[256,1024]{1,0:T(8,128)(2,1)S(1)} collective-permute-done((bf16[256,1024]{1,0:T(8,128)(2,1)}, bf16[256,1024]{1,0:T(8,128)(2,1)S(1)}, u32[]{:S(2)}, u32[]{:S(2)}) %collective-permute-start.9) | collective-permute-done | bytes 524320 | tf_op jit(solution)/shard_map/ppermute | solution.py:286
  108.3 0.2 add_convert_fusion.1
  108.5 1.2 collective-permute-start.13
  109.7 0.2 add_convert_fusion
  109.9 2.2 %collective-permute-start.14 = (bf16[256,1024]{1,0:T(8,128)(2,1)S(1)}, bf16[256,1024]{1,0:T(8,128)(2,1)S(1)}, u32[]{:S(2)}, u32[]{:S(2)}) collective-permute-start(bf16[256,1024]{1,0:T(8,128)(2,1)S(1)} %add_convert_fusion), channel_id=1, source_target_pairs={{0,3},{1,0},{2,1},{3,2},{4,7},{5,4},{6,5},{7,6},{8,11},{9,8},{10,9... | collective-permute-start | bytes 1572872 | tf_op jit(solution)/shard_map/ppermute | solution.py:286
  112.1 8.4 %collective-permute-done.13.last_top = bf16[256,1024]{1,0:T(8,128)(2,1)S(1)} collective-permute-done((bf16[256,1024]{1,0:T(8,128)(2,1)S(1)}, bf16[256,1024]{1,0:T(8,128)(2,1)S(1)}, u32[]{:S(2)}, u32[]{:S(2)}) %collective-permute-start.13) | collective-permute-done | bytes 524320 | tf_op jit(solution)/shard_map/ppermute | solution.py:286
  120.6 1.8 shard_map.109
  122.4 8.8 %all-to-all-start.1 = ((bf16[64,8,1024]{2,1,0:T(8,128)(2,1)}), bf16[64,8,1024]{2,1,0:T(8,128)(2,1)S(1)}, u32[]{:S(2)}, u32[]{:S(2)}) async-start(bf16[64,8,1024]{2,1,0:T(8,128)(2,1)} %bitcast.7), calls=%async_computation.1 | async-start | bytes 2097152 | tf_op jit(solution)/shard_map/all_to_all | solution.py:352
  131.2 0.2 collective-permute-start.15
  131.4 0.0 copy-start.2
  131.4 0.0 copy-start.3
  131.4 0.0 copy-start.4
  131.4 0.0 copy-start.5
  131.4 2.5 %collective-permute-done.15 = bf16[512,1024]{1,0:T(8,128)(2,1)S(1)} collective-permute-done((bf16[512,1024]{1,0:T(8,128)(2,1)S(1)}, bf16[512,1024]{1,0:T(8,128)(2,1)S(1)}, u32[]{:S(2)}, u32[]{:S(2)}) %collective-permute-start.15) | collective-permute-done | bytes 1048608 | tf_op jit(solution)/shard_map/ppermute | solution.py:268
  133.9 1.5 pad_maximum_fusion
  135.4 23.6 %all-to-all-done.1 = bf16[64,8,1024]{2,1,0:T(8,128)(2,1)S(1)} async-done(((bf16[64,8,1024]{2,1,0:T(8,128)(2,1)}), bf16[64,8,1024]{2,1,0:T(8,128)(2,1)S(1)}, u32[]{:S(2)}, u32[]{:S(2)}) %all-to-all-start.1) | async-done | bytes 1048608 | tf_op jit(solution)/shard_map/all_to_all | solution.py:352
  159.1 2.4 %shard_map.110 = (f32[4,1024]{1,0:T(4,128)}, bf16[32,4,1024]{2,1,0:T(4,128)(2,1)}) custom-call(s32[1,4]{1,0:T(1,128)S(1)} %copy-done.5, bf16[512,1024]{1,0:T(8,128)(2,1)S(1)} %bitcast.24, bf16[128,1024]{1,0:T(8,128)(2,1)S(1)} %copy-done, s32[2,128]{1,0:T(2,128)S(1)} %copy-done.4, f32[2,128]{1,0:T(2,128)S(1)} %bitcast.26, f32[1,1024]{1,0:T(1,128)S(1)} %bitcast.25), custom_call_target="tpu_custom_call" | custom-call | tf_op jit(solution)/shard_map/pallas_call | solution.py:208
  161.5 6.5 %all-to-all-start.3 = ((bf16[32,4,1024]{2,1,0:T(4,128)(2,1)}), bf16[32,4,1024]{2,1,0:T(4,128)(2,1)S(1)}, u32[]{:S(2)}, u32[]{:S(2)}) async-start(bf16[32,4,1024]{2,1,0:T(4,128)(2,1)} %get-tuple-element.60), calls=%async_computation.3 | async-start | bytes 524288 | tf_op jit(solution)/shard_map/all_to_all | solution.py:275
  168.0 1.4 subtract_convert_fusion.1
  169.4 10.9 %all-to-all-done.3 = bf16[32,4,1024]{2,1,0:T(4,128)(2,1)S(1)} async-done(((bf16[32,4,1024]{2,1,0:T(4,128)(2,1)}), bf16[32,4,1024]{2,1,0:T(4,128)(2,1)S(1)}, u32[]{:S(2)}, u32[]{:S(2)}) %all-to-all-start.3) | async-done | bytes 262176 | tf_op jit(solution)/shard_map/all_to_all | solution.py:275
  180.3 0.1 reshape.52
  180.4 0.1 collective-permute-start.16
  180.5 0.4 fusion.19
  180.9 1.1 collective-permute-done.16
  182.1 0.3 subtract_convert_fusion
  182.3 0.2 fusion.23
  182.6 1.4 collective-permute-start.19
  184.0 3.3 %collective-permute-start.18 = (f32[4,1024]{1,0:T(4,128)S(1)}, f32[4,1024]{1,0:T(4,128)S(1)}, u32[]{:S(2)}, u32[]{:S(2)}) collective-permute-start(f32[4,1024]{1,0:T(4,128)S(1)} %get-tuple-element.71), channel_id=1, source_target_pairs={{0,2},{1,3},{2,0},{3,1},{4,6},{5,7},{6,4},{7,5},{8,10},{9,11},{10,... | collective-permute-start | bytes 49160 | tf_op jit(solution)/shard_map/ppermute | solution.py:286
  187.3 1.0 collective-permute-start.17
  188.3 0.6 fusion.18
  189.0 0.3 collective-permute-done.18
  189.2 1.8 collective-permute-done.17
  191.1 0.6 fusion.17
  (40 shorter events, 0.2 us)
Async XLA Ops:
  0.6 15.1 %copy-start.10 = (bf16[4,1024]{1,0:T(4,128)(2,1)S(1)}, bf16[4,1024]{1,0:T(4,128)(2,1)}, u32[]{:S(2)}) copy-start(bf16[4,1024]{1,0:T(4,128)(2,1)} %param.12) | copy-start | bytes 24580
  4.0 39.6 %all-to-all-start = ((bf16[64,8,1024]{2,1,0:T(8,128)(2,1)}), bf16[64,8,1024]{2,1,0:T(8,128)(2,1)S(1)}, u32[]{:S(2)}, u32[]{:S(2)}) async-start(bf16[64,8,1024]{2,1,0:T(8,128)(2,1)} %bitcast.30), calls=%async_computation | async-start | bytes 2097152 | tf_op jit(solution)/shard_map/all_to_all | solution.py:311
  16.0 5.7 %collective-permute-start = (bf16[4,1024]{1,0:T(4,128)(2,1)S(1)}, bf16[4,1024]{1,0:T(4,128)(2,1)S(1)}, u32[]{:S(2)}, u32[]{:S(2)}) collective-permute-start(bf16[4,1024]{1,0:T(4,128)(2,1)S(1)} %fusion.15.refs_0_), channel_id=1, source_target_pairs={{0,1},{1,2},{2,3},{3,0},{4,5},{5,6},{6,7},{7,4},{8,9},{9,10},{10,1... | collective-permute-start | bytes 24584 | tf_op jit(solution)/shard_map/ppermute | solution.py:286
  17.5 5.2 %collective-permute-start.1 = (bf16[4,1024]{1,0:T(4,128)(2,1)S(1)}, bf16[4,1024]{1,0:T(4,128)(2,1)S(1)}, u32[]{:S(2)}, u32[]{:S(2)}) collective-permute-start(bf16[4,1024]{1,0:T(4,128)(2,1)S(1)} %fusion.15.refs_0_), channel_id=1, source_target_pairs={{0,2},{1,3},{2,0},{3,1},{4,6},{5,7},{6,4},{7,5},{8,10},{9,11},{10,... | collective-permute-start | bytes 24584 | tf_op jit(solution)/shard_map/ppermute | solution.py:286
  20.2 3.7 %collective-permute-start.2 = (bf16[4,1024]{1,0:T(4,128)(2,1)S(1)}, bf16[4,1024]{1,0:T(4,128)(2,1)S(1)}, u32[]{:S(2)}, u32[]{:S(2)}) collective-permute-start(bf16[4,1024]{1,0:T(4,128)(2,1)S(1)} %fusion.15.refs_0_), channel_id=1, source_target_pairs={{0,3},{1,0},{2,1},{3,2},{4,7},{5,4},{6,5},{7,6},{8,11},{9,8},{10,9... | collective-permute-start | bytes 24584 | tf_op jit(solution)/shard_map/ppermute | solution.py:286
  43.6 5.4 %copy-start.6 = (bf16[64,8,1024]{2,1,0:T(8,128)(2,1)}, bf16[64,8,1024]{2,1,0:T(8,128)(2,1)S(1)}, u32[]{:S(2)}) copy-start(bf16[64,8,1024]{2,1,0:T(8,128)(2,1)S(1)} %all-to-all-done) | copy-start | bytes 3145732
  43.7 18.1 %collective-permute-start.3 = (bf16[256,1024]{1,0:T(8,128)(2,1)S(1)}, bf16[256,1024]{1,0:T(8,128)(2,1)}, u32[]{:S(2)}, u32[]{:S(2)}) collective-permute-start(bf16[256,1024]{1,0:T(8,128)(2,1)S(1)} %get-tuple-element.68), channel_id=1, source_target_pairs={{0,1},{1,2},{2,3},{3,0},{4,5},{5,6},{6,7},{7,4},{8,9},{9,10},{10,1... | collective-permute-start | bytes 1572872 | tf_op jit(solution)/shard_map/ppermute | solution.py:286
  45.3 36.2 %collective-permute-start.7 = (bf16[256,1024]{1,0:T(8,128)(2,1)S(1)}, bf16[256,1024]{1,0:T(8,128)(2,1)}, u32[]{:S(2)}, u32[]{:S(2)}) collective-permute-start(bf16[256,1024]{1,0:T(8,128)(2,1)S(1)} %get-tuple-element.68), channel_id=1, source_target_pairs={{0,3},{1,0},{2,1},{3,2},{4,7},{5,4},{6,5},{7,6},{8,11},{9,8},{10,9... | collective-permute-start | bytes 1572872 | tf_op jit(solution)/shard_map/ppermute | solution.py:286
  47.0 23.2 %collective-permute-start.4 = (bf16[256,1024]{1,0:T(8,128)(2,1)S(1)}, bf16[256,1024]{1,0:T(8,128)(2,1)}, u32[]{:S(2)}, u32[]{:S(2)}) collective-permute-start(bf16[256,1024]{1,0:T(8,128)(2,1)S(1)} %get-tuple-element.67), channel_id=1, source_target_pairs={{0,3},{1,0},{2,1},{3,2},{4,7},{5,4},{6,5},{7,6},{8,11},{9,8},{10,9... | collective-permute-start | bytes 1572872 | tf_op jit(solution)/shard_map/ppermute | solution.py:286
  48.5 33.2 %collective-permute-start.8 = (bf16[256,1024]{1,0:T(8,128)(2,1)S(1)}, bf16[256,1024]{1,0:T(8,128)(2,1)}, u32[]{:S(2)}, u32[]{:S(2)}) collective-permute-start(bf16[256,1024]{1,0:T(8,128)(2,1)S(1)} %get-tuple-element.67), channel_id=1, source_target_pairs={{0,1},{1,2},{2,3},{3,0},{4,5},{5,6},{6,7},{7,4},{8,9},{9,10},{10,1... | collective-permute-start | bytes 1572872 | tf_op jit(solution)/shard_map/ppermute | solution.py:286
  49.0 73.3 %all-to-all-start.2 = ((bf16[32,16,1024]{2,1,0:T(8,128)(2,1)}), bf16[32,16,1024]{2,1,0:T(8,128)(2,1)S(1)}, u32[]{:S(2)}, u32[]{:S(2)}) async-start(bf16[32,16,1024]{2,1,0:T(8,128)(2,1)} %get-tuple-element.56), calls=%async_computation.2 | async-start | bytes 2097152 | tf_op jit(solution)/shard_map/all_to_all | solution.py:275
  70.2 17.8 %collective-permute-start.5 = (bf16[256,1024]{1,0:T(8,128)(2,1)}, bf16[256,1024]{1,0:T(8,128)(2,1)S(1)}, u32[]{:S(2)}, u32[]{:S(2)}) collective-permute-start(bf16[256,1024]{1,0:T(8,128)(2,1)} %collective-permute-done.3.refs_0_), channel_id=1, source_target_pairs={{0,1},{1,2},{2,3},{3,0},{4,5},{5,6},{6,7},{7,4},{8,9},{9,10},{10,1... | collective-permute-start | bytes 1572872 | tf_op jit(solution)/shard_map/ppermute | solution.py:286
  71.6 16.3 %collective-permute-start.6 = (bf16[256,1024]{1,0:T(8,128)(2,1)}, bf16[256,1024]{1,0:T(8,128)(2,1)S(1)}, u32[]{:S(2)}, u32[]{:S(2)}) collective-permute-start(bf16[256,1024]{1,0:T(8,128)(2,1)} %collective-permute-done.4.refs_1_), channel_id=1, source_target_pairs={{0,3},{1,0},{2,1},{3,2},{4,7},{5,4},{6,5},{7,6},{8,11},{9,8},{10,9... | collective-permute-start | bytes 1572872 | tf_op jit(solution)/shard_map/ppermute | solution.py:286
  79.7 18.9 %collective-permute-start.11 = (bf16[256,1024]{1,0:T(8,128)(2,1)}, bf16[256,1024]{1,0:T(8,128)(2,1)S(1)}, u32[]{:S(2)}, u32[]{:S(2)}) collective-permute-start(bf16[256,1024]{1,0:T(8,128)(2,1)} %get-tuple-element.40), channel_id=1, source_target_pairs={{0,3},{1,0},{2,1},{3,2},{4,7},{5,4},{6,5},{7,6},{8,11},{9,8},{10,9... | collective-permute-start | bytes 1572872 | tf_op jit(solution)/shard_map/ppermute | solution.py:286
  81.4 17.2 %collective-permute-start.12 = (bf16[256,1024]{1,0:T(8,128)(2,1)}, bf16[256,1024]{1,0:T(8,128)(2,1)S(1)}, u32[]{:S(2)}, u32[]{:S(2)}) collective-permute-start(bf16[256,1024]{1,0:T(8,128)(2,1)} %get-tuple-element.41), channel_id=1, source_target_pairs={{0,1},{1,2},{2,3},{3,0},{4,5},{5,6},{6,7},{7,4},{8,9},{9,10},{10,1... | collective-permute-start | bytes 1572872 | tf_op jit(solution)/shard_map/ppermute | solution.py:286
  88.0 0.8 copy-start.11
  88.0 1.0 copy-start.12
  88.9 19.4 %copy-start.9 = (bf16[256,1024]{1,0:T(8,128)(2,1)S(1)}, bf16[256,1024]{1,0:T(8,128)(2,1)}, u32[]{:S(2)}) copy-start(bf16[256,1024]{1,0:T(8,128)(2,1)} %get-tuple-element.51) | copy-start | bytes 1572868
  88.9 20.8 %copy-start.8 = (bf16[256,1024]{1,0:T(8,128)(2,1)S(1)}, bf16[256,1024]{1,0:T(8,128)(2,1)}, u32[]{:S(2)}) copy-start(bf16[256,1024]{1,0:T(8,128)(2,1)} %get-tuple-element.54) | copy-start | bytes 1572868
  95.3 25.2 %copy-start.1 = (bf16[512,1024]{1,0:T(8,128)(2,1)S(1)}, bf16[512,1024]{1,0:T(8,128)(2,1)}, u32[]{:S(2)}) copy-start(bf16[512,1024]{1,0:T(8,128)(2,1)} %shard_map.105.own_ref) | copy-start | bytes 3145732
  95.3 13.0 %collective-permute-start.9 = (bf16[256,1024]{1,0:T(8,128)(2,1)}, bf16[256,1024]{1,0:T(8,128)(2,1)S(1)}, u32[]{:S(2)}, u32[]{:S(2)}) collective-permute-start(bf16[256,1024]{1,0:T(8,128)(2,1)} %get-tuple-element.48), channel_id=1, source_target_pairs={{0,1},{1,2},{2,3},{3,0},{4,5},{5,6},{6,7},{7,4},{8,9},{9,10},{10,1... | collective-permute-start | bytes 1572872 | tf_op jit(solution)/shard_map/ppermute | solution.py:286
  95.6 12.7 %collective-permute-start.10 = (bf16[256,1024]{1,0:T(8,128)(2,1)}, bf16[256,1024]{1,0:T(8,128)(2,1)S(1)}, u32[]{:S(2)}, u32[]{:S(2)}) collective-permute-start(bf16[256,1024]{1,0:T(8,128)(2,1)} %get-tuple-element.49), channel_id=1, source_target_pairs={{0,3},{1,0},{2,1},{3,2},{4,7},{5,4},{6,5},{7,6},{8,11},{9,8},{10,9... | collective-permute-start | bytes 1572872 | tf_op jit(solution)/shard_map/ppermute | solution.py:286
  108.5 12.0 %collective-permute-start.13 = (bf16[256,1024]{1,0:T(8,128)(2,1)S(1)}, bf16[256,1024]{1,0:T(8,128)(2,1)S(1)}, u32[]{:S(2)}, u32[]{:S(2)}) collective-permute-start(bf16[256,1024]{1,0:T(8,128)(2,1)S(1)} %add_convert_fusion.1), channel_id=1, source_target_pairs={{0,1},{1,2},{2,3},{3,0},{4,5},{5,6},{6,7},{7,4},{8,9},{9,10},{10,1... | collective-permute-start | bytes 1572872 | tf_op jit(solution)/shard_map/ppermute | solution.py:286
  109.9 10.6 %collective-permute-start.14 = (bf16[256,1024]{1,0:T(8,128)(2,1)S(1)}, bf16[256,1024]{1,0:T(8,128)(2,1)S(1)}, u32[]{:S(2)}, u32[]{:S(2)}) collective-permute-start(bf16[256,1024]{1,0:T(8,128)(2,1)S(1)} %add_convert_fusion), channel_id=1, source_target_pairs={{0,3},{1,0},{2,1},{3,2},{4,7},{5,4},{6,5},{7,6},{8,11},{9,8},{10,9... | collective-permute-start | bytes 1572872 | tf_op jit(solution)/shard_map/ppermute | solution.py:286
  122.4 9.0 %copy-start.7 = (bf16[32,16,1024]{2,1,0:T(8,128)(2,1)}, bf16[32,16,1024]{2,1,0:T(8,128)(2,1)S(1)}, u32[]{:S(2)}) copy-start(bf16[32,16,1024]{2,1,0:T(8,128)(2,1)S(1)} %all-to-all-done.2) | copy-start | bytes 3145732
  122.4 36.7 %all-to-all-start.1 = ((bf16[64,8,1024]{2,1,0:T(8,128)(2,1)}), bf16[64,8,1024]{2,1,0:T(8,128)(2,1)S(1)}, u32[]{:S(2)}, u32[]{:S(2)}) async-start(bf16[64,8,1024]{2,1,0:T(8,128)(2,1)} %bitcast.7), calls=%async_computation.1 | async-start | bytes 2097152 | tf_op jit(solution)/shard_map/all_to_all | solution.py:352
  131.2 2.7 %collective-permute-start.15 = (bf16[512,1024]{1,0:T(8,128)(2,1)S(1)}, bf16[512,1024]{1,0:T(8,128)(2,1)S(1)}, u32[]{:S(2)}, u32[]{:S(2)}) collective-permute-start(bf16[512,1024]{1,0:T(8,128)(2,1)S(1)} %bitcast.28), channel_id=1, source_target_pairs={{0,4},{4,0},{8,12},{12,8},{16,20},{20,16},{24,28},{28,24},{32,36},... | collective-permute-start | bytes 3145736 | tf_op jit(solution)/shard_map/ppermute | solution.py:268
  131.4 27.7 %copy-start = (bf16[128,1024]{1,0:T(8,128)(2,1)S(1)}, bf16[128,1024]{1,0:T(8,128)(2,1)}, u32[]{:S(2)}) copy-start(bf16[128,1024]{1,0:T(8,128)(2,1)} %tokens_ref.3) | copy-start | bytes 786436
  131.4 27.7 %copy-start.2 = (f32[1024]{0:T(1024)S(1)}, f32[1024]{0:T(1024)}, u32[]{:S(2)}) copy-start(f32[1024]{0:T(1024)} %param.13) | copy-start | bytes 12292
  131.4 27.6 %copy-start.3 = (f32[128,2]{0,1:T(2,128)S(1)}, f32[128,2]{0,1:T(2,128)}, u32[]{:S(2)}) copy-start(f32[128,2]{0,1:T(2,128)} %param.10) | copy-start | bytes 3076
  131.4 27.6 %copy-start.4 = (s32[2,128]{1,0:T(2,128)S(1)}, s32[2,128]{1,0:T(2,128)}, u32[]{:S(2)}) copy-start(s32[2,128]{1,0:T(2,128)} %get-tuple-element.58.place_ref) | copy-start | bytes 3076
  131.4 27.6 %copy-start.5 = (s32[1,4]{1,0:T(1,128)S(1)}, s32[1,4]{1,0:T(1,128)}, u32[]{:S(2)}) copy-start(s32[1,4]{1,0:T(1,128)} %lengths_ref.1) | copy-start | bytes 52
  161.5 18.8 %all-to-all-start.3 = ((bf16[32,4,1024]{2,1,0:T(4,128)(2,1)}), bf16[32,4,1024]{2,1,0:T(4,128)(2,1)S(1)}, u32[]{:S(2)}, u32[]{:S(2)}) async-start(bf16[32,4,1024]{2,1,0:T(4,128)(2,1)} %get-tuple-element.60), calls=%async_computation.3 | async-start | bytes 524288 | tf_op jit(solution)/shard_map/all_to_all | solution.py:275
  180.4 1.6 collective-permute-start.16
  182.6 6.4 %collective-permute-start.19 = (f32[4,1024]{1,0:T(4,128)S(1)}, f32[4,1024]{1,0:T(4,128)S(1)}, u32[]{:S(2)}, u32[]{:S(2)}) collective-permute-start(f32[4,1024]{1,0:T(4,128)S(1)} %get-tuple-element.70), channel_id=1, source_target_pairs={{0,1},{1,2},{2,3},{3,0},{4,5},{5,6},{6,7},{7,4},{8,9},{9,10},{10,1... | collective-permute-start | bytes 49160 | tf_op jit(solution)/shard_map/ppermute | solution.py:286
  184.0 5.2 %collective-permute-start.18 = (f32[4,1024]{1,0:T(4,128)S(1)}, f32[4,1024]{1,0:T(4,128)S(1)}, u32[]{:S(2)}, u32[]{:S(2)}) collective-permute-start(f32[4,1024]{1,0:T(4,128)S(1)} %get-tuple-element.71), channel_id=1, source_target_pairs={{0,2},{1,3},{2,0},{3,1},{4,6},{5,7},{6,4},{7,5},{8,10},{9,11},{10,... | collective-permute-start | bytes 49160 | tf_op jit(solution)/shard_map/ppermute | solution.py:286
  187.3 3.7 %collective-permute-start.17 = (f32[4,1024]{1,0:T(4,128)S(1)}, f32[4,1024]{1,0:T(4,128)S(1)}, u32[]{:S(2)}, u32[]{:S(2)}) collective-permute-start(f32[4,1024]{1,0:T(4,128)S(1)} %get-tuple-element.69), channel_id=1, source_target_pairs={{0,3},{1,0},{2,1},{3,2},{4,7},{5,4},{6,5},{7,6},{8,11},{9,8},{10,9... | collective-permute-start | bytes 49160 | tf_op jit(solution)/shard_map/ppermute | solution.py:286

commit v9 on v8

--- a/solution.py
+++ b/solution.py
@@ -90,7 +90,7 @@
 
 def sum_terms(own, home_top, last_top, home_bottom, last_bottom):
     count, width = own.shape
-    steps = 4
+    steps = 2
     block = (count // steps, width)
     top = pl.BlockSpec(block, lambda i: (jnp.minimum(i, steps // 2 - 1), 0))
     bottom = pl.BlockSpec(block, lambda i: (jnp.maximum(i - steps // 2, 0), 0))
@@ -171,9 +171,10 @@
         spots == places[:, 1:2], columns[:, 3:4], 0.0
     )
     high, low = split_pair(gates)
-    mixed = tokens_ref[...].astype(F32)
-    mixed += jnp.dot(high, returned, preferred_element_type=F32)
-    mixed += jnp.dot(low, returned, preferred_element_type=F32)
+    both = jnp.dot(
+        jnp.concatenate([high, low], axis=0), returned, preferred_element_type=F32
+    )
+    mixed = tokens_ref[...].astype(F32) + both[:count] + both[count:]
     final = layer_norm(mixed) * gain_ref[...]
     padded = 8
     caption = lax.broadcasted_iota(jnp.int32, (padded, count), 0)

time: 192 us -> 192 us (level)
  transfers between devices with their start and end apart: 24 -> 24, of which waited for: 12 -> 12; matrix products, arithmetic and copies ran while one was open for 2% -> 2% of each run, Pallas kernels for 15% -> 14%
where the time goes in v9:
time: 192 us; the launch traced here: 191 us
  waiting for transfers between devices  87.7 us (46%)
  starting transfers between devices  62.4 us (32%)
  Pallas kernels  33.4 us (17%)
  other arithmetic  3.35 us (2%)
  matrix products  2.21 us (1%)
    ppermute x18, waiting for transfers between devices, ring_shift(): lax.ppermute(values, 'grid', [(i, (i + step) % size) for i in range(size)])  30.9 us
    ppermute x18, starting transfers between devices, ring_shift(): lax.ppermute(values, 'grid', [(i, (i + step) % size) for i in range(size)])  28.7 us
    pallas_call x4, Pallas kernels, expert_part(): pl.pallas_call(expert_kernel, grid=(2 * half,), in_specs=[pl.BlockSpec(bl...  25.2 us
    all_to_all x1, waiting for transfers between devices, on_device(): lax.all_to_all(results, 'expert', split_axis=0, concat_axis=0, tiled=True)  23.6 us
    all_to_all x1, waiting for transfers between devices, on_device(): lax.all_to_all(send, 'expert', split_axis=0, concat_axis=0, tiled=True)  18.6 us
    all_to_all x2, starting transfers between devices, along_expert(): lax.all_to_all(copies, 'expert', split_axis=0, concat_axis=0, axis_index_...  12.9 us
    all_to_all x1, starting transfers between devices, on_device(): lax.all_to_all(send, 'expert', split_axis=0, concat_axis=0, tiled=True)  11.8 us
    all_to_all x2, waiting for transfers between devices, along_expert(): lax.all_to_all(copies, 'expert', split_axis=0, concat_axis=0, axis_index_...  11 us
  transfers between devices with their start and end apart: 24, of which 12 were waited for; matrix products, arithmetic and copies ran while one was open for 2% of the time, Pallas kernels for 14%

profile of v9, /device:TPU:32, one launch (start us, length us, event | category | flops | bytes accessed | tf_op | source)
XLA Modules:
  0.0 191.2 jit_solution(18305125156295191399)
XLA Ops:
  0.6 3.3 %shard_map.103 = (bf16[512,1024]{1,0:T(8,128)(2,1)}, s32[2,128]{1,0:T(2,128)}) custom-call(bf16[128,1024]{1,0:T(8,128)(2,1)} %tokens_ref.3, s32[2,128]{1,0:T(2,128)} %bitcast.31), custom_call_target="tpu_custom_call" | custom-call | tf_op jit(solution)/shard_map/pallas_call | solution.py:140
  4.0 11.8 %all-to-all-start = ((bf16[64,8,1024]{2,1,0:T(8,128)(2,1)}), bf16[64,8,1024]{2,1,0:T(8,128)(2,1)S(1)}, u32[]{:S(2)}, u32[]{:S(2)}) async-start(bf16[64,8,1024]{2,1,0:T(8,128)(2,1)} %bitcast.30), calls=%async_computation | async-start | bytes 2097152 | tf_op jit(solution)/shard_map/all_to_all | solution.py:312
  15.8 0.1 fusion.13
  15.9 0.1 fusion.15.refs_0_
  16.0 1.5 collective-permute-start
  17.5 2.7 %collective-permute-start.1 = (bf16[4,1024]{1,0:T(4,128)(2,1)S(1)}, bf16[4,1024]{1,0:T(4,128)(2,1)S(1)}, u32[]{:S(2)}, u32[]{:S(2)}) collective-permute-start(bf16[4,1024]{1,0:T(4,128)(2,1)S(1)} %fusion.15.refs_0_), channel_id=1, source_target_pairs={{0,2},{1,3},{2,0},{3,1},{4,6},{5,7},{6,4},{7,5},{8,10},{9,11},{10,... | collective-permute-start | bytes 24584 | tf_op jit(solution)/shard_map/ppermute | solution.py:287
  20.2 1.4 collective-permute-start.2
  21.6 0.0 collective-permute-done.refs_1_
  21.6 1.0 collective-permute-done.1.refs_2_
  22.6 1.2 collective-permute-done.2.refs_3_
  23.9 1.1 shard_map.104
  25.0 18.6 %all-to-all-done = bf16[64,8,1024]{2,1,0:T(8,128)(2,1)S(1)} async-done(((bf16[64,8,1024]{2,1,0:T(8,128)(2,1)}), bf16[64,8,1024]{2,1,0:T(8,128)(2,1)S(1)}, u32[]{:S(2)}, u32[]{:S(2)}) %all-to-all-start) | async-done | bytes 1048608 | tf_op jit(solution)/shard_map/all_to_all | solution.py:312
  43.6 0.1 slice_bitcast_fusion
  43.7 1.6 collective-permute-start.3
  45.3 1.7 collective-permute-start.7
  47.0 1.5 collective-permute-start.4
  48.5 0.5 collective-permute-start.8
  49.0 6.5 %all-to-all-start.2 = ((bf16[32,16,1024]{2,1,0:T(8,128)(2,1)}), bf16[32,16,1024]{2,1,0:T(8,128)(2,1)S(1)}, u32[]{:S(2)}, u32[]{:S(2)}) async-start(bf16[32,16,1024]{2,1,0:T(8,128)(2,1)} %get-tuple-element.56), calls=%async_computation.2 | async-start | bytes 2097152 | tf_op jit(solution)/shard_map/all_to_all | solution.py:276
  55.5 6.3 %shard_map.105.own_ref = bf16[512,1024]{1,0:T(8,128)(2,1)} custom-call(bf16[512,1024]{1,0:T(8,128)(2,1)} %bitcast.27, bf16[1024,1024]{1,0:T(8,128)(2,1)} %bitcast.32, bf16[1024,1024]{1,0:T(8,128)(2,1)} %bitcast.36), custom_call_target="tpu_custom_call" | custom-call | flops 6442450944 | bytes 6291456 | tf_op jit(solution)/shard_map/pallas_call | solution.py:53
  61.8 8.4 %collective-permute-done.4.refs_1_ = bf16[256,1024]{1,0:T(8,128)(2,1)} collective-permute-done((bf16[256,1024]{1,0:T(8,128)(2,1)S(1)}, bf16[256,1024]{1,0:T(8,128)(2,1)}, u32[]{:S(2)}, u32[]{:S(2)}) %collective-permute-start.4) | collective-permute-done | bytes 524320 | tf_op jit(solution)/shard_map/ppermute | solution.py:287
  70.2 1.5 collective-permute-start.5
  71.6 1.7 collective-permute-start.6
  73.4 6.3 %shard_map.106 = (bf16[256,1024]{1,0:T(8,128)(2,1)}, bf16[256,1024]{1,0:T(8,128)(2,1)}) custom-call(bf16[256,1024]{1,0:T(8,128)(2,1)} %collective-permute-done.3.refs_0_, bf16[256,1024]{1,0:T(8,128)(2,1)} %collective-permute-done.4.refs_1_, bf16[1024,1024]{1,0:T(8,128)(2,1)} %bitcast.33, bf16[1024,1024]{1,0:T(8,128)(2,1)} %bitcast.37), custom_call_target="tpu_custom_call" | custom-call | flops 6442450944 | bytes 6291456 | tf_op jit(solution)/shard_map/pallas_call | solution.py:53
  79.7 1.7 collective-permute-start.11
  81.4 0.3 collective-permute-start.12
  81.7 6.2 %shard_map.107 = (bf16[256,1024]{1,0:T(8,128)(2,1)}, bf16[256,1024]{1,0:T(8,128)(2,1)}) custom-call(bf16[256,1024]{1,0:T(8,128)(2,1)} %collective-permute-done.7.refs_0_, bf16[256,1024]{1,0:T(8,128)(2,1)} %collective-permute-done.8.refs_1_, bf16[1024,1024]{1,0:T(8,128)(2,1)} %bitcast.34, bf16[1024,1024]{1,0:T(8,128)(2,1)} %bitcast.38), custom_call_target="tpu_custom_call" | custom-call | flops 6442450944 | bytes 6291456 | tf_op jit(solution)/shard_map/pallas_call | solution.py:53
  88.0 0.8 copy-done.11
  88.8 0.1 copy-done.12
  88.9 6.4 %shard_map.108 = (bf16[256,1024]{1,0:T(8,128)(2,1)}, bf16[256,1024]{1,0:T(8,128)(2,1)}) custom-call(bf16[256,1024]{1,0:T(8,128)(2,1)} %copy-done.11, bf16[256,1024]{1,0:T(8,128)(2,1)} %copy-done.12, bf16[1024,1024]{1,0:T(8,128)(2,1)} %bitcast.35, bf16[1024,1024]{1,0:T(8,128)(2,1)} %bitcast.39), custom_call_target="tpu_custom_call" | custom-call | flops 6442450944 | bytes 6291456 | tf_op jit(solution)/shard_map/pallas_call | solution.py:53
  95.3 0.3 collective-permute-start.9
  95.6 3.0 %collective-permute-start.10 = (bf16[256,1024]{1,0:T(8,128)(2,1)}, bf16[256,1024]{1,0:T(8,128)(2,1)S(1)}, u32[]{:S(2)}, u32[]{:S(2)}) collective-permute-start(bf16[256,1024]{1,0:T(8,128)(2,1)} %get-tuple-element.49), channel_id=1, source_target_pairs={{0,3},{1,0},{2,1},{3,2},{4,7},{5,4},{6,5},{7,6},{8,11},{9,8},{10,9... | collective-permute-start | bytes 1572872 | tf_op jit(solution)/shard_map/ppermute | solution.py:287
  98.6 9.8 %collective-permute-done.9 = bf16[256,1024]{1,0:T(8,128)(2,1)S(1)} collective-permute-done((bf16[256,1024]{1,0:T(8,128)(2,1)}, bf16[256,1024]{1,0:T(8,128)(2,1)S(1)}, u32[]{:S(2)}, u32[]{:S(2)}) %collective-permute-start.9) | collective-permute-done | bytes 524320 | tf_op jit(solution)/shard_map/ppermute | solution.py:287
  108.3 0.2 add_convert_fusion.1
  108.5 1.2 collective-permute-start.13
  109.7 0.2 add_convert_fusion
  109.9 2.2 %collective-permute-start.14 = (bf16[256,1024]{1,0:T(8,128)(2,1)S(1)}, bf16[256,1024]{1,0:T(8,128)(2,1)S(1)}, u32[]{:S(2)}, u32[]{:S(2)}) collective-permute-start(bf16[256,1024]{1,0:T(8,128)(2,1)S(1)} %add_convert_fusion), channel_id=1, source_target_pairs={{0,3},{1,0},{2,1},{3,2},{4,7},{5,4},{6,5},{7,6},{8,11},{9,8},{10,9... | collective-permute-start | bytes 1572872 | tf_op jit(solution)/shard_map/ppermute | solution.py:287
  112.1 8.4 %collective-permute-done.13.last_top = bf16[256,1024]{1,0:T(8,128)(2,1)S(1)} collective-permute-done((bf16[256,1024]{1,0:T(8,128)(2,1)S(1)}, bf16[256,1024]{1,0:T(8,128)(2,1)S(1)}, u32[]{:S(2)}, u32[]{:S(2)}) %collective-permute-start.13) | collective-permute-done | bytes 524320 | tf_op jit(solution)/shard_map/ppermute | solution.py:287
  120.6 1.3 shard_map.109
  121.8 8.8 %all-to-all-start.1 = ((bf16[64,8,1024]{2,1,0:T(8,128)(2,1)}), bf16[64,8,1024]{2,1,0:T(8,128)(2,1)S(1)}, u32[]{:S(2)}, u32[]{:S(2)}) async-start(bf16[64,8,1024]{2,1,0:T(8,128)(2,1)} %bitcast.7), calls=%async_computation.1 | async-start | bytes 2097152 | tf_op jit(solution)/shard_map/all_to_all | solution.py:353
  130.6 0.2 collective-permute-start.15
  130.9 0.0 copy-start.2
  130.9 0.0 copy-start.3
  130.9 0.0 copy-start.4
  130.9 0.0 copy-start.5
  130.9 2.5 %collective-permute-done.15 = bf16[512,1024]{1,0:T(8,128)(2,1)S(1)} collective-permute-done((bf16[512,1024]{1,0:T(8,128)(2,1)S(1)}, bf16[512,1024]{1,0:T(8,128)(2,1)S(1)}, u32[]{:S(2)}, u32[]{:S(2)}) %collective-permute-start.15) | collective-permute-done | bytes 1048608 | tf_op jit(solution)/shard_map/ppermute | solution.py:269
  133.4 1.5 pad_maximum_fusion
  134.9 23.6 %all-to-all-done.1 = bf16[64,8,1024]{2,1,0:T(8,128)(2,1)S(1)} async-done(((bf16[64,8,1024]{2,1,0:T(8,128)(2,1)}), bf16[64,8,1024]{2,1,0:T(8,128)(2,1)S(1)}, u32[]{:S(2)}, u32[]{:S(2)}) %all-to-all-start.1) | async-done | bytes 1048608 | tf_op jit(solution)/shard_map/all_to_all | solution.py:353
  158.5 2.4 %shard_map.110 = (f32[4,1024]{1,0:T(4,128)}, bf16[32,4,1024]{2,1,0:T(4,128)(2,1)}) custom-call(s32[1,4]{1,0:T(1,128)S(1)} %copy-done.5, bf16[512,1024]{1,0:T(8,128)(2,1)S(1)} %bitcast.24, bf16[128,1024]{1,0:T(8,128)(2,1)S(1)} %copy-done, s32[2,128]{1,0:T(2,128)S(1)} %copy-done.4, f32[2,128]{1,0:T(2,128)S(1)} %bitcast.26, f32[1,1024]{1,0:T(1,128)S(1)} %bitcast.25), custom_call_target="tpu_custom_call" | custom-call | tf_op jit(solution)/shard_map/pallas_call | solution.py:209
  161.0 6.4 %all-to-all-start.3 = ((bf16[32,4,1024]{2,1,0:T(4,128)(2,1)}), bf16[32,4,1024]{2,1,0:T(4,128)(2,1)S(1)}, u32[]{:S(2)}, u32[]{:S(2)}) async-start(bf16[32,4,1024]{2,1,0:T(4,128)(2,1)} %get-tuple-element.60), calls=%async_computation.3 | async-start | bytes 524288 | tf_op jit(solution)/shard_map/all_to_all | solution.py:276
  167.5 1.4 subtract_convert_fusion.1
  168.8 11.0 %all-to-all-done.3 = bf16[32,4,1024]{2,1,0:T(4,128)(2,1)S(1)} async-done(((bf16[32,4,1024]{2,1,0:T(4,128)(2,1)}), bf16[32,4,1024]{2,1,0:T(4,128)(2,1)S(1)}, u32[]{:S(2)}, u32[]{:S(2)}) %all-to-all-start.3) | async-done | bytes 262176 | tf_op jit(solution)/shard_map/all_to_all | solution.py:276
  179.8 0.1 reshape.52
  179.9 0.1 collective-permute-start.16
  180.0 0.4 fusion.19
  180.4 1.1 collective-permute-done.16
  181.5 0.3 subtract_convert_fusion
  181.8 0.2 fusion.23
  182.0 1.4 collective-permute-start.19
  183.5 3.3 %collective-permute-start.18 = (f32[4,1024]{1,0:T(4,128)S(1)}, f32[4,1024]{1,0:T(4,128)S(1)}, u32[]{:S(2)}, u32[]{:S(2)}) collective-permute-start(f32[4,1024]{1,0:T(4,128)S(1)} %get-tuple-element.71), channel_id=1, source_target_pairs={{0,2},{1,3},{2,0},{3,1},{4,6},{5,7},{6,4},{7,5},{8,10},{9,11},{10,... | collective-permute-start | bytes 49160 | tf_op jit(solution)/shard_map/ppermute | solution.py:287
  186.8 1.0 collective-permute-start.17
  187.8 0.6 fusion.18
  188.4 0.3 collective-permute-done.18
  188.7 1.8 collective-permute-done.17
  190.5 0.6 fusion.17
  (40 shorter events, 0.2 us)
Async XLA Ops:
  0.6 15.1 %copy-start.10 = (bf16[4,1024]{1,0:T(4,128)(2,1)S(1)}, bf16[4,1024]{1,0:T(4,128)(2,1)}, u32[]{:S(2)}) copy-start(bf16[4,1024]{1,0:T(4,128)(2,1)} %param.12) | copy-start | bytes 24580
  4.0 39.6 %all-to-all-start = ((bf16[64,8,1024]{2,1,0:T(8,128)(2,1)}), bf16[64,8,1024]{2,1,0:T(8,128)(2,1)S(1)}, u32[]{:S(2)}, u32[]{:S(2)}) async-start(bf16[64,8,1024]{2,1,0:T(8,128)(2,1)} %bitcast.30), calls=%async_computation | async-start | bytes 2097152 | tf_op jit(solution)/shard_map/all_to_all | solution.py:312
  16.0 5.7 %collective-permute-start = (bf16[4,1024]{1,0:T(4,128)(2,1)S(1)}, bf16[4,1024]{1,0:T(4,128)(2,1)S(1)}, u32[]{:S(2)}, u32[]{:S(2)}) collective-permute-start(bf16[4,1024]{1,0:T(4,128)(2,1)S(1)} %fusion.15.refs_0_), channel_id=1, source_target_pairs={{0,1},{1,2},{2,3},{3,0},{4,5},{5,6},{6,7},{7,4},{8,9},{9,10},{10,1... | collective-permute-start | bytes 24584 | tf_op jit(solution)/shard_map/ppermute | solution.py:287
  17.5 5.2 %collective-permute-start.1 = (bf16[4,1024]{1,0:T(4,128)(2,1)S(1)}, bf16[4,1024]{1,0:T(4,128)(2,1)S(1)}, u32[]{:S(2)}, u32[]{:S(2)}) collective-permute-start(bf16[4,1024]{1,0:T(4,128)(2,1)S(1)} %fusion.15.refs_0_), channel_id=1, source_target_pairs={{0,2},{1,3},{2,0},{3,1},{4,6},{5,7},{6,4},{7,5},{8,10},{9,11},{10,... | collective-permute-start | bytes 24584 | tf_op jit(solution)/shard_map/ppermute | solution.py:287
  20.2 3.7 %collective-permute-start.2 = (bf16[4,1024]{1,0:T(4,128)(2,1)S(1)}, bf16[4,1024]{1,0:T(4,128)(2,1)S(1)}, u32[]{:S(2)}, u32[]{:S(2)}) collective-permute-start(bf16[4,1024]{1,0:T(4,128)(2,1)S(1)} %fusion.15.refs_0_), channel_id=1, source_target_pairs={{0,3},{1,0},{2,1},{3,2},{4,7},{5,4},{6,5},{7,6},{8,11},{9,8},{10,9... | collective-permute-start | bytes 24584 | tf_op jit(solution)/shard_map/ppermute | solution.py:287
  43.6 5.4 %copy-start.6 = (bf16[64,8,1024]{2,1,0:T(8,128)(2,1)}, bf16[64,8,1024]{2,1,0:T(8,128)(2,1)S(1)}, u32[]{:S(2)}) copy-start(bf16[64,8,1024]{2,1,0:T(8,128)(2,1)S(1)} %all-to-all-done) | copy-start | bytes 3145732
  43.7 18.1 %collective-permute-start.3 = (bf16[256,1024]{1,0:T(8,128)(2,1)S(1)}, bf16[256,1024]{1,0:T(8,128)(2,1)}, u32[]{:S(2)}, u32[]{:S(2)}) collective-permute-start(bf16[256,1024]{1,0:T(8,128)(2,1)S(1)} %get-tuple-element.68), channel_id=1, source_target_pairs={{0,1},{1,2},{2,3},{3,0},{4,5},{5,6},{6,7},{7,4},{8,9},{9,10},{10,1... | collective-permute-start | bytes 1572872 | tf_op jit(solution)/shard_map/ppermute | solution.py:287
  45.3 36.2 %collective-permute-start.7 = (bf16[256,1024]{1,0:T(8,128)(2,1)S(1)}, bf16[256,1024]{1,0:T(8,128)(2,1)}, u32[]{:S(2)}, u32[]{:S(2)}) collective-permute-start(bf16[256,1024]{1,0:T(8,128)(2,1)S(1)} %get-tuple-element.68), channel_id=1, source_target_pairs={{0,3},{1,0},{2,1},{3,2},{4,7},{5,4},{6,5},{7,6},{8,11},{9,8},{10,9... | collective-permute-start | bytes 1572872 | tf_op jit(solution)/shard_map/ppermute | solution.py:287
  47.0 23.2 %collective-permute-start.4 = (bf16[256,1024]{1,0:T(8,128)(2,1)S(1)}, bf16[256,1024]{1,0:T(8,128)(2,1)}, u32[]{:S(2)}, u32[]{:S(2)}) collective-permute-start(bf16[256,1024]{1,0:T(8,128)(2,1)S(1)} %get-tuple-element.67), channel_id=1, source_target_pairs={{0,3},{1,0},{2,1},{3,2},{4,7},{5,4},{6,5},{7,6},{8,11},{9,8},{10,9... | collective-permute-start | bytes 1572872 | tf_op jit(solution)/shard_map/ppermute | solution.py:287
  48.5 33.2 %collective-permute-start.8 = (bf16[256,1024]{1,0:T(8,128)(2,1)S(1)}, bf16[256,1024]{1,0:T(8,128)(2,1)}, u32[]{:S(2)}, u32[]{:S(2)}) collective-permute-start(bf16[256,1024]{1,0:T(8,128)(2,1)S(1)} %get-tuple-element.67), channel_id=1, source_target_pairs={{0,1},{1,2},{2,3},{3,0},{4,5},{5,6},{6,7},{7,4},{8,9},{9,10},{10,1... | collective-permute-start | bytes 1572872 | tf_op jit(solution)/shard_map/ppermute | solution.py:287
  49.0 72.8 %all-to-all-start.2 = ((bf16[32,16,1024]{2,1,0:T(8,128)(2,1)}), bf16[32,16,1024]{2,1,0:T(8,128)(2,1)S(1)}, u32[]{:S(2)}, u32[]{:S(2)}) async-start(bf16[32,16,1024]{2,1,0:T(8,128)(2,1)} %get-tuple-element.56), calls=%async_computation.2 | async-start | bytes 2097152 | tf_op jit(solution)/shard_map/all_to_all | solution.py:276
  70.2 17.8 %collective-permute-start.5 = (bf16[256,1024]{1,0:T(8,128)(2,1)}, bf16[256,1024]{1,0:T(8,128)(2,1)S(1)}, u32[]{:S(2)}, u32[]{:S(2)}) collective-permute-start(bf16[256,1024]{1,0:T(8,128)(2,1)} %collective-permute-done.3.refs_0_), channel_id=1, source_target_pairs={{0,1},{1,2},{2,3},{3,0},{4,5},{5,6},{6,7},{7,4},{8,9},{9,10},{10,1... | collective-permute-start | bytes 1572872 | tf_op jit(solution)/shard_map/ppermute | solution.py:287
  71.6 16.3 %collective-permute-start.6 = (bf16[256,1024]{1,0:T(8,128)(2,1)}, bf16[256,1024]{1,0:T(8,128)(2,1)S(1)}, u32[]{:S(2)}, u32[]{:S(2)}) collective-permute-start(bf16[256,1024]{1,0:T(8,128)(2,1)} %collective-permute-done.4.refs_1_), channel_id=1, source_target_pairs={{0,3},{1,0},{2,1},{3,2},{4,7},{5,4},{6,5},{7,6},{8,11},{9,8},{10,9... | collective-permute-start | bytes 1572872 | tf_op jit(solution)/shard_map/ppermute | solution.py:287
  79.7 18.9 %collective-permute-start.11 = (bf16[256,1024]{1,0:T(8,128)(2,1)}, bf16[256,1024]{1,0:T(8,128)(2,1)S(1)}, u32[]{:S(2)}, u32[]{:S(2)}) collective-permute-start(bf16[256,1024]{1,0:T(8,128)(2,1)} %get-tuple-element.40), channel_id=1, source_target_pairs={{0,3},{1,0},{2,1},{3,2},{4,7},{5,4},{6,5},{7,6},{8,11},{9,8},{10,9... | collective-permute-start | bytes 1572872 | tf_op jit(solution)/shard_map/ppermute | solution.py:287
  81.4 17.2 %collective-permute-start.12 = (bf16[256,1024]{1,0:T(8,128)(2,1)}, bf16[256,1024]{1,0:T(8,128)(2,1)S(1)}, u32[]{:S(2)}, u32[]{:S(2)}) collective-permute-start(bf16[256,1024]{1,0:T(8,128)(2,1)} %get-tuple-element.41), channel_id=1, source_target_pairs={{0,1},{1,2},{2,3},{3,0},{4,5},{5,6},{6,7},{7,4},{8,9},{9,10},{10,1... | collective-permute-start | bytes 1572872 | tf_op jit(solution)/shard_map/ppermute | solution.py:287
  88.0 0.8 copy-start.11
  88.0 1.0 copy-start.12
  88.9 19.4 %copy-start.9 = (bf16[256,1024]{1,0:T(8,128)(2,1)S(1)}, bf16[256,1024]{1,0:T(8,128)(2,1)}, u32[]{:S(2)}) copy-start(bf16[256,1024]{1,0:T(8,128)(2,1)} %get-tuple-element.51) | copy-start | bytes 1572868
  88.9 20.8 %copy-start.8 = (bf16[256,1024]{1,0:T(8,128)(2,1)S(1)}, bf16[256,1024]{1,0:T(8,128)(2,1)}, u32[]{:S(2)}) copy-start(bf16[256,1024]{1,0:T(8,128)(2,1)} %get-tuple-element.54) | copy-start | bytes 1572868
  95.3 25.2 %copy-start.1 = (bf16[512,1024]{1,0:T(8,128)(2,1)S(1)}, bf16[512,1024]{1,0:T(8,128)(2,1)}, u32[]{:S(2)}) copy-start(bf16[512,1024]{1,0:T(8,128)(2,1)} %shard_map.105.own_ref) | copy-start | bytes 3145732
  95.3 13.0 %collective-permute-start.9 = (bf16[256,1024]{1,0:T(8,128)(2,1)}, bf16[256,1024]{1,0:T(8,128)(2,1)S(1)}, u32[]{:S(2)}, u32[]{:S(2)}) collective-permute-start(bf16[256,1024]{1,0:T(8,128)(2,1)} %get-tuple-element.48), channel_id=1, source_target_pairs={{0,1},{1,2},{2,3},{3,0},{4,5},{5,6},{6,7},{7,4},{8,9},{9,10},{10,1... | collective-permute-start | bytes 1572872 | tf_op jit(solution)/shard_map/ppermute | solution.py:287
  95.6 12.7 %collective-permute-start.10 = (bf16[256,1024]{1,0:T(8,128)(2,1)}, bf16[256,1024]{1,0:T(8,128)(2,1)S(1)}, u32[]{:S(2)}, u32[]{:S(2)}) collective-permute-start(bf16[256,1024]{1,0:T(8,128)(2,1)} %get-tuple-element.49), channel_id=1, source_target_pairs={{0,3},{1,0},{2,1},{3,2},{4,7},{5,4},{6,5},{7,6},{8,11},{9,8},{10,9... | collective-permute-start | bytes 1572872 | tf_op jit(solution)/shard_map/ppermute | solution.py:287
  108.5 12.0 %collective-permute-start.13 = (bf16[256,1024]{1,0:T(8,128)(2,1)S(1)}, bf16[256,1024]{1,0:T(8,128)(2,1)S(1)}, u32[]{:S(2)}, u32[]{:S(2)}) collective-permute-start(bf16[256,1024]{1,0:T(8,128)(2,1)S(1)} %add_convert_fusion.1), channel_id=1, source_target_pairs={{0,1},{1,2},{2,3},{3,0},{4,5},{5,6},{6,7},{7,4},{8,9},{9,10},{10,1... | collective-permute-start | bytes 1572872 | tf_op jit(solution)/shard_map/ppermute | solution.py:287
  109.9 10.6 %collective-permute-start.14 = (bf16[256,1024]{1,0:T(8,128)(2,1)S(1)}, bf16[256,1024]{1,0:T(8,128)(2,1)S(1)}, u32[]{:S(2)}, u32[]{:S(2)}) collective-permute-start(bf16[256,1024]{1,0:T(8,128)(2,1)S(1)} %add_convert_fusion), channel_id=1, source_target_pairs={{0,3},{1,0},{2,1},{3,2},{4,7},{5,4},{6,5},{7,6},{8,11},{9,8},{10,9... | collective-permute-start | bytes 1572872 | tf_op jit(solution)/shard_map/ppermute | solution.py:287
  121.8 9.0 %copy-start.7 = (bf16[32,16,1024]{2,1,0:T(8,128)(2,1)}, bf16[32,16,1024]{2,1,0:T(8,128)(2,1)S(1)}, u32[]{:S(2)}) copy-start(bf16[32,16,1024]{2,1,0:T(8,128)(2,1)S(1)} %all-to-all-done.2) | copy-start | bytes 3145732
  121.8 36.7 %all-to-all-start.1 = ((bf16[64,8,1024]{2,1,0:T(8,128)(2,1)}), bf16[64,8,1024]{2,1,0:T(8,128)(2,1)S(1)}, u32[]{:S(2)}, u32[]{:S(2)}) async-start(bf16[64,8,1024]{2,1,0:T(8,128)(2,1)} %bitcast.7), calls=%async_computation.1 | async-start | bytes 2097152 | tf_op jit(solution)/shard_map/all_to_all | solution.py:353
  130.6 2.7 %collective-permute-start.15 = (bf16[512,1024]{1,0:T(8,128)(2,1)S(1)}, bf16[512,1024]{1,0:T(8,128)(2,1)S(1)}, u32[]{:S(2)}, u32[]{:S(2)}) collective-permute-start(bf16[512,1024]{1,0:T(8,128)(2,1)S(1)} %bitcast.28), channel_id=1, source_target_pairs={{0,4},{4,0},{8,12},{12,8},{16,20},{20,16},{24,28},{28,24},{32,36},... | collective-permute-start | bytes 3145736 | tf_op jit(solution)/shard_map/ppermute | solution.py:269
  130.9 27.7 %copy-start = (bf16[128,1024]{1,0:T(8,128)(2,1)S(1)}, bf16[128,1024]{1,0:T(8,128)(2,1)}, u32[]{:S(2)}) copy-start(bf16[128,1024]{1,0:T(8,128)(2,1)} %tokens_ref.3) | copy-start | bytes 786436
  130.9 27.7 %copy-start.2 = (f32[1024]{0:T(1024)S(1)}, f32[1024]{0:T(1024)}, u32[]{:S(2)}) copy-start(f32[1024]{0:T(1024)} %param.13) | copy-start | bytes 12292
  130.9 27.6 %copy-start.3 = (f32[128,2]{0,1:T(2,128)S(1)}, f32[128,2]{0,1:T(2,128)}, u32[]{:S(2)}) copy-start(f32[128,2]{0,1:T(2,128)} %param.10) | copy-start | bytes 3076
  130.9 27.6 %copy-start.4 = (s32[2,128]{1,0:T(2,128)S(1)}, s32[2,128]{1,0:T(2,128)}, u32[]{:S(2)}) copy-start(s32[2,128]{1,0:T(2,128)} %get-tuple-element.58.place_ref) | copy-start | bytes 3076
  130.9 27.6 %copy-start.5 = (s32[1,4]{1,0:T(1,128)S(1)}, s32[1,4]{1,0:T(1,128)}, u32[]{:S(2)}) copy-start(s32[1,4]{1,0:T(1,128)} %lengths_ref.1) | copy-start | bytes 52
  161.0 18.8 %all-to-all-start.3 = ((bf16[32,4,1024]{2,1,0:T(4,128)(2,1)}), bf16[32,4,1024]{2,1,0:T(4,128)(2,1)S(1)}, u32[]{:S(2)}, u32[]{:S(2)}) async-start(bf16[32,4,1024]{2,1,0:T(4,128)(2,1)} %get-tuple-element.60), calls=%async_computation.3 | async-start | bytes 524288 | tf_op jit(solution)/shard_map/all_to_all | solution.py:276
  179.9 1.6 collective-permute-start.16
  182.0 6.4 %collective-permute-start.19 = (f32[4,1024]{1,0:T(4,128)S(1)}, f32[4,1024]{1,0:T(4,128)S(1)}, u32[]{:S(2)}, u32[]{:S(2)}) collective-permute-start(f32[4,1024]{1,0:T(4,128)S(1)} %get-tuple-element.70), channel_id=1, source_target_pairs={{0,1},{1,2},{2,3},{3,0},{4,5},{5,6},{6,7},{7,4},{8,9},{9,10},{10,1... | collective-permute-start | bytes 49160 | tf_op jit(solution)/shard_map/ppermute | solution.py:287
  183.5 5.2 %collective-permute-start.18 = (f32[4,1024]{1,0:T(4,128)S(1)}, f32[4,1024]{1,0:T(4,128)S(1)}, u32[]{:S(2)}, u32[]{:S(2)}) collective-permute-start(f32[4,1024]{1,0:T(4,128)S(1)} %get-tuple-element.71), channel_id=1, source_target_pairs={{0,2},{1,3},{2,0},{3,1},{4,6},{5,7},{6,4},{7,5},{8,10},{9,11},{10,... | collective-permute-start | bytes 49160 | tf_op jit(solution)/shard_map/ppermute | solution.py:287
  186.8 3.7 %collective-permute-start.17 = (f32[4,1024]{1,0:T(4,128)S(1)}, f32[4,1024]{1,0:T(4,128)S(1)}, u32[]{:S(2)}, u32[]{:S(2)}) collective-permute-start(f32[4,1024]{1,0:T(4,128)S(1)} %get-tuple-element.69), channel_id=1, source_target_pairs={{0,3},{1,0},{2,1},{3,2},{4,7},{5,4},{6,5},{7,6},{8,11},{9,8},{10,9... | collective-permute-start | bytes 49160 | tf_op jit(solution)/shard_map/ppermute | solution.py:287
